TPU v7x, 256 devices: a whole 4x4x8 slice. The times are simulated.
256 devices in a mesh: tm: 4 (over z_hi, core), height: 16 (over x, y), width: 4 (over z_lo).
Axes of the slice: x: 4, y: 4, z: 8 (z_hi: 2, z_lo: 4; z = z_hi * 4 + z_lo), core: 2. Of those that a mesh axis runs over, the one named last changes fastest.
Arguments:
- frames: bfloat16 [8, 64, 128, 384], P('tm', 'height', 'width'), may hold values from -6 to 6
- cache_in: bfloat16 [2, 64, 128, 384], P(None, 'height', 'width'), may hold values from -6 to 6
- kernel: bfloat16 [384, 3, 3, 3, 384], replicated, may hold values from -0.0625 to 0.0625
- conv_bias: float32 [384], replicated, may hold values from -3 to 3
- cotangent: bfloat16 [8, 64, 128, 384], P('tm', 'height', 'width'), may hold values from -6 to 6
Outputs:
- decoded: bfloat16 [8, 64, 128, 384], P('tm', 'height', 'width')
- frame_grad: bfloat16 [8, 64, 128, 384], P('tm', 'height', 'width')
- cache_grad: bfloat16 [8, 64, 128, 384], P('tm', 'height', 'width')
- kernel_grad: float32 [384, 3, 3, 3, 384], P('height')
All inputs are finite; a program needn't handle non-finite values.
Results may differ from a plain program's by a relative error of at most 0.0053.
Values may be sent and summed in bfloat16 or wider, within the bound.
No kernel may reach another device: no remote copies, remote signals or barrier semaphores. Data moves between devices by JAX's collectives and lax.ppermute only.
A program may use at most 256 MiB of HBM per device.

v0:
```python
import jax
import jax.numpy as jnp
from jax import lax
from jax.sharding import PartitionSpec as P


def shifted(value, axis, by):
    length = lax.axis_size(axis)
    pairs = [(i, i + by) for i in range(length) if 0 <= i + by < length]
    return lax.ppermute(value, axis, pairs)


def with_halo(value, sides, width):
    for axis, dim in sides:
        size, length = (lax.axis_size(axis), value.shape[dim])
        up = [(i, (i + 1) % size) for i in range(size - 1)]
        down = [(j, i) for i, j in up]
        last = lax.slice_in_dim(value, length - width, length, axis=dim)
        initial = lax.slice_in_dim(value, 0, width, axis=dim)
        before = lax.ppermute(last, axis, up)
        after = lax.ppermute(initial, axis, down)
        value = jnp.concatenate([before, value, after], axis=dim)
    return value


def tap_block(padded, tap_t, tap_h, tap_w, depth_count, row_count, col_count):
    block = padded[
        tap_t : tap_t + depth_count, tap_h : tap_h + row_count, tap_w : tap_w + col_count
    ]
    return block.reshape(-1, block.shape[-1])


def body(frames, cache_in, kernel, conv_bias, cotangent):
    frame_count, row_count, col_count, channels = frames.shape
    is_first = lax.axis_index("tm") == 0
    earlier = shifted(frames, "tm", 1)
    earlier = jnp.where(is_first, cache_in, earlier)
    stacked = jnp.concatenate([earlier, frames], 0)
    extended = with_halo(stacked, (("height", 1), ("width", 2)), 1)
    pre_act = jnp.zeros((frame_count * row_count * col_count, channels), jnp.float32) + conv_bias
    for tap_t in range(3):
        for tap_h in range(3):
            for tap_w in range(3):
                block = tap_block(extended, tap_t, tap_h, tap_w, frame_count, row_count, col_count)
                pre_act = pre_act + lax.dot_general(
                    block,
                    kernel[:, tap_t, tap_h, tap_w, :],
                    (((1,), (1,)), ((), ())),
                    preferred_element_type=jnp.float32,
                )
    sigma = jax.nn.sigmoid(pre_act)
    decoded = (pre_act * sigma).astype(jnp.bfloat16).reshape(frames.shape)
    scaled = (
        cotangent.reshape(-1, channels).astype(jnp.float32)
        * sigma
        * (1.0 + pre_act * (1.0 - sigma))
    ).astype(jnp.bfloat16)
    grad_rimmed = with_halo(scaled.reshape(frames.shape), (("height", 1), ("width", 2)), 1)
    partial_value = jnp.zeros((frame_count + 2, row_count, col_count, channels), jnp.float32)
    for tap_t in range(3):
        contrib = jnp.zeros((frame_count * row_count * col_count, channels), jnp.float32)
        for tap_h in range(3):
            for tap_w in range(3):
                block = grad_rimmed[
                    :, 2 - tap_h : 2 - tap_h + row_count, 2 - tap_w : 2 - tap_w + col_count
                ].reshape(-1, channels)
                contrib = contrib + jnp.dot(
                    block, kernel[:, tap_t, tap_h, tap_w, :], preferred_element_type=jnp.float32
                )
        partial_value = partial_value.at[tap_t : tap_t + frame_count].add(
            contrib.reshape(frame_count, row_count, col_count, channels)
        )
    cache_grad = partial_value[:2].astype(jnp.bfloat16)
    carried = shifted(cache_grad, "tm", -1)
    frame_grad = (
        partial_value[2:]
        .at[frame_count - 2 :]
        .add(carried.astype(jnp.float32))
        .astype(jnp.bfloat16)
    )
    pieces = []
    for tap_t in range(3):
        for tap_h in range(3):
            for tap_w in range(3):
                block = tap_block(extended, tap_t, tap_h, tap_w, frame_count, row_count, col_count)
                pieces.append(
                    lax.dot_general(
                        scaled, block, (((0,), (0,)), ((), ())), preferred_element_type=jnp.float32
                    )
                )
    owned = lax.psum_scatter(
        jnp.stack(pieces, 1).reshape(
            channels // lax.axis_size("height") * lax.axis_size("height"), 3, 3, 3, channels
        ),
        "height",
        scatter_dimension=0,
        tiled=True,
    )
    kernel_grad = lax.psum(owned, ("tm", "width"))
    return (decoded, frame_grad, cache_grad, kernel_grad)


def solution(mesh):
    in_specs = (
        P("tm", "height", "width", None),
        P(None, "height", "width", None),
        P(),
        P(),
        P("tm", "height", "width", None),
    )
    out_specs = (
        P("tm", "height", "width", None),
        P("tm", "height", "width", None),
        P("tm", "height", "width", None),
        P("height", None, None, None, None),
    )
    return jax.shard_map(body, mesh=mesh, in_specs=in_specs, out_specs=out_specs, check_vma=False)
```

profile of v0, /device:TPU:1, one launch (start us, length us, event | category | flops | bytes accessed | tf_op | source)
XLA Modules:
  0.0 323.4 jit_solution(16105572426888722058)
XLA Ops:
  7.2 10.2 %collective-permute-start = (bf16[2,4,32,384]{3,2,1,0:T(8,128)(2,1)}, bf16[2,4,32,384]{3,2,1,0:T(8,128)(2,1)S(1)}, u32[]{:S(2)}, u32[]{:S(2)}) collective-permute-start(bf16[2,4,32,384]{3,2,1,0:T(8,128)(2,1)} %param.15), channel_id=1, source_target_pairs={{0,64},{64,128},{128,192},{1,65},{65,129},{129,193},{2,66},{66,130... | collective-permute-start | bytes 589832 | tf_op jit(solution)/shard_map/ppermute | solution.py:10
  17.4 2.9 collective-permute-done
  20.4 0.9 pad_maximum_fusion.7
  21.2 3.2 collective-permute-start.1
  24.4 1.3 collective-permute-start.2
  25.7 0.9 pad_maximum_fusion.5
  26.7 3.1 collective-permute-done.2
  29.8 0.9 pad_maximum_fusion.11
  30.7 4.8 %collective-permute-start.3 = (bf16[4,6,1,384]{3,2,1,0:T(2,128)(2,1)S(1)}, bf16[4,6,1,384]{3,2,1,0:T(2,128)(2,1)S(1)}, u32[]{:S(2)}, u32[]{:S(2)}) collective-permute-start(bf16[4,6,1,384]{3,2,1,0:T(2,128)(2,1)S(1)} %get-tuple-element.80), channel_id=1, source_target_pairs={{0,1},{1,2},{2,3},{4,5},{5,6},{6,7},{8,9},{9,10},{10,11},{12,13},{... | collective-permute-start | bytes 55304 | tf_op jit(solution)/shard_map/ppermute | solution.py:20
  35.5 1.3 collective-permute-start.4
  36.8 1.1 pad_maximum_fusion.1
  38.1 2.1 collective-permute-done.4
  40.2 1.4 maximum_maximum_fusion
  41.6 0.5 fusion.150
  42.4 0.3 convolution_add_fusion.46
  46.2 0.3 convolution_add_fusion.33
  49.8 1.1 fusion.34
  50.9 1.1 fusion.26
  52.0 1.1 fusion.25
  53.1 1.1 fusion.24
  54.3 1.1 fusion.23
  55.4 1.1 fusion.22
  56.5 1.1 fusion.21
  57.6 1.1 fusion.20
  58.7 1.1 fusion.19
  59.8 1.1 fusion.18
  61.0 1.1 fusion.17
  62.1 1.1 fusion.16
  63.2 1.1 fusion.15
  64.3 1.1 fusion.14
  65.4 1.2 fusion.13
  66.6 1.2 fusion.12
  67.8 1.1 fusion.11
  68.9 1.1 fusion.10
  70.0 1.1 fusion.9
  71.1 1.1 fusion.8
  72.2 1.1 fusion.7
  73.3 1.1 fusion.6
  74.4 1.2 fusion.5
  75.6 1.1 fusion.4
  76.7 1.1 fusion.3
  77.8 1.1 fusion.2
  78.9 1.1 fusion.1
  80.0 1.1 fusion
  81.3 3.5 %collective-permute-start.5 = (bf16[2,1,32,384]{3,2,1,0:T(8,128)(2,1)S(1)}, bf16[2,1,32,384]{3,2,1,0:T(8,128)(2,1)S(1)}, u32[]{:S(2)}, u32[]{:S(2)}) collective-permute-start(bf16[2,1,32,384]{3,2,1,0:T(8,128)(2,1)S(1)} %get-tuple-element.106), channel_id=1, source_target_pairs={{0,4},{4,8},{8,12},{12,16},{16,20},{20,24},{24,28},{28,32},{32,36}... | collective-permute-start | bytes 147464 | tf_op jit(solution)/shard_map/ppermute | solution.py:20
  84.7 1.3 collective-permute-start.6
  86.1 3.5 %collective-permute-done.6 = bf16[2,1,32,384]{3,2,1,0:T(8,128)(2,1)S(1)} collective-permute-done((bf16[2,1,32,384]{3,2,1,0:T(8,128)(2,1)S(1)}, bf16[2,1,32,384]{3,2,1,0:T(8,128)(2,1)S(1)}, u32[]{:S(2)}, u32[]{:S(2)}) %collective-permute-start.6) | collective-permute-done | bytes 49184 | tf_op jit(solution)/shard_map/ppermute | solution.py:21
  89.6 1.3 collective-permute-start.7
  90.9 4.2 %collective-permute-start.8 = (bf16[2,6,1,384]{3,2,1,0:T(2,128)(2,1)S(1)}, bf16[2,6,1,384]{3,2,1,0:T(2,128)(2,1)S(1)}, u32[]{:S(2)}, u32[]{:S(2)}) collective-permute-start(bf16[2,6,1,384]{3,2,1,0:T(2,128)(2,1)S(1)} %get-tuple-element.103), channel_id=1, source_target_pairs={{0,1},{1,2},{2,3},{4,5},{5,6},{6,7},{8,9},{9,10},{10,11},{12,13},{... | collective-permute-start | bytes 27656 | tf_op jit(solution)/shard_map/ppermute | solution.py:20
  95.1 1.2 fusion.70
  96.4 1.2 fusion.91
  97.6 1.2 fusion.50
  99.2 1.5 fusion.75
  100.7 1.3 convolution_add_fusion.20
  102.0 1.2 convolution_add_fusion.19
  103.3 1.2 convolution_add_fusion.18
  104.5 1.2 convolution_add_fusion.17
  105.8 1.2 convolution_add_fusion.16
  110.0 1.9 collective-permute-start.9
  113.9 87.3 %reduce-scatter.2.cloned.1.call-done = f32[24,3,3,3,384]{4,0,3,2,1:T(8,128)} async-done(((f32[384,3,3,3,384]{4,0,3,2,1:T(8,128)}), f32[24,3,3,3,384]{4,0,3,2,1:T(8,128)}) %reduce-scatter.2.cloned.1.call-update) | async-done | bytes 995344 | tf_op jit(solution)/shard_map/reduce_scatter | solution.py:91
  201.2 1.2 fusion.30
  202.4 0.8 fusion.32
  203.2 111.2 %all-reduce.3.cloned.1.call-done = f32[24,3,3,3,384]{4,0,3,2,1:T(8,128)} async-done(((f32[24,3,3,3,384]{4,0,3,2,1:T(8,128)}), f32[24,3,3,3,384]{4,0,3,2,1:T(8,128)}) %all-reduce.3.cloned.1.call-update) | async-done | bytes 995344 | tf_op jit(solution)/shard_map/psum | solution.py:99
  314.3 2.2 copy.37
  (80 shorter events, 12.4 us)
Async XLA Ops:
  7.2 194.0 %reduce-scatter.2.cloned.1.call-start = ((), (), s32[]{:S(2)}) async-start(), calls=%async_computation.1 | async-start | bytes 16920576 | tf_op jit(solution)/shard_map/reduce_scatter | solution.py:91
  7.2 13.1 %collective-permute-start = (bf16[2,4,32,384]{3,2,1,0:T(8,128)(2,1)}, bf16[2,4,32,384]{3,2,1,0:T(8,128)(2,1)S(1)}, u32[]{:S(2)}, u32[]{:S(2)}) collective-permute-start(bf16[2,4,32,384]{3,2,1,0:T(8,128)(2,1)} %param.15), channel_id=1, source_target_pairs={{0,64},{64,128},{128,192},{1,65},{65,129},{129,193},{2,66},{66,130... | collective-permute-start | bytes 589832 | tf_op jit(solution)/shard_map/ppermute | solution.py:10
  17.4 24.6 %slice-start = ((s8[7962624]{0:T(1024)(128)(4,1)}), s8[4194304]{0:T(1024)(128)(4,1)S(1)}, s32[]{:S(2)}) async-start(s8[7962624]{0:T(1024)(128)(4,1)} %bitcast.401), calls=%async_computation.3 | async-start | bytes 8388608
  20.4 22.0 %copy-start.2 = (f32[384]{0:T(512)S(1)}, f32[384]{0:T(512)}, u32[]{:S(2)}) copy-start(f32[384]{0:T(512)} %param.18) | copy-start | bytes 4612
  21.2 5.4 %collective-permute-start.1 = (bf16[4,1,32,384]{3,2,1,0:T(8,128)(2,1)S(1)}, bf16[4,1,32,384]{3,2,1,0:T(8,128)(2,1)S(1)}, u32[]{:S(2)}, u32[]{:S(2)}) collective-permute-start(bf16[4,1,32,384]{3,2,1,0:T(8,128)(2,1)S(1)} %get-tuple-element.92), channel_id=1, source_target_pairs={{0,4},{4,8},{8,12},{12,16},{16,20},{20,24},{24,28},{28,32},{32,36}... | collective-permute-start | bytes 294920 | tf_op jit(solution)/shard_map/ppermute | solution.py:20
  24.4 5.4 %collective-permute-start.2 = (bf16[4,1,32,384]{3,2,1,0:T(8,128)(2,1)S(1)}, bf16[4,1,32,384]{3,2,1,0:T(8,128)(2,1)S(1)}, u32[]{:S(2)}, u32[]{:S(2)}) collective-permute-start(bf16[4,1,32,384]{3,2,1,0:T(8,128)(2,1)S(1)} %get-tuple-element.93), channel_id=1, source_target_pairs={{4,0},{8,4},{12,8},{16,12},{20,16},{24,20},{28,24},{32,28},{36,32}... | collective-permute-start | bytes 294920 | tf_op jit(solution)/shard_map/ppermute | solution.py:21
  30.7 7.4 %collective-permute-start.3 = (bf16[4,6,1,384]{3,2,1,0:T(2,128)(2,1)S(1)}, bf16[4,6,1,384]{3,2,1,0:T(2,128)(2,1)S(1)}, u32[]{:S(2)}, u32[]{:S(2)}) collective-permute-start(bf16[4,6,1,384]{3,2,1,0:T(2,128)(2,1)S(1)} %get-tuple-element.80), channel_id=1, source_target_pairs={{0,1},{1,2},{2,3},{4,5},{5,6},{6,7},{8,9},{9,10},{10,11},{12,13},{... | collective-permute-start | bytes 55304 | tf_op jit(solution)/shard_map/ppermute | solution.py:20
  35.5 4.7 %collective-permute-start.4 = (bf16[4,6,1,384]{3,2,1,0:T(2,128)(2,1)S(1)}, bf16[4,6,1,384]{3,2,1,0:T(2,128)(2,1)S(1)}, u32[]{:S(2)}, u32[]{:S(2)}) collective-permute-start(bf16[4,6,1,384]{3,2,1,0:T(2,128)(2,1)S(1)} %get-tuple-element.81), channel_id=1, source_target_pairs={{1,0},{2,1},{3,2},{5,4},{6,5},{7,6},{9,8},{10,9},{11,10},{13,12},{... | collective-permute-start | bytes 55304 | tf_op jit(solution)/shard_map/ppermute | solution.py:21
  38.1 4.0 %slice-start.1 = ((s8[7962624]{0:T(1024)(128)(4,1)}), s8[3768320]{0:T(1024)(128)(4,1)S(1)}, s32[]{:S(2)}) async-start(s8[7962624]{0:T(1024)(128)(4,1)} %bitcast.401), calls=%async_computation.4 | async-start | bytes 7536640
  45.0 3.6 %copy-start = (bf16[2,4,32,384]{3,2,1,0:T(8,128)(2,1)S(1)}, bf16[2,4,32,384]{3,2,1,0:T(8,128)(2,1)}, u32[]{:S(2)}) copy-start(bf16[2,4,32,384]{3,2,1,0:T(8,128)(2,1)} %param.15) | copy-start | bytes 589828
  46.2 3.6 %copy-start.3 = (bf16[2,4,32,384]{3,2,1,0:T(8,128)(2,1)S(1)}, bf16[2,4,32,384]{3,2,1,0:T(8,128)(2,1)}, u32[]{:S(2)}) copy-start(bf16[2,4,32,384]{3,2,1,0:T(8,128)(2,1)} %param.19) | copy-start | bytes 589828
  81.2 233.1 %all-reduce.3.cloned.1.call-start = ((), (), s32[]{:S(2)}) async-start(), calls=%async_computation.2 | async-start | bytes 1990656 | tf_op jit(solution)/shard_map/psum | solution.py:99
  81.2 25.8 %slice-start.2 = ((s8[7962624]{0:T(1024)(128)(4,1)}), s8[3768320]{0:T(1024)(128)(4,1)S(1)}, s32[]{:S(2)}) async-start(s8[7962624]{0:T(1024)(128)(4,1)} %bitcast.403), calls=%async_computation.5 | async-start | bytes 7536640
  81.3 4.8 %collective-permute-start.5 = (bf16[2,1,32,384]{3,2,1,0:T(8,128)(2,1)S(1)}, bf16[2,1,32,384]{3,2,1,0:T(8,128)(2,1)S(1)}, u32[]{:S(2)}, u32[]{:S(2)}) collective-permute-start(bf16[2,1,32,384]{3,2,1,0:T(8,128)(2,1)S(1)} %get-tuple-element.106), channel_id=1, source_target_pairs={{0,4},{4,8},{8,12},{12,16},{16,20},{20,24},{24,28},{28,32},{32,36}... | collective-permute-start | bytes 147464 | tf_op jit(solution)/shard_map/ppermute | solution.py:20
  84.7 4.8 %collective-permute-start.6 = (bf16[2,1,32,384]{3,2,1,0:T(8,128)(2,1)S(1)}, bf16[2,1,32,384]{3,2,1,0:T(8,128)(2,1)S(1)}, u32[]{:S(2)}, u32[]{:S(2)}) collective-permute-start(bf16[2,1,32,384]{3,2,1,0:T(8,128)(2,1)S(1)} %get-tuple-element.107), channel_id=1, source_target_pairs={{4,0},{8,4},{12,8},{16,12},{20,16},{24,20},{28,24},{32,28},{36,32}... | collective-permute-start | bytes 147464 | tf_op jit(solution)/shard_map/ppermute | solution.py:21
  89.6 9.2 %collective-permute-start.7 = (bf16[2,6,1,384]{3,2,1,0:T(2,128)(2,1)S(1)}, bf16[2,6,1,384]{3,2,1,0:T(2,128)(2,1)S(1)}, u32[]{:S(2)}, u32[]{:S(2)}) collective-permute-start(bf16[2,6,1,384]{3,2,1,0:T(2,128)(2,1)S(1)} %get-tuple-element.102), channel_id=1, source_target_pairs={{1,0},{2,1},{3,2},{5,4},{6,5},{7,6},{9,8},{10,9},{11,10},{13,12},{... | collective-permute-start | bytes 27656 | tf_op jit(solution)/shard_map/ppermute | solution.py:21
  90.9 7.9 %collective-permute-start.8 = (bf16[2,6,1,384]{3,2,1,0:T(2,128)(2,1)S(1)}, bf16[2,6,1,384]{3,2,1,0:T(2,128)(2,1)S(1)}, u32[]{:S(2)}, u32[]{:S(2)}) collective-permute-start(bf16[2,6,1,384]{3,2,1,0:T(2,128)(2,1)S(1)} %get-tuple-element.103), channel_id=1, source_target_pairs={{0,1},{1,2},{2,3},{4,5},{5,6},{6,7},{8,9},{9,10},{10,11},{12,13},{... | collective-permute-start | bytes 27656 | tf_op jit(solution)/shard_map/ppermute | solution.py:20
  99.1 7.9 %slice-start.3 = ((s8[7962624]{0:T(1024)(128)(4,1)}), s8[4194304]{0:T(1024)(128)(4,1)S(1)}, s32[]{:S(2)}) async-start(s8[7962624]{0:T(1024)(128)(4,1)} %bitcast.403), calls=%async_computation.6 | async-start | bytes 8388608
  110.0 206.6 %copy-start.1 = (bf16[2,4,32,384]{3,2,1,0:T(8,128)(2,1)}, bf16[2,4,32,384]{3,2,1,0:T(8,128)(2,1)S(1)}, u32[]{:S(2)}) copy-start(bf16[2,4,32,384]{3,2,1,0:T(8,128)(2,1)S(1)} %slice.745) | copy-start | bytes 589828
  110.0 92.4 %collective-permute-start.9 = (bf16[2,4,32,384]{3,2,1,0:T(8,128)(2,1)S(1)}, bf16[2,4,32,384]{3,2,1,0:T(8,128)(2,1)S(1)}, u32[]{:S(2)}, u32[]{:S(2)}) collective-permute-start(bf16[2,4,32,384]{3,2,1,0:T(8,128)(2,1)S(1)} %slice.745), channel_id=1, source_target_pairs={{64,0},{128,64},{192,128},{65,1},{129,65},{193,129},{66,2},{130,66... | collective-permute-start | bytes 589832 | tf_op jit(solution)/shard_map/ppermute | solution.py:10
Sparse Core Ops, SparseCore 0:
  81.3 119.7 reduce-scatter.1
  203.5 110.8 all-reduce.2
where the time goes:
time: 324 us; the launch traced here: 323 us
  waiting for transfers between devices  210 us (65%)
  matrix products  56 us (17%)
  starting transfers between devices  33 us (10%)
  between operations  14.8 us (5%)
  other arithmetic  6.37 us (2%)
    psum x1, waiting for transfers between devices, body(): kernel_grad = lax.psum(owned, ('tm', 'width'))  111 us
    reduce_scatter x1, waiting for transfers between devices, body(): lax.psum_scatter(jnp.stack(pieces, 1).reshape(channels // lax.axis_size('...  87.3 us
    dot_general x27, matrix products, body(): lax.dot_general(scaled, block, (((0,), (0,)), ((), ())), preferred_elemen...  30.3 us
    dot_general x27, matrix products, body(): jnp.dot(block, kernel[:, tap_t, tap_h, tap_w, :], preferred_element_type=...  17.2 us
    ppermute x4, starting transfers between devices, with_halo(): before = lax.ppermute(last, axis, up)  15.6 us
    ppermute x2, starting transfers between devices, shifted(): return lax.ppermute(value, axis, pairs)  12.1 us
    ppermute x4, waiting for transfers between devices, with_halo(): after = lax.ppermute(initial, axis, down)  8.73 us
    dot_general x27, matrix products, body(): lax.dot_general(block, kernel[:, tap_t, tap_h, tap_w, :], (((1,), (1,)),...  8.56 us
  transfers between devices with their start and end apart: 12, of which 6 were waited for; matrix products, arithmetic and copies ran while one was open for 6% of the time, Pallas kernels for 0%

commit v1 on v0

v1 whole, which is shorter than its diff:
```python
import jax
import jax.numpy as jnp
from jax import lax
from jax.experimental import pallas as pl
from jax.experimental.pallas import tpu as pltpu
from jax.sharding import Mesh, PartitionSpec as P

BF = jnp.bfloat16
F32 = jnp.float32
TM = ("zh", "co")
HEIGHT = ("x", "y")
RING = ("zh", "z")
STREAM_TAPS = (4, 3, 4, 3)
STREAM_START = (0, 4, 7, 11)
STREAM_ORDER = ((0, 3, 1, 2), (0, 1, 3, 2), (0, 3, 1, 2), (0, 1, 3, 2))
N_TAPS = 14


def shifted(value, axis, by):
    length = lax.axis_size(axis)
    pairs = [(i, i + by) for i in range(length) if 0 <= i + by < length]
    return lax.ppermute(value, axis, pairs)


def exchanged(value, axis, flip):
    return lax.ppermute(value, axis, [(i, i ^ flip) for i in range(lax.axis_size(axis))])


def with_halo(value, sides, width):
    for axis, dim in sides:
        size, length = (lax.axis_size(axis), value.shape[dim])
        up = [(i, (i + 1) % size) for i in range(size - 1)]
        down = [(j, i) for i, j in up]
        last = lax.slice_in_dim(value, length - width, length, axis=dim)
        initial = lax.slice_in_dim(value, 0, width, axis=dim)
        before = lax.ppermute(last, axis, up)
        after = lax.ppermute(initial, axis, down)
        value = jnp.concatenate([before, value, after], axis=dim)
    return value


def tap_block(padded, tap_t, tap_h, tap_w, depth_count, row_count, col_count):
    block = padded[
        tap_t : tap_t + depth_count, tap_h : tap_h + row_count, tap_w : tap_w + col_count
    ]
    return block.reshape(-1, block.shape[-1])


def selectors(channels):
    at_x, at_y = lax.axis_index("x"), lax.axis_index("y")
    row = lax.broadcasted_iota(jnp.int32, (channels, channels), 0)
    col = lax.broadcasted_iota(jnp.int32, (channels, channels), 1)
    outer, inner, rest = row // 96, (row // 24) % 4, row % 24
    out = []
    for stream, order in enumerate(STREAM_ORDER):
        def rel(v):
            return jnp.where(
                v == 0, order[0], jnp.where(v == 1, order[1], jnp.where(v == 2, order[2], order[3]))
            )

        if stream < 2:
            dest_x, dest_y = at_x ^ rel(outer), at_y ^ rel(inner)
        else:
            dest_y, dest_x = at_y ^ rel(outer), at_x ^ rel(inner)
        out.append((dest_x * 96 + dest_y * 24 + rest == col).astype(BF))
    return jnp.stack(out)


def weight_grad_kernel(core_ref, ext_ref, more_ref, own_ref, peer_ref, sel_ref, *rest):
    outs, (cols, lhs) = rest[:8], rest[8:]
    step = pl.program_id(0)
    core = core_ref[0]

    @pl.when(step == 0)
    def _():
        for c in range(3):
            for f in range(4):
                cols[c, f + core] = ext_ref[f, :, c : c + 32, :]
            cols[c, 4 * (1 - core)] = more_ref[:, c : c + 32, :]
        for s in range(4):
            for half, ref in enumerate((own_ref, peer_ref)):
                lhs[s, half] = lax.dot_general(
                    sel_ref[s], ref[...], (((1,), (1,)), ((), ())), preferred_element_type=F32
                ).astype(BF)

    k = step + 4 * core
    tap_t, tap_h, tap_w = k // 9, (k // 3) % 3, k % 3
    mine = cols[tap_w, pl.ds(tap_t + 2 * core, 2), pl.ds(tap_h, 4)].reshape(256, 384)
    theirs = cols[tap_w, pl.ds(tap_t + 2 * (1 - core), 2), pl.ds(tap_h, 4)].reshape(256, 384)
    for s in range(4):
        @pl.when((step >= STREAM_START[s]) & (step < STREAM_START[s] + STREAM_TAPS[s]))
        def _():
            total = jnp.dot(lhs[s, 0], mine, preferred_element_type=F32)
            total = total + jnp.dot(lhs[s, 1], theirs, preferred_element_type=F32)
            outs[2 * s][0] = total[:192].astype(BF)
            outs[2 * s + 1][0] = total[192:].astype(BF)


def weight_grad(core, ext, more, own, peer, sel):
    def whole(a):
        return pl.BlockSpec(a.shape, lambda j, *_: (0,) * a.ndim)

    def part(s):
        return pl.BlockSpec(
            (1, 192, 384),
            lambda j, *_: (jnp.clip(j - STREAM_START[s], 0, STREAM_TAPS[s] - 1), 0, 0),
        )

    shapes, specs = [], []
    for s in range(4):
        shapes += [jax.ShapeDtypeStruct((STREAM_TAPS[s], 192, 384), BF)] * 2
        specs += [part(s)] * 2
    return pl.pallas_call(
        weight_grad_kernel,
        out_shape=shapes,
        grid_spec=pltpu.PrefetchScalarGridSpec(
            num_scalar_prefetch=1,
            grid=(N_TAPS,),
            in_specs=[whole(a) for a in (ext, more, own, peer, sel)],
            out_specs=specs,
            scratch_shapes=[
                pltpu.VMEM((3, 5, 6, 32, 384), BF),
                pltpu.VMEM((4, 2, 384, 256), BF),
            ],
        ),
        compiler_params=pltpu.CompilerParams(vmem_limit_bytes=48 << 20),
        cost_estimate=pl.CostEstimate(
            flops=2 * N_TAPS * 384 * 384 * 512, bytes_accessed=8 << 20, transcendentals=0
        ),
    )(core, ext, more, own, peer, sel)


def halved(keep, sent, axes, flips):
    got = [exchanged(v, a, f) for v, a, f in zip(sent, axes, flips)]
    return [k.astype(F32) + g.astype(F32) for k, g in zip(keep, got)]


def reduced_over_xy(parts):
    keep, sent = list(parts[0::2]), list(parts[1::2])
    total = None
    for axes in (("x", "x", "y", "y"), ("y", "y", "x", "x")):
        for flips in ((1, 3, 1, 3), (3, 1, 3, 1)):
            if total is not None:
                half = [v.shape[1] // 2 for v in total]
                keep = [v[:, :h] for v, h in zip(total, half)]
                sent = [v[:, h:].astype(BF) for v, h in zip(total, half)]
            total = halved(keep, sent, axes, flips)
    return jnp.concatenate(total, 0)


def reduced_over_ring(mine):
    at = lax.axis_index(RING)
    chunks = mine.reshape(7, 2, 24, 384)
    total = lax.dynamic_index_in_dim(chunks, jnp.minimum(at, 6), 0, keepdims=False)
    for k in range(1, 8):
        out = lax.dynamic_index_in_dim(chunks, jnp.minimum((at + k) % 8, 6), 0, keepdims=False)
        pairs = [(i, (i + k) % 8) for i in range(8) if (i + k) % 8 < 7]
        total = total + lax.ppermute(out.astype(BF), RING, pairs).astype(F32)
    total = lax.optimization_barrier(total.astype(BF))
    parts = [total]
    for k in range(1, 8):
        pairs = [(i, (i + k) % 8) for i in range(7)]
        parts.append(lax.ppermute(total, RING, pairs))
    back = jnp.stack([parts[(-i) % 8] for i in range(8)])
    whole = lax.dynamic_slice_in_dim(jnp.concatenate([back, back]), (8 - at) % 8, 7, 0)
    return lax.optimization_barrier(whole.reshape(N_TAPS, 24, 384))


def body(frames, cache_in, kernel, conv_bias, cotangent):
    frame_count, row_count, col_count, channels = frames.shape
    core = lax.axis_index("co")
    is_first = lax.axis_index(TM) == 0
    weights = kernel.transpose(1, 2, 3, 0, 4)
    earlier = shifted(frames, TM, 1)
    earlier = jnp.where(is_first, cache_in, earlier)
    stacked = jnp.concatenate([earlier, frames], 0)
    extended = with_halo(stacked, ((HEIGHT, 1), ("z", 2)), 1)
    more = exchanged(jnp.where(core == 0, extended[1], extended[2]), "co", 1)
    pre_act = jnp.zeros((frame_count * row_count * col_count, channels), F32) + conv_bias
    for tap_t in range(3):
        for tap_h in range(3):
            for tap_w in range(3):
                block = tap_block(extended, tap_t, tap_h, tap_w, frame_count, row_count, col_count)
                pre_act = pre_act + lax.dot_general(
                    block,
                    weights[tap_t, tap_h, tap_w],
                    (((1,), (1,)), ((), ())),
                    preferred_element_type=F32,
                )
    sigma = jax.nn.sigmoid(pre_act)
    decoded = (pre_act * sigma).astype(BF).reshape(frames.shape)
    scaled = (
        cotangent.reshape(-1, channels).astype(F32) * sigma * (1.0 + pre_act * (1.0 - sigma))
    ).astype(BF)
    peer = exchanged(scaled, "co", 1)
    parts = weight_grad(core.reshape(1), extended, more, scaled, peer, selectors(channels))
    mine = reduced_over_ring(reduced_over_xy(parts))
    theirs = exchanged(mine, "co", 1)
    taps = jnp.where(
        core == 0,
        jnp.concatenate([mine, theirs[1:]], 0),
        jnp.concatenate([theirs, mine[1:]], 0),
    ).astype(F32)
    kernel_grad = taps.reshape(3, 3, 3, 24, channels).transpose(3, 0, 1, 2, 4)

    grad_rimmed = with_halo(scaled.reshape(frames.shape), ((HEIGHT, 1), ("z", 2)), 1)
    partial_value = jnp.zeros((frame_count + 2, row_count, col_count, channels), F32)
    for tap_t in range(3):
        contrib = jnp.zeros((frame_count * row_count * col_count, channels), F32)
        for tap_h in range(3):
            for tap_w in range(3):
                block = grad_rimmed[
                    :, 2 - tap_h : 2 - tap_h + row_count, 2 - tap_w : 2 - tap_w + col_count
                ].reshape(-1, channels)
                contrib = contrib + jnp.dot(
                    block, weights[tap_t, tap_h, tap_w], preferred_element_type=F32
                )
        partial_value = partial_value.at[tap_t : tap_t + frame_count].add(
            contrib.reshape(frame_count, row_count, col_count, channels)
        )
    cache_grad = partial_value[:2].astype(BF)
    carried = shifted(cache_grad, TM, -1)
    frame_grad = (
        partial_value[2:].at[frame_count - 2 :].add(carried.astype(F32)).astype(BF)
    )
    return (decoded, frame_grad, cache_grad, kernel_grad)


def solution(mesh):
    split = Mesh(mesh.devices.reshape(2, 2, 4, 4, 4), ("zh", "co", "x", "y", "z"))
    block = P(TM, HEIGHT, "z", None)
    return jax.shard_map(
        body,
        mesh=split,
        in_specs=(block, P(None, HEIGHT, "z", None), P(), P(), block),
        out_specs=(block, block, block, P(HEIGHT, None, None, None, None)),
        check_vma=False,
    )
```

time: 324 us -> 194 us (0.60)
  waiting for transfers between devices: 210 us -> 36.1 us
  starting transfers between devices: 33 us -> 118 us
  matrix products: 56 us -> 15.9 us
  between operations: 14.8 us -> 2.07 us
  Pallas kernels: 0 us -> 8.98 us
  other arithmetic: 6.37 us -> 10.5 us
    psum x1 -> x0, waiting for transfers between devices: 111 us -> none  [body(): kernel_grad = lax.psum(owned, ('tm', 'width'))]
    reduce_scatter x1 -> x0, waiting for transfers between devices: 87.3 us -> none  [body(): lax.psum_scatter(jnp.stack(pieces, 1).reshape(channels // lax.axis_size('...]
    ppermute x0 -> x33, starting transfers between devices: none -> 75.7 us  [the longest x7 29.7 us: reduced_over_ring(): total = total + lax.ppermute(out.astype(BF), RING, pairs).astype(F32)]
    dot_general x81 -> x54, matrix products: 56 us -> 15.9 us  [the longest x27 8.59 us: body(): lax.dot_general(block, weights[tap_t, tap_h, tap_w], (((1,), (1,)), ((),...]
    ppermute x0 -> x33, waiting for transfers between devices: none -> 28 us  [the longest x19 26.9 us: exchanged(): lax.ppermute(value, axis, [(i, i ^ flip) for i in range(lax.axis_size(axi...]
    ppermute x2, starting transfers between devices: 12.1 us -> 21.9 us  [shifted(): return lax.ppermute(value, axis, pairs)]
    pallas_call x0 -> x1, Pallas kernels: none -> 8.98 us  [weight_grad(): pl.pallas_call(weight_grad_kernel, out_shape=shapes, grid_spec=pltpu.Pref...]
  transfers between devices with their start and end apart: 12 -> 43, of which waited for: 6 -> 20; matrix products, arithmetic and copies ran while one was open for 6% -> 8% of each run, Pallas kernels for 0% -> 0%
where the time goes in v1:
time: 194 us; the launch traced here: 193 us
  starting transfers between devices  118 us (61%)
  waiting for transfers between devices  36.1 us (19%)
  matrix products  15.9 us (8%)
  other arithmetic  10.5 us (5%)
  Pallas kernels  8.98 us (5%)
  between operations  2.07 us (1%)
    ppermute x7, starting transfers between devices, reduced_over_ring(): total = total + lax.ppermute(out.astype(BF), RING, pairs).astype(F32)  29.7 us
    ppermute x19, waiting for transfers between devices, exchanged(): lax.ppermute(value, axis, [(i, i ^ flip) for i in range(lax.axis_size(axi...  26.9 us
    ppermute x7, starting transfers between devices, reduced_over_ring(): parts.append(lax.ppermute(total, RING, pairs))  26.7 us
    ppermute x2, starting transfers between devices, shifted(): return lax.ppermute(value, axis, pairs)  21.9 us
    ppermute x19, starting transfers between devices, exchanged(): lax.ppermute(value, axis, [(i, i ^ flip) for i in range(lax.axis_size(axi...  19.4 us
    ppermute x4, starting transfers between devices, with_halo(): before = lax.ppermute(last, axis, up)  15.5 us
    pallas_call x1, Pallas kernels, weight_grad(): pl.pallas_call(weight_grad_kernel, out_shape=shapes, grid_spec=pltpu.Pref...  8.98 us
    dot_general x27, matrix products, body(): lax.dot_general(block, weights[tap_t, tap_h, tap_w], (((1,), (1,)), ((),...  8.59 us
  transfers between devices with their start and end apart: 43, of which 20 were waited for; matrix products, arithmetic and copies ran while one was open for 8% of the time, Pallas kernels for 0%

profile of v1, /device:TPU:1, one launch (start us, length us, event | category | flops | bytes accessed | tf_op | source)
XLA Modules:
  0.0 193.1 jit_solution(1746937605286087952)
XLA Ops:
  0.6 10.3 %collective-permute-start = (bf16[2,4,32,384]{3,2,1,0:T(8,128)(2,1)}, bf16[2,4,32,384]{3,2,1,0:T(8,128)(2,1)S(1)}, u32[]{:S(2)}, u32[]{:S(2)}) collective-permute-start(bf16[2,4,32,384]{3,2,1,0:T(8,128)(2,1)} %param.15), channel_id=1, source_target_pairs={{0,64},{64,128},{128,192},{1,65},{65,129},{129,193},{2,66},{66,130... | collective-permute-start | bytes 589832 | tf_op jit(solution)/shard_map/ppermute | solution.py:22
  11.1 1.2 fusion.11
  12.3 1.3 add_convert_fusion.sel_ref
  13.9 1.0 pad_maximum_fusion.9
  14.9 3.2 %collective-permute-start.1 = (bf16[4,1,32,384]{3,2,1,0:T(8,128)(2,1)S(1)}, bf16[4,1,32,384]{3,2,1,0:T(8,128)(2,1)S(1)}, u32[]{:S(2)}, u32[]{:S(2)}) collective-permute-start(bf16[4,1,32,384]{3,2,1,0:T(8,128)(2,1)S(1)} %get-tuple-element.115), channel_id=1, source_target_pairs={{0,4},{4,8},{8,12},{12,16},{16,20},{20,24},{24,28},{28,32},{32,36}... | collective-permute-start | bytes 294920 | tf_op jit(solution)/shard_map/ppermute | solution.py:36
  18.2 1.3 collective-permute-start.2
  19.5 0.9 pad_maximum_fusion.7
  20.4 3.1 %collective-permute-done.2 = bf16[4,1,32,384]{3,2,1,0:T(8,128)(2,1)S(1)} collective-permute-done((bf16[4,1,32,384]{3,2,1,0:T(8,128)(2,1)S(1)}, bf16[4,1,32,384]{3,2,1,0:T(8,128)(2,1)S(1)}, u32[]{:S(2)}, u32[]{:S(2)}) %collective-permute-start.2) | collective-permute-done | bytes 98336 | tf_op jit(solution)/shard_map/ppermute | solution.py:37
  23.5 0.9 pad_maximum_fusion.13
  24.4 4.9 %collective-permute-start.3 = (bf16[4,6,1,384]{3,2,1,0:T(2,128)(2,1)S(1)}, bf16[4,6,1,384]{3,2,1,0:T(2,128)(2,1)S(1)}, u32[]{:S(2)}, u32[]{:S(2)}) collective-permute-start(bf16[4,6,1,384]{3,2,1,0:T(2,128)(2,1)S(1)} %get-tuple-element.96), channel_id=1, source_target_pairs={{0,1},{1,2},{2,3},{4,5},{5,6},{6,7},{8,9},{9,10},{10,11},{12,13},{... | collective-permute-start | bytes 55304 | tf_op jit(solution)/shard_map/ppermute | solution.py:36
  29.3 1.3 collective-permute-start.4
  30.6 1.1 pad_maximum_fusion.3
  31.9 2.1 %collective-permute-done.4 = bf16[4,6,1,384]{3,2,1,0:T(2,128)(2,1)S(1)} collective-permute-done((bf16[4,6,1,384]{3,2,1,0:T(2,128)(2,1)S(1)}, bf16[4,6,1,384]{3,2,1,0:T(2,128)(2,1)S(1)}, u32[]{:S(2)}, u32[]{:S(2)}) %collective-permute-start.4) | collective-permute-done | bytes 18464 | tf_op jit(solution)/shard_map/ppermute | solution.py:37
  34.0 0.4 maximum_maximum_fusion
  34.5 0.5 fusion.49
  42.7 1.1 fusion.18
  43.8 3.2 %collective-permute-start.5 = (bf16[2,1,32,384]{3,2,1,0:T(8,128)(2,1)S(1)}, bf16[2,1,32,384]{3,2,1,0:T(8,128)(2,1)S(1)}, u32[]{:S(2)}, u32[]{:S(2)}) collective-permute-start(bf16[2,1,32,384]{3,2,1,0:T(8,128)(2,1)S(1)} %get-tuple-element.129), channel_id=1, source_target_pairs={{0,4},{4,8},{8,12},{12,16},{16,20},{20,24},{24,28},{28,32},{32,36}... | collective-permute-start | bytes 147464 | tf_op jit(solution)/shard_map/ppermute | solution.py:36
  47.0 1.3 collective-permute-start.6
  48.3 0.4 pad_maximum_fusion.1.ext_ref
  48.7 0.9 collective-permute-start.10
  49.6 2.2 %collective-permute-done.6 = bf16[2,1,32,384]{3,2,1,0:T(8,128)(2,1)S(1)} collective-permute-done((bf16[2,1,32,384]{3,2,1,0:T(8,128)(2,1)S(1)}, bf16[2,1,32,384]{3,2,1,0:T(8,128)(2,1)S(1)}, u32[]{:S(2)}, u32[]{:S(2)}) %collective-permute-start.6) | collective-permute-done | bytes 49184 | tf_op jit(solution)/shard_map/ppermute | solution.py:37
  52.5 1.3 collective-permute-start.7
  53.8 4.2 %collective-permute-start.8 = (bf16[2,6,1,384]{3,2,1,0:T(2,128)(2,1)S(1)}, bf16[2,6,1,384]{3,2,1,0:T(2,128)(2,1)S(1)}, u32[]{:S(2)}, u32[]{:S(2)}) collective-permute-start(bf16[2,6,1,384]{3,2,1,0:T(2,128)(2,1)S(1)} %get-tuple-element.126), channel_id=1, source_target_pairs={{0,1},{1,2},{2,3},{4,5},{5,6},{6,7},{8,9},{9,10},{10,11},{12,13},{... | collective-permute-start | bytes 27656 | tf_op jit(solution)/shard_map/ppermute | solution.py:36
  58.2 0.4 collective-permute-done.8
  64.5 9.0 %shard_map.89 = (bf16[4,192,384]{2,1,0:T(8,128)(2,1)S(1)}, bf16[4,192,384]{2,1,0:T(8,128)(2,1)S(1)}, bf16[3,192,384]{2,1,0:T(8,128)(2,1)S(1)}, bf16[3,192,384]{2...) custom-call(s32[1]{0:T(128)} %bitcast.69.core_ref, ...), custom_call_target="tpu_custom_call" | custom-call | flops 2113929216 | bytes 8388608 | tf_op jit(solution)/shard_map/pallas_call | solution.py:113
  73.5 3.8 %collective-permute-start.16 = (bf16[3,192,384]{2,1,0:T(8,128)(2,1)S(1)}, bf16[3,192,384]{2,1,0:T(8,128)(2,1)S(1)}, u32[]{:S(2)}, u32[]{:S(2)}) collective-permute-start(bf16[3,192,384]{2,1,0:T(8,128)(2,1)S(1)} %get-tuple-element.71), channel_id=1, source_target_pairs={{0,48},{16,32},{32,16},{48,0},{1,49},{17,33},{33,17},{49,1},{2,50}... | collective-permute-start | bytes 1327112 | tf_op jit(solution)/shard_map/ppermute | solution.py:26
  77.7 3.4 %collective-permute-start.24 = (bf16[3,192,384]{2,1,0:T(8,128)(2,1)S(1)}, bf16[3,192,384]{2,1,0:T(8,128)(2,1)S(1)}, u32[]{:S(2)}, u32[]{:S(2)}) collective-permute-start(bf16[3,192,384]{2,1,0:T(8,128)(2,1)S(1)} %get-tuple-element.75), channel_id=1, source_target_pairs={{0,12},{4,8},{8,4},{12,0},{1,13},{5,9},{9,5},{13,1},{2,14},{6,10},... | collective-permute-start | bytes 1327112 | tf_op jit(solution)/shard_map/ppermute | solution.py:26
  81.5 4.0 %collective-permute-done.16 = bf16[3,192,384]{2,1,0:T(8,128)(2,1)S(1)} collective-permute-done((bf16[3,192,384]{2,1,0:T(8,128)(2,1)S(1)}, bf16[3,192,384]{2,1,0:T(8,128)(2,1)S(1)}, u32[]{:S(2)}, u32[]{:S(2)}) %collective-permute-start.16) | collective-permute-done | bytes 442400 | tf_op jit(solution)/shard_map/ppermute | solution.py:26
  85.7 2.5 %collective-permute-done.24 = bf16[3,192,384]{2,1,0:T(8,128)(2,1)S(1)} collective-permute-done((bf16[3,192,384]{2,1,0:T(8,128)(2,1)S(1)}, bf16[3,192,384]{2,1,0:T(8,128)(2,1)S(1)}, u32[]{:S(2)}, u32[]{:S(2)}) %collective-permute-start.24) | collective-permute-done | bytes 442400 | tf_op jit(solution)/shard_map/ppermute | solution.py:26
  88.5 1.4 collective-permute-done.12
  90.5 2.3 %collective-permute-done.20 = bf16[4,192,384]{2,1,0:T(8,128)(2,1)S(1)} collective-permute-done((bf16[4,192,384]{2,1,0:T(8,128)(2,1)S(1)}, bf16[4,192,384]{2,1,0:T(8,128)(2,1)S(1)}, u32[]{:S(2)}, u32[]{:S(2)}) %collective-permute-start.20) | collective-permute-done | bytes 589856 | tf_op jit(solution)/shard_map/ppermute | solution.py:26
  92.9 1.0 collective-permute-start.21
  93.9 0.7 collective-permute-done.17
  94.7 2.1 %collective-permute-start.18 = (bf16[3,48,384]{2,1,0:T(8,128)(2,1)S(1)}, bf16[3,48,384]{2,1,0:T(8,128)(2,1)S(1)}, u32[]{:S(2)}, u32[]{:S(2)}) collective-permute-start(bf16[3,48,384]{2,1,0:T(8,128)(2,1)S(1)} %slice.800), channel_id=1, source_target_pairs={{0,12},{4,8},{8,4},{12,0},{1,13},{5,9},{9,5},{13,1},{2,14},{6,10},... | collective-permute-start | bytes 331784 | tf_op jit(solution)/shard_map/ppermute | solution.py:26
  96.8 0.7 collective-permute-done.25
  97.6 1.2 collective-permute-start.26
  98.8 2.4 %collective-permute-done.18 = bf16[3,48,384]{2,1,0:T(8,128)(2,1)S(1)} collective-permute-done((bf16[3,48,384]{2,1,0:T(8,128)(2,1)S(1)}, bf16[3,48,384]{2,1,0:T(8,128)(2,1)S(1)}, u32[]{:S(2)}, u32[]{:S(2)}) %collective-permute-start.18) | collective-permute-done | bytes 110624 | tf_op jit(solution)/shard_map/ppermute | solution.py:26
  101.4 2.5 %collective-permute-done.26 = bf16[3,48,384]{2,1,0:T(8,128)(2,1)S(1)} collective-permute-done((bf16[3,48,384]{2,1,0:T(8,128)(2,1)S(1)}, bf16[3,48,384]{2,1,0:T(8,128)(2,1)S(1)}, u32[]{:S(2)}, u32[]{:S(2)}) %collective-permute-start.26) | collective-permute-done | bytes 110624 | tf_op jit(solution)/shard_map/ppermute | solution.py:26
  104.1 0.6 collective-permute-done.19
  104.7 2.7 %collective-permute-done.27 = bf16[3,24,384]{2,1,0:T(8,128)(2,1)S(1)} collective-permute-done((bf16[3,24,384]{2,1,0:T(8,128)(2,1)S(1)}, bf16[3,24,384]{2,1,0:T(8,128)(2,1)S(1)}, u32[]{:S(2)}, u32[]{:S(2)}) %collective-permute-start.27) | collective-permute-done | bytes 55328 | tf_op jit(solution)/shard_map/ppermute | solution.py:26
  108.1 3.5 %collective-permute-done.14 = bf16[4,48,384]{2,1,0:T(8,128)(2,1)S(1)} collective-permute-done((bf16[4,48,384]{2,1,0:T(8,128)(2,1)S(1)}, bf16[4,48,384]{2,1,0:T(8,128)(2,1)S(1)}, u32[]{:S(2)}, u32[]{:S(2)}) %collective-permute-start.14) | collective-permute-done | bytes 147488 | tf_op jit(solution)/shard_map/ppermute | solution.py:26
  111.6 0.9 collective-permute-start.15
  112.6 1.1 collective-permute-start.23
  113.7 2.5 %collective-permute-done.15 = bf16[4,24,384]{2,1,0:T(8,128)(2,1)S(1)} collective-permute-done((bf16[4,24,384]{2,1,0:T(8,128)(2,1)S(1)}, bf16[4,24,384]{2,1,0:T(8,128)(2,1)S(1)}, u32[]{:S(2)}, u32[]{:S(2)}) %collective-permute-start.15) | collective-permute-done | bytes 73760 | tf_op jit(solution)/shard_map/ppermute | solution.py:26
  116.1 1.0 collective-permute-done.23
  117.2 3.5 %collective-permute-start.28 = (bf16[2,24,384]{2,1,0:T(8,128)(2,1)S(1)}, bf16[2,24,384]{2,1,0:T(8,128)(2,1)S(1)}, u32[]{:S(2)}, u32[]{:S(2)}) collective-permute-start(bf16[2,24,384]{2,1,0:T(8,128)(2,1)S(1)} %get-tuple-element.98), channel_id=1, source_target_pairs={{0,1},{1,2},{2,3},{3,128},{128,129},{129,130},{131,0},{4,5},{5,6},... | collective-permute-start | bytes 110600 | tf_op jit(solution)/shard_map/ppermute | solution.py:158
  120.8 3.0 %collective-permute-start.29 = (bf16[2,24,384]{2,1,0:T(8,128)(2,1)S(1)}, bf16[2,24,384]{2,1,0:T(8,128)(2,1)S(1)}, u32[]{:S(2)}, u32[]{:S(2)}) collective-permute-start(bf16[2,24,384]{2,1,0:T(8,128)(2,1)S(1)} %get-tuple-element.104), channel_id=1, source_target_pairs={{0,2},{1,3},{2,128},{3,129},{128,130},{130,0},{131,1},{4,6},{5,7},... | collective-permute-start | bytes 110600 | tf_op jit(solution)/shard_map/ppermute | solution.py:158
  123.9 12.3 %collective-permute-start.30 = (bf16[2,24,384]{2,1,0:T(8,128)(2,1)S(1)}, bf16[2,24,384]{2,1,0:T(8,128)(2,1)S(1)}, u32[]{:S(2)}, u32[]{:S(2)}) collective-permute-start(bf16[2,24,384]{2,1,0:T(8,128)(2,1)S(1)} %get-tuple-element.103), channel_id=1, source_target_pairs={{0,3},{1,128},{2,129},{3,130},{129,0},{130,1},{131,2},{4,7},{5,132... | collective-permute-start | bytes 110600 | tf_op jit(solution)/shard_map/ppermute | solution.py:158
  136.2 1.9 collective-permute-start.31
  138.2 5.6 %collective-permute-start.32 = (bf16[2,24,384]{2,1,0:T(8,128)(2,1)S(1)}, bf16[2,24,384]{2,1,0:T(8,128)(2,1)S(1)}, u32[]{:S(2)}, u32[]{:S(2)}) collective-permute-start(bf16[2,24,384]{2,1,0:T(8,128)(2,1)S(1)} %get-tuple-element.101), channel_id=1, source_target_pairs={{0,129},{1,130},{3,0},{128,1},{129,2},{130,3},{131,128},{4,133},{5... | collective-permute-start | bytes 110600 | tf_op jit(solution)/shard_map/ppermute | solution.py:158
  143.8 1.9 collective-permute-start.33
  145.8 1.3 collective-permute-start.34
  147.4 11.5 %collective-permute-start.9 = (bf16[2,4,32,384]{3,2,1,0:T(8,128)(2,1)S(1)}, bf16[2,4,32,384]{3,2,1,0:T(8,128)(2,1)S(1)}, u32[]{:S(2)}, u32[]{:S(2)}) collective-permute-start(bf16[2,4,32,384]{3,2,1,0:T(8,128)(2,1)S(1)} %slice.796), channel_id=1, source_target_pairs={{64,0},{128,64},{192,128},{65,1},{129,65},{193,129},{66,2},{130,66... | collective-permute-start | bytes 589832 | tf_op jit(solution)/shard_map/ppermute | solution.py:22
  159.0 5.8 %collective-permute-start.35 = (bf16[2,24,384]{2,1,0:T(8,128)(2,1)S(1)}, bf16[2,24,384]{2,1,0:T(8,128)(2,1)S(1)}, u32[]{:S(2)}, u32[]{:S(2)}) collective-permute-start(bf16[2,24,384]{2,1,0:T(8,128)(2,1)S(1)} %fusion.33), channel_id=1, source_target_pairs={{0,131},{1,0},{2,1},{3,2},{128,3},{129,128},{130,129},{4,135},{5,4... | collective-permute-start | bytes 110600 | tf_op jit(solution)/shard_map/ppermute | solution.py:163
  164.8 2.3 %collective-permute-start.36 = (bf16[2,24,384]{2,1,0:T(8,128)(2,1)S(1)}, bf16[2,24,384]{2,1,0:T(8,128)(2,1)S(1)}, u32[]{:S(2)}, u32[]{:S(2)}) collective-permute-start(bf16[2,24,384]{2,1,0:T(8,128)(2,1)S(1)} %fusion.33), channel_id=1, source_target_pairs={{0,130},{1,131},{2,0},{3,1},{128,2},{129,3},{130,128},{4,134},{5,1... | collective-permute-start | bytes 110600 | tf_op jit(solution)/shard_map/ppermute | solution.py:163
  167.1 4.8 %collective-permute-start.37 = (bf16[2,24,384]{2,1,0:T(8,128)(2,1)S(1)}, bf16[2,24,384]{2,1,0:T(8,128)(2,1)S(1)}, u32[]{:S(2)}, u32[]{:S(2)}) collective-permute-start(bf16[2,24,384]{2,1,0:T(8,128)(2,1)S(1)} %fusion.33), channel_id=1, source_target_pairs={{0,129},{1,130},{2,131},{3,0},{128,1},{129,2},{130,3},{4,133},{5,1... | collective-permute-start | bytes 110600 | tf_op jit(solution)/shard_map/ppermute | solution.py:163
  171.9 3.4 %collective-permute-start.38 = (bf16[2,24,384]{2,1,0:T(8,128)(2,1)S(1)}, bf16[2,24,384]{2,1,0:T(8,128)(2,1)S(1)}, u32[]{:S(2)}, u32[]{:S(2)}) collective-permute-start(bf16[2,24,384]{2,1,0:T(8,128)(2,1)S(1)} %fusion.33), channel_id=1, source_target_pairs={{0,128},{1,129},{2,130},{3,131},{128,0},{129,1},{130,2},{4,132},{5... | collective-permute-start | bytes 110600 | tf_op jit(solution)/shard_map/ppermute | solution.py:163
  175.3 1.9 collective-permute-start.39
  177.3 7.2 %collective-permute-start.40 = (bf16[2,24,384]{2,1,0:T(8,128)(2,1)S(1)}, bf16[2,24,384]{2,1,0:T(8,128)(2,1)S(1)}, u32[]{:S(2)}, u32[]{:S(2)}) collective-permute-start(bf16[2,24,384]{2,1,0:T(8,128)(2,1)S(1)} %fusion.33), channel_id=1, source_target_pairs={{0,2},{1,3},{2,128},{3,129},{128,130},{129,131},{130,0},{4,6},{5,7... | collective-permute-start | bytes 110600 | tf_op jit(solution)/shard_map/ppermute | solution.py:163
  184.5 1.3 collective-permute-start.41
  185.9 1.0 collective-permute-done.40
  187.2 3.6 %collective-permute-start.42 = (bf16[14,24,384]{2,1,0:T(8,128)(2,1)S(1)}, bf16[14,24,384]{2,1,0:T(8,128)(2,1)S(1)}, u32[]{:S(2)}, u32[]{:S(2)}) collective-permute-start(bf16[14,24,384]{2,1,0:T(8,128)(2,1)S(1)} %bitcast.357), channel_id=1, source_target_pairs={{0,64},{64,0},{1,65},{65,1},{2,66},{66,2},{3,67},{67,3},{4,68},{68... | collective-permute-start | bytes 774152 | tf_op jit(solution)/shard_map/ppermute | solution.py:26
  191.1 0.8 fusion.16
  192.1 1.0 convert_bitcast_fusion
  (169 shorter events, 19.1 us)
Async XLA Ops:
  0.6 33.4 %copy-start = (bf16[2,4,32,384]{3,2,1,0:T(8,128)(2,1)S(1)}, bf16[2,4,32,384]{3,2,1,0:T(8,128)(2,1)}, u32[]{:S(2)}) copy-start(bf16[2,4,32,384]{3,2,1,0:T(8,128)(2,1)} %param.15) | copy-start | bytes 589828
  0.6 13.2 %collective-permute-start = (bf16[2,4,32,384]{3,2,1,0:T(8,128)(2,1)}, bf16[2,4,32,384]{3,2,1,0:T(8,128)(2,1)S(1)}, u32[]{:S(2)}, u32[]{:S(2)}) collective-permute-start(bf16[2,4,32,384]{3,2,1,0:T(8,128)(2,1)} %param.15), channel_id=1, source_target_pairs={{0,64},{64,128},{128,192},{1,65},{65,129},{129,193},{2,66},{66,130... | collective-permute-start | bytes 589832 | tf_op jit(solution)/shard_map/ppermute | solution.py:22
  13.6 21.3 %slice-start = ((s8[7962624]{0:T(1024)(128)(4,1)}), s8[4194304]{0:T(1024)(128)(4,1)S(1)}, s32[]{:S(2)}) async-start(s8[7962624]{0:T(1024)(128)(4,1)} %bitcast.275), calls=%async_computation | async-start | bytes 8388608
  13.9 21.3 %copy-start.2 = (f32[384]{0:T(512)S(1)}, f32[384]{0:T(512)}, u32[]{:S(2)}) copy-start(f32[384]{0:T(512)} %param.18) | copy-start | bytes 4612
  14.9 5.4 %collective-permute-start.1 = (bf16[4,1,32,384]{3,2,1,0:T(8,128)(2,1)S(1)}, bf16[4,1,32,384]{3,2,1,0:T(8,128)(2,1)S(1)}, u32[]{:S(2)}, u32[]{:S(2)}) collective-permute-start(bf16[4,1,32,384]{3,2,1,0:T(8,128)(2,1)S(1)} %get-tuple-element.115), channel_id=1, source_target_pairs={{0,4},{4,8},{8,12},{12,16},{16,20},{20,24},{24,28},{28,32},{32,36}... | collective-permute-start | bytes 294920 | tf_op jit(solution)/shard_map/ppermute | solution.py:36
  18.2 5.4 %collective-permute-start.2 = (bf16[4,1,32,384]{3,2,1,0:T(8,128)(2,1)S(1)}, bf16[4,1,32,384]{3,2,1,0:T(8,128)(2,1)S(1)}, u32[]{:S(2)}, u32[]{:S(2)}) collective-permute-start(bf16[4,1,32,384]{3,2,1,0:T(8,128)(2,1)S(1)} %get-tuple-element.116), channel_id=1, source_target_pairs={{4,0},{8,4},{12,8},{16,12},{20,16},{24,20},{28,24},{32,28},{36,32}... | collective-permute-start | bytes 294920 | tf_op jit(solution)/shard_map/ppermute | solution.py:37
  24.4 7.5 %collective-permute-start.3 = (bf16[4,6,1,384]{3,2,1,0:T(2,128)(2,1)S(1)}, bf16[4,6,1,384]{3,2,1,0:T(2,128)(2,1)S(1)}, u32[]{:S(2)}, u32[]{:S(2)}) collective-permute-start(bf16[4,6,1,384]{3,2,1,0:T(2,128)(2,1)S(1)} %get-tuple-element.96), channel_id=1, source_target_pairs={{0,1},{1,2},{2,3},{4,5},{5,6},{6,7},{8,9},{9,10},{10,11},{12,13},{... | collective-permute-start | bytes 55304 | tf_op jit(solution)/shard_map/ppermute | solution.py:36
  29.3 4.7 %collective-permute-start.4 = (bf16[4,6,1,384]{3,2,1,0:T(2,128)(2,1)S(1)}, bf16[4,6,1,384]{3,2,1,0:T(2,128)(2,1)S(1)}, u32[]{:S(2)}, u32[]{:S(2)}) collective-permute-start(bf16[4,6,1,384]{3,2,1,0:T(2,128)(2,1)S(1)} %get-tuple-element.97), channel_id=1, source_target_pairs={{1,0},{2,1},{3,2},{5,4},{6,5},{7,6},{9,8},{10,9},{11,10},{13,12},{... | collective-permute-start | bytes 55304 | tf_op jit(solution)/shard_map/ppermute | solution.py:37
  31.9 3.0 %slice-start.1 = ((s8[7962624]{0:T(1024)(128)(4,1)}), s8[3768320]{0:T(1024)(128)(4,1)S(1)}, s32[]{:S(2)}) async-start(s8[7962624]{0:T(1024)(128)(4,1)} %bitcast.275), calls=%async_computation.1 | async-start | bytes 7536640
  39.1 3.6 %copy-start.3 = (bf16[2,4,32,384]{3,2,1,0:T(8,128)(2,1)S(1)}, bf16[2,4,32,384]{3,2,1,0:T(8,128)(2,1)}, u32[]{:S(2)}) copy-start(bf16[2,4,32,384]{3,2,1,0:T(8,128)(2,1)} %param.19) | copy-start | bytes 589828
  43.8 20.7 %collective-permute-start.11 = (bf16[256,384]{1,0:T(8,128)(2,1)S(1)}, bf16[256,384]{1,0:T(8,128)(2,1)S(1)}, u32[]{:S(2)}, u32[]{:S(2)}) collective-permute-start(bf16[256,384]{1,0:T(8,128)(2,1)S(1)} %get-tuple-element.111.own_ref), channel_id=1, source_target_pairs={{0,64},{64,0},{1,65},{65,1},{2,66},{66,2},{3,67},{67,3},{4,68},{68... | collective-permute-start | bytes 589832 | tf_op jit(solution)/shard_map/ppermute | solution.py:26
  43.8 5.8 %collective-permute-start.5 = (bf16[2,1,32,384]{3,2,1,0:T(8,128)(2,1)S(1)}, bf16[2,1,32,384]{3,2,1,0:T(8,128)(2,1)S(1)}, u32[]{:S(2)}, u32[]{:S(2)}) collective-permute-start(bf16[2,1,32,384]{3,2,1,0:T(8,128)(2,1)S(1)} %get-tuple-element.129), channel_id=1, source_target_pairs={{0,4},{4,8},{8,12},{12,16},{16,20},{20,24},{24,28},{28,32},{32,36}... | collective-permute-start | bytes 147464 | tf_op jit(solution)/shard_map/ppermute | solution.py:36
  47.0 4.8 %collective-permute-start.6 = (bf16[2,1,32,384]{3,2,1,0:T(8,128)(2,1)S(1)}, bf16[2,1,32,384]{3,2,1,0:T(8,128)(2,1)S(1)}, u32[]{:S(2)}, u32[]{:S(2)}) collective-permute-start(bf16[2,1,32,384]{3,2,1,0:T(8,128)(2,1)S(1)} %get-tuple-element.130), channel_id=1, source_target_pairs={{4,0},{8,4},{12,8},{16,12},{20,16},{24,20},{28,24},{32,28},{36,32}... | collective-permute-start | bytes 147464 | tf_op jit(solution)/shard_map/ppermute | solution.py:37
  48.7 15.8 %collective-permute-start.10 = (bf16[6,34,384]{2,1,0:T(8,128)(2,1)S(1)}, bf16[6,34,384]{2,1,0:T(8,128)(2,1)S(1)}, u32[]{:S(2)}, u32[]{:S(2)}) collective-permute-start(bf16[6,34,384]{2,1,0:T(8,128)(2,1)S(1)} %fusion.26), channel_id=1, source_target_pairs={{0,64},{64,0},{1,65},{65,1},{2,66},{66,2},{3,67},{67,3},{4,68},{68... | collective-permute-start | bytes 470024 | tf_op jit(solution)/shard_map/ppermute | solution.py:26
  52.5 5.8 %collective-permute-start.7 = (bf16[2,6,1,384]{3,2,1,0:T(2,128)(2,1)S(1)}, bf16[2,6,1,384]{3,2,1,0:T(2,128)(2,1)S(1)}, u32[]{:S(2)}, u32[]{:S(2)}) collective-permute-start(bf16[2,6,1,384]{3,2,1,0:T(2,128)(2,1)S(1)} %get-tuple-element.125), channel_id=1, source_target_pairs={{1,0},{2,1},{3,2},{5,4},{6,5},{7,6},{9,8},{10,9},{11,10},{13,12},{... | collective-permute-start | bytes 27656 | tf_op jit(solution)/shard_map/ppermute | solution.py:37
  53.8 4.9 %collective-permute-start.8 = (bf16[2,6,1,384]{3,2,1,0:T(2,128)(2,1)S(1)}, bf16[2,6,1,384]{3,2,1,0:T(2,128)(2,1)S(1)}, u32[]{:S(2)}, u32[]{:S(2)}) collective-permute-start(bf16[2,6,1,384]{3,2,1,0:T(2,128)(2,1)S(1)} %get-tuple-element.126), channel_id=1, source_target_pairs={{0,1},{1,2},{2,3},{4,5},{5,6},{6,7},{8,9},{9,10},{10,11},{12,13},{... | collective-permute-start | bytes 27656 | tf_op jit(solution)/shard_map/ppermute | solution.py:36
  73.5 12.0 %collective-permute-start.16 = (bf16[3,192,384]{2,1,0:T(8,128)(2,1)S(1)}, bf16[3,192,384]{2,1,0:T(8,128)(2,1)S(1)}, u32[]{:S(2)}, u32[]{:S(2)}) collective-permute-start(bf16[3,192,384]{2,1,0:T(8,128)(2,1)S(1)} %get-tuple-element.71), channel_id=1, source_target_pairs={{0,48},{16,32},{32,16},{48,0},{1,49},{17,33},{33,17},{49,1},{2,50}... | collective-permute-start | bytes 1327112 | tf_op jit(solution)/shard_map/ppermute | solution.py:26
  77.6 12.4 %collective-permute-start.12 = (bf16[4,192,384]{2,1,0:T(8,128)(2,1)S(1)}, bf16[4,192,384]{2,1,0:T(8,128)(2,1)S(1)}, u32[]{:S(2)}, u32[]{:S(2)}) collective-permute-start(bf16[4,192,384]{2,1,0:T(8,128)(2,1)S(1)} %get-tuple-element.69), channel_id=1, source_target_pairs={{0,16},{16,0},{32,48},{48,32},{1,17},{17,1},{33,49},{49,33},{2,18}... | collective-permute-start | bytes 1769480 | tf_op jit(solution)/shard_map/ppermute | solution.py:26
  77.7 10.6 %collective-permute-start.24 = (bf16[3,192,384]{2,1,0:T(8,128)(2,1)S(1)}, bf16[3,192,384]{2,1,0:T(8,128)(2,1)S(1)}, u32[]{:S(2)}, u32[]{:S(2)}) collective-permute-start(bf16[3,192,384]{2,1,0:T(8,128)(2,1)S(1)} %get-tuple-element.75), channel_id=1, source_target_pairs={{0,12},{4,8},{8,4},{12,0},{1,13},{5,9},{9,5},{13,1},{2,14},{6,10},... | collective-permute-start | bytes 1327112 | tf_op jit(solution)/shard_map/ppermute | solution.py:26
  81.4 11.3 %collective-permute-start.20 = (bf16[4,192,384]{2,1,0:T(8,128)(2,1)S(1)}, bf16[4,192,384]{2,1,0:T(8,128)(2,1)S(1)}, u32[]{:S(2)}, u32[]{:S(2)}) collective-permute-start(bf16[4,192,384]{2,1,0:T(8,128)(2,1)S(1)} %get-tuple-element.73), channel_id=1, source_target_pairs={{0,4},{4,0},{8,12},{12,8},{1,5},{5,1},{9,13},{13,9},{2,6},{6,2},{1... | collective-permute-start | bytes 1769480 | tf_op jit(solution)/shard_map/ppermute | solution.py:26
  85.6 9.0 %collective-permute-start.17 = (bf16[3,96,384]{2,1,0:T(8,128)(2,1)S(1)}, bf16[3,96,384]{2,1,0:T(8,128)(2,1)S(1)}, u32[]{:S(2)}, u32[]{:S(2)}) collective-permute-start(bf16[3,96,384]{2,1,0:T(8,128)(2,1)S(1)} %slice.795), channel_id=1, source_target_pairs={{0,16},{16,0},{32,48},{48,32},{1,17},{17,1},{33,49},{49,33},{2,18}... | collective-permute-start | bytes 663560 | tf_op jit(solution)/shard_map/ppermute | solution.py:26
  88.4 9.1 %collective-permute-start.25 = (bf16[3,96,384]{2,1,0:T(8,128)(2,1)S(1)}, bf16[3,96,384]{2,1,0:T(8,128)(2,1)S(1)}, u32[]{:S(2)}, u32[]{:S(2)}) collective-permute-start(bf16[3,96,384]{2,1,0:T(8,128)(2,1)S(1)} %slice.794), channel_id=1, source_target_pairs={{0,4},{4,0},{8,12},{12,8},{1,5},{5,1},{9,13},{13,9},{2,6},{6,2},{1... | collective-permute-start | bytes 663560 | tf_op jit(solution)/shard_map/ppermute | solution.py:26
  90.1 17.3 %collective-permute-start.13 = (bf16[4,96,384]{2,1,0:T(8,128)(2,1)S(1)}, bf16[4,96,384]{2,1,0:T(8,128)(2,1)S(1)}, u32[]{:S(2)}, u32[]{:S(2)}) collective-permute-start(bf16[4,96,384]{2,1,0:T(8,128)(2,1)S(1)} %slice.793), channel_id=1, source_target_pairs={{0,48},{16,32},{32,16},{48,0},{1,49},{17,33},{33,17},{49,1},{2,50}... | collective-permute-start | bytes 884744 | tf_op jit(solution)/shard_map/ppermute | solution.py:26
  92.9 15.0 %collective-permute-start.21 = (bf16[4,96,384]{2,1,0:T(8,128)(2,1)S(1)}, bf16[4,96,384]{2,1,0:T(8,128)(2,1)S(1)}, u32[]{:S(2)}, u32[]{:S(2)}) collective-permute-start(bf16[4,96,384]{2,1,0:T(8,128)(2,1)S(1)} %slice.792), channel_id=1, source_target_pairs={{0,12},{4,8},{8,4},{12,0},{1,13},{5,9},{9,5},{13,1},{2,14},{6,10},... | collective-permute-start | bytes 884744 | tf_op jit(solution)/shard_map/ppermute | solution.py:26
  94.7 6.5 %collective-permute-start.18 = (bf16[3,48,384]{2,1,0:T(8,128)(2,1)S(1)}, bf16[3,48,384]{2,1,0:T(8,128)(2,1)S(1)}, u32[]{:S(2)}, u32[]{:S(2)}) collective-permute-start(bf16[3,48,384]{2,1,0:T(8,128)(2,1)S(1)} %slice.800), channel_id=1, source_target_pairs={{0,12},{4,8},{8,4},{12,0},{1,13},{5,9},{9,5},{13,1},{2,14},{6,10},... | collective-permute-start | bytes 331784 | tf_op jit(solution)/shard_map/ppermute | solution.py:26
  97.6 6.4 %collective-permute-start.26 = (bf16[3,48,384]{2,1,0:T(8,128)(2,1)S(1)}, bf16[3,48,384]{2,1,0:T(8,128)(2,1)S(1)}, u32[]{:S(2)}, u32[]{:S(2)}) collective-permute-start(bf16[3,48,384]{2,1,0:T(8,128)(2,1)S(1)} %slice.799), channel_id=1, source_target_pairs={{0,48},{16,32},{32,16},{48,0},{1,49},{17,33},{33,17},{49,1},{2,50}... | collective-permute-start | bytes 331784 | tf_op jit(solution)/shard_map/ppermute | solution.py:26
  101.3 3.4 %collective-permute-start.19 = (bf16[3,24,384]{2,1,0:T(8,128)(2,1)S(1)}, bf16[3,24,384]{2,1,0:T(8,128)(2,1)S(1)}, u32[]{:S(2)}, u32[]{:S(2)}) collective-permute-start(bf16[3,24,384]{2,1,0:T(8,128)(2,1)S(1)} %slice.804), channel_id=1, source_target_pairs={{0,4},{4,0},{8,12},{12,8},{1,5},{5,1},{9,13},{13,9},{2,6},{6,2},{1... | collective-permute-start | bytes 165896 | tf_op jit(solution)/shard_map/ppermute | solution.py:26
  104.0 3.4 %collective-permute-start.27 = (bf16[3,24,384]{2,1,0:T(8,128)(2,1)S(1)}, bf16[3,24,384]{2,1,0:T(8,128)(2,1)S(1)}, u32[]{:S(2)}, u32[]{:S(2)}) collective-permute-start(bf16[3,24,384]{2,1,0:T(8,128)(2,1)S(1)} %slice.803), channel_id=1, source_target_pairs={{0,16},{16,0},{32,48},{48,32},{1,17},{17,1},{33,49},{49,33},{2,18}... | collective-permute-start | bytes 165896 | tf_op jit(solution)/shard_map/ppermute | solution.py:26
  107.5 4.1 %collective-permute-start.14 = (bf16[4,48,384]{2,1,0:T(8,128)(2,1)S(1)}, bf16[4,48,384]{2,1,0:T(8,128)(2,1)S(1)}, u32[]{:S(2)}, u32[]{:S(2)}) collective-permute-start(bf16[4,48,384]{2,1,0:T(8,128)(2,1)S(1)} %slice.798), channel_id=1, source_target_pairs={{0,4},{4,0},{8,12},{12,8},{1,5},{5,1},{9,13},{13,9},{2,6},{6,2},{1... | collective-permute-start | bytes 442376 | tf_op jit(solution)/shard_map/ppermute | solution.py:26
  108.0 4.6 %collective-permute-start.22 = (bf16[4,48,384]{2,1,0:T(8,128)(2,1)S(1)}, bf16[4,48,384]{2,1,0:T(8,128)(2,1)S(1)}, u32[]{:S(2)}, u32[]{:S(2)}) collective-permute-start(bf16[4,48,384]{2,1,0:T(8,128)(2,1)S(1)} %slice.797), channel_id=1, source_target_pairs={{0,16},{16,0},{32,48},{48,32},{1,17},{17,1},{33,49},{49,33},{2,18}... | collective-permute-start | bytes 442376 | tf_op jit(solution)/shard_map/ppermute | solution.py:26
  111.6 4.5 %collective-permute-start.15 = (bf16[4,24,384]{2,1,0:T(8,128)(2,1)S(1)}, bf16[4,24,384]{2,1,0:T(8,128)(2,1)S(1)}, u32[]{:S(2)}, u32[]{:S(2)}) collective-permute-start(bf16[4,24,384]{2,1,0:T(8,128)(2,1)S(1)} %slice.802), channel_id=1, source_target_pairs={{0,12},{4,8},{8,4},{12,0},{1,13},{5,9},{9,5},{13,1},{2,14},{6,10},... | collective-permute-start | bytes 221192 | tf_op jit(solution)/shard_map/ppermute | solution.py:26
  112.6 4.5 %collective-permute-start.23 = (bf16[4,24,384]{2,1,0:T(8,128)(2,1)S(1)}, bf16[4,24,384]{2,1,0:T(8,128)(2,1)S(1)}, u32[]{:S(2)}, u32[]{:S(2)}) collective-permute-start(bf16[4,24,384]{2,1,0:T(8,128)(2,1)S(1)} %slice.801), channel_id=1, source_target_pairs={{0,48},{16,32},{32,16},{48,0},{1,49},{17,33},{33,17},{49,1},{2,50}... | collective-permute-start | bytes 221192 | tf_op jit(solution)/shard_map/ppermute | solution.py:26
  117.2 26.6 %collective-permute-start.28 = (bf16[2,24,384]{2,1,0:T(8,128)(2,1)S(1)}, bf16[2,24,384]{2,1,0:T(8,128)(2,1)S(1)}, u32[]{:S(2)}, u32[]{:S(2)}) collective-permute-start(bf16[2,24,384]{2,1,0:T(8,128)(2,1)S(1)} %get-tuple-element.98), channel_id=1, source_target_pairs={{0,1},{1,2},{2,3},{3,128},{128,129},{129,130},{131,0},{4,5},{5,6},... | collective-permute-start | bytes 110600 | tf_op jit(solution)/shard_map/ppermute | solution.py:158
  120.8 25.0 %collective-permute-start.29 = (bf16[2,24,384]{2,1,0:T(8,128)(2,1)S(1)}, bf16[2,24,384]{2,1,0:T(8,128)(2,1)S(1)}, u32[]{:S(2)}, u32[]{:S(2)}) collective-permute-start(bf16[2,24,384]{2,1,0:T(8,128)(2,1)S(1)} %get-tuple-element.104), channel_id=1, source_target_pairs={{0,2},{1,3},{2,128},{3,129},{128,130},{130,0},{131,1},{4,6},{5,7},... | collective-permute-start | bytes 110600 | tf_op jit(solution)/shard_map/ppermute | solution.py:158
  123.9 23.5 %collective-permute-start.30 = (bf16[2,24,384]{2,1,0:T(8,128)(2,1)S(1)}, bf16[2,24,384]{2,1,0:T(8,128)(2,1)S(1)}, u32[]{:S(2)}, u32[]{:S(2)}) collective-permute-start(bf16[2,24,384]{2,1,0:T(8,128)(2,1)S(1)} %get-tuple-element.103), channel_id=1, source_target_pairs={{0,3},{1,128},{2,129},{3,130},{129,0},{130,1},{131,2},{4,7},{5,132... | collective-permute-start | bytes 110600 | tf_op jit(solution)/shard_map/ppermute | solution.py:158
  136.2 22.7 %collective-permute-start.31 = (bf16[2,24,384]{2,1,0:T(8,128)(2,1)S(1)}, bf16[2,24,384]{2,1,0:T(8,128)(2,1)S(1)}, u32[]{:S(2)}, u32[]{:S(2)}) collective-permute-start(bf16[2,24,384]{2,1,0:T(8,128)(2,1)S(1)} %get-tuple-element.102), channel_id=1, source_target_pairs={{0,128},{1,129},{2,130},{128,0},{129,1},{130,2},{131,3},{4,132},{5... | collective-permute-start | bytes 110600 | tf_op jit(solution)/shard_map/ppermute | solution.py:158
  138.2 20.8 %collective-permute-start.32 = (bf16[2,24,384]{2,1,0:T(8,128)(2,1)S(1)}, bf16[2,24,384]{2,1,0:T(8,128)(2,1)S(1)}, u32[]{:S(2)}, u32[]{:S(2)}) collective-permute-start(bf16[2,24,384]{2,1,0:T(8,128)(2,1)S(1)} %get-tuple-element.101), channel_id=1, source_target_pairs={{0,129},{1,130},{3,0},{128,1},{129,2},{130,3},{131,128},{4,133},{5... | collective-permute-start | bytes 110600 | tf_op jit(solution)/shard_map/ppermute | solution.py:158
  143.8 15.1 %collective-permute-start.33 = (bf16[2,24,384]{2,1,0:T(8,128)(2,1)S(1)}, bf16[2,24,384]{2,1,0:T(8,128)(2,1)S(1)}, u32[]{:S(2)}, u32[]{:S(2)}) collective-permute-start(bf16[2,24,384]{2,1,0:T(8,128)(2,1)S(1)} %get-tuple-element.100), channel_id=1, source_target_pairs={{0,130},{2,0},{3,1},{128,2},{129,3},{130,128},{131,129},{4,134},{6... | collective-permute-start | bytes 110600 | tf_op jit(solution)/shard_map/ppermute | solution.py:158
  145.8 13.2 %collective-permute-start.34 = (bf16[2,24,384]{2,1,0:T(8,128)(2,1)S(1)}, bf16[2,24,384]{2,1,0:T(8,128)(2,1)S(1)}, u32[]{:S(2)}, u32[]{:S(2)}) collective-permute-start(bf16[2,24,384]{2,1,0:T(8,128)(2,1)S(1)} %get-tuple-element.99), channel_id=1, source_target_pairs={{1,0},{2,1},{3,2},{128,3},{129,128},{130,129},{131,130},{5,4},{6,5... | collective-permute-start | bytes 110600 | tf_op jit(solution)/shard_map/ppermute | solution.py:158
  147.4 45.8 %copy-start.1 = (bf16[2,4,32,384]{3,2,1,0:T(8,128)(2,1)}, bf16[2,4,32,384]{3,2,1,0:T(8,128)(2,1)S(1)}, u32[]{:S(2)}) copy-start(bf16[2,4,32,384]{3,2,1,0:T(8,128)(2,1)S(1)} %slice.796) | copy-start | bytes 589828
  147.4 43.7 %collective-permute-start.9 = (bf16[2,4,32,384]{3,2,1,0:T(8,128)(2,1)S(1)}, bf16[2,4,32,384]{3,2,1,0:T(8,128)(2,1)S(1)}, u32[]{:S(2)}, u32[]{:S(2)}) collective-permute-start(bf16[2,4,32,384]{3,2,1,0:T(8,128)(2,1)S(1)} %slice.796), channel_id=1, source_target_pairs={{64,0},{128,64},{192,128},{65,1},{129,65},{193,129},{66,2},{130,66... | collective-permute-start | bytes 589832 | tf_op jit(solution)/shard_map/ppermute | solution.py:22
  159.0 16.3 %collective-permute-start.35 = (bf16[2,24,384]{2,1,0:T(8,128)(2,1)S(1)}, bf16[2,24,384]{2,1,0:T(8,128)(2,1)S(1)}, u32[]{:S(2)}, u32[]{:S(2)}) collective-permute-start(bf16[2,24,384]{2,1,0:T(8,128)(2,1)S(1)} %fusion.33), channel_id=1, source_target_pairs={{0,131},{1,0},{2,1},{3,2},{128,3},{129,128},{130,129},{4,135},{5,4... | collective-permute-start | bytes 110600 | tf_op jit(solution)/shard_map/ppermute | solution.py:163
  164.8 12.5 %collective-permute-start.36 = (bf16[2,24,384]{2,1,0:T(8,128)(2,1)S(1)}, bf16[2,24,384]{2,1,0:T(8,128)(2,1)S(1)}, u32[]{:S(2)}, u32[]{:S(2)}) collective-permute-start(bf16[2,24,384]{2,1,0:T(8,128)(2,1)S(1)} %fusion.33), channel_id=1, source_target_pairs={{0,130},{1,131},{2,0},{3,1},{128,2},{129,3},{130,128},{4,134},{5,1... | collective-permute-start | bytes 110600 | tf_op jit(solution)/shard_map/ppermute | solution.py:163
  167.1 17.4 %collective-permute-start.37 = (bf16[2,24,384]{2,1,0:T(8,128)(2,1)S(1)}, bf16[2,24,384]{2,1,0:T(8,128)(2,1)S(1)}, u32[]{:S(2)}, u32[]{:S(2)}) collective-permute-start(bf16[2,24,384]{2,1,0:T(8,128)(2,1)S(1)} %fusion.33), channel_id=1, source_target_pairs={{0,129},{1,130},{2,131},{3,0},{128,1},{129,2},{130,3},{4,133},{5,1... | collective-permute-start | bytes 110600 | tf_op jit(solution)/shard_map/ppermute | solution.py:163
  171.9 14.0 %collective-permute-start.38 = (bf16[2,24,384]{2,1,0:T(8,128)(2,1)S(1)}, bf16[2,24,384]{2,1,0:T(8,128)(2,1)S(1)}, u32[]{:S(2)}, u32[]{:S(2)}) collective-permute-start(bf16[2,24,384]{2,1,0:T(8,128)(2,1)S(1)} %fusion.33), channel_id=1, source_target_pairs={{0,128},{1,129},{2,130},{3,131},{128,0},{129,1},{130,2},{4,132},{5... | collective-permute-start | bytes 110600 | tf_op jit(solution)/shard_map/ppermute | solution.py:163
  175.3 10.6 %collective-permute-start.39 = (bf16[2,24,384]{2,1,0:T(8,128)(2,1)S(1)}, bf16[2,24,384]{2,1,0:T(8,128)(2,1)S(1)}, u32[]{:S(2)}, u32[]{:S(2)}) collective-permute-start(bf16[2,24,384]{2,1,0:T(8,128)(2,1)S(1)} %fusion.33), channel_id=1, source_target_pairs={{0,3},{1,128},{2,129},{3,130},{128,131},{129,0},{130,1},{4,7},{5,1... | collective-permute-start | bytes 110600 | tf_op jit(solution)/shard_map/ppermute | solution.py:163
  177.3 9.7 %collective-permute-start.40 = (bf16[2,24,384]{2,1,0:T(8,128)(2,1)S(1)}, bf16[2,24,384]{2,1,0:T(8,128)(2,1)S(1)}, u32[]{:S(2)}, u32[]{:S(2)}) collective-permute-start(bf16[2,24,384]{2,1,0:T(8,128)(2,1)S(1)} %fusion.33), channel_id=1, source_target_pairs={{0,2},{1,3},{2,128},{3,129},{128,130},{129,131},{130,0},{4,6},{5,7... | collective-permute-start | bytes 110600 | tf_op jit(solution)/shard_map/ppermute | solution.py:163
  184.5 2.4 %collective-permute-start.41 = (bf16[2,24,384]{2,1,0:T(8,128)(2,1)S(1)}, bf16[2,24,384]{2,1,0:T(8,128)(2,1)S(1)}, u32[]{:S(2)}, u32[]{:S(2)}) collective-permute-start(bf16[2,24,384]{2,1,0:T(8,128)(2,1)S(1)} %fusion.33), channel_id=1, source_target_pairs={{0,1},{1,2},{2,3},{3,128},{128,129},{129,130},{130,131},{4,5},{5,6... | collective-permute-start | bytes 110600 | tf_op jit(solution)/shard_map/ppermute | solution.py:163
  187.2 4.8 %collective-permute-start.42 = (bf16[14,24,384]{2,1,0:T(8,128)(2,1)S(1)}, bf16[14,24,384]{2,1,0:T(8,128)(2,1)S(1)}, u32[]{:S(2)}, u32[]{:S(2)}) collective-permute-start(bf16[14,24,384]{2,1,0:T(8,128)(2,1)S(1)} %bitcast.357), channel_id=1, source_target_pairs={{0,64},{64,0},{1,65},{65,1},{2,66},{66,2},{3,67},{67,3},{4,68},{68... | collective-permute-start | bytes 774152 | tf_op jit(solution)/shard_map/ppermute | solution.py:26

commit v2 on v1

--- a/solution.py
+++ b/solution.py
@@ -149,21 +149,11 @@
 
 
 def reduced_over_ring(mine):
-    at = lax.axis_index(RING)
-    chunks = mine.reshape(7, 2, 24, 384)
-    total = lax.dynamic_index_in_dim(chunks, jnp.minimum(at, 6), 0, keepdims=False)
-    for k in range(1, 8):
-        out = lax.dynamic_index_in_dim(chunks, jnp.minimum((at + k) % 8, 6), 0, keepdims=False)
-        pairs = [(i, (i + k) % 8) for i in range(8) if (i + k) % 8 < 7]
-        total = total + lax.ppermute(out.astype(BF), RING, pairs).astype(F32)
-    total = lax.optimization_barrier(total.astype(BF))
-    parts = [total]
-    for k in range(1, 8):
-        pairs = [(i, (i + k) % 8) for i in range(7)]
-        parts.append(lax.ppermute(total, RING, pairs))
-    back = jnp.stack([parts[(-i) % 8] for i in range(8)])
-    whole = lax.dynamic_slice_in_dim(jnp.concatenate([back, back]), (8 - at) % 8, 7, 0)
-    return lax.optimization_barrier(whole.reshape(N_TAPS, 24, 384))
+    chunks = mine.astype(BF).reshape(8, 42, 384)
+    got = lax.all_to_all(chunks, RING, 0, 0, tiled=True)
+    total = jnp.sum(got.astype(F32), 0).astype(BF)
+    whole = lax.all_to_all(jnp.broadcast_to(total, chunks.shape), RING, 0, 0, tiled=True)
+    return whole.reshape(N_TAPS, 24, 384)
 
 
 def body(frames, cache_in, kernel, conv_bias, cotangent):
@@ -179,6 +169,8 @@
     pre_act = jnp.zeros((frame_count * row_count * col_count, channels), F32) + conv_bias
     for tap_t in range(3):
         for tap_h in range(3):
+            if tap_t * 3 + tap_h == 5:
+                pre_act, more = lax.optimization_barrier((pre_act, more))
             for tap_w in range(3):
                 block = tap_block(extended, tap_t, tap_h, tap_w, frame_count, row_count, col_count)
                 pre_act = pre_act + lax.dot_general(
@@ -194,6 +186,7 @@
     ).astype(BF)
     peer = exchanged(scaled, "co", 1)
     parts = weight_grad(core.reshape(1), extended, more, scaled, peer, selectors(channels))
+    scaled, *parts = lax.optimization_barrier((scaled, *parts))
     mine = reduced_over_ring(reduced_over_xy(parts))
     theirs = exchanged(mine, "co", 1)
     taps = jnp.where(

time: 194 us -> 169 us (0.87)
  starting transfers between devices: 118 us -> 79 us
  matrix products: 15.9 us -> 26.4 us
  local copies, waits for them, and re-layouts: 1.45 us -> 3.46 us
    ppermute x14 -> x0, starting transfers between devices: 56.3 us -> none  [the longest x7 29.7 us: reduced_over_ring(): total = total + lax.ppermute(out.astype(BF), RING, pairs).astype(F32)]
    all_to_all x0 -> x2, waiting for transfers between devices: none -> 14.3 us  [the longest x1 7.21 us: reduced_over_ring(): got = lax.all_to_all(chunks, RING, 0, 0, tiled=True)]
    all_to_all x0 -> x2, starting transfers between devices: none -> 12.8 us  [the longest x1 9.42 us: reduced_over_ring(): got = lax.all_to_all(chunks, RING, 0, 0, tiled=True)]
    ppermute x19, starting transfers between devices: 19.4 us -> 32.1 us  [exchanged(): lax.ppermute(value, axis, [(i, i ^ flip) for i in range(lax.axis_size(axi...]
    ppermute x19, waiting for transfers between devices: 26.9 us -> 15.6 us  [exchanged(): lax.ppermute(value, axis, [(i, i ^ flip) for i in range(lax.axis_size(axi...]
    dot_general x27, matrix products: 7.26 us -> 16.9 us  [body(): jnp.dot(block, weights[tap_t, tap_h, tap_w], preferred_element_type=F32)]
    ppermute x2, starting transfers between devices: 21.9 us -> 14 us  [shifted(): return lax.ppermute(value, axis, pairs)]
    ppermute x4, waiting for transfers between devices: 7.43 us -> 3.94 us  [with_halo(): after = lax.ppermute(initial, axis, down)]
  transfers between devices with their start and end apart: 43 -> 31, of which waited for: 20 -> 12; matrix products, arithmetic and copies ran while one was open for 8% -> 19% of each run, Pallas kernels for 0% -> 0%
where the time goes in v2:
time: 169 us; the launch traced here: 168 us
  starting transfers between devices  79 us (47%)
  waiting for transfers between devices  36.7 us (22%)
  matrix products  26.4 us (16%)
  other arithmetic  11.8 us (7%)
  Pallas kernels  9.11 us (5%)
  local copies, waits for them, and re-layouts  3.46 us (2%)
    ppermute x19, starting transfers between devices, exchanged(): lax.ppermute(value, axis, [(i, i ^ flip) for i in range(lax.axis_size(axi...  32.1 us
    dot_general x27, matrix products, body(): jnp.dot(block, weights[tap_t, tap_h, tap_w], preferred_element_type=F32)  16.9 us
    ppermute x19, waiting for transfers between devices, exchanged(): lax.ppermute(value, axis, [(i, i ^ flip) for i in range(lax.axis_size(axi...  15.6 us
    ppermute x4, starting transfers between devices, with_halo(): before = lax.ppermute(last, axis, up)  14.5 us
    ppermute x2, starting transfers between devices, shifted(): return lax.ppermute(value, axis, pairs)  14 us
    dot_general x27, matrix products, body(): lax.dot_general(block, weights[tap_t, tap_h, tap_w], (((1,), (1,)), ((),...  9.53 us
    all_to_all x1, starting transfers between devices, reduced_over_ring(): got = lax.all_to_all(chunks, RING, 0, 0, tiled=True)  9.42 us
    pallas_call x1, Pallas kernels, weight_grad(): pl.pallas_call(weight_grad_kernel, out_shape=shapes, grid_spec=pltpu.Pref...  9.11 us
  transfers between devices with their start and end apart: 31, of which 12 were waited for; matrix products, arithmetic and copies ran while one was open for 19% of the time, Pallas kernels for 0%

profile of v2, /device:TPU:1, one launch (start us, length us, event | category | flops | bytes accessed | tf_op | source)
XLA Modules:
  0.0 168.2 jit_solution(9658707938142268212)
XLA Ops:
  0.6 10.2 %collective-permute-start = (bf16[2,4,32,384]{3,2,1,0:T(8,128)(2,1)}, bf16[2,4,32,384]{3,2,1,0:T(8,128)(2,1)S(1)}, u32[]{:S(2)}, u32[]{:S(2)}) collective-permute-start(bf16[2,4,32,384]{3,2,1,0:T(8,128)(2,1)} %param.15), channel_id=1, source_target_pairs={{0,64},{64,128},{128,192},{1,65},{65,129},{129,193},{2,66},{66,130... | collective-permute-start | bytes 589832 | tf_op jit(solution)/shard_map/ppermute | solution.py:22
  10.9 2.8 %collective-permute-done = bf16[2,4,32,384]{3,2,1,0:T(8,128)(2,1)S(1)} collective-permute-done((bf16[2,4,32,384]{3,2,1,0:T(8,128)(2,1)}, bf16[2,4,32,384]{3,2,1,0:T(8,128)(2,1)S(1)}, u32[]{:S(2)}, u32[]{:S(2)}) %collective-permute-start) | collective-permute-done | bytes 196640 | tf_op jit(solution)/shard_map/ppermute | solution.py:22
  13.8 1.0 pad_maximum_fusion.9
  14.8 3.3 %collective-permute-start.1 = (bf16[4,1,32,384]{3,2,1,0:T(8,128)(2,1)S(1)}, bf16[4,1,32,384]{3,2,1,0:T(8,128)(2,1)S(1)}, u32[]{:S(2)}, u32[]{:S(2)}) collective-permute-start(bf16[4,1,32,384]{3,2,1,0:T(8,128)(2,1)S(1)} %get-tuple-element.130), channel_id=1, source_target_pairs={{0,4},{4,8},{8,12},{12,16},{16,20},{20,24},{24,28},{28,32},{32,36}... | collective-permute-start | bytes 294920 | tf_op jit(solution)/shard_map/ppermute | solution.py:36
  18.2 1.4 collective-permute-start.2
  19.6 0.9 pad_maximum_fusion.7
  20.5 3.1 %collective-permute-done.2 = bf16[4,1,32,384]{3,2,1,0:T(8,128)(2,1)S(1)} collective-permute-done((bf16[4,1,32,384]{3,2,1,0:T(8,128)(2,1)S(1)}, bf16[4,1,32,384]{3,2,1,0:T(8,128)(2,1)S(1)}, u32[]{:S(2)}, u32[]{:S(2)}) %collective-permute-start.2) | collective-permute-done | bytes 98336 | tf_op jit(solution)/shard_map/ppermute | solution.py:37
  23.6 0.9 pad_maximum_fusion.10
  24.5 4.8 %collective-permute-start.3 = (bf16[4,6,1,384]{3,2,1,0:T(2,128)(2,1)S(1)}, bf16[4,6,1,384]{3,2,1,0:T(2,128)(2,1)S(1)}, u32[]{:S(2)}, u32[]{:S(2)}) collective-permute-start(bf16[4,6,1,384]{3,2,1,0:T(2,128)(2,1)S(1)} %get-tuple-element.119), channel_id=1, source_target_pairs={{0,1},{1,2},{2,3},{4,5},{5,6},{6,7},{8,9},{9,10},{10,11},{12,13},{... | collective-permute-start | bytes 55304 | tf_op jit(solution)/shard_map/ppermute | solution.py:36
  29.3 1.3 collective-permute-start.4
  30.6 1.1 maximum_maximum_fusion.1
  31.9 1.3 fusion.24
  33.2 0.8 collective-permute-done.4
  34.0 1.7 %pad_maximum_fusion = (bf16[4,6,33,384]{3,2,1,0:T(8,128)(2,1)S(1)}, bf16[4,6,33,384]{3,2,1,0:T(8,128)(2,1)S(1)}) fusion(bf16[4,6,1,384]{3,2,1,0:T(2,128)(2,1)S(1)} %collective-permute-done.4, bf16[4,1,32,384]{3,2,1,0:T(8,128)(2,1)S(1)} %collective-permute-done.2, bf16[2,4,32,384]{3,2,1,0:T(8,128)(2,1)} %param.15, ...), kind=kLoop, calls=%fused_computation.67 | loop fusion | flops 6082560 | bytes 1843200 | tf_op jit(solution)/shard_map/concatenate | solution.py:38
  44.2 1.1 fusion.18
  45.3 0.5 collective-permute-start.6
  45.8 1.1 fusion.11
  46.9 1.3 add_convert_fusion.sel_ref
  48.2 9.1 %shard_map.89 = (bf16[4,192,384]{2,1,0:T(8,128)(2,1)S(1)}, bf16[4,192,384]{2,1,0:T(8,128)(2,1)S(1)}, bf16[3,192,384]{2,1,0:T(8,128)(2,1)S(1)}, bf16[3,192,384]{2...) custom-call(s32[1]{0:T(128)} %bitcast.58.core_ref, ...), custom_call_target="tpu_custom_call" | custom-call | flops 2113929216 | bytes 8388608 | tf_op jit(solution)/shard_map/pallas_call | solution.py:113
  57.3 3.2 %collective-permute-start.7 = (bf16[2,1,32,384]{3,2,1,0:T(8,128)(2,1)S(1)}, bf16[2,1,32,384]{3,2,1,0:T(8,128)(2,1)S(1)}, u32[]{:S(2)}, u32[]{:S(2)}) collective-permute-start(bf16[2,1,32,384]{3,2,1,0:T(8,128)(2,1)S(1)} %get-tuple-element.144), channel_id=1, source_target_pairs={{0,4},{4,8},{8,12},{12,16},{16,20},{20,24},{24,28},{28,32},{32,36}... | collective-permute-start | bytes 147464 | tf_op jit(solution)/shard_map/ppermute | solution.py:36
  60.5 1.6 collective-permute-start.8
  62.1 5.0 %collective-permute-start.12 = (bf16[4,192,384]{2,1,0:T(8,128)(2,1)S(1)}, bf16[4,192,384]{2,1,0:T(8,128)(2,1)S(1)}, u32[]{:S(2)}, u32[]{:S(2)}) collective-permute-start(bf16[4,192,384]{2,1,0:T(8,128)(2,1)S(1)} %get-tuple-element.91), channel_id=1, source_target_pairs={{0,16},{16,0},{32,48},{48,32},{1,17},{17,1},{33,49},{49,33},{2,18}... | collective-permute-start | bytes 1769480 | tf_op jit(solution)/shard_map/ppermute | solution.py:26
  67.1 1.8 %collective-permute-start.16 = (bf16[3,192,384]{2,1,0:T(8,128)(2,1)S(1)}, bf16[3,192,384]{2,1,0:T(8,128)(2,1)S(1)}, u32[]{:S(2)}, u32[]{:S(2)}) collective-permute-start(bf16[3,192,384]{2,1,0:T(8,128)(2,1)S(1)} %get-tuple-element.93), channel_id=1, source_target_pairs={{0,48},{16,32},{32,16},{48,0},{1,49},{17,33},{33,17},{49,1},{2,50}... | collective-permute-start | bytes 1327112 | tf_op jit(solution)/shard_map/ppermute | solution.py:26
  69.0 1.2 fusion.22
  70.2 1.2 fusion.19
  71.5 3.2 %collective-permute-start.10 = (bf16[2,6,1,384]{3,2,1,0:T(2,128)(2,1)S(1)}, bf16[2,6,1,384]{3,2,1,0:T(2,128)(2,1)S(1)}, u32[]{:S(2)}, u32[]{:S(2)}) collective-permute-start(bf16[2,6,1,384]{3,2,1,0:T(2,128)(2,1)S(1)} %get-tuple-element.141), channel_id=1, source_target_pairs={{0,1},{1,2},{2,3},{4,5},{5,6},{6,7},{8,9},{9,10},{10,11},{12,13},{... | collective-permute-start | bytes 27656 | tf_op jit(solution)/shard_map/ppermute | solution.py:36
  74.7 1.3 collective-permute-start.9
  76.0 1.2 fusion.27
  77.3 2.3 %collective-permute-start.24 = (bf16[3,192,384]{2,1,0:T(8,128)(2,1)S(1)}, bf16[3,192,384]{2,1,0:T(8,128)(2,1)S(1)}, u32[]{:S(2)}, u32[]{:S(2)}) collective-permute-start(bf16[3,192,384]{2,1,0:T(8,128)(2,1)S(1)} %get-tuple-element.97), channel_id=1, source_target_pairs={{0,12},{4,8},{8,4},{12,0},{1,13},{5,9},{9,5},{13,1},{2,14},{6,10},... | collective-permute-start | bytes 1327112 | tf_op jit(solution)/shard_map/ppermute | solution.py:26
  79.8 1.2 fusion.25
  81.1 1.2 fusion.21
  86.5 0.7 slice.804
  87.2 3.8 %collective-permute-start.11 = (bf16[2,4,32,384]{3,2,1,0:T(8,128)(2,1)}, bf16[2,4,32,384]{3,2,1,0:T(8,128)(2,1)S(1)}, u32[]{:S(2)}, u32[]{:S(2)}) collective-permute-start(bf16[2,4,32,384]{3,2,1,0:T(8,128)(2,1)} %slice.804), channel_id=1, source_target_pairs={{64,0},{128,64},{192,128},{65,1},{129,65},{193,129},{66,2},{130,66... | collective-permute-start | bytes 589832 | tf_op jit(solution)/shard_map/ppermute | solution.py:22
  92.0 0.8 collective-permute-start.17
  93.0 1.4 collective-permute-start.25
  94.5 0.7 collective-permute-start.13
  95.4 2.8 %collective-permute-start.21 = (bf16[4,96,384]{2,1,0:T(8,128)(2,1)S(1)}, bf16[4,96,384]{2,1,0:T(8,128)(2,1)S(1)}, u32[]{:S(2)}, u32[]{:S(2)}) collective-permute-start(bf16[4,96,384]{2,1,0:T(8,128)(2,1)S(1)} %slice.800), channel_id=1, source_target_pairs={{0,12},{4,8},{8,4},{12,0},{1,13},{5,9},{9,5},{13,1},{2,14},{6,10},... | collective-permute-start | bytes 884744 | tf_op jit(solution)/shard_map/ppermute | solution.py:26
  98.2 1.1 collective-permute-done.17
  99.5 2.8 %collective-permute-start.18 = (bf16[3,48,384]{2,1,0:T(8,128)(2,1)S(1)}, bf16[3,48,384]{2,1,0:T(8,128)(2,1)S(1)}, u32[]{:S(2)}, u32[]{:S(2)}) collective-permute-start(bf16[3,48,384]{2,1,0:T(8,128)(2,1)S(1)} %slice.808), channel_id=1, source_target_pairs={{0,12},{4,8},{8,4},{12,0},{1,13},{5,9},{9,5},{13,1},{2,14},{6,10},... | collective-permute-start | bytes 331784 | tf_op jit(solution)/shard_map/ppermute | solution.py:26
  102.4 1.0 collective-permute-start.26
  103.4 4.5 %collective-permute-done.18 = bf16[3,48,384]{2,1,0:T(8,128)(2,1)S(1)} collective-permute-done((bf16[3,48,384]{2,1,0:T(8,128)(2,1)S(1)}, bf16[3,48,384]{2,1,0:T(8,128)(2,1)S(1)}, u32[]{:S(2)}, u32[]{:S(2)}) %collective-permute-start.18) | collective-permute-done | bytes 110624 | tf_op jit(solution)/shard_map/ppermute | solution.py:26
  107.9 0.9 collective-permute-start.19
  108.9 2.1 %collective-permute-done.19 = bf16[3,24,384]{2,1,0:T(8,128)(2,1)S(1)} collective-permute-done((bf16[3,24,384]{2,1,0:T(8,128)(2,1)S(1)}, bf16[3,24,384]{2,1,0:T(8,128)(2,1)S(1)}, u32[]{:S(2)}, u32[]{:S(2)}) %collective-permute-start.19) | collective-permute-done | bytes 55328 | tf_op jit(solution)/shard_map/ppermute | solution.py:26
  111.0 1.2 collective-permute-done.27
  112.3 1.0 collective-permute-start.14
  113.5 3.1 %collective-permute-done.14 = bf16[4,48,384]{2,1,0:T(8,128)(2,1)S(1)} collective-permute-done((bf16[4,48,384]{2,1,0:T(8,128)(2,1)S(1)}, bf16[4,48,384]{2,1,0:T(8,128)(2,1)S(1)}, u32[]{:S(2)}, u32[]{:S(2)}) %collective-permute-start.14) | collective-permute-done | bytes 147488 | tf_op jit(solution)/shard_map/ppermute | solution.py:26
  116.7 1.8 %collective-permute-start.15 = (bf16[4,24,384]{2,1,0:T(8,128)(2,1)S(1)}, bf16[4,24,384]{2,1,0:T(8,128)(2,1)S(1)}, u32[]{:S(2)}, u32[]{:S(2)}) collective-permute-start(bf16[4,24,384]{2,1,0:T(8,128)(2,1)S(1)} %slice.810), channel_id=1, source_target_pairs={{0,12},{4,8},{8,4},{12,0},{1,13},{5,9},{9,5},{13,1},{2,14},{6,10},... | collective-permute-start | bytes 221192 | tf_op jit(solution)/shard_map/ppermute | solution.py:26
  118.5 0.8 collective-permute-start.23
  119.4 1.8 %collective-permute-done.15 = bf16[4,24,384]{2,1,0:T(8,128)(2,1)S(1)} collective-permute-done((bf16[4,24,384]{2,1,0:T(8,128)(2,1)S(1)}, bf16[4,24,384]{2,1,0:T(8,128)(2,1)S(1)}, u32[]{:S(2)}, u32[]{:S(2)}) %collective-permute-start.15) | collective-permute-done | bytes 73760 | tf_op jit(solution)/shard_map/ppermute | solution.py:26
  121.2 1.9 %collective-permute-done.23 = bf16[4,24,384]{2,1,0:T(8,128)(2,1)S(1)} collective-permute-done((bf16[4,24,384]{2,1,0:T(8,128)(2,1)S(1)}, bf16[4,24,384]{2,1,0:T(8,128)(2,1)S(1)}, u32[]{:S(2)}, u32[]{:S(2)}) %collective-permute-start.23) | collective-permute-done | bytes 73760 | tf_op jit(solution)/shard_map/ppermute | solution.py:26
  123.1 0.8 convert_element_type.161
  123.9 9.4 %all-to-all-start = ((bf16[8,42,384]{2,1,0:T(8,128)(2,1)}), bf16[8,42,384]{2,1,0:T(8,128)(2,1)S(1)}, u32[]{:S(2)}, u32[]{:S(2)}) async-start(bf16[8,42,384]{2,1,0:T(8,128)(2,1)} %convert_element_type.161), calls=%async_computation | async-start | bytes 589824 | tf_op jit(solution)/shard_map/all_to_all | solution.py:153
  133.3 1.2 convolution_add_fusion.3
  134.6 1.2 convolution_add_fusion.2
  135.8 7.2 %all-to-all-done = bf16[8,42,384]{2,1,0:T(8,128)(2,1)S(1)} async-done(((bf16[8,42,384]{2,1,0:T(8,128)(2,1)}), bf16[8,42,384]{2,1,0:T(8,128)(2,1)S(1)}, u32[]{:S(2)}, u32[]{:S(2)}) %all-to-all-start) | async-done | bytes 258080 | tf_op jit(solution)/shard_map/all_to_all | solution.py:153
  143.1 0.7 broadcast_in_dim.43
  143.8 3.4 %all-to-all-start.1 = ((bf16[8,42,384]{2,1,0:T(8,128)(2,1)}), bf16[8,42,384]{2,1,0:T(8,128)(2,1)S(1)}, u32[]{:S(2)}, u32[]{:S(2)}) async-start(bf16[8,42,384]{2,1,0:T(8,128)(2,1)} %broadcast_in_dim.43), calls=%async_computation.1 | async-start | bytes 589824 | tf_op jit(solution)/shard_map/all_to_all | solution.py:155
  147.2 1.2 fusion.28
  148.5 1.2 convolution_add_fusion.1
  149.7 7.1 %all-to-all-done.1 = bf16[8,42,384]{2,1,0:T(8,128)(2,1)S(1)} async-done(((bf16[8,42,384]{2,1,0:T(8,128)(2,1)}), bf16[8,42,384]{2,1,0:T(8,128)(2,1)S(1)}, u32[]{:S(2)}, u32[]{:S(2)}) %all-to-all-start.1) | async-done | bytes 258080 | tf_op jit(solution)/shard_map/all_to_all | solution.py:155
  156.9 8.0 %collective-permute-start.28 = (bf16[14,24,384]{2,1,0:T(8,128)(2,1)S(1)}, bf16[14,24,384]{2,1,0:T(8,128)(2,1)S(1)}, u32[]{:S(2)}, u32[]{:S(2)}) collective-permute-start(bf16[14,24,384]{2,1,0:T(8,128)(2,1)S(1)} %reshape.1176), channel_id=1, source_target_pairs={{0,64},{64,0},{1,65},{65,1},{2,66},{66,2},{3,67},{67,3},{4,68},{68... | collective-permute-start | bytes 774152 | tf_op jit(solution)/shard_map/ppermute | solution.py:26
  164.9 1.2 fusion.3
  166.2 0.7 fusion.16
  167.1 1.0 convert_bitcast_fusion
  (133 shorter events, 15.3 us)
Async XLA Ops:
  0.6 13.1 %collective-permute-start = (bf16[2,4,32,384]{3,2,1,0:T(8,128)(2,1)}, bf16[2,4,32,384]{3,2,1,0:T(8,128)(2,1)S(1)}, u32[]{:S(2)}, u32[]{:S(2)}) collective-permute-start(bf16[2,4,32,384]{3,2,1,0:T(8,128)(2,1)} %param.15), channel_id=1, source_target_pairs={{0,64},{64,128},{128,192},{1,65},{65,129},{129,193},{2,66},{66,130... | collective-permute-start | bytes 589832 | tf_op jit(solution)/shard_map/ppermute | solution.py:22
  13.8 22.4 %slice-start = ((s8[7962624]{0:T(1024)(128)(4,1)}), s8[4194304]{0:T(1024)(128)(4,1)S(1)}, s32[]{:S(2)}) async-start(s8[7962624]{0:T(1024)(128)(4,1)} %bitcast.230), calls=%async_computation.2 | async-start | bytes 8388608
  14.8 5.7 %collective-permute-start.1 = (bf16[4,1,32,384]{3,2,1,0:T(8,128)(2,1)S(1)}, bf16[4,1,32,384]{3,2,1,0:T(8,128)(2,1)S(1)}, u32[]{:S(2)}, u32[]{:S(2)}) collective-permute-start(bf16[4,1,32,384]{3,2,1,0:T(8,128)(2,1)S(1)} %get-tuple-element.130), channel_id=1, source_target_pairs={{0,4},{4,8},{8,12},{12,16},{16,20},{20,24},{24,28},{28,32},{32,36}... | collective-permute-start | bytes 294920 | tf_op jit(solution)/shard_map/ppermute | solution.py:36
  18.1 18.4 %copy-start = (bf16[2,4,32,384]{3,2,1,0:T(8,128)(2,1)S(1)}, bf16[2,4,32,384]{3,2,1,0:T(8,128)(2,1)}, u32[]{:S(2)}) copy-start(bf16[2,4,32,384]{3,2,1,0:T(8,128)(2,1)} %param.15) | copy-start | bytes 589828
  18.2 5.5 %collective-permute-start.2 = (bf16[4,1,32,384]{3,2,1,0:T(8,128)(2,1)S(1)}, bf16[4,1,32,384]{3,2,1,0:T(8,128)(2,1)S(1)}, u32[]{:S(2)}, u32[]{:S(2)}) collective-permute-start(bf16[4,1,32,384]{3,2,1,0:T(8,128)(2,1)S(1)} %get-tuple-element.131), channel_id=1, source_target_pairs={{4,0},{8,4},{12,8},{16,12},{20,16},{24,20},{28,24},{32,28},{36,32}... | collective-permute-start | bytes 294920 | tf_op jit(solution)/shard_map/ppermute | solution.py:37
  24.5 8.7 %collective-permute-start.3 = (bf16[4,6,1,384]{3,2,1,0:T(2,128)(2,1)S(1)}, bf16[4,6,1,384]{3,2,1,0:T(2,128)(2,1)S(1)}, u32[]{:S(2)}, u32[]{:S(2)}) collective-permute-start(bf16[4,6,1,384]{3,2,1,0:T(2,128)(2,1)S(1)} %get-tuple-element.119), channel_id=1, source_target_pairs={{0,1},{1,2},{2,3},{4,5},{5,6},{6,7},{8,9},{9,10},{10,11},{12,13},{... | collective-permute-start | bytes 55304 | tf_op jit(solution)/shard_map/ppermute | solution.py:36
  29.3 4.7 %collective-permute-start.4 = (bf16[4,6,1,384]{3,2,1,0:T(2,128)(2,1)S(1)}, bf16[4,6,1,384]{3,2,1,0:T(2,128)(2,1)S(1)}, u32[]{:S(2)}, u32[]{:S(2)}) collective-permute-start(bf16[4,6,1,384]{3,2,1,0:T(2,128)(2,1)S(1)} %get-tuple-element.118), channel_id=1, source_target_pairs={{1,0},{2,1},{3,2},{5,4},{6,5},{7,6},{9,8},{10,9},{11,10},{13,12},{... | collective-permute-start | bytes 55304 | tf_op jit(solution)/shard_map/ppermute | solution.py:37
  31.7 5.6 %copy-start.1 = (f32[384]{0:T(512)S(1)}, f32[384]{0:T(512)}, u32[]{:S(2)}) copy-start(f32[384]{0:T(512)} %param.18) | copy-start | bytes 4612
  33.2 3.0 %slice-start.1 = ((s8[7962624]{0:T(1024)(128)(4,1)}), s8[3768320]{0:T(1024)(128)(4,1)S(1)}, s32[]{:S(2)}) async-start(s8[7962624]{0:T(1024)(128)(4,1)} %bitcast.230), calls=%async_computation.3 | async-start | bytes 7536640
  37.0 4.8 %collective-permute-start.5 = (bf16[6,34,384]{2,1,0:T(8,128)(2,1)S(1)}, bf16[6,34,384]{2,1,0:T(8,128)(2,1)S(1)}, u32[]{:S(2)}, u32[]{:S(2)}) collective-permute-start(bf16[6,34,384]{2,1,0:T(8,128)(2,1)S(1)} %fusion.29), channel_id=1, source_target_pairs={{0,64},{64,0},{1,65},{65,1},{2,66},{66,2},{3,67},{67,3},{4,68},{68... | collective-permute-start | bytes 470024 | tf_op jit(solution)/shard_map/ppermute | solution.py:26
  40.6 3.6 %copy-start.2 = (bf16[2,4,32,384]{3,2,1,0:T(8,128)(2,1)S(1)}, bf16[2,4,32,384]{3,2,1,0:T(8,128)(2,1)}, u32[]{:S(2)}) copy-start(bf16[2,4,32,384]{3,2,1,0:T(8,128)(2,1)} %param.19) | copy-start | bytes 589828
  45.3 2.9 %collective-permute-start.6 = (bf16[256,384]{1,0:T(8,128)(2,1)S(1)}, bf16[256,384]{1,0:T(8,128)(2,1)S(1)}, u32[]{:S(2)}, u32[]{:S(2)}) collective-permute-start(bf16[256,384]{1,0:T(8,128)(2,1)S(1)} %get-tuple-element.89.own_ref), channel_id=1, source_target_pairs={{0,64},{64,0},{1,65},{65,1},{2,66},{66,2},{3,67},{67,3},{4,68},{68... | collective-permute-start | bytes 589832 | tf_op jit(solution)/shard_map/ppermute | solution.py:26
  48.2 34.2 %slice-start.2 = ((s8[7962624]{0:T(1024)(128)(4,1)}), s8[3768320]{0:T(1024)(128)(4,1)S(1)}, s32[]{:S(2)}) async-start(s8[7962624]{0:T(1024)(128)(4,1)} %bitcast.258), calls=%async_computation.4 | async-start | bytes 7536640
  57.3 11.6 %collective-permute-start.7 = (bf16[2,1,32,384]{3,2,1,0:T(8,128)(2,1)S(1)}, bf16[2,1,32,384]{3,2,1,0:T(8,128)(2,1)S(1)}, u32[]{:S(2)}, u32[]{:S(2)}) collective-permute-start(bf16[2,1,32,384]{3,2,1,0:T(8,128)(2,1)S(1)} %get-tuple-element.144), channel_id=1, source_target_pairs={{0,4},{4,8},{8,12},{12,16},{16,20},{20,24},{24,28},{28,32},{32,36}... | collective-permute-start | bytes 147464 | tf_op jit(solution)/shard_map/ppermute | solution.py:36
  60.5 21.9 %slice-start.3 = ((s8[7962624]{0:T(1024)(128)(4,1)}), s8[4194304]{0:T(1024)(128)(4,1)S(1)}, s32[]{:S(2)}) async-start(s8[7962624]{0:T(1024)(128)(4,1)} %bitcast.258), calls=%async_computation.5 | async-start | bytes 8388608
  60.5 8.4 %collective-permute-start.8 = (bf16[2,1,32,384]{3,2,1,0:T(8,128)(2,1)S(1)}, bf16[2,1,32,384]{3,2,1,0:T(8,128)(2,1)S(1)}, u32[]{:S(2)}, u32[]{:S(2)}) collective-permute-start(bf16[2,1,32,384]{3,2,1,0:T(8,128)(2,1)S(1)} %get-tuple-element.145), channel_id=1, source_target_pairs={{4,0},{8,4},{12,8},{16,12},{20,16},{24,20},{28,24},{32,28},{36,32}... | collective-permute-start | bytes 147464 | tf_op jit(solution)/shard_map/ppermute | solution.py:37
  62.1 32.3 %collective-permute-start.12 = (bf16[4,192,384]{2,1,0:T(8,128)(2,1)S(1)}, bf16[4,192,384]{2,1,0:T(8,128)(2,1)S(1)}, u32[]{:S(2)}, u32[]{:S(2)}) collective-permute-start(bf16[4,192,384]{2,1,0:T(8,128)(2,1)S(1)} %get-tuple-element.91), channel_id=1, source_target_pairs={{0,16},{16,0},{32,48},{48,32},{1,17},{17,1},{33,49},{49,33},{2,18}... | collective-permute-start | bytes 1769480 | tf_op jit(solution)/shard_map/ppermute | solution.py:26
  67.1 24.7 %collective-permute-start.16 = (bf16[3,192,384]{2,1,0:T(8,128)(2,1)S(1)}, bf16[3,192,384]{2,1,0:T(8,128)(2,1)S(1)}, u32[]{:S(2)}, u32[]{:S(2)}) collective-permute-start(bf16[3,192,384]{2,1,0:T(8,128)(2,1)S(1)} %get-tuple-element.93), channel_id=1, source_target_pairs={{0,48},{16,32},{32,16},{48,0},{1,49},{17,33},{33,17},{49,1},{2,50}... | collective-permute-start | bytes 1327112 | tf_op jit(solution)/shard_map/ppermute | solution.py:26
  68.9 26.3 %collective-permute-start.20 = (bf16[4,192,384]{2,1,0:T(8,128)(2,1)S(1)}, bf16[4,192,384]{2,1,0:T(8,128)(2,1)S(1)}, u32[]{:S(2)}, u32[]{:S(2)}) collective-permute-start(bf16[4,192,384]{2,1,0:T(8,128)(2,1)S(1)} %get-tuple-element.95), channel_id=1, source_target_pairs={{0,4},{4,0},{8,12},{12,8},{1,5},{5,1},{9,13},{13,9},{2,6},{6,2},{1... | collective-permute-start | bytes 1769480 | tf_op jit(solution)/shard_map/ppermute | solution.py:26
  71.5 5.7 %collective-permute-start.10 = (bf16[2,6,1,384]{3,2,1,0:T(2,128)(2,1)S(1)}, bf16[2,6,1,384]{3,2,1,0:T(2,128)(2,1)S(1)}, u32[]{:S(2)}, u32[]{:S(2)}) collective-permute-start(bf16[2,6,1,384]{3,2,1,0:T(2,128)(2,1)S(1)} %get-tuple-element.141), channel_id=1, source_target_pairs={{0,1},{1,2},{2,3},{4,5},{5,6},{6,7},{8,9},{9,10},{10,11},{12,13},{... | collective-permute-start | bytes 27656 | tf_op jit(solution)/shard_map/ppermute | solution.py:36
  74.7 4.9 %collective-permute-start.9 = (bf16[2,6,1,384]{3,2,1,0:T(2,128)(2,1)S(1)}, bf16[2,6,1,384]{3,2,1,0:T(2,128)(2,1)S(1)}, u32[]{:S(2)}, u32[]{:S(2)}) collective-permute-start(bf16[2,6,1,384]{3,2,1,0:T(2,128)(2,1)S(1)} %get-tuple-element.140), channel_id=1, source_target_pairs={{1,0},{2,1},{3,2},{5,4},{6,5},{7,6},{9,8},{10,9},{11,10},{13,12},{... | collective-permute-start | bytes 27656 | tf_op jit(solution)/shard_map/ppermute | solution.py:37
  77.3 15.6 %collective-permute-start.24 = (bf16[3,192,384]{2,1,0:T(8,128)(2,1)S(1)}, bf16[3,192,384]{2,1,0:T(8,128)(2,1)S(1)}, u32[]{:S(2)}, u32[]{:S(2)}) collective-permute-start(bf16[3,192,384]{2,1,0:T(8,128)(2,1)S(1)} %get-tuple-element.97), channel_id=1, source_target_pairs={{0,12},{4,8},{8,4},{12,0},{1,13},{5,9},{9,5},{13,1},{2,14},{6,10},... | collective-permute-start | bytes 1327112 | tf_op jit(solution)/shard_map/ppermute | solution.py:26
  87.2 79.0 %collective-permute-start.11 = (bf16[2,4,32,384]{3,2,1,0:T(8,128)(2,1)}, bf16[2,4,32,384]{3,2,1,0:T(8,128)(2,1)S(1)}, u32[]{:S(2)}, u32[]{:S(2)}) collective-permute-start(bf16[2,4,32,384]{3,2,1,0:T(8,128)(2,1)} %slice.804), channel_id=1, source_target_pairs={{64,0},{128,64},{192,128},{65,1},{129,65},{193,129},{66,2},{130,66... | collective-permute-start | bytes 589832 | tf_op jit(solution)/shard_map/ppermute | solution.py:22
  92.0 7.4 %collective-permute-start.17 = (bf16[3,96,384]{2,1,0:T(8,128)(2,1)S(1)}, bf16[3,96,384]{2,1,0:T(8,128)(2,1)S(1)}, u32[]{:S(2)}, u32[]{:S(2)}) collective-permute-start(bf16[3,96,384]{2,1,0:T(8,128)(2,1)S(1)} %slice.803), channel_id=1, source_target_pairs={{0,16},{16,0},{32,48},{48,32},{1,17},{17,1},{33,49},{49,33},{2,18}... | collective-permute-start | bytes 663560 | tf_op jit(solution)/shard_map/ppermute | solution.py:26
  93.0 9.3 %collective-permute-start.25 = (bf16[3,96,384]{2,1,0:T(8,128)(2,1)S(1)}, bf16[3,96,384]{2,1,0:T(8,128)(2,1)S(1)}, u32[]{:S(2)}, u32[]{:S(2)}) collective-permute-start(bf16[3,96,384]{2,1,0:T(8,128)(2,1)S(1)} %slice.802), channel_id=1, source_target_pairs={{0,4},{4,0},{8,12},{12,8},{1,5},{5,1},{9,13},{13,9},{2,6},{6,2},{1... | collective-permute-start | bytes 663560 | tf_op jit(solution)/shard_map/ppermute | solution.py:26
  94.5 17.7 %collective-permute-start.13 = (bf16[4,96,384]{2,1,0:T(8,128)(2,1)S(1)}, bf16[4,96,384]{2,1,0:T(8,128)(2,1)S(1)}, u32[]{:S(2)}, u32[]{:S(2)}) collective-permute-start(bf16[4,96,384]{2,1,0:T(8,128)(2,1)S(1)} %slice.801), channel_id=1, source_target_pairs={{0,48},{16,32},{32,16},{48,0},{1,49},{17,33},{33,17},{49,1},{2,50}... | collective-permute-start | bytes 884744 | tf_op jit(solution)/shard_map/ppermute | solution.py:26
  95.4 17.9 %collective-permute-start.21 = (bf16[4,96,384]{2,1,0:T(8,128)(2,1)S(1)}, bf16[4,96,384]{2,1,0:T(8,128)(2,1)S(1)}, u32[]{:S(2)}, u32[]{:S(2)}) collective-permute-start(bf16[4,96,384]{2,1,0:T(8,128)(2,1)S(1)} %slice.800), channel_id=1, source_target_pairs={{0,12},{4,8},{8,4},{12,0},{1,13},{5,9},{9,5},{13,1},{2,14},{6,10},... | collective-permute-start | bytes 884744 | tf_op jit(solution)/shard_map/ppermute | solution.py:26
  99.5 8.4 %collective-permute-start.18 = (bf16[3,48,384]{2,1,0:T(8,128)(2,1)S(1)}, bf16[3,48,384]{2,1,0:T(8,128)(2,1)S(1)}, u32[]{:S(2)}, u32[]{:S(2)}) collective-permute-start(bf16[3,48,384]{2,1,0:T(8,128)(2,1)S(1)} %slice.808), channel_id=1, source_target_pairs={{0,12},{4,8},{8,4},{12,0},{1,13},{5,9},{9,5},{13,1},{2,14},{6,10},... | collective-permute-start | bytes 331784 | tf_op jit(solution)/shard_map/ppermute | solution.py:26
  102.4 6.4 %collective-permute-start.26 = (bf16[3,48,384]{2,1,0:T(8,128)(2,1)S(1)}, bf16[3,48,384]{2,1,0:T(8,128)(2,1)S(1)}, u32[]{:S(2)}, u32[]{:S(2)}) collective-permute-start(bf16[3,48,384]{2,1,0:T(8,128)(2,1)S(1)} %slice.807), channel_id=1, source_target_pairs={{0,48},{16,32},{32,16},{48,0},{1,49},{17,33},{33,17},{49,1},{2,50}... | collective-permute-start | bytes 331784 | tf_op jit(solution)/shard_map/ppermute | solution.py:26
  107.9 3.1 %collective-permute-start.19 = (bf16[3,24,384]{2,1,0:T(8,128)(2,1)S(1)}, bf16[3,24,384]{2,1,0:T(8,128)(2,1)S(1)}, u32[]{:S(2)}, u32[]{:S(2)}) collective-permute-start(bf16[3,24,384]{2,1,0:T(8,128)(2,1)S(1)} %slice.812), channel_id=1, source_target_pairs={{0,4},{4,0},{8,12},{12,8},{1,5},{5,1},{9,13},{13,9},{2,6},{6,2},{1... | collective-permute-start | bytes 165896 | tf_op jit(solution)/shard_map/ppermute | solution.py:26
  108.8 3.4 %collective-permute-start.27 = (bf16[3,24,384]{2,1,0:T(8,128)(2,1)S(1)}, bf16[3,24,384]{2,1,0:T(8,128)(2,1)S(1)}, u32[]{:S(2)}, u32[]{:S(2)}) collective-permute-start(bf16[3,24,384]{2,1,0:T(8,128)(2,1)S(1)} %slice.811), channel_id=1, source_target_pairs={{0,16},{16,0},{32,48},{48,32},{1,17},{17,1},{33,49},{49,33},{2,18}... | collective-permute-start | bytes 165896 | tf_op jit(solution)/shard_map/ppermute | solution.py:26
  112.3 4.3 %collective-permute-start.14 = (bf16[4,48,384]{2,1,0:T(8,128)(2,1)S(1)}, bf16[4,48,384]{2,1,0:T(8,128)(2,1)S(1)}, u32[]{:S(2)}, u32[]{:S(2)}) collective-permute-start(bf16[4,48,384]{2,1,0:T(8,128)(2,1)S(1)} %slice.806), channel_id=1, source_target_pairs={{0,4},{4,0},{8,12},{12,8},{1,5},{5,1},{9,13},{13,9},{2,6},{6,2},{1... | collective-permute-start | bytes 442376 | tf_op jit(solution)/shard_map/ppermute | solution.py:26
  113.4 5.1 %collective-permute-start.22 = (bf16[4,48,384]{2,1,0:T(8,128)(2,1)S(1)}, bf16[4,48,384]{2,1,0:T(8,128)(2,1)S(1)}, u32[]{:S(2)}, u32[]{:S(2)}) collective-permute-start(bf16[4,48,384]{2,1,0:T(8,128)(2,1)S(1)} %slice.805), channel_id=1, source_target_pairs={{0,16},{16,0},{32,48},{48,32},{1,17},{17,1},{33,49},{49,33},{2,18}... | collective-permute-start | bytes 442376 | tf_op jit(solution)/shard_map/ppermute | solution.py:26
  116.7 4.5 %collective-permute-start.15 = (bf16[4,24,384]{2,1,0:T(8,128)(2,1)S(1)}, bf16[4,24,384]{2,1,0:T(8,128)(2,1)S(1)}, u32[]{:S(2)}, u32[]{:S(2)}) collective-permute-start(bf16[4,24,384]{2,1,0:T(8,128)(2,1)S(1)} %slice.810), channel_id=1, source_target_pairs={{0,12},{4,8},{8,4},{12,0},{1,13},{5,9},{9,5},{13,1},{2,14},{6,10},... | collective-permute-start | bytes 221192 | tf_op jit(solution)/shard_map/ppermute | solution.py:26
  118.5 4.5 %collective-permute-start.23 = (bf16[4,24,384]{2,1,0:T(8,128)(2,1)S(1)}, bf16[4,24,384]{2,1,0:T(8,128)(2,1)S(1)}, u32[]{:S(2)}, u32[]{:S(2)}) collective-permute-start(bf16[4,24,384]{2,1,0:T(8,128)(2,1)S(1)} %slice.809), channel_id=1, source_target_pairs={{0,48},{16,32},{32,16},{48,0},{1,49},{17,33},{33,17},{49,1},{2,50}... | collective-permute-start | bytes 221192 | tf_op jit(solution)/shard_map/ppermute | solution.py:26
  123.9 19.1 %all-to-all-start = ((bf16[8,42,384]{2,1,0:T(8,128)(2,1)}), bf16[8,42,384]{2,1,0:T(8,128)(2,1)S(1)}, u32[]{:S(2)}, u32[]{:S(2)}) async-start(bf16[8,42,384]{2,1,0:T(8,128)(2,1)} %convert_element_type.161), calls=%async_computation | async-start | bytes 589824 | tf_op jit(solution)/shard_map/all_to_all | solution.py:153
  143.8 13.0 %all-to-all-start.1 = ((bf16[8,42,384]{2,1,0:T(8,128)(2,1)}), bf16[8,42,384]{2,1,0:T(8,128)(2,1)S(1)}, u32[]{:S(2)}, u32[]{:S(2)}) async-start(bf16[8,42,384]{2,1,0:T(8,128)(2,1)} %broadcast_in_dim.43), calls=%async_computation.1 | async-start | bytes 589824 | tf_op jit(solution)/shard_map/all_to_all | solution.py:155
  156.9 10.0 %collective-permute-start.28 = (bf16[14,24,384]{2,1,0:T(8,128)(2,1)S(1)}, bf16[14,24,384]{2,1,0:T(8,128)(2,1)S(1)}, u32[]{:S(2)}, u32[]{:S(2)}) collective-permute-start(bf16[14,24,384]{2,1,0:T(8,128)(2,1)S(1)} %reshape.1176), channel_id=1, source_target_pairs={{0,64},{64,0},{1,65},{65,1},{2,66},{66,2},{3,67},{67,3},{4,68},{68... | collective-permute-start | bytes 774152 | tf_op jit(solution)/shard_map/ppermute | solution.py:26

commit v3 on v2

v3 whole, which is shorter than its diff:
```python
import jax
import jax.numpy as jnp
from jax import lax
from jax.experimental import pallas as pl
from jax.experimental.pallas import tpu as pltpu
from jax.sharding import Mesh, PartitionSpec as P

BF = jnp.bfloat16
F32 = jnp.float32
TM = ("zh", "co")
HEIGHT = ("x", "y")
RING = ("zh", "z")
N_TAPS = 14


def shifted(value, axis, by):
    length = lax.axis_size(axis)
    pairs = [(i, i + by) for i in range(length) if 0 <= i + by < length]
    return lax.ppermute(value, axis, pairs)


def exchanged(value, axis, flip):
    return lax.ppermute(value, axis, [(i, i ^ flip) for i in range(lax.axis_size(axis))])


def with_halo(value, sides, width):
    for axis, dim in sides:
        size, length = (lax.axis_size(axis), value.shape[dim])
        up = [(i, (i + 1) % size) for i in range(size - 1)]
        down = [(j, i) for i, j in up]
        last = lax.slice_in_dim(value, length - width, length, axis=dim)
        initial = lax.slice_in_dim(value, 0, width, axis=dim)
        before = lax.ppermute(last, axis, up)
        after = lax.ppermute(initial, axis, down)
        value = jnp.concatenate([before, value, after], axis=dim)
    return value


def tap_block(padded, tap_t, tap_h, tap_w, depth_count, row_count, col_count):
    block = padded[
        tap_t : tap_t + depth_count, tap_h : tap_h + row_count, tap_w : tap_w + col_count
    ]
    return block.reshape(-1, block.shape[-1])


def spread_kernel(where_ref, *refs):
    lines, peer_ref, out_ref = refs[:4], refs[4], refs[5]
    core = where_ref[0]
    for k, flip in enumerate((0, 1, 3, 2)):
        src = where_ref[1] ^ flip
        at = jnp.where(src == 0, 0, 1 + 4 * src)
        for c in range(3):
            for f in range(3):
                out_ref[c, f + 2 * core, pl.ds(at, 5)] = lines[k][f, :, c : c + 32, :]
            for f in range(2):
                out_ref[c, f + 3 * (1 - core), pl.ds(at, 5)] = peer_ref[k, f, :, c : c + 32, :]


def spread(where, lines, peer):
    shape = (3, 5, 18, 32, 384)
    args = (*lines, peer)

    def whole(shape):
        return pl.BlockSpec(shape, lambda i, *_: (0,) * len(shape))

    return pl.pallas_call(
        spread_kernel,
        out_shape=jax.ShapeDtypeStruct(shape, BF),
        grid_spec=pltpu.PrefetchScalarGridSpec(
            num_scalar_prefetch=1,
            grid=(1,),
            in_specs=[whole(a.shape) for a in args],
            out_specs=whole(shape),
        ),
        compiler_params=pltpu.CompilerParams(vmem_limit_bytes=48 << 20),
        cost_estimate=pl.CostEstimate(flops=0, bytes_accessed=12 << 20, transcendentals=0),
    )(where, *args)


def weight_grad_kernel(core_ref, cols, own_ref, peer_ref, out_ref):
    core = core_ref[0]
    k = pl.program_id(0) + 4 * core
    tap_t, tap_h, tap_w = k // 9, (k // 3) % 3, k % 3
    total = None
    for ref, first in ((own_ref, 2 * core), (peer_ref, 2 * (1 - core))):
        for src in range(4):
            patch = cols[tap_w, pl.ds(tap_t + first, 2), pl.ds(4 * src + tap_h, 4)]
            term = jnp.dot(ref[src], patch.reshape(256, 384), preferred_element_type=F32)
            total = term if total is None else total + term
    for q in range(4):
        out_ref[q, 0] = total[24 * q : 24 * q + 24].astype(BF)


def weight_grad(core, cols, own, peer):
    def whole(a):
        return pl.BlockSpec(a.shape, lambda j, *_: (0,) * a.ndim)

    return pl.pallas_call(
        weight_grad_kernel,
        out_shape=jax.ShapeDtypeStruct((4, N_TAPS, 24, 384), BF),
        grid_spec=pltpu.PrefetchScalarGridSpec(
            num_scalar_prefetch=1,
            grid=(N_TAPS,),
            in_specs=[whole(a) for a in (cols, own, peer)],
            out_specs=pl.BlockSpec((4, 1, 24, 384), lambda j, *_: (0, j, 0, 0)),
        ),
        compiler_params=pltpu.CompilerParams(vmem_limit_bytes=48 << 20),
        cost_estimate=pl.CostEstimate(
            flops=2 * N_TAPS * 384 * 384 * 512, bytes_accessed=9 << 20, transcendentals=0
        ),
    )(core, cols, own, peer)


def across(value, axes):
    return lax.all_to_all(value, axes, 0, 0, tiled=True)


def reduced_over_ring(mine):
    chunks = mine.astype(BF).reshape(8, 42, 384)
    got = across(chunks, RING)
    total = jnp.sum(got.astype(F32), 0).astype(BF)
    whole = across(jnp.broadcast_to(total, chunks.shape), RING)
    return whole.reshape(N_TAPS, 24, 384)


def program(frames, cache_in, kernel, conv_bias, cotangent):
    frame_count, row_count, col_count, channels = frames.shape
    core = lax.axis_index("co")
    is_first = lax.axis_index(TM) == 0
    weights = kernel.transpose(1, 2, 3, 0, 4)
    earlier = shifted(frames, TM, 1)
    earlier = jnp.where(is_first, cache_in, earlier)
    stacked = jnp.concatenate([earlier, frames], 0)
    extended = with_halo(stacked, ((HEIGHT, 1), ("z", 2)), 1)
    rows = lax.dynamic_slice(
        extended,
        (core, (lax.axis_index("y") != 0).astype(jnp.int32), 0, 0),
        (3, 5, col_count + 2, channels),
    )
    rows = jnp.pad(rows, ((0, 0), (0, 0), (0, 6), (0, 0)))
    line = [rows] + [exchanged(rows, "y", flip) for flip in (1, 3, 2)]
    pre_act = jnp.zeros((frame_count * row_count * col_count, channels), F32) + conv_bias
    for tap_t in range(3):
        for tap_h in range(3):
            for tap_w in range(3):
                block = tap_block(extended, tap_t, tap_h, tap_w, frame_count, row_count, col_count)
                pre_act = pre_act + lax.dot_general(
                    block,
                    weights[tap_t, tap_h, tap_w],
                    (((1,), (1,)), ((), ())),
                    preferred_element_type=F32,
                )
    sigma = jax.nn.sigmoid(pre_act)
    decoded = (pre_act * sigma).astype(BF).reshape(frames.shape)
    scaled = (
        cotangent.reshape(-1, channels).astype(F32) * sigma * (1.0 + pre_act * (1.0 - sigma))
    ).astype(BF)
    row = lax.broadcasted_iota(jnp.int32, (channels, channels), 0)
    col = lax.broadcasted_iota(jnp.int32, (channels, channels), 1)
    order = (row // 24 % 4 * 96 + row // 96 * 24 + row % 24 == col).astype(BF)
    own = lax.dot_general(order, scaled, (((1,), (1,)), ((), ())), preferred_element_type=F32)
    own = across(own.astype(BF).reshape(4, 96, -1), "y")
    own, *line = lax.optimization_barrier((own, *line))
    line_peer = jnp.stack([jnp.where(core == 0, v[1:3], v[0:2]) for v in line])
    line_peer = exchanged(line_peer, "co", 1)
    cols = spread(jnp.stack([core, lax.axis_index("y")]), line, line_peer)
    parts = weight_grad(core.reshape(1), cols, own, exchanged(own, "co", 1))
    scaled, parts = lax.optimization_barrier((scaled, parts))
    parts = across(parts, "x")
    mine = reduced_over_ring(jnp.sum(parts.astype(F32), 0))
    theirs = exchanged(mine, "co", 1)
    taps = jnp.where(
        core == 0,
        jnp.concatenate([mine, theirs[1:]], 0),
        jnp.concatenate([theirs, mine[1:]], 0),
    ).astype(F32)
    kernel_grad = taps.reshape(3, 3, 3, 24, channels).transpose(3, 0, 1, 2, 4)

    grad_rimmed = with_halo(scaled.reshape(frames.shape), ((HEIGHT, 1), ("z", 2)), 1)
    partial_value = jnp.zeros((frame_count + 2, row_count, col_count, channels), F32)
    for tap_t in range(3):
        contrib = jnp.zeros((frame_count * row_count * col_count, channels), F32)
        for tap_h in range(3):
            for tap_w in range(3):
                block = grad_rimmed[
                    :, 2 - tap_h : 2 - tap_h + row_count, 2 - tap_w : 2 - tap_w + col_count
                ].reshape(-1, channels)
                contrib = contrib + jnp.dot(
                    block, weights[tap_t, tap_h, tap_w], preferred_element_type=F32
                )
        partial_value = partial_value.at[tap_t : tap_t + frame_count].add(
            contrib.reshape(frame_count, row_count, col_count, channels)
        )
    cache_grad = partial_value[:2].astype(BF)
    carried = shifted(cache_grad, TM, -1)
    frame_grad = (
        partial_value[2:].at[frame_count - 2 :].add(carried.astype(F32)).astype(BF)
    )
    return (decoded, frame_grad, cache_grad, kernel_grad)


def solution(mesh):
    split = Mesh(mesh.devices.reshape(2, 2, 4, 4, 4), ("zh", "co", "x", "y", "z"))
    block = P(TM, HEIGHT, "z", None)
    return jax.shard_map(
        program,
        mesh=split,
        in_specs=(block, P(None, HEIGHT, "z", None), P(), P(), block),
        out_specs=(block, block, block, P(HEIGHT, None, None, None, None)),
        check_vma=False,
    )
```

time: 169 us -> 181 us (1.071)
  matrix products: 26.4 us -> 43.8 us
  starting transfers between devices: 79 us -> 69.6 us
  Pallas kernels: 9.11 us -> 15.7 us
  waiting for transfers between devices: 36.7 us -> 34.5 us
    ppermute x19 -> x6, starting transfers between devices: 32.1 us -> 7.26 us  [exchanged(): lax.ppermute(value, axis, [(i, i ^ flip) for i in range(lax.axis_size(axi...]
    dot_general x54 -> x55, matrix products: 26.4 us -> 43.8 us  [the longest x27 33.2 us: program(): jnp.dot(block, weights[tap_t, tap_h, tap_w], preferred_element_type=F32)]
    all_to_all x2 -> x4, starting transfers between devices: 12.8 us -> 26.5 us  [across(): return lax.all_to_all(value, axes, 0, 0, tiled=True)]
    ppermute x19 -> x6, waiting for transfers between devices: 15.6 us -> 2.34 us  [exchanged(): lax.ppermute(value, axis, [(i, i ^ flip) for i in range(lax.axis_size(axi...]
    all_to_all x2 -> x4, waiting for transfers between devices: 14.3 us -> 26.3 us  [across(): return lax.all_to_all(value, axes, 0, 0, tiled=True)]
    pallas_call x1 -> x2, Pallas kernels: 9.11 us -> 15.7 us  [the longest x1 10.7 us: weight_grad(): pl.pallas_call(weight_grad_kernel, out_shape=jax.ShapeDtypeStruct((4, N_T...]
    ppermute x4, starting transfers between devices: 14.5 us -> 16.7 us  [with_halo(): before = lax.ppermute(last, axis, up)]
    concatenate x6 -> x5, other arithmetic: 4.37 us -> 3.27 us  [with_halo(): value = jnp.concatenate([before, value, after], axis=dim)]
  transfers between devices with their start and end apart: 31 -> 20, of which waited for: 12 -> 7; matrix products, arithmetic and copies ran while one was open for 19% -> 29% of each run, Pallas kernels for 0% -> 3%
where the time goes in v3:
time: 181 us; the launch traced here: 178 us
  starting transfers between devices  69.6 us (38%)
  matrix products  43.8 us (24%)
  waiting for transfers between devices  34.5 us (19%)
  Pallas kernels  15.7 us (9%)
  other arithmetic  10.1 us (6%)
  local copies, waits for them, and re-layouts  3.26 us (2%)
    dot_general x27, matrix products, program(): jnp.dot(block, weights[tap_t, tap_h, tap_w], preferred_element_type=F32)  33.2 us
    all_to_all x4, starting transfers between devices, across(): return lax.all_to_all(value, axes, 0, 0, tiled=True)  26.5 us
    all_to_all x4, waiting for transfers between devices, across(): return lax.all_to_all(value, axes, 0, 0, tiled=True)  26.3 us
    ppermute x4, starting transfers between devices, with_halo(): before = lax.ppermute(last, axis, up)  16.7 us
    ppermute x2, starting transfers between devices, shifted(): return lax.ppermute(value, axis, pairs)  14 us
    pallas_call x1, Pallas kernels, weight_grad(): pl.pallas_call(weight_grad_kernel, out_shape=jax.ShapeDtypeStruct((4, N_T...  10.7 us
    dot_general x27, matrix products, program(): lax.dot_general(block, weights[tap_t, tap_h, tap_w], (((1,), (1,)), ((),...  8.56 us
    ppermute x6, starting transfers between devices, exchanged(): lax.ppermute(value, axis, [(i, i ^ flip) for i in range(lax.axis_size(axi...  7.26 us
  transfers between devices with their start and end apart: 20, of which 7 were waited for; matrix products, arithmetic and copies ran while one was open for 29% of the time, Pallas kernels for 3%

profile of v3, /device:TPU:1, one launch (start us, length us, event | category | flops | bytes accessed | tf_op | source)
XLA Modules:
  0.0 178.4 jit_solution(6237722353295898494)
XLA Ops:
  0.6 10.3 %collective-permute-start = (bf16[2,4,32,384]{3,2,1,0:T(8,128)(2,1)}, bf16[2,4,32,384]{3,2,1,0:T(8,128)(2,1)S(1)}, u32[]{:S(2)}, u32[]{:S(2)}) collective-permute-start(bf16[2,4,32,384]{3,2,1,0:T(8,128)(2,1)} %param.15), channel_id=1, source_target_pairs={{0,64},{64,128},{128,192},{1,65},{65,129},{129,193},{2,66},{66,130... | collective-permute-start | bytes 589832 | tf_op jit(solution)/shard_map/ppermute | solution.py:19
  11.1 2.8 %collective-permute-done = bf16[2,4,32,384]{3,2,1,0:T(8,128)(2,1)S(1)} collective-permute-done((bf16[2,4,32,384]{3,2,1,0:T(8,128)(2,1)}, bf16[2,4,32,384]{3,2,1,0:T(8,128)(2,1)S(1)}, u32[]{:S(2)}, u32[]{:S(2)}) %collective-permute-start) | collective-permute-done | bytes 196640 | tf_op jit(solution)/shard_map/ppermute | solution.py:19
  13.9 0.9 pad_maximum_fusion.8
  14.8 1.3 collective-permute-start.2
  16.1 4.0 %collective-permute-start.1 = (bf16[4,1,32,384]{3,2,1,0:T(8,128)(2,1)S(1)}, bf16[4,1,32,384]{3,2,1,0:T(8,128)(2,1)S(1)}, u32[]{:S(2)}, u32[]{:S(2)}) collective-permute-start(bf16[4,1,32,384]{3,2,1,0:T(8,128)(2,1)S(1)} %get-tuple-element.106), channel_id=1, source_target_pairs={{0,4},{4,8},{8,12},{12,16},{16,20},{20,24},{24,28},{28,32},{32,36}... | collective-permute-start | bytes 294920 | tf_op jit(solution)/shard_map/ppermute | solution.py:33
  20.1 0.9 pad_maximum_fusion.6
  21.7 1.2 pad_maximum_fusion.12
  22.9 4.8 %collective-permute-start.3 = (bf16[4,6,1,384]{3,2,1,0:T(2,128)(2,1)S(1)}, bf16[4,6,1,384]{3,2,1,0:T(2,128)(2,1)S(1)}, u32[]{:S(2)}, u32[]{:S(2)}) collective-permute-start(bf16[4,6,1,384]{3,2,1,0:T(2,128)(2,1)S(1)} %get-tuple-element.94), channel_id=1, source_target_pairs={{0,1},{1,2},{2,3},{4,5},{5,6},{6,7},{8,9},{9,10},{10,11},{12,13},{... | collective-permute-start | bytes 55304 | tf_op jit(solution)/shard_map/ppermute | solution.py:33
  27.7 1.3 collective-permute-start.4
  29.0 1.1 pad_maximum_fusion.2
  30.3 2.4 %collective-permute-done.4 = bf16[4,6,1,384]{3,2,1,0:T(2,128)(2,1)S(1)} collective-permute-done((bf16[4,6,1,384]{3,2,1,0:T(2,128)(2,1)S(1)}, bf16[4,6,1,384]{3,2,1,0:T(2,128)(2,1)S(1)}, u32[]{:S(2)}, u32[]{:S(2)}) %collective-permute-start.4) | collective-permute-done | bytes 18464 | tf_op jit(solution)/shard_map/ppermute | solution.py:34
  32.7 1.5 fusion.11
  34.2 1.6 collective-permute-start.5
  35.8 3.4 %collective-permute-start.6 = (bf16[3,5,40,384]{3,2,1,0:T(8,128)(2,1)S(1)}, bf16[3,5,40,384]{3,2,1,0:T(8,128)(2,1)S(1)}, u32[]{:S(2)}, u32[]{:S(2)}) collective-permute-start(bf16[3,5,40,384]{3,2,1,0:T(8,128)(2,1)S(1)} %pad.14.refs_0_), channel_id=1, source_target_pairs={{0,12},{4,8},{8,4},{12,0},{1,13},{5,9},{9,5},{13,1},{2,14},{6,10},... | collective-permute-start | bytes 1382408 | tf_op jit(solution)/shard_map/ppermute | solution.py:23
  39.3 1.1 collective-permute-start.7
  49.0 1.1 fusion.18
  50.1 2.0 %convolution_convert_fusion = bf16[384,256]{1,0:T(8,128)(2,1)} fusion(bf16[256,384]{1,0:T(8,128)(2,1)S(1)} %get-tuple-element.72, s32[384]{0:T(512)S(1)} %get-tuple-element.138, s32[384]{0:T(512)S(1)} %get-tuple-element.139, s32[384]{0:T(512)S(1)} %get-tuple-element.136, s32[384]{0:T(512)S(1)} %get-tuple-element.140, s32[384]{0:T(512)S(1)} %get-tuple-element.137, ...), kind=kOutput, calls=%fused_computation.52 | convolution fusion | flops 78397440 | bytes 403584 | tf_op jit(solution)/shard_map/dot_general | solution.py:161
  52.1 3.4 %all-to-all-start = ((bf16[4,96,256]{2,1,0:T(8,128)(2,1)}), bf16[4,96,256]{2,1,0:T(8,128)(2,1)S(1)}, u32[]{:S(2)}, u32[]{:S(2)}) async-start(bf16[4,96,256]{2,1,0:T(8,128)(2,1)} %bitcast.59), calls=%async_computation | async-start | bytes 393216 | tf_op jit(solution)/shard_map/all_to_all | solution.py:115
  55.5 5.1 %all-to-all-done.own_ref = bf16[4,96,256]{2,1,0:T(8,128)(2,1)S(1)} async-done(((bf16[4,96,256]{2,1,0:T(8,128)(2,1)}), bf16[4,96,256]{2,1,0:T(8,128)(2,1)S(1)}, u32[]{:S(2)}, u32[]{:S(2)}) %all-to-all-start) | async-done | bytes 196640 | tf_op jit(solution)/shard_map/all_to_all | solution.py:115
  61.8 2.3 %collective-permute-done.8.refs_4_ = bf16[4,2,5,40,384]{4,3,2,1,0:T(8,128)(2,1)S(1)} collective-permute-done((bf16[4,2,5,40,384]{4,3,2,1,0:T(8,128)(2,1)S(1)}, bf16[4,2,5,40,384]{4,3,2,1,0:T(8,128)(2,1)S(1)}, u32[]{:S(2)}, u32[]{:S(2)}) %collective-permute-start.8) | collective-permute-done | bytes 1228832 | tf_op jit(solution)/shard_map/ppermute | solution.py:23
  64.1 4.9 %shard_map.89.cols = bf16[3,5,18,32,384]{4,3,2,1,0:T(8,128)(2,1)} custom-call(s32[2]{0:T(128)S(1)} %pad_add_fusion.where_ref, bf16[3,5,40,384]{3,2,1,0:T(8,128)(2,1)S(1)} %pad.14.refs_0_, bf16[3,5,40,384]{3,2,1,0:T(8,128)(2,1)S(1)} %collective-permute-done.5.refs_1_, bf16[3,5,40,384]{3,2,1,0:T(8,128)(2,1)S(1)} %collective-permute-done.6.refs_2_, ...), custom_call_target="tpu_custom_call" | custom-call | bytes 12582912 | tf_op jit(solution)/shard_map/pallas_call | solution.py:66
  69.0 10.7 %shard_map.90 = bf16[4,14,24,384]{3,2,1,0:T(8,128)(2,1)} custom-call(s32[1]{0:T(128)} %bitcast.57.core_ref, bf16[3,5,18,32,384]{4,3,2,1,0:T(8,128)(2,1)} %shard_map.89.cols, bf16[4,96,256]{2,1,0:T(8,128)(2,1)S(1)} %all-to-all-done.own_ref, bf16[4,96,256]{2,1,0:T(8,128)(2,1)S(1)} %collective-permute-done.9.peer_ref), custom_call_target="tpu_custom_call" | custom-call | flops 2113929216 | bytes 9437184 | tf_op jit(solution)/shard_map/pallas_call | solution.py:98
  79.8 1.3 collective-permute-start.11
  81.1 4.0 %collective-permute-start.10 = (bf16[2,1,32,384]{3,2,1,0:T(8,128)(2,1)S(1)}, bf16[2,1,32,384]{3,2,1,0:T(8,128)(2,1)S(1)}, u32[]{:S(2)}, u32[]{:S(2)}) collective-permute-start(bf16[2,1,32,384]{3,2,1,0:T(8,128)(2,1)S(1)} %get-tuple-element.120), channel_id=1, source_target_pairs={{0,4},{4,8},{8,12},{12,16},{16,20},{20,24},{24,28},{28,32},{32,36}... | collective-permute-start | bytes 147464 | tf_op jit(solution)/shard_map/ppermute | solution.py:33
  85.1 6.1 %all-to-all-start.1 = ((bf16[4,14,24,384]{3,2,1,0:T(8,128)(2,1)}), bf16[4,14,24,384]{3,2,1,0:T(8,128)(2,1)S(1)}, u32[]{:S(2)}, u32[]{:S(2)}) async-start(bf16[4,14,24,384]{3,2,1,0:T(8,128)(2,1)} %shard_map.90), calls=%async_computation.1 | async-start | bytes 2064384 | tf_op jit(solution)/shard_map/all_to_all | solution.py:115
  91.2 1.2 fusion.38
  92.5 1.2 fusion.33
  93.8 1.3 collective-permute-start.12
  95.1 4.0 %collective-permute-start.13 = (bf16[2,6,1,384]{3,2,1,0:T(2,128)(2,1)S(1)}, bf16[2,6,1,384]{3,2,1,0:T(2,128)(2,1)S(1)}, u32[]{:S(2)}, u32[]{:S(2)}) collective-permute-start(bf16[2,6,1,384]{3,2,1,0:T(2,128)(2,1)S(1)} %get-tuple-element.117), channel_id=1, source_target_pairs={{0,1},{1,2},{2,3},{4,5},{5,6},{6,7},{8,9},{9,10},{10,11},{12,13},{... | collective-permute-start | bytes 27656 | tf_op jit(solution)/shard_map/ppermute | solution.py:33
  99.1 1.2 fusion.36
  100.6 1.2 fusion.35
  101.8 1.2 fusion.37
  103.1 1.2 convolution_add_fusion.20
  104.4 1.2 convolution_add_fusion.19
  105.6 1.2 convolution_add_fusion.18
  106.8 1.2 convolution_add_fusion.17
  108.1 1.2 convolution_add_fusion.13
  109.3 1.2 convolution_add_fusion.12
  110.6 1.2 convolution_add_fusion.11
  111.8 1.2 convolution_add_fusion.10
  113.0 1.2 convolution_add_fusion.16
  114.3 1.2 convolution_add_fusion.9
  115.5 1.2 convolution_add_fusion.15
  116.8 1.2 convolution_add_fusion.8
  118.0 1.2 fusion.1
  119.3 1.2 fusion.2
  120.7 0.7 slice.662
  121.4 3.6 %collective-permute-start.14 = (bf16[2,4,32,384]{3,2,1,0:T(8,128)(2,1)}, bf16[2,4,32,384]{3,2,1,0:T(8,128)(2,1)}, u32[]{:S(2)}, u32[]{:S(2)}) collective-permute-start(bf16[2,4,32,384]{3,2,1,0:T(8,128)(2,1)} %slice.662), channel_id=1, source_target_pairs={{64,0},{128,64},{192,128},{65,1},{129,65},{193,129},{66,2},{130,66... | collective-permute-start | bytes 589832 | tf_op jit(solution)/shard_map/ppermute | solution.py:19
  125.0 1.2 convolution_add_fusion.6
  126.2 1.2 convolution_add_fusion.5
  127.5 1.2 convolution_add_fusion.4
  129.0 0.8 reshape.346
  129.8 13.6 %all-to-all-start.2 = ((bf16[8,42,384]{2,1,0:T(8,128)(2,1)}), bf16[8,42,384]{2,1,0:T(8,128)(2,1)S(1)}, u32[]{:S(2)}, u32[]{:S(2)}) async-start(bf16[8,42,384]{2,1,0:T(8,128)(2,1)} %reshape.346), calls=%async_computation.2 | async-start | bytes 589824 | tf_op jit(solution)/shard_map/all_to_all | solution.py:115
  143.3 1.2 convolution_add_fusion.3
  144.6 1.2 convolution_add_fusion.2
  145.8 10.7 %all-to-all-done.2 = bf16[8,42,384]{2,1,0:T(8,128)(2,1)S(1)} async-done(((bf16[8,42,384]{2,1,0:T(8,128)(2,1)}), bf16[8,42,384]{2,1,0:T(8,128)(2,1)S(1)}, u32[]{:S(2)}, u32[]{:S(2)}) %all-to-all-start.2) | async-done | bytes 258080 | tf_op jit(solution)/shard_map/all_to_all | solution.py:115
  156.5 0.7 broadcast_in_dim.2
  157.2 3.4 %all-to-all-start.3 = ((bf16[8,42,384]{2,1,0:T(8,128)(2,1)}), bf16[8,42,384]{2,1,0:T(8,128)(2,1)S(1)}, u32[]{:S(2)}, u32[]{:S(2)}) async-start(bf16[8,42,384]{2,1,0:T(8,128)(2,1)} %broadcast_in_dim.2), calls=%async_computation.3 | async-start | bytes 589824 | tf_op jit(solution)/shard_map/all_to_all | solution.py:115
  160.7 1.2 fusion.39
  161.9 1.2 convolution_add_fusion.1
  163.2 10.5 %all-to-all-done.3 = bf16[8,42,384]{2,1,0:T(8,128)(2,1)S(1)} async-done(((bf16[8,42,384]{2,1,0:T(8,128)(2,1)}), bf16[8,42,384]{2,1,0:T(8,128)(2,1)S(1)}, u32[]{:S(2)}, u32[]{:S(2)}) %all-to-all-start.3) | async-done | bytes 258080 | tf_op jit(solution)/shard_map/all_to_all | solution.py:115
  174.3 1.2 fusion.3
  175.5 1.7 fusion.16
  177.4 1.0 convert_bitcast_fusion
  (84 shorter events, 12.1 us)
Async XLA Ops:
  0.6 39.7 %copy-start = (bf16[2,4,32,384]{3,2,1,0:T(8,128)(2,1)S(1)}, bf16[2,4,32,384]{3,2,1,0:T(8,128)(2,1)}, u32[]{:S(2)}) copy-start(bf16[2,4,32,384]{3,2,1,0:T(8,128)(2,1)} %param.15) | copy-start | bytes 589828
  0.6 13.2 %collective-permute-start = (bf16[2,4,32,384]{3,2,1,0:T(8,128)(2,1)}, bf16[2,4,32,384]{3,2,1,0:T(8,128)(2,1)S(1)}, u32[]{:S(2)}, u32[]{:S(2)}) collective-permute-start(bf16[2,4,32,384]{3,2,1,0:T(8,128)(2,1)} %param.15), channel_id=1, source_target_pairs={{0,64},{64,128},{128,192},{1,65},{65,129},{129,193},{2,66},{66,130... | collective-permute-start | bytes 589832 | tf_op jit(solution)/shard_map/ppermute | solution.py:19
  14.8 6.2 %collective-permute-start.2 = (bf16[4,1,32,384]{3,2,1,0:T(8,128)(2,1)S(1)}, bf16[4,1,32,384]{3,2,1,0:T(8,128)(2,1)S(1)}, u32[]{:S(2)}, u32[]{:S(2)}) collective-permute-start(bf16[4,1,32,384]{3,2,1,0:T(8,128)(2,1)S(1)} %get-tuple-element.107), channel_id=1, source_target_pairs={{4,0},{8,4},{12,8},{16,12},{20,16},{24,20},{28,24},{32,28},{36,32}... | collective-permute-start | bytes 294920 | tf_op jit(solution)/shard_map/ppermute | solution.py:34
  16.1 5.6 %collective-permute-start.1 = (bf16[4,1,32,384]{3,2,1,0:T(8,128)(2,1)S(1)}, bf16[4,1,32,384]{3,2,1,0:T(8,128)(2,1)S(1)}, u32[]{:S(2)}, u32[]{:S(2)}) collective-permute-start(bf16[4,1,32,384]{3,2,1,0:T(8,128)(2,1)S(1)} %get-tuple-element.106), channel_id=1, source_target_pairs={{0,4},{4,8},{8,12},{12,16},{16,20},{20,24},{24,28},{28,32},{32,36}... | collective-permute-start | bytes 294920 | tf_op jit(solution)/shard_map/ppermute | solution.py:33
  21.0 20.3 %slice-start = ((s8[7962624]{0:T(1024)(128)(4,1)}), s8[4194304]{0:T(1024)(128)(4,1)S(1)}, s32[]{:S(2)}) async-start(s8[7962624]{0:T(1024)(128)(4,1)} %bitcast.251), calls=%async_computation.4 | async-start | bytes 8388608
  22.9 7.4 %collective-permute-start.3 = (bf16[4,6,1,384]{3,2,1,0:T(2,128)(2,1)S(1)}, bf16[4,6,1,384]{3,2,1,0:T(2,128)(2,1)S(1)}, u32[]{:S(2)}, u32[]{:S(2)}) collective-permute-start(bf16[4,6,1,384]{3,2,1,0:T(2,128)(2,1)S(1)} %get-tuple-element.94), channel_id=1, source_target_pairs={{0,1},{1,2},{2,3},{4,5},{5,6},{6,7},{8,9},{9,10},{10,11},{12,13},{... | collective-permute-start | bytes 55304 | tf_op jit(solution)/shard_map/ppermute | solution.py:33
  27.7 13.9 %copy-start.1 = (f32[384]{0:T(512)S(1)}, f32[384]{0:T(512)}, u32[]{:S(2)}) copy-start(f32[384]{0:T(512)} %param.18) | copy-start | bytes 4612
  27.7 5.0 %collective-permute-start.4 = (bf16[4,6,1,384]{3,2,1,0:T(2,128)(2,1)S(1)}, bf16[4,6,1,384]{3,2,1,0:T(2,128)(2,1)S(1)}, u32[]{:S(2)}, u32[]{:S(2)}) collective-permute-start(bf16[4,6,1,384]{3,2,1,0:T(2,128)(2,1)S(1)} %get-tuple-element.95), channel_id=1, source_target_pairs={{1,0},{2,1},{3,2},{5,4},{6,5},{7,6},{9,8},{10,9},{11,10},{13,12},{... | collective-permute-start | bytes 55304 | tf_op jit(solution)/shard_map/ppermute | solution.py:34
  34.2 7.1 %slice-start.1 = ((s8[7962624]{0:T(1024)(128)(4,1)}), s8[3768320]{0:T(1024)(128)(4,1)S(1)}, s32[]{:S(2)}) async-start(s8[7962624]{0:T(1024)(128)(4,1)} %bitcast.251), calls=%async_computation.5 | async-start | bytes 7536640
  34.2 26.4 %collective-permute-start.5 = (bf16[3,5,40,384]{3,2,1,0:T(8,128)(2,1)S(1)}, bf16[3,5,40,384]{3,2,1,0:T(8,128)(2,1)S(1)}, u32[]{:S(2)}, u32[]{:S(2)}) collective-permute-start(bf16[3,5,40,384]{3,2,1,0:T(8,128)(2,1)S(1)} %pad.14.refs_0_), channel_id=1, source_target_pairs={{0,4},{4,0},{8,12},{12,8},{1,5},{5,1},{9,13},{13,9},{2,6},{6,2},{1... | collective-permute-start | bytes 1382408 | tf_op jit(solution)/shard_map/ppermute | solution.py:23
  35.8 24.8 %collective-permute-start.6 = (bf16[3,5,40,384]{3,2,1,0:T(8,128)(2,1)S(1)}, bf16[3,5,40,384]{3,2,1,0:T(8,128)(2,1)S(1)}, u32[]{:S(2)}, u32[]{:S(2)}) collective-permute-start(bf16[3,5,40,384]{3,2,1,0:T(8,128)(2,1)S(1)} %pad.14.refs_0_), channel_id=1, source_target_pairs={{0,12},{4,8},{8,4},{12,0},{1,13},{5,9},{9,5},{13,1},{2,14},{6,10},... | collective-permute-start | bytes 1382408 | tf_op jit(solution)/shard_map/ppermute | solution.py:23
  39.3 21.4 %collective-permute-start.7 = (bf16[3,5,40,384]{3,2,1,0:T(8,128)(2,1)S(1)}, bf16[3,5,40,384]{3,2,1,0:T(8,128)(2,1)S(1)}, u32[]{:S(2)}, u32[]{:S(2)}) collective-permute-start(bf16[3,5,40,384]{3,2,1,0:T(8,128)(2,1)S(1)} %pad.14.refs_0_), channel_id=1, source_target_pairs={{0,8},{4,12},{8,0},{12,4},{1,9},{5,13},{9,1},{13,5},{2,10},{6,14},... | collective-permute-start | bytes 1382408 | tf_op jit(solution)/shard_map/ppermute | solution.py:23
  45.4 3.6 %copy-start.2 = (bf16[2,4,32,384]{3,2,1,0:T(8,128)(2,1)S(1)}, bf16[2,4,32,384]{3,2,1,0:T(8,128)(2,1)}, u32[]{:S(2)}) copy-start(bf16[2,4,32,384]{3,2,1,0:T(8,128)(2,1)} %param.19) | copy-start | bytes 589828
  52.1 8.5 %all-to-all-start = ((bf16[4,96,256]{2,1,0:T(8,128)(2,1)}), bf16[4,96,256]{2,1,0:T(8,128)(2,1)S(1)}, u32[]{:S(2)}, u32[]{:S(2)}) async-start(bf16[4,96,256]{2,1,0:T(8,128)(2,1)} %bitcast.59), calls=%async_computation | async-start | bytes 393216 | tf_op jit(solution)/shard_map/all_to_all | solution.py:115
  61.1 3.0 %collective-permute-start.8 = (bf16[4,2,5,40,384]{4,3,2,1,0:T(8,128)(2,1)S(1)}, bf16[4,2,5,40,384]{4,3,2,1,0:T(8,128)(2,1)S(1)}, u32[]{:S(2)}, u32[]{:S(2)}) collective-permute-start(bf16[4,2,5,40,384]{4,3,2,1,0:T(8,128)(2,1)S(1)} %pad_maximum_fusion), channel_id=1, source_target_pairs={{0,64},{64,0},{1,65},{65,1},{2,66},{66,2},{3,67},{67,3},{4,68},{68... | collective-permute-start | bytes 3686408 | tf_op jit(solution)/shard_map/ppermute | solution.py:23
  61.2 7.8 %collective-permute-start.9 = (bf16[4,96,256]{2,1,0:T(8,128)(2,1)S(1)}, bf16[4,96,256]{2,1,0:T(8,128)(2,1)S(1)}, u32[]{:S(2)}, u32[]{:S(2)}) collective-permute-start(bf16[4,96,256]{2,1,0:T(8,128)(2,1)S(1)} %all-to-all-done.own_ref), channel_id=1, source_target_pairs={{0,64},{64,0},{1,65},{65,1},{2,66},{66,2},{3,67},{67,3},{4,68},{68... | collective-permute-start | bytes 589832 | tf_op jit(solution)/shard_map/ppermute | solution.py:23
  79.8 11.4 %collective-permute-start.11 = (bf16[2,1,32,384]{3,2,1,0:T(8,128)(2,1)S(1)}, bf16[2,1,32,384]{3,2,1,0:T(8,128)(2,1)S(1)}, u32[]{:S(2)}, u32[]{:S(2)}) collective-permute-start(bf16[2,1,32,384]{3,2,1,0:T(8,128)(2,1)S(1)} %get-tuple-element.121), channel_id=1, source_target_pairs={{4,0},{8,4},{12,8},{16,12},{20,16},{24,20},{28,24},{32,28},{36,32}... | collective-permute-start | bytes 147464 | tf_op jit(solution)/shard_map/ppermute | solution.py:34
  81.1 10.1 %collective-permute-start.10 = (bf16[2,1,32,384]{3,2,1,0:T(8,128)(2,1)S(1)}, bf16[2,1,32,384]{3,2,1,0:T(8,128)(2,1)S(1)}, u32[]{:S(2)}, u32[]{:S(2)}) collective-permute-start(bf16[2,1,32,384]{3,2,1,0:T(8,128)(2,1)S(1)} %get-tuple-element.120), channel_id=1, source_target_pairs={{0,4},{4,8},{8,12},{12,16},{16,20},{20,24},{24,28},{28,32},{32,36}... | collective-permute-start | bytes 147464 | tf_op jit(solution)/shard_map/ppermute | solution.py:33
  85.1 43.7 %all-to-all-start.1 = ((bf16[4,14,24,384]{3,2,1,0:T(8,128)(2,1)}), bf16[4,14,24,384]{3,2,1,0:T(8,128)(2,1)S(1)}, u32[]{:S(2)}, u32[]{:S(2)}) async-start(bf16[4,14,24,384]{3,2,1,0:T(8,128)(2,1)} %shard_map.90), calls=%async_computation.1 | async-start | bytes 2064384 | tf_op jit(solution)/shard_map/all_to_all | solution.py:115
  93.8 6.5 %collective-permute-start.12 = (bf16[2,6,1,384]{3,2,1,0:T(2,128)(2,1)S(1)}, bf16[2,6,1,384]{3,2,1,0:T(2,128)(2,1)S(1)}, u32[]{:S(2)}, u32[]{:S(2)}) collective-permute-start(bf16[2,6,1,384]{3,2,1,0:T(2,128)(2,1)S(1)} %get-tuple-element.116), channel_id=1, source_target_pairs={{1,0},{2,1},{3,2},{5,4},{6,5},{7,6},{9,8},{10,9},{11,10},{13,12},{... | collective-permute-start | bytes 27656 | tf_op jit(solution)/shard_map/ppermute | solution.py:34
  95.1 5.2 %collective-permute-start.13 = (bf16[2,6,1,384]{3,2,1,0:T(2,128)(2,1)S(1)}, bf16[2,6,1,384]{3,2,1,0:T(2,128)(2,1)S(1)}, u32[]{:S(2)}, u32[]{:S(2)}) collective-permute-start(bf16[2,6,1,384]{3,2,1,0:T(2,128)(2,1)S(1)} %get-tuple-element.117), channel_id=1, source_target_pairs={{0,1},{1,2},{2,3},{4,5},{5,6},{6,7},{8,9},{9,10},{10,11},{12,13},{... | collective-permute-start | bytes 27656 | tf_op jit(solution)/shard_map/ppermute | solution.py:33
  121.4 54.2 %collective-permute-start.14 = (bf16[2,4,32,384]{3,2,1,0:T(8,128)(2,1)}, bf16[2,4,32,384]{3,2,1,0:T(8,128)(2,1)}, u32[]{:S(2)}, u32[]{:S(2)}) collective-permute-start(bf16[2,4,32,384]{3,2,1,0:T(8,128)(2,1)} %slice.662), channel_id=1, source_target_pairs={{64,0},{128,64},{192,128},{65,1},{129,65},{193,129},{66,2},{130,66... | collective-permute-start | bytes 589832 | tf_op jit(solution)/shard_map/ppermute | solution.py:19
  129.8 26.7 %all-to-all-start.2 = ((bf16[8,42,384]{2,1,0:T(8,128)(2,1)}), bf16[8,42,384]{2,1,0:T(8,128)(2,1)S(1)}, u32[]{:S(2)}, u32[]{:S(2)}) async-start(bf16[8,42,384]{2,1,0:T(8,128)(2,1)} %reshape.346), calls=%async_computation.2 | async-start | bytes 589824 | tf_op jit(solution)/shard_map/all_to_all | solution.py:115
  157.2 16.4 %all-to-all-start.3 = ((bf16[8,42,384]{2,1,0:T(8,128)(2,1)}), bf16[8,42,384]{2,1,0:T(8,128)(2,1)S(1)}, u32[]{:S(2)}, u32[]{:S(2)}) async-start(bf16[8,42,384]{2,1,0:T(8,128)(2,1)} %broadcast_in_dim.2), calls=%async_computation.3 | async-start | bytes 589824 | tf_op jit(solution)/shard_map/all_to_all | solution.py:115
  173.7 3.5 %collective-permute-start.15 = (bf16[14,24,384]{2,1,0:T(8,128)(2,1)S(1)}, bf16[14,24,384]{2,1,0:T(8,128)(2,1)S(1)}, u32[]{:S(2)}, u32[]{:S(2)}) collective-permute-start(bf16[14,24,384]{2,1,0:T(8,128)(2,1)S(1)} %reshape.347), channel_id=1, source_target_pairs={{0,64},{64,0},{1,65},{65,1},{2,66},{66,2},{3,67},{67,3},{4,68},{68... | collective-permute-start | bytes 774152 | tf_op jit(solution)/shard_map/ppermute | solution.py:23

commit v4 on v3

--- a/solution.py
+++ b/solution.py
@@ -57,24 +57,15 @@
 
 
 def spread(where, lines, peer):
-    shape = (3, 5, 18, 32, 384)
-    args = (*lines, peer)
-
-    def whole(shape):
-        return pl.BlockSpec(shape, lambda i, *_: (0,) * len(shape))
-
     return pl.pallas_call(
         spread_kernel,
-        out_shape=jax.ShapeDtypeStruct(shape, BF),
-        grid_spec=pltpu.PrefetchScalarGridSpec(
-            num_scalar_prefetch=1,
-            grid=(1,),
-            in_specs=[whole(a.shape) for a in args],
-            out_specs=whole(shape),
-        ),
-        compiler_params=pltpu.CompilerParams(vmem_limit_bytes=48 << 20),
+        out_shape=jax.ShapeDtypeStruct((3, 5, 18, 32, 384), BF),
+        in_specs=[pl.BlockSpec(memory_space=pltpu.SMEM)]
+        + [pl.BlockSpec(memory_space=pltpu.VMEM)] * 5,
+        out_specs=pl.BlockSpec(memory_space=pltpu.VMEM),
+        compiler_params=pltpu.CompilerParams(vmem_limit_bytes=14 << 20),
         cost_estimate=pl.CostEstimate(flops=0, bytes_accessed=12 << 20, transcendentals=0),
-    )(where, *args)
+    )(where, *lines, peer)
 
 
 def weight_grad_kernel(core_ref, cols, own_ref, peer_ref, out_ref):
@@ -92,23 +83,67 @@
 
 
 def weight_grad(core, cols, own, peer):
-    def whole(a):
-        return pl.BlockSpec(a.shape, lambda j, *_: (0,) * a.ndim)
-
     return pl.pallas_call(
         weight_grad_kernel,
         out_shape=jax.ShapeDtypeStruct((4, N_TAPS, 24, 384), BF),
         grid_spec=pltpu.PrefetchScalarGridSpec(
             num_scalar_prefetch=1,
             grid=(N_TAPS,),
-            in_specs=[whole(a) for a in (cols, own, peer)],
+            in_specs=[pl.BlockSpec(memory_space=pltpu.VMEM)] * 3,
             out_specs=pl.BlockSpec((4, 1, 24, 384), lambda j, *_: (0, j, 0, 0)),
         ),
-        compiler_params=pltpu.CompilerParams(vmem_limit_bytes=48 << 20),
+        compiler_params=pltpu.CompilerParams(vmem_limit_bytes=14 << 20),
         cost_estimate=pl.CostEstimate(
             flops=2 * N_TAPS * 384 * 384 * 512, bytes_accessed=9 << 20, transcendentals=0
         ),
     )(core, cols, own, peer)
+
+
+def input_grad_kernel(rim_ref, weight_ref, head_ref, tail_ref, cols, total):
+    step = pl.program_id(0)
+
+    @pl.when(step == 0)
+    def _():
+        total[...] = jnp.zeros_like(total)
+        for c in range(3):
+            cols[c] = rim_ref[:, :, 2 - c : 34 - c, :]
+
+    tap_t, tap_h = step // 3, step % 3
+    term = None
+    for c in range(3):
+        block = cols[c, :, pl.ds(2 - tap_h, 4)].reshape(256, 384)
+        part = jnp.dot(block, weight_ref[0, 0, c], preferred_element_type=F32)
+        term = part if term is None else term + part
+    total[pl.ds(tap_t, 2)] += term.reshape(2, 128, 384)
+
+    @pl.when(step == 8)
+    def _():
+        head_ref[...] = total[:2].astype(BF)
+        tail_ref[...] = total[2:]
+
+
+def input_grad(rimmed, weights):
+    def whole(shape):
+        return pl.BlockSpec(shape, lambda j: (0,) * len(shape))
+
+    return pl.pallas_call(
+        input_grad_kernel,
+        out_shape=[
+            jax.ShapeDtypeStruct((2, 128, 384), BF),
+            jax.ShapeDtypeStruct((2, 128, 384), F32),
+        ],
+        grid=(9,),
+        in_specs=[
+            pl.BlockSpec(memory_space=pltpu.VMEM),
+            pl.BlockSpec((1, 1, 3, 384, 384), lambda j: (j // 3, j % 3, 0, 0, 0)),
+        ],
+        out_specs=[whole((2, 128, 384)), whole((2, 128, 384))],
+        scratch_shapes=[pltpu.VMEM((3, 2, 6, 32, 384), BF), pltpu.VMEM((4, 128, 384), F32)],
+        compiler_params=pltpu.CompilerParams(vmem_limit_bytes=60 << 20),
+        cost_estimate=pl.CostEstimate(
+            flops=2 * 27 * 256 * 384 * 384, bytes_accessed=9 << 20, transcendentals=0
+        ),
+    )(rimmed, weights)
 
 
 def across(value, axes):
@@ -127,6 +162,10 @@
     frame_count, row_count, col_count, channels = frames.shape
     core = lax.axis_index("co")
     is_first = lax.axis_index(TM) == 0
+    row = lax.broadcasted_iota(jnp.int32, (channels, channels), 0)
+    col = lax.broadcasted_iota(jnp.int32, (channels, channels), 1)
+    order = (row // 24 % 4 * 96 + row // 96 * 24 + row % 24 == col).astype(BF)
+    order, frames = lax.optimization_barrier((order, frames))
     weights = kernel.transpose(1, 2, 3, 0, 4)
     earlier = shifted(frames, TM, 1)
     earlier = jnp.where(is_first, cache_in, earlier)
@@ -138,9 +177,15 @@
         (3, 5, col_count + 2, channels),
     )
     rows = jnp.pad(rows, ((0, 0), (0, 0), (0, 6), (0, 0)))
-    line = [rows] + [exchanged(rows, "y", flip) for flip in (1, 3, 2)]
+    near = [exchanged(rows, "y", flip) for flip in (1, 3)]
     pre_act = jnp.zeros((frame_count * row_count * col_count, channels), F32) + conv_bias
     for tap_t in range(3):
+        if tap_t == 2:
+            pre_act, *near = lax.optimization_barrier((pre_act, *near))
+            far = [
+                exchanged(near[0][:, :, :16], "y", 3),
+                exchanged(near[1][:, :, 16:], "y", 1),
+            ]
         for tap_h in range(3):
             for tap_w in range(3):
                 block = tap_block(extended, tap_t, tap_h, tap_w, frame_count, row_count, col_count)
@@ -155,12 +200,10 @@
     scaled = (
         cotangent.reshape(-1, channels).astype(F32) * sigma * (1.0 + pre_act * (1.0 - sigma))
     ).astype(BF)
-    row = lax.broadcasted_iota(jnp.int32, (channels, channels), 0)
-    col = lax.broadcasted_iota(jnp.int32, (channels, channels), 1)
-    order = (row // 24 % 4 * 96 + row // 96 * 24 + row % 24 == col).astype(BF)
     own = lax.dot_general(order, scaled, (((1,), (1,)), ((), ())), preferred_element_type=F32)
-    own = across(own.astype(BF).reshape(4, 96, -1), "y")
-    own, *line = lax.optimization_barrier((own, *line))
+    own, *far = lax.optimization_barrier((own.astype(BF).reshape(4, 96, -1), *far))
+    own = across(own, "y")
+    line = [rows, *near, jnp.concatenate(far, 2)]
     line_peer = jnp.stack([jnp.where(core == 0, v[1:3], v[0:2]) for v in line])
     line_peer = exchanged(line_peer, "co", 1)
     cols = spread(jnp.stack([core, lax.axis_index("y")]), line, line_peer)
@@ -176,26 +219,14 @@
     ).astype(F32)
     kernel_grad = taps.reshape(3, 3, 3, 24, channels).transpose(3, 0, 1, 2, 4)
 
-    grad_rimmed = with_halo(scaled.reshape(frames.shape), ((HEIGHT, 1), ("z", 2)), 1)
-    partial_value = jnp.zeros((frame_count + 2, row_count, col_count, channels), F32)
-    for tap_t in range(3):
-        contrib = jnp.zeros((frame_count * row_count * col_count, channels), F32)
-        for tap_h in range(3):
-            for tap_w in range(3):
-                block = grad_rimmed[
-                    :, 2 - tap_h : 2 - tap_h + row_count, 2 - tap_w : 2 - tap_w + col_count
-                ].reshape(-1, channels)
-                contrib = contrib + jnp.dot(
-                    block, weights[tap_t, tap_h, tap_w], preferred_element_type=F32
-                )
-        partial_value = partial_value.at[tap_t : tap_t + frame_count].add(
-            contrib.reshape(frame_count, row_count, col_count, channels)
-        )
-    cache_grad = partial_value[:2].astype(BF)
+    tall = with_halo(scaled.reshape(frames.shape), ((HEIGHT, 1),), 1)
+    left = shifted(tall[:, :, -1:], "z", 1)
+    right = shifted(tall[:, :, :1], "z", -1)
+    grad_rimmed = jnp.concatenate([left, tall, right], 2)
+    head, tail = input_grad(grad_rimmed, weights)
+    cache_grad = head.reshape(frames.shape)
     carried = shifted(cache_grad, TM, -1)
-    frame_grad = (
-        partial_value[2:].at[frame_count - 2 :].add(carried.astype(F32)).astype(BF)
-    )
+    frame_grad = (tail.reshape(frames.shape) + carried.astype(F32)).astype(BF)
     return (decoded, frame_grad, cache_grad, kernel_grad)
 
 

time: 181 us -> 158 us (0.87)
  the two profiles are of different devices: /device:TPU:1 before, /device:TPU:35 now
where the time goes in v4:
time: 158 us; the launch traced here: 157 us
  starting transfers between devices  57.4 us (36%)
  waiting for transfers between devices  29 us (18%)
  blocking collectives  26.4 us (17%)
  Pallas kernels  18.4 us (12%)
  other arithmetic  11.1 us (7%)
  matrix products  9.86 us (6%)
  local copies, waits for them, and re-layouts  3.37 us (2%)
    all_to_all x2, blocking collectives, across(): return lax.all_to_all(value, axes, 0, 0, tiled=True)  26.4 us
    ppermute x4, starting transfers between devices, shifted(): return lax.ppermute(value, axis, pairs)  19.9 us
    all_to_all x2, starting transfers between devices, across(): return lax.all_to_all(value, axes, 0, 0, tiled=True)  16.8 us
    ppermute x4, waiting for transfers between devices, shifted(): return lax.ppermute(value, axis, pairs)  14.5 us
    ppermute x3, starting transfers between devices, with_halo(): after = lax.ppermute(initial, axis, down)  10.2 us
    ppermute x3, waiting for transfers between devices, with_halo(): before = lax.ppermute(last, axis, up)  9.91 us
    pallas_call x1, Pallas kernels, input_grad(): pl.pallas_call(input_grad_kernel, out_shape=[jax.ShapeDtypeStruct((2, 128...  9.75 us
    dot_general x27, matrix products, program(): lax.dot_general(block, weights[tap_t, tap_h, tap_w], (((1,), (1,)), ((),...  9.58 us
  transfers between devices with their start and end apart: 19, of which 7 were waited for; matrix products, arithmetic and copies ran while one was open for 11% of the time, Pallas kernels for 8%

profile of v4, /device:TPU:35, one launch (start us, length us, event | category | flops | bytes accessed | tf_op | source)
XLA Modules:
  0.0 156.8 jit_solution(937334608686254865)
XLA Ops:
  0.7 0.7 fusion.6
  1.5 8.5 %collective-permute-start = (bf16[2,4,32,384]{3,2,1,0:T(8,128)(2,1)}, bf16[2,4,32,384]{3,2,1,0:T(8,128)(2,1)S(1)}, u32[]{:S(2)}, u32[]{:S(2)}) collective-permute-start(bf16[2,4,32,384]{3,2,1,0:T(8,128)(2,1)} %param.5), channel_id=1, source_target_pairs={{0,64},{64,128},{128,192},{1,65},{65,129},{129,193},{2,66},{66,130... | collective-permute-start | bytes 589832 | tf_op jit(solution)/shard_map/ppermute | solution.py:19
  10.0 5.0 %collective-permute-done = bf16[2,4,32,384]{3,2,1,0:T(8,128)(2,1)S(1)} collective-permute-done((bf16[2,4,32,384]{3,2,1,0:T(8,128)(2,1)}, bf16[2,4,32,384]{3,2,1,0:T(8,128)(2,1)S(1)}, u32[]{:S(2)}, u32[]{:S(2)}) %collective-permute-start) | collective-permute-done | bytes 196640 | tf_op jit(solution)/shard_map/ppermute | solution.py:19
  15.0 0.9 pad_maximum_fusion.6
  15.9 4.6 %collective-permute-start.2 = (bf16[4,1,32,384]{3,2,1,0:T(8,128)(2,1)S(1)}, bf16[4,1,32,384]{3,2,1,0:T(8,128)(2,1)S(1)}, u32[]{:S(2)}, u32[]{:S(2)}) collective-permute-start(bf16[4,1,32,384]{3,2,1,0:T(8,128)(2,1)S(1)} %get-tuple-element.61), channel_id=1, source_target_pairs={{4,0},{8,4},{12,8},{16,12},{20,16},{24,20},{28,24},{32,28},{36,32}... | collective-permute-start | bytes 294920 | tf_op jit(solution)/shard_map/ppermute | solution.py:34
  20.5 1.9 %collective-permute-start.1 = (bf16[4,1,32,384]{3,2,1,0:T(8,128)(2,1)S(1)}, bf16[4,1,32,384]{3,2,1,0:T(8,128)(2,1)S(1)}, u32[]{:S(2)}, u32[]{:S(2)}) collective-permute-start(bf16[4,1,32,384]{3,2,1,0:T(8,128)(2,1)S(1)} %get-tuple-element.60), channel_id=1, source_target_pairs={{0,4},{4,8},{8,12},{12,16},{16,20},{20,24},{24,28},{28,32},{32,36}... | collective-permute-start | bytes 294920 | tf_op jit(solution)/shard_map/ppermute | solution.py:33
  22.4 0.9 pad_maximum_fusion.4
  23.3 4.6 %collective-permute-done.1 = bf16[4,1,32,384]{3,2,1,0:T(8,128)(2,1)S(1)} collective-permute-done((bf16[4,1,32,384]{3,2,1,0:T(8,128)(2,1)S(1)}, bf16[4,1,32,384]{3,2,1,0:T(8,128)(2,1)S(1)}, u32[]{:S(2)}, u32[]{:S(2)}) %collective-permute-start.1) | collective-permute-done | bytes 98336 | tf_op jit(solution)/shard_map/ppermute | solution.py:33
  27.9 0.9 pad_maximum_fusion.7
  28.8 1.9 %collective-permute-start.4 = (bf16[4,6,1,384]{3,2,1,0:T(2,128)(2,1)S(1)}, bf16[4,6,1,384]{3,2,1,0:T(2,128)(2,1)S(1)}, u32[]{:S(2)}, u32[]{:S(2)}) collective-permute-start(bf16[4,6,1,384]{3,2,1,0:T(2,128)(2,1)S(1)} %get-tuple-element.48), channel_id=1, source_target_pairs={{1,0},{2,1},{3,2},{5,4},{6,5},{7,6},{9,8},{10,9},{11,10},{13,12},{... | collective-permute-start | bytes 55304 | tf_op jit(solution)/shard_map/ppermute | solution.py:34
  30.8 3.6 %collective-permute-start.3 = (bf16[4,6,1,384]{3,2,1,0:T(2,128)(2,1)S(1)}, bf16[4,6,1,384]{3,2,1,0:T(2,128)(2,1)S(1)}, u32[]{:S(2)}, u32[]{:S(2)}) collective-permute-start(bf16[4,6,1,384]{3,2,1,0:T(2,128)(2,1)S(1)} %get-tuple-element.49), channel_id=1, source_target_pairs={{0,1},{1,2},{2,3},{4,5},{5,6},{6,7},{8,9},{9,10},{10,11},{12,13},{... | collective-permute-start | bytes 55304 | tf_op jit(solution)/shard_map/ppermute | solution.py:33
  34.4 1.1 pad_maximum_fusion.2
  35.6 1.3 fusion.16
  37.0 1.5 fusion.8
  38.8 0.4 pad_maximum_fusion.1
  39.7 0.9 slice-done.1
  40.6 0.3 fusion.15
  41.3 0.3 convolution_add_fusion.22
  41.6 0.3 convolution_add_fusion.21
  41.9 0.3 convolution_add_fusion.20
  42.2 0.3 convolution_add_fusion.19
  42.5 0.3 fusion
  42.8 0.3 convolution_add_fusion.17
  43.1 0.3 convolution_add_fusion.16
  43.4 0.3 convolution_add_fusion.15
  43.7 0.3 convolution_add_fusion.14
  44.0 0.3 convolution_add_fusion.13
  44.3 0.3 convolution_add_fusion.12
  44.6 0.3 convolution_add_fusion.11
  44.9 0.3 convolution_add_fusion.10
  45.2 0.3 convolution_add_fusion.9
  45.5 0.3 convolution_add_fusion.8
  45.8 0.3 convolution_add_fusion.7
  46.1 0.3 fusion.17
  46.6 0.6 collective-permute-done.5.refs_1_
  47.2 1.9 %collective-permute-done.6.refs_2_ = bf16[3,5,40,384]{3,2,1,0:T(8,128)(2,1)S(1)} collective-permute-done((bf16[3,5,40,384]{3,2,1,0:T(8,128)(2,1)S(1)}, bf16[3,5,40,384]{3,2,1,0:T(8,128)(2,1)S(1)}, u32[]{:S(2)}, u32[]{:S(2)}) %collective-permute-start.6) | collective-permute-done | bytes 460832 | tf_op jit(solution)/shard_map/ppermute | solution.py:23
  49.3 0.6 collective-permute-start.8
  50.0 0.3 convolution_add_fusion.5
  50.3 0.3 convolution_add_fusion.4
  50.6 0.3 convolution_add_fusion.3
  50.9 0.3 convolution_add_fusion.2
  51.2 0.3 convolution_add_fusion.1
  51.5 1.1 fusion.13
  52.9 2.0 %collective-permute-done.7 = bf16[3,5,16,384]{3,2,1,0:T(8,128)(2,1)S(1)} collective-permute-done((bf16[3,5,16,384]{3,2,1,0:T(8,128)(2,1)S(1)}, bf16[3,5,16,384]{3,2,1,0:T(8,128)(2,1)S(1)}, u32[]{:S(2)}, u32[]{:S(2)}) %collective-permute-start.7) | collective-permute-done | bytes 184352 | tf_op jit(solution)/shard_map/ppermute | solution.py:23
  55.4 8.7 %all_to_all.20.own_ref = bf16[4,96,256]{2,1,0:T(8,128)(2,1)S(1)} all-to-all(bf16[4,96,256]{2,1,0:T(8,128)(2,1)S(1)} %bitcast.222), channel_id=1, replica_groups=mesh['zh'=2,'co'=2,'x'=4,'y'=4,'z'=4] {'y'}, dimensions={0} | all-to-all | bytes 393216 | tf_op jit(solution)/shard_map/all_to_all | solution.py:150
  64.1 1.9 %collective-permute-start.10 = (bf16[4,96,256]{2,1,0:T(8,128)(2,1)S(1)}, bf16[4,96,256]{2,1,0:T(8,128)(2,1)S(1)}, u32[]{:S(2)}, u32[]{:S(2)}) collective-permute-start(bf16[4,96,256]{2,1,0:T(8,128)(2,1)S(1)} %all_to_all.20.own_ref), channel_id=1, source_target_pairs={{0,64},{64,0},{1,65},{65,1},{2,66},{66,2},{3,67},{67,3},{4,68},{68... | collective-permute-start | bytes 589832 | tf_op jit(solution)/shard_map/ppermute | solution.py:23
  66.1 2.2 %shard_map.84.cols = bf16[3,5,18,32,384]{4,3,2,1,0:T(8,128)(2,1)S(1)} custom-call(s32[2]{0:T(128)S(1)} %pad_add_fusion.where_ref, bf16[3,5,40,384]{3,2,1,0:T(8,128)(2,1)S(1)} %pad.4.refs_0_, bf16[3,5,40,384]{3,2,1,0:T(8,128)(2,1)S(1)} %collective-permute-done.5.refs_1_, bf16[3,5,40,384]{3,2,1,0:T(8,128)(2,1)S(1)} %collective-permute-done.6.refs_2_, ...), custom_call_target="tpu_custom_call" | custom-call | bytes 12582912 | tf_op jit(solution)/shard_map/pallas_call | solution.py:60
  68.3 6.5 %shard_map.85 = bf16[4,14,24,384]{3,2,1,0:T(8,128)(2,1)S(1)} custom-call(s32[1]{0:T(128)} %bitcast.57.core_ref, bf16[3,5,18,32,384]{4,3,2,1,0:T(8,128)(2,1)S(1)} %shard_map.84.cols, bf16[4,96,256]{2,1,0:T(8,128)(2,1)S(1)} %all_to_all.20.own_ref, bf16[4,96,256]{2,1,0:T(8,128)(2,1)S(1)} %collective-permute-done.10.peer_ref), custom_call_target="tpu_custom_call" | custom-call | flops 2113929216 | bytes 9437184 | tf_op jit(solution)/shard_map/pallas_call | solution.py:86
  74.7 17.6 %all_to_all.21 = bf16[4,14,24,384]{3,2,1,0:T(8,128)(2,1)S(1)} all-to-all(bf16[4,14,24,384]{3,2,1,0:T(8,128)(2,1)S(1)} %shard_map.85), channel_id=1, replica_groups=mesh['zh'=2,'co'=2,'x'=4,'y'=4,'z'=4] {'x'}, dimensions={0} | all-to-all | bytes 2064384 | tf_op jit(solution)/shard_map/all_to_all | solution.py:150
  92.6 0.8 reshape.157
  93.4 10.5 %all-to-all-start.2 = ((bf16[8,42,384]{2,1,0:T(8,128)(2,1)}), bf16[8,42,384]{2,1,0:T(8,128)(2,1)S(1)}, u32[]{:S(2)}, u32[]{:S(2)}) async-start(bf16[8,42,384]{2,1,0:T(8,128)(2,1)} %reshape.157), calls=%async_computation.2 | async-start | bytes 589824 | tf_op jit(solution)/shard_map/all_to_all | solution.py:150
  103.9 3.7 %collective-permute-start.12 = (bf16[2,1,32,384]{3,2,1,0:T(8,128)(2,1)S(1)}, bf16[2,1,32,384]{3,2,1,0:T(8,128)(2,1)S(1)}, u32[]{:S(2)}, u32[]{:S(2)}) collective-permute-start(bf16[2,1,32,384]{3,2,1,0:T(8,128)(2,1)S(1)} %get-tuple-element.65), channel_id=1, source_target_pairs={{4,0},{8,4},{12,8},{16,12},{20,16},{24,20},{28,24},{32,28},{36,32}... | collective-permute-start | bytes 147464 | tf_op jit(solution)/shard_map/ppermute | solution.py:34
  107.6 1.9 %collective-permute-start.11 = (bf16[2,1,32,384]{3,2,1,0:T(8,128)(2,1)S(1)}, bf16[2,1,32,384]{3,2,1,0:T(8,128)(2,1)S(1)}, u32[]{:S(2)}, u32[]{:S(2)}) collective-permute-start(bf16[2,1,32,384]{3,2,1,0:T(8,128)(2,1)S(1)} %get-tuple-element.64), channel_id=1, source_target_pairs={{0,4},{4,8},{8,12},{12,16},{16,20},{20,24},{24,28},{28,32},{32,36}... | collective-permute-start | bytes 147464 | tf_op jit(solution)/shard_map/ppermute | solution.py:33
  109.5 5.3 %collective-permute-done.11 = bf16[2,1,32,384]{3,2,1,0:T(8,128)(2,1)S(1)} collective-permute-done((bf16[2,1,32,384]{3,2,1,0:T(8,128)(2,1)S(1)}, bf16[2,1,32,384]{3,2,1,0:T(8,128)(2,1)S(1)}, u32[]{:S(2)}, u32[]{:S(2)}) %collective-permute-start.11) | collective-permute-done | bytes 49184 | tf_op jit(solution)/shard_map/ppermute | solution.py:33
  114.8 1.9 %collective-permute-start.14 = (bf16[2,6,1,384]{3,2,1,0:T(2,128)(2,1)S(1)}, bf16[2,6,1,384]{3,2,1,0:T(2,128)(2,1)S(1)}, u32[]{:S(2)}, u32[]{:S(2)}) collective-permute-start(bf16[2,6,1,384]{3,2,1,0:T(2,128)(2,1)S(1)} %get-tuple-element.63), channel_id=1, source_target_pairs={{1,0},{2,1},{3,2},{5,4},{6,5},{7,6},{9,8},{10,9},{11,10},{13,12},{... | collective-permute-start | bytes 27656 | tf_op jit(solution)/shard_map/ppermute | solution.py:19
  116.8 3.4 %collective-permute-start.13 = (bf16[2,6,1,384]{3,2,1,0:T(2,128)(2,1)S(1)}, bf16[2,6,1,384]{3,2,1,0:T(2,128)(2,1)S(1)}, u32[]{:S(2)}, u32[]{:S(2)}) collective-permute-start(bf16[2,6,1,384]{3,2,1,0:T(2,128)(2,1)S(1)} %get-tuple-element.62), channel_id=1, source_target_pairs={{0,1},{1,2},{2,3},{4,5},{5,6},{6,7},{8,9},{9,10},{10,11},{12,13},{... | collective-permute-start | bytes 27656 | tf_op jit(solution)/shard_map/ppermute | solution.py:19
  120.2 0.7 broadcast_in_dim.4
  121.0 6.3 %all-to-all-start.3 = ((bf16[8,42,384]{2,1,0:T(8,128)(2,1)}), bf16[8,42,384]{2,1,0:T(8,128)(2,1)S(1)}, u32[]{:S(2)}, u32[]{:S(2)}) async-start(bf16[8,42,384]{2,1,0:T(8,128)(2,1)} %broadcast_in_dim.4), calls=%async_computation.3 | async-start | bytes 589824 | tf_op jit(solution)/shard_map/all_to_all | solution.py:150
  127.3 0.9 pad_maximum_fusion.3.rim_ref
  128.2 9.7 %shard_map.86 = (bf16[2,128,384]{2,1,0:T(8,128)(2,1)}, f32[2,128,384]{2,1,0:T(8,128)}) custom-call(bf16[2,6,34,384]{3,2,1,0:T(8,128)(2,1)} %pad_maximum_fusion.3.rim_ref, bf16[3,3,3,384,384]{4,3,2,1,0:T(8,128)(2,1)} %bitcast.163), custom_call_target="tpu_custom_call" | custom-call | flops 2038431744 | bytes 9437184 | tf_op jit(solution)/shard_map/pallas_call | solution.py:129
  138.0 6.2 %collective-permute-start.15 = (bf16[2,4,32,384]{3,2,1,0:T(8,128)(2,1)}, bf16[2,4,32,384]{3,2,1,0:T(8,128)(2,1)S(1)}, u32[]{:S(2)}, u32[]{:S(2)}) collective-permute-start(bf16[2,4,32,384]{3,2,1,0:T(8,128)(2,1)} %bitcast.225), channel_id=1, source_target_pairs={{64,0},{128,64},{192,128},{65,1},{129,65},{193,129},{66,2},{130,66... | collective-permute-start | bytes 589832 | tf_op jit(solution)/shard_map/ppermute | solution.py:19
  144.3 9.5 %collective-permute-done.15 = bf16[2,4,32,384]{3,2,1,0:T(8,128)(2,1)S(1)} collective-permute-done((bf16[2,4,32,384]{3,2,1,0:T(8,128)(2,1)}, bf16[2,4,32,384]{3,2,1,0:T(8,128)(2,1)S(1)}, u32[]{:S(2)}, u32[]{:S(2)}) %collective-permute-start.15) | collective-permute-done | bytes 196640 | tf_op jit(solution)/shard_map/ppermute | solution.py:19
  153.9 1.7 %add_convert_fusion = bf16[2,4,32,384]{3,2,1,0:T(8,128)(2,1)} fusion(f32[2,4,32,384]{3,2,1,0:T(8,128)} %bitcast.223, bf16[2,4,32,384]{3,2,1,0:T(8,128)(2,1)S(1)} %collective-permute-done.15), kind=kLoop, calls=%fused_computation.57 | loop fusion | flops 294912 | bytes 786432 | tf_op jit(solution)/shard_map/convert_element_type | solution.py:229
  155.8 1.0 convert_bitcast_fusion
  (59 shorter events, 3.3 us)
Async XLA Ops:
  0.6 38.1 %copy-start = (bf16[2,4,32,384]{3,2,1,0:T(8,128)(2,1)S(1)}, bf16[2,4,32,384]{3,2,1,0:T(8,128)(2,1)}, u32[]{:S(2)}) copy-start(bf16[2,4,32,384]{3,2,1,0:T(8,128)(2,1)} %param.5) | copy-start | bytes 589828
  1.5 13.5 %collective-permute-start = (bf16[2,4,32,384]{3,2,1,0:T(8,128)(2,1)}, bf16[2,4,32,384]{3,2,1,0:T(8,128)(2,1)S(1)}, u32[]{:S(2)}, u32[]{:S(2)}) collective-permute-start(bf16[2,4,32,384]{3,2,1,0:T(8,128)(2,1)} %param.5), channel_id=1, source_target_pairs={{0,64},{64,128},{128,192},{1,65},{65,129},{129,193},{2,66},{66,130... | collective-permute-start | bytes 589832 | tf_op jit(solution)/shard_map/ppermute | solution.py:19
  15.9 7.5 %collective-permute-start.2 = (bf16[4,1,32,384]{3,2,1,0:T(8,128)(2,1)S(1)}, bf16[4,1,32,384]{3,2,1,0:T(8,128)(2,1)S(1)}, u32[]{:S(2)}, u32[]{:S(2)}) collective-permute-start(bf16[4,1,32,384]{3,2,1,0:T(8,128)(2,1)S(1)} %get-tuple-element.61), channel_id=1, source_target_pairs={{4,0},{8,4},{12,8},{16,12},{20,16},{24,20},{28,24},{32,28},{36,32}... | collective-permute-start | bytes 294920 | tf_op jit(solution)/shard_map/ppermute | solution.py:34
  20.5 7.5 %collective-permute-start.1 = (bf16[4,1,32,384]{3,2,1,0:T(8,128)(2,1)S(1)}, bf16[4,1,32,384]{3,2,1,0:T(8,128)(2,1)S(1)}, u32[]{:S(2)}, u32[]{:S(2)}) collective-permute-start(bf16[4,1,32,384]{3,2,1,0:T(8,128)(2,1)S(1)} %get-tuple-element.60), channel_id=1, source_target_pairs={{0,4},{4,8},{8,12},{12,16},{16,20},{20,24},{24,28},{28,32},{32,36}... | collective-permute-start | bytes 294920 | tf_op jit(solution)/shard_map/ppermute | solution.py:33
  28.8 8.2 %collective-permute-start.4 = (bf16[4,6,1,384]{3,2,1,0:T(2,128)(2,1)S(1)}, bf16[4,6,1,384]{3,2,1,0:T(2,128)(2,1)S(1)}, u32[]{:S(2)}, u32[]{:S(2)}) collective-permute-start(bf16[4,6,1,384]{3,2,1,0:T(2,128)(2,1)S(1)} %get-tuple-element.48), channel_id=1, source_target_pairs={{1,0},{2,1},{3,2},{5,4},{6,5},{7,6},{9,8},{10,9},{11,10},{13,12},{... | collective-permute-start | bytes 55304 | tf_op jit(solution)/shard_map/ppermute | solution.py:34
  30.8 8.9 %slice-start = ((s8[7962624]{0:T(1024)(128)(4,1)}), s8[4194304]{0:T(1024)(128)(4,1)S(1)}, s32[]{:S(2)}) async-start(s8[7962624]{0:T(1024)(128)(4,1)} %bitcast.164), calls=%async_computation.4 | async-start | bytes 8388608
  30.8 6.2 %collective-permute-start.3 = (bf16[4,6,1,384]{3,2,1,0:T(2,128)(2,1)S(1)}, bf16[4,6,1,384]{3,2,1,0:T(2,128)(2,1)S(1)}, u32[]{:S(2)}, u32[]{:S(2)}) collective-permute-start(bf16[4,6,1,384]{3,2,1,0:T(2,128)(2,1)S(1)} %get-tuple-element.49), channel_id=1, source_target_pairs={{0,1},{1,2},{2,3},{4,5},{5,6},{6,7},{8,9},{9,10},{10,11},{12,13},{... | collective-permute-start | bytes 55304 | tf_op jit(solution)/shard_map/ppermute | solution.py:33
  35.6 5.7 %copy-start.1 = (f32[384]{0:T(512)S(1)}, f32[384]{0:T(512)}, u32[]{:S(2)}) copy-start(f32[384]{0:T(512)} %param.8) | copy-start | bytes 4612
  38.6 2.1 %slice-start.1 = ((s8[7962624]{0:T(1024)(128)(4,1)}), s8[3768320]{0:T(1024)(128)(4,1)S(1)}, s32[]{:S(2)}) async-start(s8[7962624]{0:T(1024)(128)(4,1)} %bitcast.164), calls=%async_computation.5 | async-start | bytes 7536640
  38.6 8.6 %collective-permute-start.5 = (bf16[3,5,40,384]{3,2,1,0:T(8,128)(2,1)S(1)}, bf16[3,5,40,384]{3,2,1,0:T(8,128)(2,1)S(1)}, u32[]{:S(2)}, u32[]{:S(2)}) collective-permute-start(bf16[3,5,40,384]{3,2,1,0:T(8,128)(2,1)S(1)} %pad.4.refs_0_), channel_id=1, source_target_pairs={{0,4},{4,0},{8,12},{12,8},{1,5},{5,1},{9,13},{13,9},{2,6},{6,2},{1... | collective-permute-start | bytes 1382408 | tf_op jit(solution)/shard_map/ppermute | solution.py:23
  38.7 10.4 %collective-permute-start.6 = (bf16[3,5,40,384]{3,2,1,0:T(8,128)(2,1)S(1)}, bf16[3,5,40,384]{3,2,1,0:T(8,128)(2,1)S(1)}, u32[]{:S(2)}, u32[]{:S(2)}) collective-permute-start(bf16[3,5,40,384]{3,2,1,0:T(8,128)(2,1)S(1)} %pad.4.refs_0_), channel_id=1, source_target_pairs={{0,12},{4,8},{8,4},{12,0},{1,13},{5,9},{9,5},{13,1},{2,14},{6,10},... | collective-permute-start | bytes 1382408 | tf_op jit(solution)/shard_map/ppermute | solution.py:23
  45.1 6.3 %copy-start.2 = (bf16[2,4,32,384]{3,2,1,0:T(8,128)(2,1)S(1)}, bf16[2,4,32,384]{3,2,1,0:T(8,128)(2,1)}, u32[]{:S(2)}) copy-start(bf16[2,4,32,384]{3,2,1,0:T(8,128)(2,1)} %param.9) | copy-start | bytes 589828
  49.2 5.7 %collective-permute-start.7 = (bf16[3,5,16,384]{3,2,1,0:T(8,128)(2,1)S(1)}, bf16[3,5,16,384]{3,2,1,0:T(8,128)(2,1)S(1)}, u32[]{:S(2)}, u32[]{:S(2)}) collective-permute-start(bf16[3,5,16,384]{3,2,1,0:T(8,128)(2,1)S(1)} %slice.296), channel_id=1, source_target_pairs={{0,12},{4,8},{8,4},{12,0},{1,13},{5,9},{9,5},{13,1},{2,14},{6,10},... | collective-permute-start | bytes 552968 | tf_op jit(solution)/shard_map/ppermute | solution.py:23
  49.3 5.6 %collective-permute-start.8 = (bf16[3,5,24,384]{3,2,1,0:T(8,128)(2,1)S(1)}, bf16[3,5,24,384]{3,2,1,0:T(8,128)(2,1)S(1)}, u32[]{:S(2)}, u32[]{:S(2)}) collective-permute-start(bf16[3,5,24,384]{3,2,1,0:T(8,128)(2,1)S(1)} %slice.297), channel_id=1, source_target_pairs={{0,4},{4,0},{8,12},{12,8},{1,5},{5,1},{9,13},{13,9},{2,6},{6,2},{1... | collective-permute-start | bytes 829448 | tf_op jit(solution)/shard_map/ppermute | solution.py:23
  55.3 10.8 %collective-permute-start.9 = (bf16[4,2,5,40,384]{4,3,2,1,0:T(8,128)(2,1)S(1)}, bf16[4,2,5,40,384]{4,3,2,1,0:T(8,128)(2,1)S(1)}, u32[]{:S(2)}, u32[]{:S(2)}) collective-permute-start(bf16[4,2,5,40,384]{4,3,2,1,0:T(8,128)(2,1)S(1)} %pad_maximum_fusion), channel_id=1, source_target_pairs={{0,64},{64,0},{1,65},{65,1},{2,66},{66,2},{3,67},{67,3},{4,68},{68... | collective-permute-start | bytes 3686408 | tf_op jit(solution)/shard_map/ppermute | solution.py:23
  64.1 4.2 %collective-permute-start.10 = (bf16[4,96,256]{2,1,0:T(8,128)(2,1)S(1)}, bf16[4,96,256]{2,1,0:T(8,128)(2,1)S(1)}, u32[]{:S(2)}, u32[]{:S(2)}) collective-permute-start(bf16[4,96,256]{2,1,0:T(8,128)(2,1)S(1)} %all_to_all.20.own_ref), channel_id=1, source_target_pairs={{0,64},{64,0},{1,65},{65,1},{2,66},{66,2},{3,67},{67,3},{4,68},{68... | collective-permute-start | bytes 589832 | tf_op jit(solution)/shard_map/ppermute | solution.py:23
  93.4 26.8 %all-to-all-start.2 = ((bf16[8,42,384]{2,1,0:T(8,128)(2,1)}), bf16[8,42,384]{2,1,0:T(8,128)(2,1)S(1)}, u32[]{:S(2)}, u32[]{:S(2)}) async-start(bf16[8,42,384]{2,1,0:T(8,128)(2,1)} %reshape.157), calls=%async_computation.2 | async-start | bytes 589824 | tf_op jit(solution)/shard_map/all_to_all | solution.py:150
  103.9 5.6 %collective-permute-start.12 = (bf16[2,1,32,384]{3,2,1,0:T(8,128)(2,1)S(1)}, bf16[2,1,32,384]{3,2,1,0:T(8,128)(2,1)S(1)}, u32[]{:S(2)}, u32[]{:S(2)}) collective-permute-start(bf16[2,1,32,384]{3,2,1,0:T(8,128)(2,1)S(1)} %get-tuple-element.65), channel_id=1, source_target_pairs={{4,0},{8,4},{12,8},{16,12},{20,16},{24,20},{28,24},{32,28},{36,32}... | collective-permute-start | bytes 147464 | tf_op jit(solution)/shard_map/ppermute | solution.py:34
  107.6 7.2 %collective-permute-start.11 = (bf16[2,1,32,384]{3,2,1,0:T(8,128)(2,1)S(1)}, bf16[2,1,32,384]{3,2,1,0:T(8,128)(2,1)S(1)}, u32[]{:S(2)}, u32[]{:S(2)}) collective-permute-start(bf16[2,1,32,384]{3,2,1,0:T(8,128)(2,1)S(1)} %get-tuple-element.64), channel_id=1, source_target_pairs={{0,4},{4,8},{8,12},{12,16},{16,20},{20,24},{24,28},{28,32},{32,36}... | collective-permute-start | bytes 147464 | tf_op jit(solution)/shard_map/ppermute | solution.py:33
  114.8 12.5 %collective-permute-start.14 = (bf16[2,6,1,384]{3,2,1,0:T(2,128)(2,1)S(1)}, bf16[2,6,1,384]{3,2,1,0:T(2,128)(2,1)S(1)}, u32[]{:S(2)}, u32[]{:S(2)}) collective-permute-start(bf16[2,6,1,384]{3,2,1,0:T(2,128)(2,1)S(1)} %get-tuple-element.63), channel_id=1, source_target_pairs={{1,0},{2,1},{3,2},{5,4},{6,5},{7,6},{9,8},{10,9},{11,10},{13,12},{... | collective-permute-start | bytes 27656 | tf_op jit(solution)/shard_map/ppermute | solution.py:19
  116.8 10.5 %collective-permute-start.13 = (bf16[2,6,1,384]{3,2,1,0:T(2,128)(2,1)S(1)}, bf16[2,6,1,384]{3,2,1,0:T(2,128)(2,1)S(1)}, u32[]{:S(2)}, u32[]{:S(2)}) collective-permute-start(bf16[2,6,1,384]{3,2,1,0:T(2,128)(2,1)S(1)} %get-tuple-element.62), channel_id=1, source_target_pairs={{0,1},{1,2},{2,3},{4,5},{5,6},{6,7},{8,9},{9,10},{10,11},{12,13},{... | collective-permute-start | bytes 27656 | tf_op jit(solution)/shard_map/ppermute | solution.py:19
  121.0 23.2 %all-to-all-start.3 = ((bf16[8,42,384]{2,1,0:T(8,128)(2,1)}), bf16[8,42,384]{2,1,0:T(8,128)(2,1)S(1)}, u32[]{:S(2)}, u32[]{:S(2)}) async-start(bf16[8,42,384]{2,1,0:T(8,128)(2,1)} %broadcast_in_dim.4), calls=%async_computation.3 | async-start | bytes 589824 | tf_op jit(solution)/shard_map/all_to_all | solution.py:150
  138.0 15.9 %collective-permute-start.15 = (bf16[2,4,32,384]{3,2,1,0:T(8,128)(2,1)}, bf16[2,4,32,384]{3,2,1,0:T(8,128)(2,1)S(1)}, u32[]{:S(2)}, u32[]{:S(2)}) collective-permute-start(bf16[2,4,32,384]{3,2,1,0:T(8,128)(2,1)} %bitcast.225), channel_id=1, source_target_pairs={{64,0},{128,64},{192,128},{65,1},{129,65},{193,129},{66,2},{130,66... | collective-permute-start | bytes 589832 | tf_op jit(solution)/shard_map/ppermute | solution.py:19
  144.2 11.4 %collective-permute-start.16 = (bf16[14,24,384]{2,1,0:T(8,128)(2,1)S(1)}, bf16[14,24,384]{2,1,0:T(8,128)(2,1)S(1)}, u32[]{:S(2)}, u32[]{:S(2)}) collective-permute-start(bf16[14,24,384]{2,1,0:T(8,128)(2,1)S(1)} %reshape.158), channel_id=1, source_target_pairs={{0,64},{64,0},{1,65},{65,1},{2,66},{66,2},{3,67},{67,3},{4,68},{68... | collective-permute-start | bytes 774152 | tf_op jit(solution)/shard_map/ppermute | solution.py:23

commit v5 on v4

--- a/solution.py
+++ b/solution.py
@@ -43,33 +43,21 @@
     return block.reshape(-1, block.shape[-1])
 
 
-def spread_kernel(where_ref, *refs):
-    lines, peer_ref, out_ref = refs[:4], refs[4], refs[5]
+def weight_grad_kernel(where_ref, own_ref, peer_ref, *refs):
+    lines, both_ref, out_ref, cols = refs[:4], refs[4], refs[5], refs[6]
     core = where_ref[0]
-    for k, flip in enumerate((0, 1, 3, 2)):
-        src = where_ref[1] ^ flip
-        at = jnp.where(src == 0, 0, 1 + 4 * src)
-        for c in range(3):
-            for f in range(3):
-                out_ref[c, f + 2 * core, pl.ds(at, 5)] = lines[k][f, :, c : c + 32, :]
-            for f in range(2):
-                out_ref[c, f + 3 * (1 - core), pl.ds(at, 5)] = peer_ref[k, f, :, c : c + 32, :]
-
-
-def spread(where, lines, peer):
-    return pl.pallas_call(
-        spread_kernel,
-        out_shape=jax.ShapeDtypeStruct((3, 5, 18, 32, 384), BF),
-        in_specs=[pl.BlockSpec(memory_space=pltpu.SMEM)]
-        + [pl.BlockSpec(memory_space=pltpu.VMEM)] * 5,
-        out_specs=pl.BlockSpec(memory_space=pltpu.VMEM),
-        compiler_params=pltpu.CompilerParams(vmem_limit_bytes=14 << 20),
-        cost_estimate=pl.CostEstimate(flops=0, bytes_accessed=12 << 20, transcendentals=0),
-    )(where, *lines, peer)
-
-
-def weight_grad_kernel(core_ref, cols, own_ref, peer_ref, out_ref):
-    core = core_ref[0]
+
+    @pl.when(pl.program_id(0) == 0)
+    def _():
+        for n, flip in enumerate((0, 1, 3, 2)):
+            src = where_ref[1] ^ flip
+            at = jnp.where(src == 0, 0, 1 + 4 * src)
+            for c in range(3):
+                for f in range(3):
+                    cols[c, f + 2 * core, pl.ds(at, 5)] = lines[n][f, :, c : c + 32, :]
+                for f in range(2):
+                    cols[c, f + 3 * (1 - core), pl.ds(at, 5)] = both_ref[n, f, :, c : c + 32, :]
+
     k = pl.program_id(0) + 4 * core
     tap_t, tap_h, tap_w = k // 9, (k // 3) % 3, k % 3
     total = None
@@ -82,21 +70,22 @@
         out_ref[q, 0] = total[24 * q : 24 * q + 24].astype(BF)
 
 
-def weight_grad(core, cols, own, peer):
+def weight_grad(where, own, peer, lines, both):
     return pl.pallas_call(
         weight_grad_kernel,
         out_shape=jax.ShapeDtypeStruct((4, N_TAPS, 24, 384), BF),
         grid_spec=pltpu.PrefetchScalarGridSpec(
             num_scalar_prefetch=1,
             grid=(N_TAPS,),
-            in_specs=[pl.BlockSpec(memory_space=pltpu.VMEM)] * 3,
+            in_specs=[pl.BlockSpec(memory_space=pltpu.VMEM)] * 7,
             out_specs=pl.BlockSpec((4, 1, 24, 384), lambda j, *_: (0, j, 0, 0)),
+            scratch_shapes=[pltpu.VMEM((3, 5, 18, 32, 384), BF)],
         ),
-        compiler_params=pltpu.CompilerParams(vmem_limit_bytes=14 << 20),
+        compiler_params=pltpu.CompilerParams(vmem_limit_bytes=16 << 20),
         cost_estimate=pl.CostEstimate(
             flops=2 * N_TAPS * 384 * 384 * 512, bytes_accessed=9 << 20, transcendentals=0
         ),
-    )(core, cols, own, peer)
+    )(where, own, peer, *lines, both)
 
 
 def input_grad_kernel(rim_ref, weight_ref, head_ref, tail_ref, cols, total):
@@ -206,9 +195,12 @@
     line = [rows, *near, jnp.concatenate(far, 2)]
     line_peer = jnp.stack([jnp.where(core == 0, v[1:3], v[0:2]) for v in line])
     line_peer = exchanged(line_peer, "co", 1)
-    cols = spread(jnp.stack([core, lax.axis_index("y")]), line, line_peer)
-    parts = weight_grad(core.reshape(1), cols, own, exchanged(own, "co", 1))
-    scaled, parts = lax.optimization_barrier((scaled, parts))
+    scaled_rows = scaled.reshape(frames.shape)
+    above = shifted(scaled_rows[:, -1:], HEIGHT, 1)
+    below = shifted(scaled_rows[:, :1], HEIGHT, -1)
+    line_peer, above, below = lax.optimization_barrier((line_peer, above, below))
+    where = jnp.stack([core, lax.axis_index("y")])
+    parts = weight_grad(where, own, exchanged(own, "co", 1), line, line_peer)
     parts = across(parts, "x")
     mine = reduced_over_ring(jnp.sum(parts.astype(F32), 0))
     theirs = exchanged(mine, "co", 1)
@@ -219,7 +211,7 @@
     ).astype(F32)
     kernel_grad = taps.reshape(3, 3, 3, 24, channels).transpose(3, 0, 1, 2, 4)
 
-    tall = with_halo(scaled.reshape(frames.shape), ((HEIGHT, 1),), 1)
+    tall = jnp.concatenate([above, scaled_rows, below], 1)
     left = shifted(tall[:, :, -1:], "z", 1)
     right = shifted(tall[:, :, :1], "z", -1)
     grad_rimmed = jnp.concatenate([left, tall, right], 2)

time: 158 us -> 156 us (0.987)
  the two profiles are of different devices: /device:TPU:35 before, /device:TPU:1 now
where the time goes in v5:
time: 156 us; the launch traced here: 155 us
  starting transfers between devices  59.9 us (38%)
  blocking collectives  26.3 us (17%)
  waiting for transfers between devices  25.5 us (16%)
  Pallas kernels  18.4 us (12%)
  other arithmetic  11.1 us (7%)
  matrix products  9.85 us (6%)
  local copies, waits for them, and re-layouts  2.45 us (2%)
    all_to_all x2, blocking collectives, across(): return lax.all_to_all(value, axes, 0, 0, tiled=True)  26.3 us
    ppermute x6, starting transfers between devices, shifted(): return lax.ppermute(value, axis, pairs)  24.2 us
    all_to_all x2, starting transfers between devices, across(): return lax.all_to_all(value, axes, 0, 0, tiled=True)  15.5 us
    ppermute x6, waiting for transfers between devices, shifted(): return lax.ppermute(value, axis, pairs)  15.3 us
    pallas_call x1, Pallas kernels, input_grad(): pl.pallas_call(input_grad_kernel, out_shape=[jax.ShapeDtypeStruct((2, 128...  9.75 us
    dot_general x27, matrix products, program(): lax.dot_general(block, weights[tap_t, tap_h, tap_w], (((1,), (1,)), ((),...  9.57 us
    ppermute x7, starting transfers between devices, exchanged(): lax.ppermute(value, axis, [(i, i ^ flip) for i in range(lax.axis_size(axi...  9.36 us
    pallas_call x1, Pallas kernels, weight_grad(): pl.pallas_call(weight_grad_kernel, out_shape=jax.ShapeDtypeStruct((4, N_T...  8.67 us
  transfers between devices with their start and end apart: 19, of which 7 were waited for; matrix products, arithmetic and copies ran while one was open for 11% of the time, Pallas kernels for 6%

profile of v5, /device:TPU:1, one launch (start us, length us, event | category | flops | bytes accessed | tf_op | source)
XLA Modules:
  0.0 154.9 jit_solution(13982949202781752230)
XLA Ops:
  0.7 0.7 fusion.6
  1.5 10.2 %collective-permute-start = (bf16[2,4,32,384]{3,2,1,0:T(8,128)(2,1)}, bf16[2,4,32,384]{3,2,1,0:T(8,128)(2,1)S(1)}, u32[]{:S(2)}, u32[]{:S(2)}) collective-permute-start(bf16[2,4,32,384]{3,2,1,0:T(8,128)(2,1)} %param.5), channel_id=1, source_target_pairs={{0,64},{64,128},{128,192},{1,65},{65,129},{129,193},{2,66},{66,130... | collective-permute-start | bytes 589832 | tf_op jit(solution)/shard_map/ppermute | solution.py:19
  11.7 2.9 %collective-permute-done = bf16[2,4,32,384]{3,2,1,0:T(8,128)(2,1)S(1)} collective-permute-done((bf16[2,4,32,384]{3,2,1,0:T(8,128)(2,1)}, bf16[2,4,32,384]{3,2,1,0:T(8,128)(2,1)S(1)}, u32[]{:S(2)}, u32[]{:S(2)}) %collective-permute-start) | collective-permute-done | bytes 196640 | tf_op jit(solution)/shard_map/ppermute | solution.py:19
  14.6 0.9 pad_maximum_fusion.6
  15.5 3.2 %collective-permute-start.1 = (bf16[4,1,32,384]{3,2,1,0:T(8,128)(2,1)S(1)}, bf16[4,1,32,384]{3,2,1,0:T(8,128)(2,1)S(1)}, u32[]{:S(2)}, u32[]{:S(2)}) collective-permute-start(bf16[4,1,32,384]{3,2,1,0:T(8,128)(2,1)S(1)} %get-tuple-element.62), channel_id=1, source_target_pairs={{0,4},{4,8},{8,12},{12,16},{16,20},{20,24},{24,28},{28,32},{32,36}... | collective-permute-start | bytes 294920 | tf_op jit(solution)/shard_map/ppermute | solution.py:33
  18.7 1.3 collective-permute-start.2
  20.0 0.9 pad_maximum_fusion.4
  20.9 3.1 %collective-permute-done.2 = bf16[4,1,32,384]{3,2,1,0:T(8,128)(2,1)S(1)} collective-permute-done((bf16[4,1,32,384]{3,2,1,0:T(8,128)(2,1)S(1)}, bf16[4,1,32,384]{3,2,1,0:T(8,128)(2,1)S(1)}, u32[]{:S(2)}, u32[]{:S(2)}) %collective-permute-start.2) | collective-permute-done | bytes 98336 | tf_op jit(solution)/shard_map/ppermute | solution.py:34
  24.0 0.9 pad_maximum_fusion.7
  24.9 4.8 %collective-permute-start.3 = (bf16[4,6,1,384]{3,2,1,0:T(2,128)(2,1)S(1)}, bf16[4,6,1,384]{3,2,1,0:T(2,128)(2,1)S(1)}, u32[]{:S(2)}, u32[]{:S(2)}) collective-permute-start(bf16[4,6,1,384]{3,2,1,0:T(2,128)(2,1)S(1)} %get-tuple-element.51), channel_id=1, source_target_pairs={{0,1},{1,2},{2,3},{4,5},{5,6},{6,7},{8,9},{9,10},{10,11},{12,13},{... | collective-permute-start | bytes 55304 | tf_op jit(solution)/shard_map/ppermute | solution.py:33
  29.7 1.6 %collective-permute-start.4 = (bf16[4,6,1,384]{3,2,1,0:T(2,128)(2,1)S(1)}, bf16[4,6,1,384]{3,2,1,0:T(2,128)(2,1)S(1)}, u32[]{:S(2)}, u32[]{:S(2)}) collective-permute-start(bf16[4,6,1,384]{3,2,1,0:T(2,128)(2,1)S(1)} %get-tuple-element.50), channel_id=1, source_target_pairs={{1,0},{2,1},{3,2},{5,4},{6,5},{7,6},{9,8},{10,9},{11,10},{13,12},{... | collective-permute-start | bytes 55304 | tf_op jit(solution)/shard_map/ppermute | solution.py:34
  31.3 1.1 pad_maximum_fusion.2
  32.5 1.3 fusion.16
  33.8 1.1 collective-permute-done.4
  35.0 1.5 fusion.8
  36.5 1.4 collective-permute-start.5
  37.9 3.2 %collective-permute-start.6 = (bf16[3,5,40,384]{3,2,1,0:T(8,128)(2,1)S(1)}, bf16[3,5,40,384]{3,2,1,0:T(8,128)(2,1)S(1)}, u32[]{:S(2)}, u32[]{:S(2)}) collective-permute-start(bf16[3,5,40,384]{3,2,1,0:T(8,128)(2,1)S(1)} %pad.4.refs_0_), channel_id=1, source_target_pairs={{0,12},{4,8},{8,4},{12,0},{1,13},{5,9},{9,5},{13,1},{2,14},{6,10},... | collective-permute-start | bytes 1382408 | tf_op jit(solution)/shard_map/ppermute | solution.py:23
  41.1 0.4 pad_maximum_fusion.1
  42.3 0.3 fusion.15
  42.7 0.3 convolution_add_fusion.22
  43.0 0.3 convolution_add_fusion.21
  43.3 0.3 convolution_add_fusion.20
  43.6 0.3 convolution_add_fusion.19
  43.9 0.3 fusion
  44.2 0.3 convolution_add_fusion.17
  44.5 0.3 convolution_add_fusion.16
  44.8 0.3 convolution_add_fusion.15
  45.1 0.3 convolution_add_fusion.14
  45.4 0.3 convolution_add_fusion.13
  45.7 0.3 convolution_add_fusion.12
  46.0 0.3 convolution_add_fusion.11
  46.3 0.3 convolution_add_fusion.10
  46.6 0.3 convolution_add_fusion.9
  46.9 0.3 convolution_add_fusion.8
  47.2 0.3 convolution_add_fusion.7
  48.2 0.9 collective-permute-start.8
  49.1 1.8 %collective-permute-start.7 = (bf16[3,5,16,384]{3,2,1,0:T(8,128)(2,1)S(1)}, bf16[3,5,16,384]{3,2,1,0:T(8,128)(2,1)S(1)}, u32[]{:S(2)}, u32[]{:S(2)}) collective-permute-start(bf16[3,5,16,384]{3,2,1,0:T(8,128)(2,1)S(1)} %slice.302), channel_id=1, source_target_pairs={{0,12},{4,8},{8,4},{12,0},{1,13},{5,9},{9,5},{13,1},{2,14},{6,10},... | collective-permute-start | bytes 552968 | tf_op jit(solution)/shard_map/ppermute | solution.py:23
  50.9 0.3 convolution_add_fusion.5
  51.2 0.3 convolution_add_fusion.4
  51.5 0.3 convolution_add_fusion.3
  51.8 0.3 convolution_add_fusion.2
  52.1 0.3 convolution_add_fusion.1
  52.4 1.1 fusion.13
  53.8 0.9 collective-permute-done.7
  55.2 8.0 %all_to_all.20.own_ref = bf16[4,96,256]{2,1,0:T(8,128)(2,1)S(1)} all-to-all(bf16[4,96,256]{2,1,0:T(8,128)(2,1)S(1)} %bitcast.222), channel_id=1, replica_groups=mesh['zh'=2,'co'=2,'x'=4,'y'=4,'z'=4] {'y'}, dimensions={0} | all-to-all | bytes 393216 | tf_op jit(solution)/shard_map/all_to_all | solution.py:139
  63.2 1.9 %collective-permute-start.15 = (bf16[4,96,256]{2,1,0:T(8,128)(2,1)S(1)}, bf16[4,96,256]{2,1,0:T(8,128)(2,1)S(1)}, u32[]{:S(2)}, u32[]{:S(2)}) collective-permute-start(bf16[4,96,256]{2,1,0:T(8,128)(2,1)S(1)} %all_to_all.20.own_ref), channel_id=1, source_target_pairs={{0,64},{64,0},{1,65},{65,1},{2,66},{66,2},{3,67},{67,3},{4,68},{68... | collective-permute-start | bytes 589832 | tf_op jit(solution)/shard_map/ppermute | solution.py:23
  65.1 2.2 %collective-permute-start.10 = (bf16[2,1,32,384]{3,2,1,0:T(8,128)(2,1)S(1)}, bf16[2,1,32,384]{3,2,1,0:T(8,128)(2,1)S(1)}, u32[]{:S(2)}, u32[]{:S(2)}) collective-permute-start(bf16[2,1,32,384]{3,2,1,0:T(8,128)(2,1)S(1)} %get-tuple-element.67), channel_id=1, source_target_pairs={{0,4},{4,8},{8,12},{12,16},{16,20},{20,24},{24,28},{28,32},{32,36}... | collective-permute-start | bytes 147464 | tf_op jit(solution)/shard_map/ppermute | solution.py:19
  67.3 1.3 collective-permute-start.11
  68.7 3.5 %collective-permute-done.11 = bf16[2,1,32,384]{3,2,1,0:T(8,128)(2,1)S(1)} collective-permute-done((bf16[2,1,32,384]{3,2,1,0:T(8,128)(2,1)S(1)}, bf16[2,1,32,384]{3,2,1,0:T(8,128)(2,1)S(1)}, u32[]{:S(2)}, u32[]{:S(2)}) %collective-permute-start.11) | collective-permute-done | bytes 49184 | tf_op jit(solution)/shard_map/ppermute | solution.py:19
  72.1 8.7 %shard_map.85 = bf16[4,14,24,384]{3,2,1,0:T(8,128)(2,1)S(1)} custom-call(s32[2]{0:T(128)S(1)} %pad_add_fusion.where_ref, bf16[4,96,256]{2,1,0:T(8,128)(2,1)S(1)} %all_to_all.20.own_ref, bf16[4,96,256]{2,1,0:T(8,128)(2,1)S(1)} %collective-permute-done.15.peer_ref, bf16[3,5,40,384]{3,2,1,0:T(8,128)(2,1)S(1)} %pad.4.refs_0_, ...), custom_call_target="tpu_custom_call" | custom-call | flops 2113929216 | bytes 9437184 | tf_op jit(solution)/shard_map/pallas_call | solution.py:74
  80.8 18.4 %all_to_all.21 = bf16[4,14,24,384]{3,2,1,0:T(8,128)(2,1)S(1)} all-to-all(bf16[4,14,24,384]{3,2,1,0:T(8,128)(2,1)S(1)} %shard_map.85), channel_id=1, replica_groups=mesh['zh'=2,'co'=2,'x'=4,'y'=4,'z'=4] {'x'}, dimensions={0} | all-to-all | bytes 2064384 | tf_op jit(solution)/shard_map/all_to_all | solution.py:139
  99.4 0.8 reshape.153
  100.2 12.1 %all-to-all-start.2 = ((bf16[8,42,384]{2,1,0:T(8,128)(2,1)}), bf16[8,42,384]{2,1,0:T(8,128)(2,1)S(1)}, u32[]{:S(2)}, u32[]{:S(2)}) async-start(bf16[8,42,384]{2,1,0:T(8,128)(2,1)} %reshape.153), calls=%async_computation.2 | async-start | bytes 589824 | tf_op jit(solution)/shard_map/all_to_all | solution.py:139
  112.3 3.4 %collective-permute-start.12 = (bf16[2,6,1,384]{3,2,1,0:T(2,128)(2,1)S(1)}, bf16[2,6,1,384]{3,2,1,0:T(2,128)(2,1)S(1)}, u32[]{:S(2)}, u32[]{:S(2)}) collective-permute-start(bf16[2,6,1,384]{3,2,1,0:T(2,128)(2,1)S(1)} %get-tuple-element.64), channel_id=1, source_target_pairs={{0,1},{1,2},{2,3},{4,5},{5,6},{6,7},{8,9},{9,10},{10,11},{12,13},{... | collective-permute-start | bytes 27656 | tf_op jit(solution)/shard_map/ppermute | solution.py:19
  115.7 1.3 collective-permute-start.13
  117.0 5.1 %all-to-all-done.2 = bf16[8,42,384]{2,1,0:T(8,128)(2,1)S(1)} async-done(((bf16[8,42,384]{2,1,0:T(8,128)(2,1)}), bf16[8,42,384]{2,1,0:T(8,128)(2,1)S(1)}, u32[]{:S(2)}, u32[]{:S(2)}) %all-to-all-start.2) | async-done | bytes 258080 | tf_op jit(solution)/shard_map/all_to_all | solution.py:139
  122.1 0.7 broadcast_in_dim.4
  122.9 3.4 %all-to-all-start.3 = ((bf16[8,42,384]{2,1,0:T(8,128)(2,1)}), bf16[8,42,384]{2,1,0:T(8,128)(2,1)S(1)}, u32[]{:S(2)}, u32[]{:S(2)}) async-start(bf16[8,42,384]{2,1,0:T(8,128)(2,1)} %broadcast_in_dim.4), calls=%async_computation.3 | async-start | bytes 589824 | tf_op jit(solution)/shard_map/all_to_all | solution.py:139
  126.3 0.9 pad_maximum_fusion.3.rim_ref
  127.2 9.7 %shard_map.84 = (bf16[2,128,384]{2,1,0:T(8,128)(2,1)}, f32[2,128,384]{2,1,0:T(8,128)}) custom-call(bf16[2,6,34,384]{3,2,1,0:T(8,128)(2,1)} %pad_maximum_fusion.3.rim_ref, bf16[3,3,3,384,384]{4,3,2,1,0:T(8,128)(2,1)} %bitcast.163), custom_call_target="tpu_custom_call" | custom-call | flops 2038431744 | bytes 9437184 | tf_op jit(solution)/shard_map/pallas_call | solution.py:118
  137.0 5.9 %collective-permute-start.14 = (bf16[2,4,32,384]{3,2,1,0:T(8,128)(2,1)}, bf16[2,4,32,384]{3,2,1,0:T(8,128)(2,1)S(1)}, u32[]{:S(2)}, u32[]{:S(2)}) collective-permute-start(bf16[2,4,32,384]{3,2,1,0:T(8,128)(2,1)} %bitcast.225), channel_id=1, source_target_pairs={{64,0},{128,64},{192,128},{65,1},{129,65},{193,129},{66,2},{130,66... | collective-permute-start | bytes 589832 | tf_op jit(solution)/shard_map/ppermute | solution.py:19
  143.0 8.9 %collective-permute-done.14 = bf16[2,4,32,384]{3,2,1,0:T(8,128)(2,1)S(1)} collective-permute-done((bf16[2,4,32,384]{3,2,1,0:T(8,128)(2,1)}, bf16[2,4,32,384]{3,2,1,0:T(8,128)(2,1)S(1)}, u32[]{:S(2)}, u32[]{:S(2)}) %collective-permute-start.14) | collective-permute-done | bytes 196640 | tf_op jit(solution)/shard_map/ppermute | solution.py:19
  151.9 1.7 %add_convert_fusion = bf16[2,4,32,384]{3,2,1,0:T(8,128)(2,1)} fusion(f32[2,4,32,384]{3,2,1,0:T(8,128)} %bitcast.223, bf16[2,4,32,384]{3,2,1,0:T(8,128)(2,1)S(1)} %collective-permute-done.14), kind=kLoop, calls=%fused_computation.57 | loop fusion | flops 294912 | bytes 786432 | tf_op jit(solution)/shard_map/convert_element_type | solution.py:221
  153.9 1.0 convert_bitcast_fusion
  (58 shorter events, 3.3 us)
Async XLA Ops:
  0.6 40.5 %copy-start = (bf16[2,4,32,384]{3,2,1,0:T(8,128)(2,1)S(1)}, bf16[2,4,32,384]{3,2,1,0:T(8,128)(2,1)}, u32[]{:S(2)}) copy-start(bf16[2,4,32,384]{3,2,1,0:T(8,128)(2,1)} %param.5) | copy-start | bytes 589828
  1.5 13.1 %collective-permute-start = (bf16[2,4,32,384]{3,2,1,0:T(8,128)(2,1)}, bf16[2,4,32,384]{3,2,1,0:T(8,128)(2,1)S(1)}, u32[]{:S(2)}, u32[]{:S(2)}) collective-permute-start(bf16[2,4,32,384]{3,2,1,0:T(8,128)(2,1)} %param.5), channel_id=1, source_target_pairs={{0,64},{64,128},{128,192},{1,65},{65,129},{129,193},{2,66},{66,130... | collective-permute-start | bytes 589832 | tf_op jit(solution)/shard_map/ppermute | solution.py:19
  15.5 5.4 %collective-permute-start.1 = (bf16[4,1,32,384]{3,2,1,0:T(8,128)(2,1)S(1)}, bf16[4,1,32,384]{3,2,1,0:T(8,128)(2,1)S(1)}, u32[]{:S(2)}, u32[]{:S(2)}) collective-permute-start(bf16[4,1,32,384]{3,2,1,0:T(8,128)(2,1)S(1)} %get-tuple-element.62), channel_id=1, source_target_pairs={{0,4},{4,8},{8,12},{12,16},{16,20},{20,24},{24,28},{28,32},{32,36}... | collective-permute-start | bytes 294920 | tf_op jit(solution)/shard_map/ppermute | solution.py:33
  18.7 5.4 %collective-permute-start.2 = (bf16[4,1,32,384]{3,2,1,0:T(8,128)(2,1)S(1)}, bf16[4,1,32,384]{3,2,1,0:T(8,128)(2,1)S(1)}, u32[]{:S(2)}, u32[]{:S(2)}) collective-permute-start(bf16[4,1,32,384]{3,2,1,0:T(8,128)(2,1)S(1)} %get-tuple-element.63), channel_id=1, source_target_pairs={{4,0},{8,4},{12,8},{16,12},{20,16},{24,20},{28,24},{32,28},{36,32}... | collective-permute-start | bytes 294920 | tf_op jit(solution)/shard_map/ppermute | solution.py:34
  24.9 8.9 %collective-permute-start.3 = (bf16[4,6,1,384]{3,2,1,0:T(2,128)(2,1)S(1)}, bf16[4,6,1,384]{3,2,1,0:T(2,128)(2,1)S(1)}, u32[]{:S(2)}, u32[]{:S(2)}) collective-permute-start(bf16[4,6,1,384]{3,2,1,0:T(2,128)(2,1)S(1)} %get-tuple-element.51), channel_id=1, source_target_pairs={{0,1},{1,2},{2,3},{4,5},{5,6},{6,7},{8,9},{9,10},{10,11},{12,13},{... | collective-permute-start | bytes 55304 | tf_op jit(solution)/shard_map/ppermute | solution.py:33
  29.7 12.3 %slice-start = ((s8[7962624]{0:T(1024)(128)(4,1)}), s8[4194304]{0:T(1024)(128)(4,1)S(1)}, s32[]{:S(2)}) async-start(s8[7962624]{0:T(1024)(128)(4,1)} %bitcast.164), calls=%async_computation.4 | async-start | bytes 8388608
  29.7 5.3 %collective-permute-start.4 = (bf16[4,6,1,384]{3,2,1,0:T(2,128)(2,1)S(1)}, bf16[4,6,1,384]{3,2,1,0:T(2,128)(2,1)S(1)}, u32[]{:S(2)}, u32[]{:S(2)}) collective-permute-start(bf16[4,6,1,384]{3,2,1,0:T(2,128)(2,1)S(1)} %get-tuple-element.50), channel_id=1, source_target_pairs={{1,0},{2,1},{3,2},{5,4},{6,5},{7,6},{9,8},{10,9},{11,10},{13,12},{... | collective-permute-start | bytes 55304 | tf_op jit(solution)/shard_map/ppermute | solution.py:34
  32.5 10.2 %copy-start.1 = (f32[384]{0:T(512)S(1)}, f32[384]{0:T(512)}, u32[]{:S(2)}) copy-start(f32[384]{0:T(512)} %param.8) | copy-start | bytes 4612
  36.5 5.5 %slice-start.1 = ((s8[7962624]{0:T(1024)(128)(4,1)}), s8[3768320]{0:T(1024)(128)(4,1)S(1)}, s32[]{:S(2)}) async-start(s8[7962624]{0:T(1024)(128)(4,1)} %bitcast.164), calls=%async_computation.5 | async-start | bytes 7536640
  36.5 11.6 %collective-permute-start.5 = (bf16[3,5,40,384]{3,2,1,0:T(8,128)(2,1)S(1)}, bf16[3,5,40,384]{3,2,1,0:T(8,128)(2,1)S(1)}, u32[]{:S(2)}, u32[]{:S(2)}) collective-permute-start(bf16[3,5,40,384]{3,2,1,0:T(8,128)(2,1)S(1)} %pad.4.refs_0_), channel_id=1, source_target_pairs={{0,4},{4,0},{8,12},{12,8},{1,5},{5,1},{9,13},{13,9},{2,6},{6,2},{1... | collective-permute-start | bytes 1382408 | tf_op jit(solution)/shard_map/ppermute | solution.py:23
  37.9 10.2 %collective-permute-start.6 = (bf16[3,5,40,384]{3,2,1,0:T(8,128)(2,1)S(1)}, bf16[3,5,40,384]{3,2,1,0:T(8,128)(2,1)S(1)}, u32[]{:S(2)}, u32[]{:S(2)}) collective-permute-start(bf16[3,5,40,384]{3,2,1,0:T(8,128)(2,1)S(1)} %pad.4.refs_0_), channel_id=1, source_target_pairs={{0,12},{4,8},{8,4},{12,0},{1,13},{5,9},{9,5},{13,1},{2,14},{6,10},... | collective-permute-start | bytes 1382408 | tf_op jit(solution)/shard_map/ppermute | solution.py:23
  46.6 5.8 %copy-start.2 = (bf16[2,4,32,384]{3,2,1,0:T(8,128)(2,1)S(1)}, bf16[2,4,32,384]{3,2,1,0:T(8,128)(2,1)}, u32[]{:S(2)}) copy-start(bf16[2,4,32,384]{3,2,1,0:T(8,128)(2,1)} %param.9) | copy-start | bytes 589828
  48.2 6.6 %collective-permute-start.8 = (bf16[3,5,24,384]{3,2,1,0:T(8,128)(2,1)S(1)}, bf16[3,5,24,384]{3,2,1,0:T(8,128)(2,1)S(1)}, u32[]{:S(2)}, u32[]{:S(2)}) collective-permute-start(bf16[3,5,24,384]{3,2,1,0:T(8,128)(2,1)S(1)} %slice.303), channel_id=1, source_target_pairs={{0,4},{4,0},{8,12},{12,8},{1,5},{5,1},{9,13},{13,9},{2,6},{6,2},{1... | collective-permute-start | bytes 829448 | tf_op jit(solution)/shard_map/ppermute | solution.py:23
  49.1 5.7 %collective-permute-start.7 = (bf16[3,5,16,384]{3,2,1,0:T(8,128)(2,1)S(1)}, bf16[3,5,16,384]{3,2,1,0:T(8,128)(2,1)S(1)}, u32[]{:S(2)}, u32[]{:S(2)}) collective-permute-start(bf16[3,5,16,384]{3,2,1,0:T(8,128)(2,1)S(1)} %slice.302), channel_id=1, source_target_pairs={{0,12},{4,8},{8,4},{12,0},{1,13},{5,9},{9,5},{13,1},{2,14},{6,10},... | collective-permute-start | bytes 552968 | tf_op jit(solution)/shard_map/ppermute | solution.py:23
  55.1 17.0 %collective-permute-start.9 = (bf16[4,2,5,40,384]{4,3,2,1,0:T(8,128)(2,1)S(1)}, bf16[4,2,5,40,384]{4,3,2,1,0:T(8,128)(2,1)S(1)}, u32[]{:S(2)}, u32[]{:S(2)}) collective-permute-start(bf16[4,2,5,40,384]{4,3,2,1,0:T(8,128)(2,1)S(1)} %pad_maximum_fusion), channel_id=1, source_target_pairs={{0,64},{64,0},{1,65},{65,1},{2,66},{66,2},{3,67},{67,3},{4,68},{68... | collective-permute-start | bytes 3686408 | tf_op jit(solution)/shard_map/ppermute | solution.py:23
  63.2 9.0 %collective-permute-start.15 = (bf16[4,96,256]{2,1,0:T(8,128)(2,1)S(1)}, bf16[4,96,256]{2,1,0:T(8,128)(2,1)S(1)}, u32[]{:S(2)}, u32[]{:S(2)}) collective-permute-start(bf16[4,96,256]{2,1,0:T(8,128)(2,1)S(1)} %all_to_all.20.own_ref), channel_id=1, source_target_pairs={{0,64},{64,0},{1,65},{65,1},{2,66},{66,2},{3,67},{67,3},{4,68},{68... | collective-permute-start | bytes 589832 | tf_op jit(solution)/shard_map/ppermute | solution.py:23
  65.1 3.6 %collective-permute-start.10 = (bf16[2,1,32,384]{3,2,1,0:T(8,128)(2,1)S(1)}, bf16[2,1,32,384]{3,2,1,0:T(8,128)(2,1)S(1)}, u32[]{:S(2)}, u32[]{:S(2)}) collective-permute-start(bf16[2,1,32,384]{3,2,1,0:T(8,128)(2,1)S(1)} %get-tuple-element.67), channel_id=1, source_target_pairs={{0,4},{4,8},{8,12},{12,16},{16,20},{20,24},{24,28},{28,32},{32,36}... | collective-permute-start | bytes 147464 | tf_op jit(solution)/shard_map/ppermute | solution.py:19
  67.3 4.8 %collective-permute-start.11 = (bf16[2,1,32,384]{3,2,1,0:T(8,128)(2,1)S(1)}, bf16[2,1,32,384]{3,2,1,0:T(8,128)(2,1)S(1)}, u32[]{:S(2)}, u32[]{:S(2)}) collective-permute-start(bf16[2,1,32,384]{3,2,1,0:T(8,128)(2,1)S(1)} %get-tuple-element.66), channel_id=1, source_target_pairs={{4,0},{8,4},{12,8},{16,12},{20,16},{24,20},{28,24},{32,28},{36,32}... | collective-permute-start | bytes 147464 | tf_op jit(solution)/shard_map/ppermute | solution.py:19
  100.2 21.9 %all-to-all-start.2 = ((bf16[8,42,384]{2,1,0:T(8,128)(2,1)}), bf16[8,42,384]{2,1,0:T(8,128)(2,1)S(1)}, u32[]{:S(2)}, u32[]{:S(2)}) async-start(bf16[8,42,384]{2,1,0:T(8,128)(2,1)} %reshape.153), calls=%async_computation.2 | async-start | bytes 589824 | tf_op jit(solution)/shard_map/all_to_all | solution.py:139
  112.3 14.0 %collective-permute-start.12 = (bf16[2,6,1,384]{3,2,1,0:T(2,128)(2,1)S(1)}, bf16[2,6,1,384]{3,2,1,0:T(2,128)(2,1)S(1)}, u32[]{:S(2)}, u32[]{:S(2)}) collective-permute-start(bf16[2,6,1,384]{3,2,1,0:T(2,128)(2,1)S(1)} %get-tuple-element.64), channel_id=1, source_target_pairs={{0,1},{1,2},{2,3},{4,5},{5,6},{6,7},{8,9},{9,10},{10,11},{12,13},{... | collective-permute-start | bytes 27656 | tf_op jit(solution)/shard_map/ppermute | solution.py:19
  115.7 10.6 %collective-permute-start.13 = (bf16[2,6,1,384]{3,2,1,0:T(2,128)(2,1)S(1)}, bf16[2,6,1,384]{3,2,1,0:T(2,128)(2,1)S(1)}, u32[]{:S(2)}, u32[]{:S(2)}) collective-permute-start(bf16[2,6,1,384]{3,2,1,0:T(2,128)(2,1)S(1)} %get-tuple-element.65), channel_id=1, source_target_pairs={{1,0},{2,1},{3,2},{5,4},{6,5},{7,6},{9,8},{10,9},{11,10},{13,12},{... | collective-permute-start | bytes 27656 | tf_op jit(solution)/shard_map/ppermute | solution.py:19
  122.9 20.0 %all-to-all-start.3 = ((bf16[8,42,384]{2,1,0:T(8,128)(2,1)}), bf16[8,42,384]{2,1,0:T(8,128)(2,1)S(1)}, u32[]{:S(2)}, u32[]{:S(2)}) async-start(bf16[8,42,384]{2,1,0:T(8,128)(2,1)} %broadcast_in_dim.4), calls=%async_computation.3 | async-start | bytes 589824 | tf_op jit(solution)/shard_map/all_to_all | solution.py:139
  137.0 15.0 %collective-permute-start.14 = (bf16[2,4,32,384]{3,2,1,0:T(8,128)(2,1)}, bf16[2,4,32,384]{3,2,1,0:T(8,128)(2,1)S(1)}, u32[]{:S(2)}, u32[]{:S(2)}) collective-permute-start(bf16[2,4,32,384]{3,2,1,0:T(8,128)(2,1)} %bitcast.225), channel_id=1, source_target_pairs={{64,0},{128,64},{192,128},{65,1},{129,65},{193,129},{66,2},{130,66... | collective-permute-start | bytes 589832 | tf_op jit(solution)/shard_map/ppermute | solution.py:19
  142.9 10.8 %collective-permute-start.16 = (bf16[14,24,384]{2,1,0:T(8,128)(2,1)S(1)}, bf16[14,24,384]{2,1,0:T(8,128)(2,1)S(1)}, u32[]{:S(2)}, u32[]{:S(2)}) collective-permute-start(bf16[14,24,384]{2,1,0:T(8,128)(2,1)S(1)} %reshape.154), channel_id=1, source_target_pairs={{0,64},{64,0},{1,65},{65,1},{2,66},{66,2},{3,67},{67,3},{4,68},{68... | collective-permute-start | bytes 774152 | tf_op jit(solution)/shard_map/ppermute | solution.py:23

commit v6 on v5

--- a/solution.py
+++ b/solution.py
@@ -36,11 +36,97 @@
     return value
 
 
-def tap_block(padded, tap_t, tap_h, tap_w, depth_count, row_count, col_count):
-    block = padded[
-        tap_t : tap_t + depth_count, tap_h : tap_h + row_count, tap_w : tap_w + col_count
-    ]
-    return block.reshape(-1, block.shape[-1])
+def whole(shape):
+    return pl.BlockSpec(shape, lambda j: (0,) * len(shape))
+
+
+def three_taps(cols, frame, tap_h, weight_ref):
+    total = None
+    for c in range(3):
+        block = cols[c, pl.ds(frame, 2), pl.ds(tap_h, 4)].reshape(256, 384)
+        term = lax.dot_general(
+            block, weight_ref[0, 0, c], (((1,), (1,)), ((), ())), preferred_element_type=F32
+        )
+        total = term if total is None else total + term
+    return total
+
+
+def forward_own_kernel(own_ref, bias_ref, weight_ref, out_ref, cols):
+    tap_h = pl.program_id(0)
+
+    @pl.when(tap_h == 0)
+    def _():
+        out_ref[...] = jnp.broadcast_to(bias_ref[...], out_ref.shape)
+        for c in range(3):
+            cols[c] = own_ref[:, :, c : c + 32, :]
+
+    out_ref[...] += three_taps(cols, 0, tap_h, weight_ref)
+
+
+def forward_own(own_ext, bias, weights):
+    return pl.pallas_call(
+        forward_own_kernel,
+        out_shape=jax.ShapeDtypeStruct((256, 384), F32),
+        grid=(3,),
+        in_specs=[
+            pl.BlockSpec(memory_space=pltpu.VMEM),
+            whole((1, 384)),
+            pl.BlockSpec((1, 1, 3, 384, 384), lambda j: (2, j, 0, 0, 0)),
+        ],
+        out_specs=whole((256, 384)),
+        scratch_shapes=[pltpu.VMEM((3, 2, 6, 32, 384), BF)],
+        compiler_params=pltpu.CompilerParams(vmem_limit_bytes=60 << 20),
+        cost_estimate=pl.CostEstimate(
+            flops=2 * 9 * 256 * 384 * 384, bytes_accessed=3 << 20, transcendentals=0
+        ),
+    )(own_ext, bias.reshape(1, -1), weights)
+
+
+def forward_rest_kernel(
+    early_ref, own_ref, so_far_ref, cotangent_ref, order_ref, weight_ref,
+    decoded_ref, scaled_ref, turned_ref, cols, total,
+):
+    step = pl.program_id(0)
+
+    @pl.when(step == 0)
+    def _():
+        total[...] = so_far_ref[...]
+        for c in range(3):
+            cols[c, :2] = early_ref[:, :, c : c + 32, :]
+            cols[c, 2] = own_ref[0, :, c : c + 32, :]
+
+    total[...] += three_taps(cols, 1 - step // 3, step % 3, weight_ref)
+
+    @pl.when(step == 5)
+    def _():
+        pre_act = total[...]
+        sigma = jax.nn.sigmoid(pre_act)
+        decoded_ref[...] = (pre_act * sigma).astype(BF)
+        scaled = cotangent_ref[...].astype(F32) * sigma * (1.0 + pre_act * (1.0 - sigma))
+        scaled_ref[...] = scaled.astype(BF)
+        turned_ref[...] = lax.dot_general(
+            order_ref[...], scaled.astype(BF), (((1,), (1,)), ((), ())), preferred_element_type=F32
+        ).astype(BF)
+
+
+def forward_rest(early_ext, own_ext, so_far, cotangent, order, weights):
+    return pl.pallas_call(
+        forward_rest_kernel,
+        out_shape=[
+            jax.ShapeDtypeStruct((256, 384), BF),
+            jax.ShapeDtypeStruct((256, 384), BF),
+            jax.ShapeDtypeStruct((384, 256), BF),
+        ],
+        grid=(6,),
+        in_specs=[pl.BlockSpec(memory_space=pltpu.VMEM)] * 5
+        + [pl.BlockSpec((1, 1, 3, 384, 384), lambda j: (1 - j // 3, j % 3, 0, 0, 0))],
+        out_specs=[whole((256, 384)), whole((256, 384)), whole((384, 256))],
+        scratch_shapes=[pltpu.VMEM((3, 3, 6, 32, 384), BF), pltpu.VMEM((256, 384), F32)],
+        compiler_params=pltpu.CompilerParams(vmem_limit_bytes=60 << 20),
+        cost_estimate=pl.CostEstimate(
+            flops=2 * 18 * 256 * 384 * 384, bytes_accessed=6 << 20, transcendentals=1 << 17
+        ),
+    )(early_ext, own_ext, so_far, cotangent, order, weights)
 
 
 def weight_grad_kernel(where_ref, own_ref, peer_ref, *refs):
@@ -112,9 +198,6 @@
 
 
 def input_grad(rimmed, weights):
-    def whole(shape):
-        return pl.BlockSpec(shape, lambda j: (0,) * len(shape))
-
     return pl.pallas_call(
         input_grad_kernel,
         out_shape=[
@@ -148,7 +231,7 @@
 
 
 def program(frames, cache_in, kernel, conv_bias, cotangent):
-    frame_count, row_count, col_count, channels = frames.shape
+    _, _, col_count, channels = frames.shape
     core = lax.axis_index("co")
     is_first = lax.axis_index(TM) == 0
     row = lax.broadcasted_iota(jnp.int32, (channels, channels), 0)
@@ -156,10 +239,13 @@
     order = (row // 24 % 4 * 96 + row // 96 * 24 + row % 24 == col).astype(BF)
     order, frames = lax.optimization_barrier((order, frames))
     weights = kernel.transpose(1, 2, 3, 0, 4)
+    own_ext = with_halo(frames, ((HEIGHT, 1),), 1)
     earlier = shifted(frames, TM, 1)
+    own_ext = with_halo(own_ext, (("z", 2),), 1)
+    so_far = forward_own(own_ext, conv_bias, weights)
     earlier = jnp.where(is_first, cache_in, earlier)
-    stacked = jnp.concatenate([earlier, frames], 0)
-    extended = with_halo(stacked, ((HEIGHT, 1), ("z", 2)), 1)
+    early_ext = with_halo(earlier, ((HEIGHT, 1), ("z", 2)), 1)
+    extended = jnp.concatenate([early_ext, own_ext], 0)
     rows = lax.dynamic_slice(
         extended,
         (core, (lax.axis_index("y") != 0).astype(jnp.int32), 0, 0),
@@ -167,40 +253,22 @@
     )
     rows = jnp.pad(rows, ((0, 0), (0, 0), (0, 6), (0, 0)))
     near = [exchanged(rows, "y", flip) for flip in (1, 3)]
-    pre_act = jnp.zeros((frame_count * row_count * col_count, channels), F32) + conv_bias
-    for tap_t in range(3):
-        if tap_t == 2:
-            pre_act, *near = lax.optimization_barrier((pre_act, *near))
-            far = [
-                exchanged(near[0][:, :, :16], "y", 3),
-                exchanged(near[1][:, :, 16:], "y", 1),
-            ]
-        for tap_h in range(3):
-            for tap_w in range(3):
-                block = tap_block(extended, tap_t, tap_h, tap_w, frame_count, row_count, col_count)
-                pre_act = pre_act + lax.dot_general(
-                    block,
-                    weights[tap_t, tap_h, tap_w],
-                    (((1,), (1,)), ((), ())),
-                    preferred_element_type=F32,
-                )
-    sigma = jax.nn.sigmoid(pre_act)
-    decoded = (pre_act * sigma).astype(BF).reshape(frames.shape)
-    scaled = (
-        cotangent.reshape(-1, channels).astype(F32) * sigma * (1.0 + pre_act * (1.0 - sigma))
-    ).astype(BF)
-    own = lax.dot_general(order, scaled, (((1,), (1,)), ((), ())), preferred_element_type=F32)
-    own, *far = lax.optimization_barrier((own.astype(BF).reshape(4, 96, -1), *far))
+    decoded, scaled, own = forward_rest(
+        early_ext, own_ext, so_far, cotangent.reshape(-1, channels), order, weights
+    )
+    decoded = decoded.reshape(frames.shape)
+    own = own.reshape(4, 96, -1)
     own = across(own, "y")
+    far = [exchanged(near[0][:, :, :16], "y", 3), exchanged(near[1][:, :, 16:], "y", 1)]
     line = [rows, *near, jnp.concatenate(far, 2)]
     line_peer = jnp.stack([jnp.where(core == 0, v[1:3], v[0:2]) for v in line])
     line_peer = exchanged(line_peer, "co", 1)
     scaled_rows = scaled.reshape(frames.shape)
     above = shifted(scaled_rows[:, -1:], HEIGHT, 1)
     below = shifted(scaled_rows[:, :1], HEIGHT, -1)
-    line_peer, above, below = lax.optimization_barrier((line_peer, above, below))
     where = jnp.stack([core, lax.axis_index("y")])
-    parts = weight_grad(where, own, exchanged(own, "co", 1), line, line_peer)
+    own_peer = exchanged(own, "co", 1)
+    parts = weight_grad(where, own, own_peer, line, line_peer)
     parts = across(parts, "x")
     mine = reduced_over_ring(jnp.sum(parts.astype(F32), 0))
     theirs = exchanged(mine, "co", 1)

time: 156 us -> 178 us (1.14)
  the two profiles are of different devices: /device:TPU:1 before, /device:TPU:35 now
where the time goes in v6:
time: 178 us; the launch traced here: 177 us
  starting transfers between devices  70.1 us (39%)
  waiting for transfers between devices  35.2 us (20%)
  Pallas kernels  30.7 us (17%)
  blocking collectives  25.9 us (15%)
  other arithmetic  9.89 us (6%)
  local copies, waits for them, and re-layouts  4.26 us (2%)
    ppermute x6, starting transfers between devices, shifted(): return lax.ppermute(value, axis, pairs)  26.5 us
    all_to_all x2, blocking collectives, across(): return lax.all_to_all(value, axes, 0, 0, tiled=True)  25.9 us
    ppermute x7, waiting for transfers between devices, exchanged(): lax.ppermute(value, axis, [(i, i ^ flip) for i in range(lax.axis_size(axi...  18.3 us
    ppermute x6, waiting for transfers between devices, shifted(): return lax.ppermute(value, axis, pairs)  14.8 us
    ppermute x4, starting transfers between devices, with_halo(): after = lax.ppermute(initial, axis, down)  14.2 us
    all_to_all x2, starting transfers between devices, across(): return lax.all_to_all(value, axes, 0, 0, tiled=True)  12.6 us
    ppermute x4, starting transfers between devices, with_halo(): before = lax.ppermute(last, axis, up)  11.5 us
    pallas_call x1, Pallas kernels, input_grad(): pl.pallas_call(input_grad_kernel, out_shape=[jax.ShapeDtypeStruct((2, 128...  9.75 us
  transfers between devices with their start and end apart: 23, of which 8 were waited for; matrix products, arithmetic and copies ran while one was open for 4% of the time, Pallas kernels for 12%

profile of v6, /device:TPU:35, one launch (start us, length us, event | category | flops | bytes accessed | tf_op | source)
XLA Modules:
  0.0 177.2 jit_solution(12181361401015555865)
XLA Ops:
  0.7 1.8 fusion.5.order_ref
  2.5 0.8 fusion.26
  3.3 3.2 %collective-permute-start.5 = (bf16[2,1,32,384]{3,2,1,0:T(8,128)(2,1)S(1)}, bf16[2,1,32,384]{3,2,1,0:T(8,128)(2,1)S(1)}, u32[]{:S(2)}, u32[]{:S(2)}) collective-permute-start(bf16[2,1,32,384]{3,2,1,0:T(8,128)(2,1)S(1)} %get-tuple-element.27), channel_id=1, source_target_pairs={{0,4},{4,8},{8,12},{12,16},{16,20},{20,24},{24,28},{28,32},{32,36}... | collective-permute-start | bytes 147464 | tf_op jit(solution)/shard_map/ppermute | solution.py:33
  6.5 8.8 %collective-permute-start = (bf16[2,4,32,384]{3,2,1,0:T(8,128)(2,1)}, bf16[2,4,32,384]{3,2,1,0:T(8,128)(2,1)S(1)}, u32[]{:S(2)}, u32[]{:S(2)}) collective-permute-start(bf16[2,4,32,384]{3,2,1,0:T(8,128)(2,1)} %param.5), channel_id=1, source_target_pairs={{0,64},{64,128},{128,192},{1,65},{65,129},{129,193},{2,66},{66,130... | collective-permute-start | bytes 589832 | tf_op jit(solution)/shard_map/ppermute | solution.py:19
  15.3 4.2 %collective-permute-start.6 = (bf16[2,1,32,384]{3,2,1,0:T(8,128)(2,1)S(1)}, bf16[2,1,32,384]{3,2,1,0:T(8,128)(2,1)S(1)}, u32[]{:S(2)}, u32[]{:S(2)}) collective-permute-start(bf16[2,1,32,384]{3,2,1,0:T(8,128)(2,1)S(1)} %get-tuple-element.26), channel_id=1, source_target_pairs={{4,0},{8,4},{12,8},{16,12},{20,16},{24,20},{28,24},{32,28},{36,32}... | collective-permute-start | bytes 147464 | tf_op jit(solution)/shard_map/ppermute | solution.py:34
  19.5 1.0 constant_dynamic-update-slice_fusion.1
  20.5 0.2 collective-permute-done.6
  20.6 0.0 collective-permute-done
  20.7 3.0 %collective-permute-start.1 = (bf16[2,1,32,384]{3,2,1,0:T(8,128)(2,1)S(1)}, bf16[2,1,32,384]{3,2,1,0:T(8,128)(2,1)S(1)}, u32[]{:S(2)}, u32[]{:S(2)}) collective-permute-start(bf16[2,1,32,384]{3,2,1,0:T(8,128)(2,1)S(1)} %get-tuple-element.28), channel_id=1, source_target_pairs={{0,4},{4,8},{8,12},{12,16},{16,20},{20,24},{24,28},{28,32},{32,36}... | collective-permute-start | bytes 147464 | tf_op jit(solution)/shard_map/ppermute | solution.py:33
  23.7 4.7 %collective-permute-start.2 = (bf16[2,1,32,384]{3,2,1,0:T(8,128)(2,1)S(1)}, bf16[2,1,32,384]{3,2,1,0:T(8,128)(2,1)S(1)}, u32[]{:S(2)}, u32[]{:S(2)}) collective-permute-start(bf16[2,1,32,384]{3,2,1,0:T(8,128)(2,1)S(1)} %get-tuple-element.29), channel_id=1, source_target_pairs={{4,0},{8,4},{12,8},{16,12},{20,16},{24,20},{28,24},{32,28},{36,32}... | collective-permute-start | bytes 147464 | tf_op jit(solution)/shard_map/ppermute | solution.py:34
  28.5 2.6 %collective-permute-start.7 = (bf16[2,6,1,384]{3,2,1,0:T(2,128)(2,1)S(1)}, bf16[2,6,1,384]{3,2,1,0:T(2,128)(2,1)S(1)}, u32[]{:S(2)}, u32[]{:S(2)}) collective-permute-start(bf16[2,6,1,384]{3,2,1,0:T(2,128)(2,1)S(1)} %get-tuple-element.20), channel_id=1, source_target_pairs={{0,1},{1,2},{2,3},{4,5},{5,6},{6,7},{8,9},{9,10},{10,11},{12,13},{... | collective-permute-start | bytes 27656 | tf_op jit(solution)/shard_map/ppermute | solution.py:33
  31.1 2.6 %collective-permute-start.8 = (bf16[2,6,1,384]{3,2,1,0:T(2,128)(2,1)S(1)}, bf16[2,6,1,384]{3,2,1,0:T(2,128)(2,1)S(1)}, u32[]{:S(2)}, u32[]{:S(2)}) collective-permute-start(bf16[2,6,1,384]{3,2,1,0:T(2,128)(2,1)S(1)} %get-tuple-element.21), channel_id=1, source_target_pairs={{1,0},{2,1},{3,2},{5,4},{6,5},{7,6},{9,8},{10,9},{11,10},{13,12},{... | collective-permute-start | bytes 27656 | tf_op jit(solution)/shard_map/ppermute | solution.py:34
  33.8 2.6 %collective-permute-start.3 = (bf16[2,6,1,384]{3,2,1,0:T(2,128)(2,1)S(1)}, bf16[2,6,1,384]{3,2,1,0:T(2,128)(2,1)S(1)}, u32[]{:S(2)}, u32[]{:S(2)}) collective-permute-start(bf16[2,6,1,384]{3,2,1,0:T(2,128)(2,1)S(1)} %get-tuple-element.22), channel_id=1, source_target_pairs={{0,1},{1,2},{2,3},{4,5},{5,6},{6,7},{8,9},{9,10},{10,11},{12,13},{... | collective-permute-start | bytes 27656 | tf_op jit(solution)/shard_map/ppermute | solution.py:33
  36.5 2.6 %collective-permute-start.4 = (bf16[2,6,1,384]{3,2,1,0:T(2,128)(2,1)S(1)}, bf16[2,6,1,384]{3,2,1,0:T(2,128)(2,1)S(1)}, u32[]{:S(2)}, u32[]{:S(2)}) collective-permute-start(bf16[2,6,1,384]{3,2,1,0:T(2,128)(2,1)S(1)} %get-tuple-element.23), channel_id=1, source_target_pairs={{1,0},{2,1},{3,2},{5,4},{6,5},{7,6},{9,8},{10,9},{11,10},{13,12},{... | collective-permute-start | bytes 27656 | tf_op jit(solution)/shard_map/ppermute | solution.py:34
  39.2 0.0 collective-permute-done.8
  39.2 0.0 collective-permute-done.3
  39.2 1.8 %collective-permute-done.4 = bf16[2,6,1,384]{3,2,1,0:T(2,128)(2,1)S(1)} collective-permute-done((bf16[2,6,1,384]{3,2,1,0:T(2,128)(2,1)S(1)}, bf16[2,6,1,384]{3,2,1,0:T(2,128)(2,1)S(1)}, u32[]{:S(2)}, u32[]{:S(2)}) %collective-permute-start.4) | collective-permute-done | bytes 9248 | tf_op jit(solution)/shard_map/ppermute | solution.py:34
  41.0 0.7 fusion.8
  41.7 0.1 pad.4.refs_0_
  41.7 0.1 collective-permute-start.15
  41.8 1.6 collective-permute-start.16
  43.4 0.1 select_bitcast_fusion
  43.5 9.1 %collective-permute-done.15.refs_1_ = bf16[3,5,40,384]{3,2,1,0:T(8,128)(2,1)S(1)} collective-permute-done((bf16[3,5,40,384]{3,2,1,0:T(8,128)(2,1)S(1)}, bf16[3,5,40,384]{3,2,1,0:T(8,128)(2,1)S(1)}, u32[]{:S(2)}, u32[]{:S(2)}) %collective-permute-start.15) | collective-permute-done | bytes 460832 | tf_op jit(solution)/shard_map/ppermute | solution.py:23
  52.6 2.1 %collective-permute-start.17 = (bf16[3,5,16,384]{3,2,1,0:T(8,128)(2,1)S(1)}, bf16[3,5,16,384]{3,2,1,0:T(8,128)(2,1)S(1)}, u32[]{:S(2)}, u32[]{:S(2)}) collective-permute-start(bf16[3,5,16,384]{3,2,1,0:T(8,128)(2,1)S(1)} %slice.102), channel_id=1, source_target_pairs={{0,12},{4,8},{8,4},{12,0},{1,13},{5,9},{9,5},{13,1},{2,14},{6,10},... | collective-permute-start | bytes 552968 | tf_op jit(solution)/shard_map/ppermute | solution.py:23
  54.7 0.0 collective-permute-done.16.refs_2_
  54.8 0.1 collective-permute-start.18
  55.0 4.8 %collective-permute-done.17 = bf16[3,5,16,384]{3,2,1,0:T(8,128)(2,1)S(1)} collective-permute-done((bf16[3,5,16,384]{3,2,1,0:T(8,128)(2,1)S(1)}, bf16[3,5,16,384]{3,2,1,0:T(8,128)(2,1)S(1)}, u32[]{:S(2)}, u32[]{:S(2)}) %collective-permute-start.17) | collective-permute-done | bytes 184352 | tf_op jit(solution)/shard_map/ppermute | solution.py:23
  59.9 3.3 %collective-permute-done.18 = bf16[3,5,24,384]{3,2,1,0:T(8,128)(2,1)S(1)} collective-permute-done((bf16[3,5,24,384]{3,2,1,0:T(8,128)(2,1)S(1)}, bf16[3,5,24,384]{3,2,1,0:T(8,128)(2,1)S(1)}, u32[]{:S(2)}, u32[]{:S(2)}) %collective-permute-start.18) | collective-permute-done | bytes 276512 | tf_op jit(solution)/shard_map/ppermute | solution.py:23
  63.3 0.0 copy-start.2
  63.3 1.2 pad_maximum_fusion
  64.6 0.4 collective-permute-start.19
  65.0 0.6 reshape.42.bias_ref
  65.5 0.9 pad_maximum_fusion.2.own_ref
  66.4 4.5 %shard_map.84.so_far_ref = f32[256,384]{1,0:T(8,128)} custom-call(bf16[2,6,34,384]{3,2,1,0:T(8,128)(2,1)} %pad_maximum_fusion.2.own_ref, f32[1,384]{1,0:T(1,128)} %reshape.42.bias_ref, bf16[3,3,3,384,384]{4,3,2,1,0:T(8,128)(2,1)} %bitcast.21), custom_call_target="tpu_custom_call" | custom-call | flops 679477248 | bytes 3145728 | tf_op jit(solution)/shard_map/pallas_call | solution.py:67
  70.9 0.9 pad_maximum_fusion.1.early_ref
  71.7 7.8 %shard_map.85 = (bf16[256,384]{1,0:T(8,128)(2,1)}, bf16[256,384]{1,0:T(8,128)(2,1)}, bf16[384,256]{1,0:T(8,128)(2,1)}) custom-call(bf16[2,6,34,384]{3,2,1,0:T(8,128)(2,1)} %pad_maximum_fusion.1.early_ref, bf16[2,6,34,384]{3,2,1,0:T(8,128)(2,1)} %pad_maximum_fusion.2.own_ref, f32[256,384]{1,0:T(8,128)} %shard_map.84.so_far_ref, bf16[256,384]{1,0:T(8,128)(2,1)} %bitcast.30, ...), custom_call_target="tpu_custom_call" | custom-call | flops 1358954496 | bytes 6291456 | tf_op jit(solution)/shard_map/pallas_call | solution.py:113
  79.6 9.3 %all_to_all.20.own_ref = bf16[4,96,256]{2,1,0:T(8,128)(2,1)S(1)} all-to-all(bf16[4,96,256]{2,1,0:T(8,128)(2,1)} %bitcast.29), channel_id=1, replica_groups=mesh['zh'=2,'co'=2,'x'=4,'y'=4,'z'=4] {'y'}, dimensions={0} | all-to-all | bytes 393216 | tf_op jit(solution)/shard_map/all_to_all | solution.py:222
  88.8 1.0 collective-permute-start.14
  89.8 0.1 pad_add_fusion.where_ref
  89.9 1.0 collective-permute-done.14.peer_ref
  90.9 8.7 %shard_map.87 = bf16[4,14,24,384]{3,2,1,0:T(8,128)(2,1)S(1)} custom-call(s32[2]{0:T(128)S(1)} %pad_add_fusion.where_ref, bf16[4,96,256]{2,1,0:T(8,128)(2,1)S(1)} %all_to_all.20.own_ref, bf16[4,96,256]{2,1,0:T(8,128)(2,1)S(1)} %collective-permute-done.14.peer_ref, bf16[3,5,40,384]{3,2,1,0:T(8,128)(2,1)S(1)} %pad.4.refs_0_, ...), custom_call_target="tpu_custom_call" | custom-call | flops 2113929216 | bytes 9437184 | tf_op jit(solution)/shard_map/pallas_call | solution.py:160
  99.6 16.7 %all_to_all.21 = bf16[4,14,24,384]{3,2,1,0:T(8,128)(2,1)S(1)} all-to-all(bf16[4,14,24,384]{3,2,1,0:T(8,128)(2,1)S(1)} %shard_map.87), channel_id=1, replica_groups=mesh['zh'=2,'co'=2,'x'=4,'y'=4,'z'=4] {'x'}, dimensions={0} | all-to-all | bytes 2064384 | tf_op jit(solution)/shard_map/all_to_all | solution.py:222
  116.3 0.2 reduce_sum.24
  116.5 0.8 reshape.49
  117.3 7.2 %all-to-all-start.2 = ((bf16[8,42,384]{2,1,0:T(8,128)(2,1)}), bf16[8,42,384]{2,1,0:T(8,128)(2,1)S(1)}, u32[]{:S(2)}, u32[]{:S(2)}) async-start(bf16[8,42,384]{2,1,0:T(8,128)(2,1)} %reshape.49), calls=%async_computation.2 | async-start | bytes 589824 | tf_op jit(solution)/shard_map/all_to_all | solution.py:222
  124.5 3.7 %collective-permute-start.10 = (bf16[2,1,32,384]{3,2,1,0:T(8,128)(2,1)S(1)}, bf16[2,1,32,384]{3,2,1,0:T(8,128)(2,1)S(1)}, u32[]{:S(2)}, u32[]{:S(2)}) collective-permute-start(bf16[2,1,32,384]{3,2,1,0:T(8,128)(2,1)S(1)} %get-tuple-element.25), channel_id=1, source_target_pairs={{4,0},{8,4},{12,8},{16,12},{20,16},{24,20},{28,24},{32,28},{36,32}... | collective-permute-start | bytes 147464 | tf_op jit(solution)/shard_map/ppermute | solution.py:19
  128.2 1.9 %collective-permute-start.9 = (bf16[2,1,32,384]{3,2,1,0:T(8,128)(2,1)S(1)}, bf16[2,1,32,384]{3,2,1,0:T(8,128)(2,1)S(1)}, u32[]{:S(2)}, u32[]{:S(2)}) collective-permute-start(bf16[2,1,32,384]{3,2,1,0:T(8,128)(2,1)S(1)} %get-tuple-element.24), channel_id=1, source_target_pairs={{0,4},{4,8},{8,12},{12,16},{16,20},{20,24},{24,28},{28,32},{32,36}... | collective-permute-start | bytes 147464 | tf_op jit(solution)/shard_map/ppermute | solution.py:19
  130.1 0.0 collective-permute-done.10
  130.1 5.3 %collective-permute-done.9 = bf16[2,1,32,384]{3,2,1,0:T(8,128)(2,1)S(1)} collective-permute-done((bf16[2,1,32,384]{3,2,1,0:T(8,128)(2,1)S(1)}, bf16[2,1,32,384]{3,2,1,0:T(8,128)(2,1)S(1)}, u32[]{:S(2)}, u32[]{:S(2)}) %collective-permute-start.9) | collective-permute-done | bytes 49184 | tf_op jit(solution)/shard_map/ppermute | solution.py:19
  135.5 2.8 %collective-permute-start.11 = (bf16[2,6,1,384]{3,2,1,0:T(2,128)(2,1)S(1)}, bf16[2,6,1,384]{3,2,1,0:T(2,128)(2,1)S(1)}, u32[]{:S(2)}, u32[]{:S(2)}) collective-permute-start(bf16[2,6,1,384]{3,2,1,0:T(2,128)(2,1)S(1)} %get-tuple-element.18), channel_id=1, source_target_pairs={{0,1},{1,2},{2,3},{4,5},{5,6},{6,7},{8,9},{9,10},{10,11},{12,13},{... | collective-permute-start | bytes 27656 | tf_op jit(solution)/shard_map/ppermute | solution.py:19
  138.3 2.5 %collective-permute-start.12 = (bf16[2,6,1,384]{3,2,1,0:T(2,128)(2,1)S(1)}, bf16[2,6,1,384]{3,2,1,0:T(2,128)(2,1)S(1)}, u32[]{:S(2)}, u32[]{:S(2)}) collective-permute-start(bf16[2,6,1,384]{3,2,1,0:T(2,128)(2,1)S(1)} %get-tuple-element.19), channel_id=1, source_target_pairs={{1,0},{2,1},{3,2},{5,4},{6,5},{7,6},{9,8},{10,9},{11,10},{13,12},{... | collective-permute-start | bytes 27656 | tf_op jit(solution)/shard_map/ppermute | solution.py:19
  140.8 0.0 all-to-all-done.2
  140.8 0.7 broadcast_in_dim.3
  141.6 5.5 %all-to-all-start.3 = ((bf16[8,42,384]{2,1,0:T(8,128)(2,1)}), bf16[8,42,384]{2,1,0:T(8,128)(2,1)S(1)}, u32[]{:S(2)}, u32[]{:S(2)}) async-start(bf16[8,42,384]{2,1,0:T(8,128)(2,1)} %broadcast_in_dim.3), calls=%async_computation.3 | async-start | bytes 589824 | tf_op jit(solution)/shard_map/all_to_all | solution.py:222
  147.0 0.0 collective-permute-done.11
  147.0 0.9 pad_maximum_fusion.3.rim_ref
  147.9 9.7 %shard_map.86 = (bf16[2,128,384]{2,1,0:T(8,128)(2,1)}, f32[2,128,384]{2,1,0:T(8,128)}) custom-call(bf16[2,6,34,384]{3,2,1,0:T(8,128)(2,1)} %pad_maximum_fusion.3.rim_ref, bf16[3,3,3,384,384]{4,3,2,1,0:T(8,128)(2,1)} %bitcast.23), custom_call_target="tpu_custom_call" | custom-call | flops 2038431744 | bytes 9437184 | tf_op jit(solution)/shard_map/pallas_call | solution.py:201
  157.7 6.8 %collective-permute-start.13 = (bf16[2,4,32,384]{3,2,1,0:T(8,128)(2,1)}, bf16[2,4,32,384]{3,2,1,0:T(8,128)(2,1)S(1)}, u32[]{:S(2)}, u32[]{:S(2)}) collective-permute-start(bf16[2,4,32,384]{3,2,1,0:T(8,128)(2,1)} %bitcast.32), channel_id=1, source_target_pairs={{64,0},{128,64},{192,128},{65,1},{129,65},{193,129},{66,2},{130,66... | collective-permute-start | bytes 589832 | tf_op jit(solution)/shard_map/ppermute | solution.py:19
  164.5 0.1 reshape.50
  164.6 0.1 collective-permute-start.20
  164.7 9.5 %collective-permute-done.13 = bf16[2,4,32,384]{3,2,1,0:T(8,128)(2,1)S(1)} collective-permute-done((bf16[2,4,32,384]{3,2,1,0:T(8,128)(2,1)}, bf16[2,4,32,384]{3,2,1,0:T(8,128)(2,1)S(1)}, u32[]{:S(2)}, u32[]{:S(2)}) %collective-permute-start.13) | collective-permute-done | bytes 196640 | tf_op jit(solution)/shard_map/ppermute | solution.py:19
  174.2 1.7 add_convert_fusion
  176.0 0.1 maximum_select_fusion
  176.2 1.0 convert_bitcast_fusion
  (36 shorter events, 0.6 us)
Async XLA Ops:
  0.6 20.0 %copy-start.1 = (bf16[2,4,32,384]{3,2,1,0:T(8,128)(2,1)S(1)}, bf16[2,4,32,384]{3,2,1,0:T(8,128)(2,1)}, u32[]{:S(2)}) copy-start(bf16[2,4,32,384]{3,2,1,0:T(8,128)(2,1)} %param.6) | copy-start | bytes 589828
  3.3 16.2 %collective-permute-start.5 = (bf16[2,1,32,384]{3,2,1,0:T(8,128)(2,1)S(1)}, bf16[2,1,32,384]{3,2,1,0:T(8,128)(2,1)S(1)}, u32[]{:S(2)}, u32[]{:S(2)}) collective-permute-start(bf16[2,1,32,384]{3,2,1,0:T(8,128)(2,1)S(1)} %get-tuple-element.27), channel_id=1, source_target_pairs={{0,4},{4,8},{8,12},{12,16},{16,20},{20,24},{24,28},{28,32},{32,36}... | collective-permute-start | bytes 147464 | tf_op jit(solution)/shard_map/ppermute | solution.py:33
  6.5 14.1 %collective-permute-start = (bf16[2,4,32,384]{3,2,1,0:T(8,128)(2,1)}, bf16[2,4,32,384]{3,2,1,0:T(8,128)(2,1)S(1)}, u32[]{:S(2)}, u32[]{:S(2)}) collective-permute-start(bf16[2,4,32,384]{3,2,1,0:T(8,128)(2,1)} %param.5), channel_id=1, source_target_pairs={{0,64},{64,128},{128,192},{1,65},{65,129},{129,193},{2,66},{66,130... | collective-permute-start | bytes 589832 | tf_op jit(solution)/shard_map/ppermute | solution.py:19
  15.3 5.4 %collective-permute-start.6 = (bf16[2,1,32,384]{3,2,1,0:T(8,128)(2,1)S(1)}, bf16[2,1,32,384]{3,2,1,0:T(8,128)(2,1)S(1)}, u32[]{:S(2)}, u32[]{:S(2)}) collective-permute-start(bf16[2,1,32,384]{3,2,1,0:T(8,128)(2,1)S(1)} %get-tuple-element.26), channel_id=1, source_target_pairs={{4,0},{8,4},{12,8},{16,12},{20,16},{24,20},{28,24},{32,28},{36,32}... | collective-permute-start | bytes 147464 | tf_op jit(solution)/shard_map/ppermute | solution.py:34
  20.7 13.1 %collective-permute-start.1 = (bf16[2,1,32,384]{3,2,1,0:T(8,128)(2,1)S(1)}, bf16[2,1,32,384]{3,2,1,0:T(8,128)(2,1)S(1)}, u32[]{:S(2)}, u32[]{:S(2)}) collective-permute-start(bf16[2,1,32,384]{3,2,1,0:T(8,128)(2,1)S(1)} %get-tuple-element.28), channel_id=1, source_target_pairs={{0,4},{4,8},{8,12},{12,16},{16,20},{20,24},{24,28},{28,32},{32,36}... | collective-permute-start | bytes 147464 | tf_op jit(solution)/shard_map/ppermute | solution.py:33
  23.7 10.1 %collective-permute-start.2 = (bf16[2,1,32,384]{3,2,1,0:T(8,128)(2,1)S(1)}, bf16[2,1,32,384]{3,2,1,0:T(8,128)(2,1)S(1)}, u32[]{:S(2)}, u32[]{:S(2)}) collective-permute-start(bf16[2,1,32,384]{3,2,1,0:T(8,128)(2,1)S(1)} %get-tuple-element.29), channel_id=1, source_target_pairs={{4,0},{8,4},{12,8},{16,12},{20,16},{24,20},{28,24},{32,28},{36,32}... | collective-permute-start | bytes 147464 | tf_op jit(solution)/shard_map/ppermute | solution.py:34
  28.5 10.7 %collective-permute-start.7 = (bf16[2,6,1,384]{3,2,1,0:T(2,128)(2,1)S(1)}, bf16[2,6,1,384]{3,2,1,0:T(2,128)(2,1)S(1)}, u32[]{:S(2)}, u32[]{:S(2)}) collective-permute-start(bf16[2,6,1,384]{3,2,1,0:T(2,128)(2,1)S(1)} %get-tuple-element.20), channel_id=1, source_target_pairs={{0,1},{1,2},{2,3},{4,5},{5,6},{6,7},{8,9},{9,10},{10,11},{12,13},{... | collective-permute-start | bytes 27656 | tf_op jit(solution)/shard_map/ppermute | solution.py:33
  31.1 8.0 %collective-permute-start.8 = (bf16[2,6,1,384]{3,2,1,0:T(2,128)(2,1)S(1)}, bf16[2,6,1,384]{3,2,1,0:T(2,128)(2,1)S(1)}, u32[]{:S(2)}, u32[]{:S(2)}) collective-permute-start(bf16[2,6,1,384]{3,2,1,0:T(2,128)(2,1)S(1)} %get-tuple-element.21), channel_id=1, source_target_pairs={{1,0},{2,1},{3,2},{5,4},{6,5},{7,6},{9,8},{10,9},{11,10},{13,12},{... | collective-permute-start | bytes 27656 | tf_op jit(solution)/shard_map/ppermute | solution.py:34
  33.8 5.3 %collective-permute-start.3 = (bf16[2,6,1,384]{3,2,1,0:T(2,128)(2,1)S(1)}, bf16[2,6,1,384]{3,2,1,0:T(2,128)(2,1)S(1)}, u32[]{:S(2)}, u32[]{:S(2)}) collective-permute-start(bf16[2,6,1,384]{3,2,1,0:T(2,128)(2,1)S(1)} %get-tuple-element.22), channel_id=1, source_target_pairs={{0,1},{1,2},{2,3},{4,5},{5,6},{6,7},{8,9},{9,10},{10,11},{12,13},{... | collective-permute-start | bytes 27656 | tf_op jit(solution)/shard_map/ppermute | solution.py:33
  36.5 4.5 %collective-permute-start.4 = (bf16[2,6,1,384]{3,2,1,0:T(2,128)(2,1)S(1)}, bf16[2,6,1,384]{3,2,1,0:T(2,128)(2,1)S(1)}, u32[]{:S(2)}, u32[]{:S(2)}) collective-permute-start(bf16[2,6,1,384]{3,2,1,0:T(2,128)(2,1)S(1)} %get-tuple-element.23), channel_id=1, source_target_pairs={{1,0},{2,1},{3,2},{5,4},{6,5},{7,6},{9,8},{10,9},{11,10},{13,12},{... | collective-permute-start | bytes 27656 | tf_op jit(solution)/shard_map/ppermute | solution.py:34
  41.7 10.9 %collective-permute-start.15 = (bf16[3,5,40,384]{3,2,1,0:T(8,128)(2,1)S(1)}, bf16[3,5,40,384]{3,2,1,0:T(8,128)(2,1)S(1)}, u32[]{:S(2)}, u32[]{:S(2)}) collective-permute-start(bf16[3,5,40,384]{3,2,1,0:T(8,128)(2,1)S(1)} %pad.4.refs_0_), channel_id=1, source_target_pairs={{0,4},{4,0},{8,12},{12,8},{1,5},{5,1},{9,13},{13,9},{2,6},{6,2},{1... | collective-permute-start | bytes 1382408 | tf_op jit(solution)/shard_map/ppermute | solution.py:23
  41.8 12.9 %collective-permute-start.16 = (bf16[3,5,40,384]{3,2,1,0:T(8,128)(2,1)S(1)}, bf16[3,5,40,384]{3,2,1,0:T(8,128)(2,1)S(1)}, u32[]{:S(2)}, u32[]{:S(2)}) collective-permute-start(bf16[3,5,40,384]{3,2,1,0:T(8,128)(2,1)S(1)} %pad.4.refs_0_), channel_id=1, source_target_pairs={{0,12},{4,8},{8,4},{12,0},{1,13},{5,9},{9,5},{13,1},{2,14},{6,10},... | collective-permute-start | bytes 1382408 | tf_op jit(solution)/shard_map/ppermute | solution.py:23
  52.6 7.2 %collective-permute-start.17 = (bf16[3,5,16,384]{3,2,1,0:T(8,128)(2,1)S(1)}, bf16[3,5,16,384]{3,2,1,0:T(8,128)(2,1)S(1)}, u32[]{:S(2)}, u32[]{:S(2)}) collective-permute-start(bf16[3,5,16,384]{3,2,1,0:T(8,128)(2,1)S(1)} %slice.102), channel_id=1, source_target_pairs={{0,12},{4,8},{8,4},{12,0},{1,13},{5,9},{9,5},{13,1},{2,14},{6,10},... | collective-permute-start | bytes 552968 | tf_op jit(solution)/shard_map/ppermute | solution.py:23
  54.8 8.4 %collective-permute-start.18 = (bf16[3,5,24,384]{3,2,1,0:T(8,128)(2,1)S(1)}, bf16[3,5,24,384]{3,2,1,0:T(8,128)(2,1)S(1)}, u32[]{:S(2)}, u32[]{:S(2)}) collective-permute-start(bf16[3,5,24,384]{3,2,1,0:T(8,128)(2,1)S(1)} %slice.103), channel_id=1, source_target_pairs={{0,4},{4,0},{8,12},{12,8},{1,5},{5,1},{9,13},{13,9},{2,6},{6,2},{1... | collective-permute-start | bytes 829448 | tf_op jit(solution)/shard_map/ppermute | solution.py:23
  63.3 1.7 copy-start.2
  64.6 26.3 %collective-permute-start.19 = (bf16[4,2,5,40,384]{4,3,2,1,0:T(8,128)(2,1)}, bf16[4,2,5,40,384]{4,3,2,1,0:T(8,128)(2,1)S(1)}, u32[]{:S(2)}, u32[]{:S(2)}) collective-permute-start(bf16[4,2,5,40,384]{4,3,2,1,0:T(8,128)(2,1)} %pad_maximum_fusion), channel_id=1, source_target_pairs={{0,64},{64,0},{1,65},{65,1},{2,66},{66,2},{3,67},{67,3},{4,68},{68... | collective-permute-start | bytes 3686408 | tf_op jit(solution)/shard_map/ppermute | solution.py:23
  88.8 2.1 %collective-permute-start.14 = (bf16[4,96,256]{2,1,0:T(8,128)(2,1)S(1)}, bf16[4,96,256]{2,1,0:T(8,128)(2,1)S(1)}, u32[]{:S(2)}, u32[]{:S(2)}) collective-permute-start(bf16[4,96,256]{2,1,0:T(8,128)(2,1)S(1)} %all_to_all.20.own_ref), channel_id=1, source_target_pairs={{0,64},{64,0},{1,65},{65,1},{2,66},{66,2},{3,67},{67,3},{4,68},{68... | collective-permute-start | bytes 589832 | tf_op jit(solution)/shard_map/ppermute | solution.py:23
  116.3 8.2 %copy-start = (bf16[256,384]{1,0:T(8,128)(2,1)S(1)}, bf16[256,384]{1,0:T(8,128)(2,1)}, u32[]{:S(2)}) copy-start(bf16[256,384]{1,0:T(8,128)(2,1)} %get-tuple-element.14) | copy-start | bytes 589828
  117.3 23.5 %all-to-all-start.2 = ((bf16[8,42,384]{2,1,0:T(8,128)(2,1)}), bf16[8,42,384]{2,1,0:T(8,128)(2,1)S(1)}, u32[]{:S(2)}, u32[]{:S(2)}) async-start(bf16[8,42,384]{2,1,0:T(8,128)(2,1)} %reshape.49), calls=%async_computation.2 | async-start | bytes 589824 | tf_op jit(solution)/shard_map/all_to_all | solution.py:222
  124.5 5.7 %collective-permute-start.10 = (bf16[2,1,32,384]{3,2,1,0:T(8,128)(2,1)S(1)}, bf16[2,1,32,384]{3,2,1,0:T(8,128)(2,1)S(1)}, u32[]{:S(2)}, u32[]{:S(2)}) collective-permute-start(bf16[2,1,32,384]{3,2,1,0:T(8,128)(2,1)S(1)} %get-tuple-element.25), channel_id=1, source_target_pairs={{4,0},{8,4},{12,8},{16,12},{20,16},{24,20},{28,24},{32,28},{36,32}... | collective-permute-start | bytes 147464 | tf_op jit(solution)/shard_map/ppermute | solution.py:19
  128.2 7.2 %collective-permute-start.9 = (bf16[2,1,32,384]{3,2,1,0:T(8,128)(2,1)S(1)}, bf16[2,1,32,384]{3,2,1,0:T(8,128)(2,1)S(1)}, u32[]{:S(2)}, u32[]{:S(2)}) collective-permute-start(bf16[2,1,32,384]{3,2,1,0:T(8,128)(2,1)S(1)} %get-tuple-element.24), channel_id=1, source_target_pairs={{0,4},{4,8},{8,12},{12,16},{16,20},{20,24},{24,28},{28,32},{32,36}... | collective-permute-start | bytes 147464 | tf_op jit(solution)/shard_map/ppermute | solution.py:19
  135.5 11.6 %collective-permute-start.11 = (bf16[2,6,1,384]{3,2,1,0:T(2,128)(2,1)S(1)}, bf16[2,6,1,384]{3,2,1,0:T(2,128)(2,1)S(1)}, u32[]{:S(2)}, u32[]{:S(2)}) collective-permute-start(bf16[2,6,1,384]{3,2,1,0:T(2,128)(2,1)S(1)} %get-tuple-element.18), channel_id=1, source_target_pairs={{0,1},{1,2},{2,3},{4,5},{5,6},{6,7},{8,9},{9,10},{10,11},{12,13},{... | collective-permute-start | bytes 27656 | tf_op jit(solution)/shard_map/ppermute | solution.py:19
  138.3 8.8 %collective-permute-start.12 = (bf16[2,6,1,384]{3,2,1,0:T(2,128)(2,1)S(1)}, bf16[2,6,1,384]{3,2,1,0:T(2,128)(2,1)S(1)}, u32[]{:S(2)}, u32[]{:S(2)}) collective-permute-start(bf16[2,6,1,384]{3,2,1,0:T(2,128)(2,1)S(1)} %get-tuple-element.19), channel_id=1, source_target_pairs={{1,0},{2,1},{3,2},{5,4},{6,5},{7,6},{9,8},{10,9},{11,10},{13,12},{... | collective-permute-start | bytes 27656 | tf_op jit(solution)/shard_map/ppermute | solution.py:19
  141.6 22.9 %all-to-all-start.3 = ((bf16[8,42,384]{2,1,0:T(8,128)(2,1)}), bf16[8,42,384]{2,1,0:T(8,128)(2,1)S(1)}, u32[]{:S(2)}, u32[]{:S(2)}) async-start(bf16[8,42,384]{2,1,0:T(8,128)(2,1)} %broadcast_in_dim.3), calls=%async_computation.3 | async-start | bytes 589824 | tf_op jit(solution)/shard_map/all_to_all | solution.py:222
  157.7 16.5 %collective-permute-start.13 = (bf16[2,4,32,384]{3,2,1,0:T(8,128)(2,1)}, bf16[2,4,32,384]{3,2,1,0:T(8,128)(2,1)S(1)}, u32[]{:S(2)}, u32[]{:S(2)}) collective-permute-start(bf16[2,4,32,384]{3,2,1,0:T(8,128)(2,1)} %bitcast.32), channel_id=1, source_target_pairs={{64,0},{128,64},{192,128},{65,1},{129,65},{193,129},{66,2},{130,66... | collective-permute-start | bytes 589832 | tf_op jit(solution)/shard_map/ppermute | solution.py:19
  164.6 11.4 %collective-permute-start.20 = (bf16[14,24,384]{2,1,0:T(8,128)(2,1)S(1)}, bf16[14,24,384]{2,1,0:T(8,128)(2,1)S(1)}, u32[]{:S(2)}, u32[]{:S(2)}) collective-permute-start(bf16[14,24,384]{2,1,0:T(8,128)(2,1)S(1)} %reshape.50), channel_id=1, source_target_pairs={{0,64},{64,0},{1,65},{65,1},{2,66},{66,2},{3,67},{67,3},{4,68},{68... | collective-permute-start | bytes 774152 | tf_op jit(solution)/shard_map/ppermute | solution.py:23

commit v7 on v5

--- a/solution.py
+++ b/solution.py
@@ -43,7 +43,7 @@
     return block.reshape(-1, block.shape[-1])
 
 
-def weight_grad_kernel(where_ref, own_ref, peer_ref, *refs):
+def weight_grad_kernel(where_ref, scaled_ref, *refs):
     lines, both_ref, out_ref, cols = refs[:4], refs[4], refs[5], refs[6]
     core = where_ref[0]
 
@@ -61,23 +61,22 @@
     k = pl.program_id(0) + 4 * core
     tap_t, tap_h, tap_w = k // 9, (k // 3) % 3, k % 3
     total = None
-    for ref, first in ((own_ref, 2 * core), (peer_ref, 2 * (1 - core))):
-        for src in range(4):
-            patch = cols[tap_w, pl.ds(tap_t + first, 2), pl.ds(4 * src + tap_h, 4)]
-            term = jnp.dot(ref[src], patch.reshape(256, 384), preferred_element_type=F32)
-            total = term if total is None else total + term
+    for src in range(8):
+        patch = cols[tap_w, pl.ds(tap_t + src // 4 * 2, 2), pl.ds(src % 4 * 4 + tap_h, 4)]
+        term = jnp.dot(scaled_ref[src], patch.reshape(256, 384), preferred_element_type=F32)
+        total = term if total is None else total + term
     for q in range(4):
         out_ref[q, 0] = total[24 * q : 24 * q + 24].astype(BF)
 
 
-def weight_grad(where, own, peer, lines, both):
+def weight_grad(where, scaled, lines, both):
     return pl.pallas_call(
         weight_grad_kernel,
         out_shape=jax.ShapeDtypeStruct((4, N_TAPS, 24, 384), BF),
         grid_spec=pltpu.PrefetchScalarGridSpec(
             num_scalar_prefetch=1,
             grid=(N_TAPS,),
-            in_specs=[pl.BlockSpec(memory_space=pltpu.VMEM)] * 7,
+            in_specs=[pl.BlockSpec(memory_space=pltpu.VMEM)] * 6,
             out_specs=pl.BlockSpec((4, 1, 24, 384), lambda j, *_: (0, j, 0, 0)),
             scratch_shapes=[pltpu.VMEM((3, 5, 18, 32, 384), BF)],
         ),
@@ -85,7 +84,7 @@
         cost_estimate=pl.CostEstimate(
             flops=2 * N_TAPS * 384 * 384 * 512, bytes_accessed=9 << 20, transcendentals=0
         ),
-    )(where, own, peer, *lines, both)
+    )(where, scaled, *lines, both)
 
 
 def input_grad_kernel(rim_ref, weight_ref, head_ref, tail_ref, cols, total):
@@ -191,16 +190,15 @@
     ).astype(BF)
     own = lax.dot_general(order, scaled, (((1,), (1,)), ((), ())), preferred_element_type=F32)
     own, *far = lax.optimization_barrier((own.astype(BF).reshape(4, 96, -1), *far))
-    own = across(own, "y")
+    both = across(jnp.concatenate([own, own]), ("co", "y"))
     line = [rows, *near, jnp.concatenate(far, 2)]
     line_peer = jnp.stack([jnp.where(core == 0, v[1:3], v[0:2]) for v in line])
     line_peer = exchanged(line_peer, "co", 1)
     scaled_rows = scaled.reshape(frames.shape)
     above = shifted(scaled_rows[:, -1:], HEIGHT, 1)
     below = shifted(scaled_rows[:, :1], HEIGHT, -1)
-    line_peer, above, below = lax.optimization_barrier((line_peer, above, below))
     where = jnp.stack([core, lax.axis_index("y")])
-    parts = weight_grad(where, own, exchanged(own, "co", 1), line, line_peer)
+    parts = weight_grad(where, both, line, line_peer)
     parts = across(parts, "x")
     mine = reduced_over_ring(jnp.sum(parts.astype(F32), 0))
     theirs = exchanged(mine, "co", 1)

time: 156 us -> 162 us (1.038)
  blocking collectives: 26.3 us -> 17.7 us
  starting transfers between devices: 59.9 us -> 65.9 us
  other arithmetic: 11.1 us -> 14.7 us
  waiting for transfers between devices: 25.5 us -> 28.8 us
    all_to_all x2 -> x1, blocking collectives: 26.3 us -> 17.7 us  [across(): return lax.all_to_all(value, axes, 0, 0, tiled=True)]
    all_to_all x2 -> x3, starting transfers between devices: 15.5 us -> 22 us  [across(): return lax.all_to_all(value, axes, 0, 0, tiled=True)]
    all_to_all x2 -> x3, waiting for transfers between devices: 5.06 us -> 7.88 us  [across(): return lax.all_to_all(value, axes, 0, 0, tiled=True)]
    ppermute x7 -> x6, starting transfers between devices: 9.36 us -> 7.36 us  [exchanged(): lax.ppermute(value, axis, [(i, i ^ flip) for i in range(lax.axis_size(axi...]
  transfers between devices with their start and end apart: 19 -> 19, of which waited for: 7 -> 7; matrix products, arithmetic and copies ran while one was open for 11% -> 13% of each run, Pallas kernels for 6% -> 6%
where the time goes in v7:
time: 162 us; the launch traced here: 160 us
  starting transfers between devices  65.9 us (41%)
  waiting for transfers between devices  28.8 us (18%)
  Pallas kernels  18.4 us (11%)
  blocking collectives  17.7 us (11%)
  other arithmetic  14.7 us (9%)
  matrix products  9.84 us (6%)
  local copies, waits for them, and re-layouts  3.31 us (2%)
    ppermute x6, starting transfers between devices, shifted(): return lax.ppermute(value, axis, pairs)  25.7 us
    all_to_all x3, starting transfers between devices, across(): return lax.all_to_all(value, axes, 0, 0, tiled=True)  22 us
    all_to_all x1, blocking collectives, across(): return lax.all_to_all(value, axes, 0, 0, tiled=True)  17.7 us
    ppermute x6, waiting for transfers between devices, shifted(): return lax.ppermute(value, axis, pairs)  15.7 us
    pallas_call x1, Pallas kernels, input_grad(): pl.pallas_call(input_grad_kernel, out_shape=[jax.ShapeDtypeStruct((2, 128...  9.75 us
    dot_general x27, matrix products, program(): lax.dot_general(block, weights[tap_t, tap_h, tap_w], (((1,), (1,)), ((),...  9.55 us
    pallas_call x1, Pallas kernels, weight_grad(): pl.pallas_call(weight_grad_kernel, out_shape=jax.ShapeDtypeStruct((4, N_T...  8.67 us
    ppermute x2, starting transfers between devices, with_halo(): before = lax.ppermute(last, axis, up)  7.96 us
  transfers between devices with their start and end apart: 19, of which 7 were waited for; matrix products, arithmetic and copies ran while one was open for 13% of the time, Pallas kernels for 6%

profile of v7, /device:TPU:1, one launch (start us, length us, event | category | flops | bytes accessed | tf_op | source)
XLA Modules:
  0.0 159.9 jit_solution(14654385783604948504)
XLA Ops:
  0.7 0.7 fusion.6
  1.5 10.2 %collective-permute-start = (bf16[2,4,32,384]{3,2,1,0:T(8,128)(2,1)}, bf16[2,4,32,384]{3,2,1,0:T(8,128)(2,1)S(1)}, u32[]{:S(2)}, u32[]{:S(2)}) collective-permute-start(bf16[2,4,32,384]{3,2,1,0:T(8,128)(2,1)} %param.5), channel_id=1, source_target_pairs={{0,64},{64,128},{128,192},{1,65},{65,129},{129,193},{2,66},{66,130... | collective-permute-start | bytes 589832 | tf_op jit(solution)/shard_map/ppermute | solution.py:19
  11.7 2.9 %collective-permute-done = bf16[2,4,32,384]{3,2,1,0:T(8,128)(2,1)S(1)} collective-permute-done((bf16[2,4,32,384]{3,2,1,0:T(8,128)(2,1)}, bf16[2,4,32,384]{3,2,1,0:T(8,128)(2,1)S(1)}, u32[]{:S(2)}, u32[]{:S(2)}) %collective-permute-start) | collective-permute-done | bytes 196640 | tf_op jit(solution)/shard_map/ppermute | solution.py:19
  14.6 0.9 pad_maximum_fusion.7
  15.5 3.2 %collective-permute-start.1 = (bf16[4,1,32,384]{3,2,1,0:T(8,128)(2,1)S(1)}, bf16[4,1,32,384]{3,2,1,0:T(8,128)(2,1)S(1)}, u32[]{:S(2)}, u32[]{:S(2)}) collective-permute-start(bf16[4,1,32,384]{3,2,1,0:T(8,128)(2,1)S(1)} %get-tuple-element.56), channel_id=1, source_target_pairs={{0,4},{4,8},{8,12},{12,16},{16,20},{20,24},{24,28},{28,32},{32,36}... | collective-permute-start | bytes 294920 | tf_op jit(solution)/shard_map/ppermute | solution.py:33
  18.7 1.3 collective-permute-start.2
  20.0 0.9 pad_maximum_fusion.5
  20.9 3.1 %collective-permute-done.2 = bf16[4,1,32,384]{3,2,1,0:T(8,128)(2,1)S(1)} collective-permute-done((bf16[4,1,32,384]{3,2,1,0:T(8,128)(2,1)S(1)}, bf16[4,1,32,384]{3,2,1,0:T(8,128)(2,1)S(1)}, u32[]{:S(2)}, u32[]{:S(2)}) %collective-permute-start.2) | collective-permute-done | bytes 98336 | tf_op jit(solution)/shard_map/ppermute | solution.py:34
  24.0 0.9 pad_maximum_fusion.8
  24.9 4.8 %collective-permute-start.3 = (bf16[4,6,1,384]{3,2,1,0:T(2,128)(2,1)S(1)}, bf16[4,6,1,384]{3,2,1,0:T(2,128)(2,1)S(1)}, u32[]{:S(2)}, u32[]{:S(2)}) collective-permute-start(bf16[4,6,1,384]{3,2,1,0:T(2,128)(2,1)S(1)} %get-tuple-element.45), channel_id=1, source_target_pairs={{0,1},{1,2},{2,3},{4,5},{5,6},{6,7},{8,9},{9,10},{10,11},{12,13},{... | collective-permute-start | bytes 55304 | tf_op jit(solution)/shard_map/ppermute | solution.py:33
  29.7 1.6 collective-permute-start.4
  31.3 1.1 pad_maximum_fusion.2
  32.5 1.2 fusion.16
  33.8 1.1 collective-permute-done.4
  35.0 1.5 fusion.8
  36.5 1.4 collective-permute-start.5
  37.9 3.2 %collective-permute-start.6 = (bf16[3,5,40,384]{3,2,1,0:T(8,128)(2,1)S(1)}, bf16[3,5,40,384]{3,2,1,0:T(8,128)(2,1)S(1)}, u32[]{:S(2)}, u32[]{:S(2)}) collective-permute-start(bf16[3,5,40,384]{3,2,1,0:T(8,128)(2,1)S(1)} %pad.4.refs_0_), channel_id=1, source_target_pairs={{0,12},{4,8},{8,4},{12,0},{1,13},{5,9},{9,5},{13,1},{2,14},{6,10},... | collective-permute-start | bytes 1382408 | tf_op jit(solution)/shard_map/ppermute | solution.py:23
  41.1 0.4 pad_maximum_fusion.1
  42.3 0.3 fusion.15
  42.7 0.3 convolution_add_fusion.22
  43.0 0.3 convolution_add_fusion.21
  43.3 0.3 convolution_add_fusion.20
  43.6 0.3 convolution_add_fusion.19
  43.9 0.3 fusion
  44.2 0.3 convolution_add_fusion.17
  44.5 0.3 convolution_add_fusion.16
  45.1 0.3 convolution_add_fusion.14
  45.4 0.3 convolution_add_fusion.13
  45.7 0.3 convolution_add_fusion.12
  46.0 0.3 convolution_add_fusion.11
  46.3 0.3 convolution_add_fusion.10
  46.6 0.3 convolution_add_fusion.9
  46.9 0.3 convolution_add_fusion.8
  47.2 0.3 convolution_add_fusion.7
  48.2 0.9 collective-permute-start.13
  49.1 1.8 %collective-permute-start.12 = (bf16[3,5,16,384]{3,2,1,0:T(8,128)(2,1)S(1)}, bf16[3,5,16,384]{3,2,1,0:T(8,128)(2,1)S(1)}, u32[]{:S(2)}, u32[]{:S(2)}) collective-permute-start(bf16[3,5,16,384]{3,2,1,0:T(8,128)(2,1)S(1)} %slice.300), channel_id=1, source_target_pairs={{0,12},{4,8},{8,4},{12,0},{1,13},{5,9},{9,5},{13,1},{2,14},{6,10},... | collective-permute-start | bytes 552968 | tf_op jit(solution)/shard_map/ppermute | solution.py:23
  50.9 0.3 convolution_add_fusion.5
  51.8 0.3 convolution_add_fusion.2
  52.1 0.3 convolution_add_fusion.1
  52.4 1.1 fusion.13
  53.8 0.9 collective-permute-done.12
  54.9 1.3 pad_maximum_fusion
  56.2 0.8 pad_maximum_fusion.3
  56.9 3.9 %all-to-all-start = ((bf16[8,96,256]{2,1,0:T(8,128)(2,1)}), bf16[8,96,256]{2,1,0:T(8,128)(2,1)S(1)}, u32[]{:S(2)}, u32[]{:S(2)}) async-start(bf16[8,96,256]{2,1,0:T(8,128)(2,1)} %pad_maximum_fusion.3), calls=%async_computation | async-start | bytes 786432 | tf_op jit(solution)/shard_map/all_to_all | solution.py:138
  60.9 7.9 %all-to-all-done.scaled_ref = bf16[8,96,256]{2,1,0:T(8,128)(2,1)S(1)} async-done(((bf16[8,96,256]{2,1,0:T(8,128)(2,1)}), bf16[8,96,256]{2,1,0:T(8,128)(2,1)S(1)}, u32[]{:S(2)}, u32[]{:S(2)}) %all-to-all-start) | async-done | bytes 393248 | tf_op jit(solution)/shard_map/all_to_all | solution.py:138
  68.8 8.7 %shard_map.85 = bf16[4,14,24,384]{3,2,1,0:T(8,128)(2,1)S(1)} custom-call(s32[2]{0:T(128)S(1)} %pad_add_fusion.where_ref, bf16[8,96,256]{2,1,0:T(8,128)(2,1)S(1)} %all-to-all-done.scaled_ref, bf16[3,5,40,384]{3,2,1,0:T(8,128)(2,1)S(1)} %pad.4.refs_0_, bf16[3,5,40,384]{3,2,1,0:T(8,128)(2,1)S(1)} %collective-permute-done.5.refs_1_, ...), custom_call_target="tpu_custom_call" | custom-call | flops 2113929216 | bytes 9437184 | tf_op jit(solution)/shard_map/pallas_call | solution.py:73
  77.4 17.7 %all_to_all.20 = bf16[4,14,24,384]{3,2,1,0:T(8,128)(2,1)S(1)} all-to-all(bf16[4,14,24,384]{3,2,1,0:T(8,128)(2,1)S(1)} %shard_map.85), channel_id=1, replica_groups=mesh['zh'=2,'co'=2,'x'=4,'y'=4,'z'=4] {'x'}, dimensions={0} | all-to-all | bytes 2064384 | tf_op jit(solution)/shard_map/all_to_all | solution.py:138
  95.3 0.8 reshape.153
  96.1 11.8 %all-to-all-start.2 = ((bf16[8,42,384]{2,1,0:T(8,128)(2,1)}), bf16[8,42,384]{2,1,0:T(8,128)(2,1)S(1)}, u32[]{:S(2)}, u32[]{:S(2)}) async-start(bf16[8,42,384]{2,1,0:T(8,128)(2,1)} %reshape.153), calls=%async_computation.2 | async-start | bytes 589824 | tf_op jit(solution)/shard_map/all_to_all | solution.py:138
  107.9 0.8 fusion.31
  108.8 2.9 %collective-permute-start.7 = (bf16[2,1,32,384]{3,2,1,0:T(8,128)(2,1)S(1)}, bf16[2,1,32,384]{3,2,1,0:T(8,128)(2,1)S(1)}, u32[]{:S(2)}, u32[]{:S(2)}) collective-permute-start(bf16[2,1,32,384]{3,2,1,0:T(8,128)(2,1)S(1)} %get-tuple-element.60), channel_id=1, source_target_pairs={{0,4},{4,8},{8,12},{12,16},{16,20},{20,24},{24,28},{28,32},{32,36}... | collective-permute-start | bytes 147464 | tf_op jit(solution)/shard_map/ppermute | solution.py:19
  111.7 1.3 collective-permute-start.8
  113.0 3.8 %collective-permute-done.8 = bf16[2,1,32,384]{3,2,1,0:T(8,128)(2,1)S(1)} collective-permute-done((bf16[2,1,32,384]{3,2,1,0:T(8,128)(2,1)S(1)}, bf16[2,1,32,384]{3,2,1,0:T(8,128)(2,1)S(1)}, u32[]{:S(2)}, u32[]{:S(2)}) %collective-permute-start.8) | collective-permute-done | bytes 49184 | tf_op jit(solution)/shard_map/ppermute | solution.py:19
  116.8 0.9 pad_maximum_fusion.14
  117.7 1.3 collective-permute-start.10
  119.0 4.0 %collective-permute-start.9 = (bf16[2,6,1,384]{3,2,1,0:T(2,128)(2,1)S(1)}, bf16[2,6,1,384]{3,2,1,0:T(2,128)(2,1)S(1)}, u32[]{:S(2)}, u32[]{:S(2)}) collective-permute-start(bf16[2,6,1,384]{3,2,1,0:T(2,128)(2,1)S(1)} %get-tuple-element.58), channel_id=1, source_target_pairs={{0,1},{1,2},{2,3},{4,5},{5,6},{6,7},{8,9},{9,10},{10,11},{12,13},{... | collective-permute-start | bytes 27656 | tf_op jit(solution)/shard_map/ppermute | solution.py:19
  123.0 0.8 broadcast_in_dim.4
  123.8 6.4 %all-to-all-start.3 = ((bf16[8,42,384]{2,1,0:T(8,128)(2,1)}), bf16[8,42,384]{2,1,0:T(8,128)(2,1)S(1)}, u32[]{:S(2)}, u32[]{:S(2)}) async-start(bf16[8,42,384]{2,1,0:T(8,128)(2,1)} %broadcast_in_dim.4), calls=%async_computation.3 | async-start | bytes 589824 | tf_op jit(solution)/shard_map/all_to_all | solution.py:138
  130.1 1.8 %pad_maximum_fusion.4.rim_ref = bf16[2,6,34,384]{3,2,1,0:T(8,128)(2,1)} fusion(bf16[2,6,1,384]{3,2,1,0:T(2,128)(2,1)S(1)} %collective-permute-done.10, bf16[2,1,32,384]{3,2,1,0:T(8,128)(2,1)S(1)} %collective-permute-done.8, bf16[2,4,32,384]{3,2,1,0:T(8,128)(2,1)} %bitcast.196, bf16[2,1,32,384]{3,2,1,0:T(8,128)(2,1)S(1)} %collective-permute-done.7, ...), kind=kLoop, calls=%fused_computation.61 | loop fusion | flops 1566720 | bytes 626688 | tf_op jit(solution)/shard_map/concatenate | solution.py:215
  132.0 9.7 %shard_map.84 = (bf16[2,128,384]{2,1,0:T(8,128)(2,1)}, f32[2,128,384]{2,1,0:T(8,128)}) custom-call(bf16[2,6,34,384]{3,2,1,0:T(8,128)(2,1)} %pad_maximum_fusion.4.rim_ref, bf16[3,3,3,384,384]{4,3,2,1,0:T(8,128)(2,1)} %bitcast.163), custom_call_target="tpu_custom_call" | custom-call | flops 2038431744 | bytes 9437184 | tf_op jit(solution)/shard_map/pallas_call | solution.py:117
  141.7 6.0 %collective-permute-start.11 = (bf16[2,4,32,384]{3,2,1,0:T(8,128)(2,1)}, bf16[2,4,32,384]{3,2,1,0:T(8,128)(2,1)S(1)}, u32[]{:S(2)}, u32[]{:S(2)}) collective-permute-start(bf16[2,4,32,384]{3,2,1,0:T(8,128)(2,1)} %bitcast.225), channel_id=1, source_target_pairs={{64,0},{128,64},{192,128},{65,1},{129,65},{193,129},{66,2},{130,66... | collective-permute-start | bytes 589832 | tf_op jit(solution)/shard_map/ppermute | solution.py:19
  148.0 9.0 %collective-permute-done.11 = bf16[2,4,32,384]{3,2,1,0:T(8,128)(2,1)S(1)} collective-permute-done((bf16[2,4,32,384]{3,2,1,0:T(8,128)(2,1)}, bf16[2,4,32,384]{3,2,1,0:T(8,128)(2,1)S(1)}, u32[]{:S(2)}, u32[]{:S(2)}) %collective-permute-start.11) | collective-permute-done | bytes 196640 | tf_op jit(solution)/shard_map/ppermute | solution.py:19
  156.9 1.7 %add_convert_fusion = bf16[2,4,32,384]{3,2,1,0:T(8,128)(2,1)} fusion(f32[2,4,32,384]{3,2,1,0:T(8,128)} %bitcast.223, bf16[2,4,32,384]{3,2,1,0:T(8,128)(2,1)S(1)} %collective-permute-done.11), kind=kLoop, calls=%fused_computation.58 | loop fusion | flops 294912 | bytes 786432 | tf_op jit(solution)/shard_map/convert_element_type | solution.py:219
  158.9 1.0 convert_bitcast_fusion
  (60 shorter events, 3.8 us)
Async XLA Ops:
  0.6 40.5 %copy-start = (bf16[2,4,32,384]{3,2,1,0:T(8,128)(2,1)S(1)}, bf16[2,4,32,384]{3,2,1,0:T(8,128)(2,1)}, u32[]{:S(2)}) copy-start(bf16[2,4,32,384]{3,2,1,0:T(8,128)(2,1)} %param.5) | copy-start | bytes 589828
  1.5 13.1 %collective-permute-start = (bf16[2,4,32,384]{3,2,1,0:T(8,128)(2,1)}, bf16[2,4,32,384]{3,2,1,0:T(8,128)(2,1)S(1)}, u32[]{:S(2)}, u32[]{:S(2)}) collective-permute-start(bf16[2,4,32,384]{3,2,1,0:T(8,128)(2,1)} %param.5), channel_id=1, source_target_pairs={{0,64},{64,128},{128,192},{1,65},{65,129},{129,193},{2,66},{66,130... | collective-permute-start | bytes 589832 | tf_op jit(solution)/shard_map/ppermute | solution.py:19
  15.5 5.4 %collective-permute-start.1 = (bf16[4,1,32,384]{3,2,1,0:T(8,128)(2,1)S(1)}, bf16[4,1,32,384]{3,2,1,0:T(8,128)(2,1)S(1)}, u32[]{:S(2)}, u32[]{:S(2)}) collective-permute-start(bf16[4,1,32,384]{3,2,1,0:T(8,128)(2,1)S(1)} %get-tuple-element.56), channel_id=1, source_target_pairs={{0,4},{4,8},{8,12},{12,16},{16,20},{20,24},{24,28},{28,32},{32,36}... | collective-permute-start | bytes 294920 | tf_op jit(solution)/shard_map/ppermute | solution.py:33
  18.7 5.4 %collective-permute-start.2 = (bf16[4,1,32,384]{3,2,1,0:T(8,128)(2,1)S(1)}, bf16[4,1,32,384]{3,2,1,0:T(8,128)(2,1)S(1)}, u32[]{:S(2)}, u32[]{:S(2)}) collective-permute-start(bf16[4,1,32,384]{3,2,1,0:T(8,128)(2,1)S(1)} %get-tuple-element.57), channel_id=1, source_target_pairs={{4,0},{8,4},{12,8},{16,12},{20,16},{24,20},{28,24},{32,28},{36,32}... | collective-permute-start | bytes 294920 | tf_op jit(solution)/shard_map/ppermute | solution.py:34
  24.9 8.9 %collective-permute-start.3 = (bf16[4,6,1,384]{3,2,1,0:T(2,128)(2,1)S(1)}, bf16[4,6,1,384]{3,2,1,0:T(2,128)(2,1)S(1)}, u32[]{:S(2)}, u32[]{:S(2)}) collective-permute-start(bf16[4,6,1,384]{3,2,1,0:T(2,128)(2,1)S(1)} %get-tuple-element.45), channel_id=1, source_target_pairs={{0,1},{1,2},{2,3},{4,5},{5,6},{6,7},{8,9},{9,10},{10,11},{12,13},{... | collective-permute-start | bytes 55304 | tf_op jit(solution)/shard_map/ppermute | solution.py:33
  29.7 12.3 %slice-start = ((s8[7962624]{0:T(1024)(128)(4,1)}), s8[4194304]{0:T(1024)(128)(4,1)S(1)}, s32[]{:S(2)}) async-start(s8[7962624]{0:T(1024)(128)(4,1)} %bitcast.164), calls=%async_computation.4 | async-start | bytes 8388608
  29.7 5.3 %collective-permute-start.4 = (bf16[4,6,1,384]{3,2,1,0:T(2,128)(2,1)S(1)}, bf16[4,6,1,384]{3,2,1,0:T(2,128)(2,1)S(1)}, u32[]{:S(2)}, u32[]{:S(2)}) collective-permute-start(bf16[4,6,1,384]{3,2,1,0:T(2,128)(2,1)S(1)} %get-tuple-element.44), channel_id=1, source_target_pairs={{1,0},{2,1},{3,2},{5,4},{6,5},{7,6},{9,8},{10,9},{11,10},{13,12},{... | collective-permute-start | bytes 55304 | tf_op jit(solution)/shard_map/ppermute | solution.py:34
  32.5 10.2 %copy-start.2 = (f32[384]{0:T(512)S(1)}, f32[384]{0:T(512)}, u32[]{:S(2)}) copy-start(f32[384]{0:T(512)} %param.8) | copy-start | bytes 4612
  36.5 5.6 %slice-start.1 = ((s8[7962624]{0:T(1024)(128)(4,1)}), s8[3768320]{0:T(1024)(128)(4,1)S(1)}, s32[]{:S(2)}) async-start(s8[7962624]{0:T(1024)(128)(4,1)} %bitcast.164), calls=%async_computation.5 | async-start | bytes 7536640
  36.5 11.6 %collective-permute-start.5 = (bf16[3,5,40,384]{3,2,1,0:T(8,128)(2,1)S(1)}, bf16[3,5,40,384]{3,2,1,0:T(8,128)(2,1)S(1)}, u32[]{:S(2)}, u32[]{:S(2)}) collective-permute-start(bf16[3,5,40,384]{3,2,1,0:T(8,128)(2,1)S(1)} %pad.4.refs_0_), channel_id=1, source_target_pairs={{0,4},{4,0},{8,12},{12,8},{1,5},{5,1},{9,13},{13,9},{2,6},{6,2},{1... | collective-permute-start | bytes 1382408 | tf_op jit(solution)/shard_map/ppermute | solution.py:23
  37.9 10.2 %collective-permute-start.6 = (bf16[3,5,40,384]{3,2,1,0:T(8,128)(2,1)S(1)}, bf16[3,5,40,384]{3,2,1,0:T(8,128)(2,1)S(1)}, u32[]{:S(2)}, u32[]{:S(2)}) collective-permute-start(bf16[3,5,40,384]{3,2,1,0:T(8,128)(2,1)S(1)} %pad.4.refs_0_), channel_id=1, source_target_pairs={{0,12},{4,8},{8,4},{12,0},{1,13},{5,9},{9,5},{13,1},{2,14},{6,10},... | collective-permute-start | bytes 1382408 | tf_op jit(solution)/shard_map/ppermute | solution.py:23
  46.6 5.8 %copy-start.3 = (bf16[2,4,32,384]{3,2,1,0:T(8,128)(2,1)S(1)}, bf16[2,4,32,384]{3,2,1,0:T(8,128)(2,1)}, u32[]{:S(2)}) copy-start(bf16[2,4,32,384]{3,2,1,0:T(8,128)(2,1)} %param.9) | copy-start | bytes 589828
  48.2 6.6 %collective-permute-start.13 = (bf16[3,5,24,384]{3,2,1,0:T(8,128)(2,1)S(1)}, bf16[3,5,24,384]{3,2,1,0:T(8,128)(2,1)S(1)}, u32[]{:S(2)}, u32[]{:S(2)}) collective-permute-start(bf16[3,5,24,384]{3,2,1,0:T(8,128)(2,1)S(1)} %slice.301), channel_id=1, source_target_pairs={{0,4},{4,0},{8,12},{12,8},{1,5},{5,1},{9,13},{13,9},{2,6},{6,2},{1... | collective-permute-start | bytes 829448 | tf_op jit(solution)/shard_map/ppermute | solution.py:23
  49.1 5.7 %collective-permute-start.12 = (bf16[3,5,16,384]{3,2,1,0:T(8,128)(2,1)S(1)}, bf16[3,5,16,384]{3,2,1,0:T(8,128)(2,1)S(1)}, u32[]{:S(2)}, u32[]{:S(2)}) collective-permute-start(bf16[3,5,16,384]{3,2,1,0:T(8,128)(2,1)S(1)} %slice.300), channel_id=1, source_target_pairs={{0,12},{4,8},{8,4},{12,0},{1,13},{5,9},{9,5},{13,1},{2,14},{6,10},... | collective-permute-start | bytes 552968 | tf_op jit(solution)/shard_map/ppermute | solution.py:23
  53.5 1.4 copy-start.1
  56.1 12.6 %collective-permute-start.14 = (bf16[4,2,5,40,384]{4,3,2,1,0:T(8,128)(2,1)}, bf16[4,2,5,40,384]{4,3,2,1,0:T(8,128)(2,1)S(1)}, u32[]{:S(2)}, u32[]{:S(2)}) collective-permute-start(bf16[4,2,5,40,384]{4,3,2,1,0:T(8,128)(2,1)} %pad_maximum_fusion), channel_id=1, source_target_pairs={{0,64},{64,0},{1,65},{65,1},{2,66},{66,2},{3,67},{67,3},{4,68},{68... | collective-permute-start | bytes 3686408 | tf_op jit(solution)/shard_map/ppermute | solution.py:23
  56.9 11.8 %all-to-all-start = ((bf16[8,96,256]{2,1,0:T(8,128)(2,1)}), bf16[8,96,256]{2,1,0:T(8,128)(2,1)S(1)}, u32[]{:S(2)}, u32[]{:S(2)}) async-start(bf16[8,96,256]{2,1,0:T(8,128)(2,1)} %pad_maximum_fusion.3), calls=%async_computation | async-start | bytes 786432 | tf_op jit(solution)/shard_map/all_to_all | solution.py:138
  96.1 26.8 %all-to-all-start.2 = ((bf16[8,42,384]{2,1,0:T(8,128)(2,1)}), bf16[8,42,384]{2,1,0:T(8,128)(2,1)S(1)}, u32[]{:S(2)}, u32[]{:S(2)}) async-start(bf16[8,42,384]{2,1,0:T(8,128)(2,1)} %reshape.153), calls=%async_computation.2 | async-start | bytes 589824 | tf_op jit(solution)/shard_map/all_to_all | solution.py:138
  108.8 4.2 %collective-permute-start.7 = (bf16[2,1,32,384]{3,2,1,0:T(8,128)(2,1)S(1)}, bf16[2,1,32,384]{3,2,1,0:T(8,128)(2,1)S(1)}, u32[]{:S(2)}, u32[]{:S(2)}) collective-permute-start(bf16[2,1,32,384]{3,2,1,0:T(8,128)(2,1)S(1)} %get-tuple-element.60), channel_id=1, source_target_pairs={{0,4},{4,8},{8,12},{12,16},{16,20},{20,24},{24,28},{28,32},{32,36}... | collective-permute-start | bytes 147464 | tf_op jit(solution)/shard_map/ppermute | solution.py:19
  111.7 5.1 %collective-permute-start.8 = (bf16[2,1,32,384]{3,2,1,0:T(8,128)(2,1)S(1)}, bf16[2,1,32,384]{3,2,1,0:T(8,128)(2,1)S(1)}, u32[]{:S(2)}, u32[]{:S(2)}) collective-permute-start(bf16[2,1,32,384]{3,2,1,0:T(8,128)(2,1)S(1)} %get-tuple-element.61), channel_id=1, source_target_pairs={{4,0},{8,4},{12,8},{16,12},{20,16},{24,20},{28,24},{32,28},{36,32}... | collective-permute-start | bytes 147464 | tf_op jit(solution)/shard_map/ppermute | solution.py:19
  117.7 12.5 %collective-permute-start.10 = (bf16[2,6,1,384]{3,2,1,0:T(2,128)(2,1)S(1)}, bf16[2,6,1,384]{3,2,1,0:T(2,128)(2,1)S(1)}, u32[]{:S(2)}, u32[]{:S(2)}) collective-permute-start(bf16[2,6,1,384]{3,2,1,0:T(2,128)(2,1)S(1)} %get-tuple-element.59), channel_id=1, source_target_pairs={{1,0},{2,1},{3,2},{5,4},{6,5},{7,6},{9,8},{10,9},{11,10},{13,12},{... | collective-permute-start | bytes 27656 | tf_op jit(solution)/shard_map/ppermute | solution.py:19
  119.0 11.2 %collective-permute-start.9 = (bf16[2,6,1,384]{3,2,1,0:T(2,128)(2,1)S(1)}, bf16[2,6,1,384]{3,2,1,0:T(2,128)(2,1)S(1)}, u32[]{:S(2)}, u32[]{:S(2)}) collective-permute-start(bf16[2,6,1,384]{3,2,1,0:T(2,128)(2,1)S(1)} %get-tuple-element.58), channel_id=1, source_target_pairs={{0,1},{1,2},{2,3},{4,5},{5,6},{6,7},{8,9},{9,10},{10,11},{12,13},{... | collective-permute-start | bytes 27656 | tf_op jit(solution)/shard_map/ppermute | solution.py:19
  123.8 24.0 %all-to-all-start.3 = ((bf16[8,42,384]{2,1,0:T(8,128)(2,1)}), bf16[8,42,384]{2,1,0:T(8,128)(2,1)S(1)}, u32[]{:S(2)}, u32[]{:S(2)}) async-start(bf16[8,42,384]{2,1,0:T(8,128)(2,1)} %broadcast_in_dim.4), calls=%async_computation.3 | async-start | bytes 589824 | tf_op jit(solution)/shard_map/all_to_all | solution.py:138
  141.7 15.2 %collective-permute-start.11 = (bf16[2,4,32,384]{3,2,1,0:T(8,128)(2,1)}, bf16[2,4,32,384]{3,2,1,0:T(8,128)(2,1)S(1)}, u32[]{:S(2)}, u32[]{:S(2)}) collective-permute-start(bf16[2,4,32,384]{3,2,1,0:T(8,128)(2,1)} %bitcast.225), channel_id=1, source_target_pairs={{64,0},{128,64},{192,128},{65,1},{129,65},{193,129},{66,2},{130,66... | collective-permute-start | bytes 589832 | tf_op jit(solution)/shard_map/ppermute | solution.py:19
  147.9 10.8 %collective-permute-start.15 = (bf16[14,24,384]{2,1,0:T(8,128)(2,1)S(1)}, bf16[14,24,384]{2,1,0:T(8,128)(2,1)S(1)}, u32[]{:S(2)}, u32[]{:S(2)}) collective-permute-start(bf16[14,24,384]{2,1,0:T(8,128)(2,1)S(1)} %reshape.154), channel_id=1, source_target_pairs={{0,64},{64,0},{1,65},{65,1},{2,66},{66,2},{3,67},{67,3},{4,68},{68... | collective-permute-start | bytes 774152 | tf_op jit(solution)/shard_map/ppermute | solution.py:23

commit v8 on v7

--- a/solution.py
+++ b/solution.py
@@ -1,3 +1,5 @@
+import functools
+
 import jax
 import jax.numpy as jnp
 from jax import lax
@@ -58,15 +60,22 @@
                 for f in range(2):
                     cols[c, f + 3 * (1 - core), pl.ds(at, 5)] = both_ref[n, f, :, c : c + 32, :]
 
-    k = pl.program_id(0) + 4 * core
-    tap_t, tap_h, tap_w = k // 9, (k // 3) % 3, k % 3
     total = None
+    taps = [2 * pl.program_id(0) + n + 4 * core for n in range(2)]
     for src in range(8):
-        patch = cols[tap_w, pl.ds(tap_t + src // 4 * 2, 2), pl.ds(src % 4 * 4 + tap_h, 4)]
-        term = jnp.dot(scaled_ref[src], patch.reshape(256, 384), preferred_element_type=F32)
+        patch = jnp.concatenate(
+            [
+                cols[k % 3, pl.ds(k // 9 + src // 4 * 2, 2), pl.ds(src % 4 * 4 + k // 3 % 3, 4)]
+                .reshape(256, 384)
+                for k in taps
+            ],
+            1,
+        )
+        term = jnp.dot(scaled_ref[src], patch, preferred_element_type=F32)
         total = term if total is None else total + term
-    for q in range(4):
-        out_ref[q, 0] = total[24 * q : 24 * q + 24].astype(BF)
+    for n in range(2):
+        for q in range(4):
+            out_ref[q, n] = total[24 * q : 24 * q + 24, 384 * n : 384 * n + 384].astype(BF)
 
 
 def weight_grad(where, scaled, lines, both):
@@ -75,9 +84,9 @@
         out_shape=jax.ShapeDtypeStruct((4, N_TAPS, 24, 384), BF),
         grid_spec=pltpu.PrefetchScalarGridSpec(
             num_scalar_prefetch=1,
-            grid=(N_TAPS,),
+            grid=(N_TAPS // 2,),
             in_specs=[pl.BlockSpec(memory_space=pltpu.VMEM)] * 6,
-            out_specs=pl.BlockSpec((4, 1, 24, 384), lambda j, *_: (0, j, 0, 0)),
+            out_specs=pl.BlockSpec((4, 2, 24, 384), lambda j, *_: (0, j, 0, 0)),
             scratch_shapes=[pltpu.VMEM((3, 5, 18, 32, 384), BF)],
         ),
         compiler_params=pltpu.CompilerParams(vmem_limit_bytes=16 << 20),
@@ -87,7 +96,8 @@
     )(where, scaled, *lines, both)
 
 
-def input_grad_kernel(rim_ref, weight_ref, head_ref, tail_ref, cols, total):
+def input_grad_kernel(one_frame, one_slot, rim_ref, *refs):
+    more, weight_ref, out_ref, cols, total = refs[:-4], refs[-4], refs[-3], refs[-2], refs[-1]
     step = pl.program_id(0)
 
     @pl.when(step == 0)
@@ -96,42 +106,46 @@
         for c in range(3):
             cols[c] = rim_ref[:, :, 2 - c : 34 - c, :]
 
-    tap_t, tap_h = step // 3, step % 3
-    term = None
-    for c in range(3):
-        block = cols[c, :, pl.ds(2 - tap_h, 4)].reshape(256, 384)
-        part = jnp.dot(block, weight_ref[0, 0, c], preferred_element_type=F32)
-        term = part if term is None else term + part
-    total[pl.ds(tap_t, 2)] += term.reshape(2, 128, 384)
-
-    @pl.when(step == 8)
-    def _():
-        head_ref[...] = total[:2].astype(BF)
-        tail_ref[...] = total[2:]
-
-
-def input_grad(rimmed, weights):
-    def whole(shape):
-        return pl.BlockSpec(shape, lambda j: (0,) * len(shape))
-
+    rows = pl.ds(2 - step % 3, 4)
+    weight = weight_ref[0, 0].reshape(1152, 384)
+
+    @pl.when(step < 3)
+    def _():
+        block = jnp.concatenate([cols[c, :, rows].reshape(256, 384) for c in range(3)], 1)
+        term = jnp.dot(block, weight, preferred_element_type=F32)
+        total[...] += term.reshape(2, 128, 384)
+
+    @pl.when(step >= 3)
+    def _():
+        block = jnp.concatenate([cols[c, one_frame, rows].reshape(128, 384) for c in range(3)], 1)
+        total[one_slot] += jnp.dot(block, weight, preferred_element_type=F32)
+
+    @pl.when(step == 5)
+    def _():
+        result = total[...]
+        for ref in more:
+            result = result + ref[...].astype(F32)
+        out_ref[...] = result.astype(BF)
+
+
+def input_grad(rimmed, weights, tap_t, one_frame, one_slot, more=()):
     return pl.pallas_call(
-        input_grad_kernel,
-        out_shape=[
-            jax.ShapeDtypeStruct((2, 128, 384), BF),
-            jax.ShapeDtypeStruct((2, 128, 384), F32),
+        functools.partial(input_grad_kernel, one_frame, one_slot),
+        out_shape=jax.ShapeDtypeStruct((2, 128, 384), BF),
+        grid=(6,),
+        in_specs=[pl.BlockSpec(memory_space=pltpu.VMEM)] * (1 + len(more))
+        + [
+            pl.BlockSpec(
+                (1, 1, 3, 384, 384), lambda j: (jnp.where(j < 3, tap_t, 1), j % 3, 0, 0, 0)
+            )
         ],
-        grid=(9,),
-        in_specs=[
-            pl.BlockSpec(memory_space=pltpu.VMEM),
-            pl.BlockSpec((1, 1, 3, 384, 384), lambda j: (j // 3, j % 3, 0, 0, 0)),
-        ],
-        out_specs=[whole((2, 128, 384)), whole((2, 128, 384))],
-        scratch_shapes=[pltpu.VMEM((3, 2, 6, 32, 384), BF), pltpu.VMEM((4, 128, 384), F32)],
+        out_specs=pl.BlockSpec((2, 128, 384), lambda j: (0, 0, 0)),
+        scratch_shapes=[pltpu.VMEM((3, 2, 6, 32, 384), BF), pltpu.VMEM((2, 128, 384), F32)],
         compiler_params=pltpu.CompilerParams(vmem_limit_bytes=60 << 20),
         cost_estimate=pl.CostEstimate(
-            flops=2 * 27 * 256 * 384 * 384, bytes_accessed=9 << 20, transcendentals=0
+            flops=27 * 256 * 384 * 384, bytes_accessed=6 << 20, transcendentals=0
         ),
-    )(rimmed, weights)
+    )(rimmed, *more, weights)
 
 
 def across(value, axes):
@@ -213,10 +227,10 @@
     left = shifted(tall[:, :, -1:], "z", 1)
     right = shifted(tall[:, :, :1], "z", -1)
     grad_rimmed = jnp.concatenate([left, tall, right], 2)
-    head, tail = input_grad(grad_rimmed, weights)
-    cache_grad = head.reshape(frames.shape)
-    carried = shifted(cache_grad, TM, -1)
-    frame_grad = (tail.reshape(frames.shape) + carried.astype(F32)).astype(BF)
+    head = input_grad(grad_rimmed, weights, 0, 0, 1)
+    carried = shifted(head, TM, -1)
+    tail = input_grad(grad_rimmed, weights, 2, 1, 0, (carried,))
+    cache_grad, frame_grad = head.reshape(frames.shape), tail.reshape(frames.shape)
     return (decoded, frame_grad, cache_grad, kernel_grad)
 
 

time: 162 us -> 173 us (1.068)
  the two profiles are of different devices: /device:TPU:1 before, /device:TPU:57 now
where the time goes in v8:
time: 173 us; the launch traced here: 172 us
  starting transfers between devices  51.8 us (30%)
  blocking collectives  37.5 us (22%)
  waiting for transfers between devices  34 us (20%)
  Pallas kernels  20.4 us (12%)
  other arithmetic  12.9 us (7%)
  matrix products  9.87 us (6%)
  local copies, waits for them, and re-layouts  4.16 us (2%)
    all_to_all x2, blocking collectives, across(): return lax.all_to_all(value, axes, 0, 0, tiled=True)  37.5 us
    ppermute x6, starting transfers between devices, shifted(): return lax.ppermute(value, axis, pairs)  29 us
    ppermute x6, waiting for transfers between devices, shifted(): return lax.ppermute(value, axis, pairs)  22.1 us
    pallas_call x2, Pallas kernels, input_grad(): pl.pallas_call(functools.partial(input_grad_kernel, one_frame, one_slot),...  13.3 us
    all_to_all x2, starting transfers between devices, across(): return lax.all_to_all(value, axes, 0, 0, tiled=True)  9.68 us
    dot_general x27, matrix products, program(): lax.dot_general(block, weights[tap_t, tap_h, tap_w], (((1,), (1,)), ((),...  9.59 us
    pallas_call x1, Pallas kernels, weight_grad(): pl.pallas_call(weight_grad_kernel, out_shape=jax.ShapeDtypeStruct((4, N_T...  7.09 us
    all_to_all x2, waiting for transfers between devices, across(): return lax.all_to_all(value, axes, 0, 0, tiled=True)  5.94 us
  transfers between devices with their start and end apart: 18, of which 8 were waited for; matrix products, arithmetic and copies ran while one was open for 10% of the time, Pallas kernels for 8%

profile of v8, /device:TPU:57, one launch (start us, length us, event | category | flops | bytes accessed | tf_op | source)
XLA Modules:
  0.0 171.9 jit_solution(16424037763404232849)
XLA Ops:
  0.7 0.7 fusion.6
  1.5 8.5 %collective-permute-start = (bf16[2,4,32,384]{3,2,1,0:T(8,128)(2,1)}, bf16[2,4,32,384]{3,2,1,0:T(8,128)(2,1)S(1)}, u32[]{:S(2)}, u32[]{:S(2)}) collective-permute-start(bf16[2,4,32,384]{3,2,1,0:T(8,128)(2,1)} %param.5), channel_id=1, source_target_pairs={{0,64},{64,128},{128,192},{1,65},{65,129},{129,193},{2,66},{66,130... | collective-permute-start | bytes 589832 | tf_op jit(solution)/shard_map/ppermute | solution.py:21
  10.0 5.0 %collective-permute-done = bf16[2,4,32,384]{3,2,1,0:T(8,128)(2,1)S(1)} collective-permute-done((bf16[2,4,32,384]{3,2,1,0:T(8,128)(2,1)}, bf16[2,4,32,384]{3,2,1,0:T(8,128)(2,1)S(1)}, u32[]{:S(2)}, u32[]{:S(2)}) %collective-permute-start) | collective-permute-done | bytes 196640 | tf_op jit(solution)/shard_map/ppermute | solution.py:21
  15.0 0.9 pad_maximum_fusion.7
  15.9 2.8 %collective-permute-start.1 = (bf16[4,1,32,384]{3,2,1,0:T(8,128)(2,1)S(1)}, bf16[4,1,32,384]{3,2,1,0:T(8,128)(2,1)S(1)}, u32[]{:S(2)}, u32[]{:S(2)}) collective-permute-start(bf16[4,1,32,384]{3,2,1,0:T(8,128)(2,1)S(1)} %get-tuple-element.52), channel_id=1, source_target_pairs={{0,4},{4,8},{8,12},{12,16},{16,20},{20,24},{24,28},{28,32},{32,36}... | collective-permute-start | bytes 294920 | tf_op jit(solution)/shard_map/ppermute | solution.py:35
  18.6 2.5 %collective-permute-start.2 = (bf16[4,1,32,384]{3,2,1,0:T(8,128)(2,1)S(1)}, bf16[4,1,32,384]{3,2,1,0:T(8,128)(2,1)S(1)}, u32[]{:S(2)}, u32[]{:S(2)}) collective-permute-start(bf16[4,1,32,384]{3,2,1,0:T(8,128)(2,1)S(1)} %get-tuple-element.53), channel_id=1, source_target_pairs={{4,0},{8,4},{12,8},{16,12},{20,16},{24,20},{28,24},{32,28},{36,32}... | collective-permute-start | bytes 294920 | tf_op jit(solution)/shard_map/ppermute | solution.py:36
  21.2 0.9 pad_maximum_fusion.5
  22.1 4.0 %collective-permute-done.2 = bf16[4,1,32,384]{3,2,1,0:T(8,128)(2,1)S(1)} collective-permute-done((bf16[4,1,32,384]{3,2,1,0:T(8,128)(2,1)S(1)}, bf16[4,1,32,384]{3,2,1,0:T(8,128)(2,1)S(1)}, u32[]{:S(2)}, u32[]{:S(2)}) %collective-permute-start.2) | collective-permute-done | bytes 98336 | tf_op jit(solution)/shard_map/ppermute | solution.py:36
  26.1 0.9 pad_maximum_fusion.8
  27.0 2.6 %collective-permute-start.3 = (bf16[4,6,1,384]{3,2,1,0:T(2,128)(2,1)S(1)}, bf16[4,6,1,384]{3,2,1,0:T(2,128)(2,1)S(1)}, u32[]{:S(2)}, u32[]{:S(2)}) collective-permute-start(bf16[4,6,1,384]{3,2,1,0:T(2,128)(2,1)S(1)} %get-tuple-element.41), channel_id=1, source_target_pairs={{0,1},{1,2},{2,3},{4,5},{5,6},{6,7},{8,9},{9,10},{10,11},{12,13},{... | collective-permute-start | bytes 55304 | tf_op jit(solution)/shard_map/ppermute | solution.py:35
  29.7 2.9 %collective-permute-start.4 = (bf16[4,6,1,384]{3,2,1,0:T(2,128)(2,1)S(1)}, bf16[4,6,1,384]{3,2,1,0:T(2,128)(2,1)S(1)}, u32[]{:S(2)}, u32[]{:S(2)}) collective-permute-start(bf16[4,6,1,384]{3,2,1,0:T(2,128)(2,1)S(1)} %get-tuple-element.40), channel_id=1, source_target_pairs={{1,0},{2,1},{3,2},{5,4},{6,5},{7,6},{9,8},{10,9},{11,10},{13,12},{... | collective-permute-start | bytes 55304 | tf_op jit(solution)/shard_map/ppermute | solution.py:36
  32.6 1.1 pad_maximum_fusion.2
  33.8 1.3 fusion.16
  35.2 1.5 fusion.8
  36.9 0.4 pad_maximum_fusion.1
  37.9 0.9 slice-done.1
  39.1 0.3 fusion.15
  39.5 0.3 convolution_add_fusion.22
  39.8 0.3 convolution_add_fusion.21
  40.1 0.3 convolution_add_fusion.20
  40.4 0.3 convolution_add_fusion.19
  40.7 0.3 fusion
  41.0 0.3 convolution_add_fusion.17
  41.3 0.3 convolution_add_fusion.16
  41.6 0.3 convolution_add_fusion.15
  41.8 0.3 convolution_add_fusion.14
  42.1 0.3 convolution_add_fusion.13
  42.4 0.3 convolution_add_fusion.12
  42.7 0.3 convolution_add_fusion.11
  43.0 0.3 convolution_add_fusion.10
  43.3 0.3 convolution_add_fusion.9
  43.6 0.3 convolution_add_fusion.8
  44.5 0.3 convolution_add_fusion.6
  44.8 0.7 collective-permute-done.6.refs_2_
  45.6 0.5 collective-permute-start.13
  46.1 1.5 collective-permute-start.12
  47.6 0.3 convolution_add_fusion.5
  47.9 0.3 convolution_add_fusion.4
  49.1 1.1 fusion.13
  50.6 1.2 collective-permute-done.12
  52.0 1.2 pad_maximum_fusion
  53.2 0.8 pad_maximum_fusion.3
  54.0 5.2 %all-to-all-start = ((bf16[8,96,256]{2,1,0:T(8,128)(2,1)}), bf16[8,96,256]{2,1,0:T(8,128)(2,1)S(1)}, u32[]{:S(2)}, u32[]{:S(2)}) async-start(bf16[8,96,256]{2,1,0:T(8,128)(2,1)} %pad_maximum_fusion.3), calls=%async_computation | async-start | bytes 786432 | tf_op jit(solution)/shard_map/all_to_all | solution.py:152
  59.2 5.9 %all-to-all-done.scaled_ref = bf16[8,96,256]{2,1,0:T(8,128)(2,1)S(1)} async-done(((bf16[8,96,256]{2,1,0:T(8,128)(2,1)}), bf16[8,96,256]{2,1,0:T(8,128)(2,1)S(1)}, u32[]{:S(2)}, u32[]{:S(2)}) %all-to-all-start) | async-done | bytes 393248 | tf_op jit(solution)/shard_map/all_to_all | solution.py:152
  65.2 7.1 %shard_map.86 = bf16[4,14,24,384]{3,2,1,0:T(8,128)(2,1)S(1)} custom-call(s32[2]{0:T(128)S(1)} %pad_add_fusion.where_ref, bf16[8,96,256]{2,1,0:T(8,128)(2,1)S(1)} %all-to-all-done.scaled_ref, bf16[3,5,40,384]{3,2,1,0:T(8,128)(2,1)S(1)} %pad.4.refs_0_, bf16[3,5,40,384]{3,2,1,0:T(8,128)(2,1)S(1)} %collective-permute-done.5.refs_1_, ...), custom_call_target="tpu_custom_call" | custom-call | flops 2113929216 | bytes 9437184 | tf_op jit(solution)/shard_map/pallas_call | solution.py:82
  72.3 16.9 %all_to_all.20 = bf16[4,14,24,384]{3,2,1,0:T(8,128)(2,1)S(1)} all-to-all(bf16[4,14,24,384]{3,2,1,0:T(8,128)(2,1)S(1)} %shard_map.86), channel_id=1, replica_groups=mesh['zh'=2,'co'=2,'x'=4,'y'=4,'z'=4] {'x'}, dimensions={0} | all-to-all | bytes 2064384 | tf_op jit(solution)/shard_map/all_to_all | solution.py:152
  89.5 20.6 %all_to_all.21 = bf16[8,42,384]{2,1,0:T(8,128)(2,1)S(1)} all-to-all(bf16[8,42,384]{2,1,0:T(8,128)(2,1)S(1)} %reshape.153), channel_id=1, replica_groups=mesh['zh'=2,'co'=2,'x'=4,'y'=4,'z'=4] {'zh','z'}, dimensions={0} | all-to-all | bytes 516096 | tf_op jit(solution)/shard_map/all_to_all | solution.py:152
  110.2 0.7 broadcast_in_dim.4
  110.9 4.5 %all-to-all-start.3 = ((bf16[8,42,384]{2,1,0:T(8,128)(2,1)}), bf16[8,42,384]{2,1,0:T(8,128)(2,1)S(1)}, u32[]{:S(2)}, u32[]{:S(2)}) async-start(bf16[8,42,384]{2,1,0:T(8,128)(2,1)} %broadcast_in_dim.4), calls=%async_computation.3 | async-start | bytes 589824 | tf_op jit(solution)/shard_map/all_to_all | solution.py:152
  115.4 0.8 fusion.31
  116.2 4.9 %collective-permute-start.7 = (bf16[2,1,32,384]{3,2,1,0:T(8,128)(2,1)S(1)}, bf16[2,1,32,384]{3,2,1,0:T(8,128)(2,1)S(1)}, u32[]{:S(2)}, u32[]{:S(2)}) collective-permute-start(bf16[2,1,32,384]{3,2,1,0:T(8,128)(2,1)S(1)} %get-tuple-element.56), channel_id=1, source_target_pairs={{0,4},{4,8},{8,12},{12,16},{16,20},{20,24},{24,28},{28,32},{32,36}... | collective-permute-start | bytes 147464 | tf_op jit(solution)/shard_map/ppermute | solution.py:21
  121.2 1.9 %collective-permute-start.8 = (bf16[2,1,32,384]{3,2,1,0:T(8,128)(2,1)S(1)}, bf16[2,1,32,384]{3,2,1,0:T(8,128)(2,1)S(1)}, u32[]{:S(2)}, u32[]{:S(2)}) collective-permute-start(bf16[2,1,32,384]{3,2,1,0:T(8,128)(2,1)S(1)} %get-tuple-element.57), channel_id=1, source_target_pairs={{4,0},{8,4},{12,8},{16,12},{20,16},{24,20},{28,24},{32,28},{36,32}... | collective-permute-start | bytes 147464 | tf_op jit(solution)/shard_map/ppermute | solution.py:21
  123.1 5.1 %collective-permute-done.8 = bf16[2,1,32,384]{3,2,1,0:T(8,128)(2,1)S(1)} collective-permute-done((bf16[2,1,32,384]{3,2,1,0:T(8,128)(2,1)S(1)}, bf16[2,1,32,384]{3,2,1,0:T(8,128)(2,1)S(1)}, u32[]{:S(2)}, u32[]{:S(2)}) %collective-permute-start.8) | collective-permute-done | bytes 49184 | tf_op jit(solution)/shard_map/ppermute | solution.py:21
  128.2 0.9 pad_maximum_fusion.14
  129.1 1.9 %collective-permute-start.10 = (bf16[2,6,1,384]{3,2,1,0:T(2,128)(2,1)S(1)}, bf16[2,6,1,384]{3,2,1,0:T(2,128)(2,1)S(1)}, u32[]{:S(2)}, u32[]{:S(2)}) collective-permute-start(bf16[2,6,1,384]{3,2,1,0:T(2,128)(2,1)S(1)} %get-tuple-element.55), channel_id=1, source_target_pairs={{1,0},{2,1},{3,2},{5,4},{6,5},{7,6},{9,8},{10,9},{11,10},{13,12},{... | collective-permute-start | bytes 27656 | tf_op jit(solution)/shard_map/ppermute | solution.py:21
  131.0 3.4 %collective-permute-start.9 = (bf16[2,6,1,384]{3,2,1,0:T(2,128)(2,1)S(1)}, bf16[2,6,1,384]{3,2,1,0:T(2,128)(2,1)S(1)}, u32[]{:S(2)}, u32[]{:S(2)}) collective-permute-start(bf16[2,6,1,384]{3,2,1,0:T(2,128)(2,1)S(1)} %get-tuple-element.54), channel_id=1, source_target_pairs={{0,1},{1,2},{2,3},{4,5},{5,6},{6,7},{8,9},{9,10},{10,11},{12,13},{... | collective-permute-start | bytes 27656 | tf_op jit(solution)/shard_map/ppermute | solution.py:21
  134.4 1.1 collective-permute-done.9
  135.5 1.8 %pad_maximum_fusion.4.rim_ref = bf16[2,6,34,384]{3,2,1,0:T(8,128)(2,1)} fusion(bf16[2,6,1,384]{3,2,1,0:T(2,128)(2,1)S(1)} %collective-permute-done.10, bf16[2,1,32,384]{3,2,1,0:T(8,128)(2,1)S(1)} %collective-permute-done.8, bf16[2,4,32,384]{3,2,1,0:T(8,128)(2,1)} %bitcast.197, bf16[2,1,32,384]{3,2,1,0:T(8,128)(2,1)S(1)} %collective-permute-done.7, ...), kind=kLoop, calls=%fused_computation.60 | loop fusion | flops 1566720 | bytes 626688 | tf_op jit(solution)/shard_map/concatenate | solution.py:229
  137.3 6.6 %shard_map.84 = bf16[2,128,384]{2,1,0:T(8,128)(2,1)} custom-call(bf16[2,6,34,384]{3,2,1,0:T(8,128)(2,1)} %pad_maximum_fusion.4.rim_ref, bf16[3,3,3,384,384]{4,3,2,1,0:T(8,128)(2,1)} %bitcast.163), custom_call_target="tpu_custom_call" | custom-call | flops 1019215872 | bytes 6291456 | tf_op jit(solution)/shard_map/pallas_call | solution.py:132
  143.9 8.4 %collective-permute-start.11 = (bf16[2,128,384]{2,1,0:T(8,128)(2,1)}, bf16[2,128,384]{2,1,0:T(8,128)(2,1)S(1)}, u32[]{:S(2)}, u32[]{:S(2)}) collective-permute-start(bf16[2,128,384]{2,1,0:T(8,128)(2,1)} %shard_map.84), channel_id=1, source_target_pairs={{64,0},{128,64},{192,128},{65,1},{129,65},{193,129},{66,2},{130,66... | collective-permute-start | bytes 589832 | tf_op jit(solution)/shard_map/ppermute | solution.py:21
  152.5 10.9 %collective-permute-done.11.refs_0_ = bf16[2,128,384]{2,1,0:T(8,128)(2,1)S(1)} collective-permute-done((bf16[2,128,384]{2,1,0:T(8,128)(2,1)}, bf16[2,128,384]{2,1,0:T(8,128)(2,1)S(1)}, u32[]{:S(2)}, u32[]{:S(2)}) %collective-permute-start.11) | collective-permute-done | bytes 196640 | tf_op jit(solution)/shard_map/ppermute | solution.py:21
  163.4 0.7 copy-done.2
  164.0 6.7 %shard_map.85 = bf16[2,128,384]{2,1,0:T(8,128)(2,1)} custom-call(bf16[2,6,34,384]{3,2,1,0:T(8,128)(2,1)} %pad_maximum_fusion.4.rim_ref, bf16[2,128,384]{2,1,0:T(8,128)(2,1)} %copy-done.2, bf16[3,3,3,384,384]{4,3,2,1,0:T(8,128)(2,1)} %bitcast.164), custom_call_target="tpu_custom_call" | custom-call | flops 1019215872 | bytes 6291456 | tf_op jit(solution)/shard_map/pallas_call | solution.py:132
  170.9 1.0 convert_bitcast_fusion
  (61 shorter events, 4.1 us)
Async XLA Ops:
  0.6 36.3 %copy-start = (bf16[2,4,32,384]{3,2,1,0:T(8,128)(2,1)S(1)}, bf16[2,4,32,384]{3,2,1,0:T(8,128)(2,1)}, u32[]{:S(2)}) copy-start(bf16[2,4,32,384]{3,2,1,0:T(8,128)(2,1)} %param.5) | copy-start | bytes 589828
  1.5 13.5 %collective-permute-start = (bf16[2,4,32,384]{3,2,1,0:T(8,128)(2,1)}, bf16[2,4,32,384]{3,2,1,0:T(8,128)(2,1)S(1)}, u32[]{:S(2)}, u32[]{:S(2)}) collective-permute-start(bf16[2,4,32,384]{3,2,1,0:T(8,128)(2,1)} %param.5), channel_id=1, source_target_pairs={{0,64},{64,128},{128,192},{1,65},{65,129},{129,193},{2,66},{66,130... | collective-permute-start | bytes 589832 | tf_op jit(solution)/shard_map/ppermute | solution.py:21
  15.9 6.2 %collective-permute-start.1 = (bf16[4,1,32,384]{3,2,1,0:T(8,128)(2,1)S(1)}, bf16[4,1,32,384]{3,2,1,0:T(8,128)(2,1)S(1)}, u32[]{:S(2)}, u32[]{:S(2)}) collective-permute-start(bf16[4,1,32,384]{3,2,1,0:T(8,128)(2,1)S(1)} %get-tuple-element.52), channel_id=1, source_target_pairs={{0,4},{4,8},{8,12},{12,16},{16,20},{20,24},{24,28},{28,32},{32,36}... | collective-permute-start | bytes 294920 | tf_op jit(solution)/shard_map/ppermute | solution.py:35
  18.6 7.5 %collective-permute-start.2 = (bf16[4,1,32,384]{3,2,1,0:T(8,128)(2,1)S(1)}, bf16[4,1,32,384]{3,2,1,0:T(8,128)(2,1)S(1)}, u32[]{:S(2)}, u32[]{:S(2)}) collective-permute-start(bf16[4,1,32,384]{3,2,1,0:T(8,128)(2,1)S(1)} %get-tuple-element.53), channel_id=1, source_target_pairs={{4,0},{8,4},{12,8},{16,12},{20,16},{24,20},{28,24},{32,28},{36,32}... | collective-permute-start | bytes 294920 | tf_op jit(solution)/shard_map/ppermute | solution.py:36
  27.0 8.1 %collective-permute-start.3 = (bf16[4,6,1,384]{3,2,1,0:T(2,128)(2,1)S(1)}, bf16[4,6,1,384]{3,2,1,0:T(2,128)(2,1)S(1)}, u32[]{:S(2)}, u32[]{:S(2)}) collective-permute-start(bf16[4,6,1,384]{3,2,1,0:T(2,128)(2,1)S(1)} %get-tuple-element.41), channel_id=1, source_target_pairs={{0,1},{1,2},{2,3},{4,5},{5,6},{6,7},{8,9},{9,10},{10,11},{12,13},{... | collective-permute-start | bytes 55304 | tf_op jit(solution)/shard_map/ppermute | solution.py:35
  29.7 8.2 %slice-start = ((s8[7962624]{0:T(1024)(128)(4,1)}), s8[4194304]{0:T(1024)(128)(4,1)S(1)}, s32[]{:S(2)}) async-start(s8[7962624]{0:T(1024)(128)(4,1)} %bitcast.165), calls=%async_computation.4 | async-start | bytes 8388608
  29.7 5.5 %collective-permute-start.4 = (bf16[4,6,1,384]{3,2,1,0:T(2,128)(2,1)S(1)}, bf16[4,6,1,384]{3,2,1,0:T(2,128)(2,1)S(1)}, u32[]{:S(2)}, u32[]{:S(2)}) collective-permute-start(bf16[4,6,1,384]{3,2,1,0:T(2,128)(2,1)S(1)} %get-tuple-element.40), channel_id=1, source_target_pairs={{1,0},{2,1},{3,2},{5,4},{6,5},{7,6},{9,8},{10,9},{11,10},{13,12},{... | collective-permute-start | bytes 55304 | tf_op jit(solution)/shard_map/ppermute | solution.py:36
  33.8 5.7 %copy-start.3 = (f32[384]{0:T(512)S(1)}, f32[384]{0:T(512)}, u32[]{:S(2)}) copy-start(f32[384]{0:T(512)} %param.8) | copy-start | bytes 4612
  36.7 2.1 %slice-start.1 = ((s8[7962624]{0:T(1024)(128)(4,1)}), s8[3768320]{0:T(1024)(128)(4,1)S(1)}, s32[]{:S(2)}) async-start(s8[7962624]{0:T(1024)(128)(4,1)} %bitcast.165), calls=%async_computation.5 | async-start | bytes 7536640
  36.7 8.1 %collective-permute-start.5 = (bf16[3,5,40,384]{3,2,1,0:T(8,128)(2,1)S(1)}, bf16[3,5,40,384]{3,2,1,0:T(8,128)(2,1)S(1)}, u32[]{:S(2)}, u32[]{:S(2)}) collective-permute-start(bf16[3,5,40,384]{3,2,1,0:T(8,128)(2,1)S(1)} %pad.4.refs_0_), channel_id=1, source_target_pairs={{0,4},{4,0},{8,12},{12,8},{1,5},{5,1},{9,13},{13,9},{2,6},{6,2},{1... | collective-permute-start | bytes 1382408 | tf_op jit(solution)/shard_map/ppermute | solution.py:25
  36.8 8.6 %collective-permute-start.6 = (bf16[3,5,40,384]{3,2,1,0:T(8,128)(2,1)S(1)}, bf16[3,5,40,384]{3,2,1,0:T(8,128)(2,1)S(1)}, u32[]{:S(2)}, u32[]{:S(2)}) collective-permute-start(bf16[3,5,40,384]{3,2,1,0:T(8,128)(2,1)S(1)} %pad.4.refs_0_), channel_id=1, source_target_pairs={{0,12},{4,8},{8,4},{12,0},{1,13},{5,9},{9,5},{13,1},{2,14},{6,10},... | collective-permute-start | bytes 1382408 | tf_op jit(solution)/shard_map/ppermute | solution.py:25
  43.3 5.8 %copy-start.4 = (bf16[2,4,32,384]{3,2,1,0:T(8,128)(2,1)S(1)}, bf16[2,4,32,384]{3,2,1,0:T(8,128)(2,1)}, u32[]{:S(2)}) copy-start(bf16[2,4,32,384]{3,2,1,0:T(8,128)(2,1)} %param.9) | copy-start | bytes 589828
  45.6 6.2 %collective-permute-start.13 = (bf16[3,5,24,384]{3,2,1,0:T(8,128)(2,1)S(1)}, bf16[3,5,24,384]{3,2,1,0:T(8,128)(2,1)S(1)}, u32[]{:S(2)}, u32[]{:S(2)}) collective-permute-start(bf16[3,5,24,384]{3,2,1,0:T(8,128)(2,1)S(1)} %slice.301), channel_id=1, source_target_pairs={{0,4},{4,0},{8,12},{12,8},{1,5},{5,1},{9,13},{13,9},{2,6},{6,2},{1... | collective-permute-start | bytes 829448 | tf_op jit(solution)/shard_map/ppermute | solution.py:25
  46.1 5.7 %collective-permute-start.12 = (bf16[3,5,16,384]{3,2,1,0:T(8,128)(2,1)S(1)}, bf16[3,5,16,384]{3,2,1,0:T(8,128)(2,1)S(1)}, u32[]{:S(2)}, u32[]{:S(2)}) collective-permute-start(bf16[3,5,16,384]{3,2,1,0:T(8,128)(2,1)S(1)} %slice.300), channel_id=1, source_target_pairs={{0,12},{4,8},{8,4},{12,0},{1,13},{5,9},{9,5},{13,1},{2,14},{6,10},... | collective-permute-start | bytes 552968 | tf_op jit(solution)/shard_map/ppermute | solution.py:25
  50.2 1.7 copy-start.1
  53.2 12.0 %collective-permute-start.14 = (bf16[4,2,5,40,384]{4,3,2,1,0:T(8,128)(2,1)}, bf16[4,2,5,40,384]{4,3,2,1,0:T(8,128)(2,1)S(1)}, u32[]{:S(2)}, u32[]{:S(2)}) collective-permute-start(bf16[4,2,5,40,384]{4,3,2,1,0:T(8,128)(2,1)} %pad_maximum_fusion), channel_id=1, source_target_pairs={{0,64},{64,0},{1,65},{65,1},{2,66},{66,2},{3,67},{67,3},{4,68},{68... | collective-permute-start | bytes 3686408 | tf_op jit(solution)/shard_map/ppermute | solution.py:25
  54.0 11.2 %all-to-all-start = ((bf16[8,96,256]{2,1,0:T(8,128)(2,1)}), bf16[8,96,256]{2,1,0:T(8,128)(2,1)S(1)}, u32[]{:S(2)}, u32[]{:S(2)}) async-start(bf16[8,96,256]{2,1,0:T(8,128)(2,1)} %pad_maximum_fusion.3), calls=%async_computation | async-start | bytes 786432 | tf_op jit(solution)/shard_map/all_to_all | solution.py:152
  110.9 41.4 %all-to-all-start.3 = ((bf16[8,42,384]{2,1,0:T(8,128)(2,1)}), bf16[8,42,384]{2,1,0:T(8,128)(2,1)S(1)}, u32[]{:S(2)}, u32[]{:S(2)}) async-start(bf16[8,42,384]{2,1,0:T(8,128)(2,1)} %broadcast_in_dim.4), calls=%async_computation.3 | async-start | bytes 589824 | tf_op jit(solution)/shard_map/all_to_all | solution.py:152
  116.2 6.9 %collective-permute-start.7 = (bf16[2,1,32,384]{3,2,1,0:T(8,128)(2,1)S(1)}, bf16[2,1,32,384]{3,2,1,0:T(8,128)(2,1)S(1)}, u32[]{:S(2)}, u32[]{:S(2)}) collective-permute-start(bf16[2,1,32,384]{3,2,1,0:T(8,128)(2,1)S(1)} %get-tuple-element.56), channel_id=1, source_target_pairs={{0,4},{4,8},{8,12},{12,16},{16,20},{20,24},{24,28},{28,32},{32,36}... | collective-permute-start | bytes 147464 | tf_op jit(solution)/shard_map/ppermute | solution.py:21
  121.2 7.0 %collective-permute-start.8 = (bf16[2,1,32,384]{3,2,1,0:T(8,128)(2,1)S(1)}, bf16[2,1,32,384]{3,2,1,0:T(8,128)(2,1)S(1)}, u32[]{:S(2)}, u32[]{:S(2)}) collective-permute-start(bf16[2,1,32,384]{3,2,1,0:T(8,128)(2,1)S(1)} %get-tuple-element.57), channel_id=1, source_target_pairs={{4,0},{8,4},{12,8},{16,12},{20,16},{24,20},{28,24},{32,28},{36,32}... | collective-permute-start | bytes 147464 | tf_op jit(solution)/shard_map/ppermute | solution.py:21
  129.1 5.3 %collective-permute-start.10 = (bf16[2,6,1,384]{3,2,1,0:T(2,128)(2,1)S(1)}, bf16[2,6,1,384]{3,2,1,0:T(2,128)(2,1)S(1)}, u32[]{:S(2)}, u32[]{:S(2)}) collective-permute-start(bf16[2,6,1,384]{3,2,1,0:T(2,128)(2,1)S(1)} %get-tuple-element.55), channel_id=1, source_target_pairs={{1,0},{2,1},{3,2},{5,4},{6,5},{7,6},{9,8},{10,9},{11,10},{13,12},{... | collective-permute-start | bytes 27656 | tf_op jit(solution)/shard_map/ppermute | solution.py:21
  131.0 4.5 %collective-permute-start.9 = (bf16[2,6,1,384]{3,2,1,0:T(2,128)(2,1)S(1)}, bf16[2,6,1,384]{3,2,1,0:T(2,128)(2,1)S(1)}, u32[]{:S(2)}, u32[]{:S(2)}) collective-permute-start(bf16[2,6,1,384]{3,2,1,0:T(2,128)(2,1)S(1)} %get-tuple-element.54), channel_id=1, source_target_pairs={{0,1},{1,2},{2,3},{4,5},{5,6},{6,7},{8,9},{9,10},{10,11},{12,13},{... | collective-permute-start | bytes 27656 | tf_op jit(solution)/shard_map/ppermute | solution.py:21
  143.9 19.5 %collective-permute-start.11 = (bf16[2,128,384]{2,1,0:T(8,128)(2,1)}, bf16[2,128,384]{2,1,0:T(8,128)(2,1)S(1)}, u32[]{:S(2)}, u32[]{:S(2)}) collective-permute-start(bf16[2,128,384]{2,1,0:T(8,128)(2,1)} %shard_map.84), channel_id=1, source_target_pairs={{64,0},{128,64},{192,128},{65,1},{129,65},{193,129},{66,2},{130,66... | collective-permute-start | bytes 589832 | tf_op jit(solution)/shard_map/ppermute | solution.py:21
  152.4 18.4 %collective-permute-start.15 = (bf16[14,24,384]{2,1,0:T(8,128)(2,1)S(1)}, bf16[14,24,384]{2,1,0:T(8,128)(2,1)S(1)}, u32[]{:S(2)}, u32[]{:S(2)}) collective-permute-start(bf16[14,24,384]{2,1,0:T(8,128)(2,1)S(1)} %reshape.154), channel_id=1, source_target_pairs={{0,64},{64,0},{1,65},{65,1},{2,66},{66,2},{3,67},{67,3},{4,68},{68... | collective-permute-start | bytes 774152 | tf_op jit(solution)/shard_map/ppermute | solution.py:25
  163.4 0.7 copy-start.2

commit v9 on v8

--- a/solution.py
+++ b/solution.py
@@ -164,10 +164,10 @@
     frame_count, row_count, col_count, channels = frames.shape
     core = lax.axis_index("co")
     is_first = lax.axis_index(TM) == 0
-    row = lax.broadcasted_iota(jnp.int32, (channels, channels), 0)
-    col = lax.broadcasted_iota(jnp.int32, (channels, channels), 1)
+    row = lax.broadcasted_iota(jnp.int32, (2 * channels, channels), 0) % channels
+    col = lax.broadcasted_iota(jnp.int32, (2 * channels, channels), 1)
     order = (row // 24 % 4 * 96 + row // 96 * 24 + row % 24 == col).astype(BF)
-    order, frames = lax.optimization_barrier((order, frames))
+    order, conv_bias = lax.optimization_barrier((order, conv_bias))
     weights = kernel.transpose(1, 2, 3, 0, 4)
     earlier = shifted(frames, TM, 1)
     earlier = jnp.where(is_first, cache_in, earlier)
@@ -182,13 +182,10 @@
     near = [exchanged(rows, "y", flip) for flip in (1, 3)]
     pre_act = jnp.zeros((frame_count * row_count * col_count, channels), F32) + conv_bias
     for tap_t in range(3):
-        if tap_t == 2:
-            pre_act, *near = lax.optimization_barrier((pre_act, *near))
-            far = [
-                exchanged(near[0][:, :, :16], "y", 3),
-                exchanged(near[1][:, :, 16:], "y", 1),
-            ]
         for tap_h in range(3):
+            if tap_t == 2 and tap_h == 2:
+                pre_act, *near = lax.optimization_barrier((pre_act, *near))
+                far = [exchanged(near[0][:, :, :16], "y", 3), exchanged(near[1][:, :, 16:], "y", 1)]
             for tap_w in range(3):
                 block = tap_block(extended, tap_t, tap_h, tap_w, frame_count, row_count, col_count)
                 pre_act = pre_act + lax.dot_general(
@@ -203,8 +200,7 @@
         cotangent.reshape(-1, channels).astype(F32) * sigma * (1.0 + pre_act * (1.0 - sigma))
     ).astype(BF)
     own = lax.dot_general(order, scaled, (((1,), (1,)), ((), ())), preferred_element_type=F32)
-    own, *far = lax.optimization_barrier((own.astype(BF).reshape(4, 96, -1), *far))
-    both = across(jnp.concatenate([own, own]), ("co", "y"))
+    both = across(own.astype(BF).reshape(8, 96, -1), ("co", "y"))
     line = [rows, *near, jnp.concatenate(far, 2)]
     line_peer = jnp.stack([jnp.where(core == 0, v[1:3], v[0:2]) for v in line])
     line_peer = exchanged(line_peer, "co", 1)

time: 173 us -> 173 us (level)
  the two profiles are of different devices: /device:TPU:57 before, /device:TPU:35 now
where the time goes in v9:
time: 173 us; the launch traced here: 172 us
  starting transfers between devices  50.6 us (29%)
  waiting for transfers between devices  40 us (23%)
  blocking collectives  37.8 us (22%)
  Pallas kernels  20.3 us (12%)
  matrix products  9.79 us (6%)
  other arithmetic  8.44 us (5%)
  local copies, waits for them, and re-layouts  3.9 us (2%)
    all_to_all x2, blocking collectives, across(): return lax.all_to_all(value, axes, 0, 0, tiled=True)  37.8 us
    ppermute x6, starting transfers between devices, shifted(): return lax.ppermute(value, axis, pairs)  27.6 us
    ppermute x6, waiting for transfers between devices, shifted(): return lax.ppermute(value, axis, pairs)  18.9 us
    pallas_call x2, Pallas kernels, input_grad(): pl.pallas_call(functools.partial(input_grad_kernel, one_frame, one_slot),...  13.3 us
    dot_general x27, matrix products, program(): lax.dot_general(block, weights[tap_t, tap_h, tap_w], (((1,), (1,)), ((),...  8.66 us
    all_to_all x2, starting transfers between devices, across(): return lax.all_to_all(value, axes, 0, 0, tiled=True)  8.4 us
    all_to_all x2, waiting for transfers between devices, across(): return lax.all_to_all(value, axes, 0, 0, tiled=True)  7.86 us
    ppermute x2, starting transfers between devices, with_halo(): after = lax.ppermute(initial, axis, down)  7.25 us
  transfers between devices with their start and end apart: 18, of which 10 were waited for; matrix products, arithmetic and copies ran while one was open for 9% of the time, Pallas kernels for 8%

profile of v9, /device:TPU:35, one launch (start us, length us, event | category | flops | bytes accessed | tf_op | source)
XLA Modules:
  0.0 172.0 jit_solution(12329161399472716304)
XLA Ops:
  0.6 8.6 %collective-permute-start = (bf16[2,4,32,384]{3,2,1,0:T(8,128)(2,1)}, bf16[2,4,32,384]{3,2,1,0:T(8,128)(2,1)S(1)}, u32[]{:S(2)}, u32[]{:S(2)}) collective-permute-start(bf16[2,4,32,384]{3,2,1,0:T(8,128)(2,1)} %param.5), channel_id=1, source_target_pairs={{0,64},{64,128},{128,192},{1,65},{65,129},{129,193},{2,66},{66,130... | collective-permute-start | bytes 589832 | tf_op jit(solution)/shard_map/ppermute | solution.py:21
  9.3 2.5 %fusion.15 = bf16[768,384]{1,0:T(8,128)(2,1)} fusion(s32[768]{0:T(1024)S(1)} %get-tuple-element.64, s32[768]{0:T(1024)S(1)} %get-tuple-element.65, pred[768]{0:T(1024)(128)(4,1)S(1)} %fusion.31), kind=kLoop, calls=%fused_computation.50 | loop fusion | flops 10616832 | bytes 596736 | tf_op jit(solution)/shard_map/convert_element_type | solution.py:169
  11.8 2.5 %collective-permute-done = bf16[2,4,32,384]{3,2,1,0:T(8,128)(2,1)S(1)} collective-permute-done((bf16[2,4,32,384]{3,2,1,0:T(8,128)(2,1)}, bf16[2,4,32,384]{3,2,1,0:T(8,128)(2,1)S(1)}, u32[]{:S(2)}, u32[]{:S(2)}) %collective-permute-start) | collective-permute-done | bytes 196640 | tf_op jit(solution)/shard_map/ppermute | solution.py:21
  14.3 0.9 pad_maximum_fusion.6
  15.2 4.6 %collective-permute-start.2 = (bf16[4,1,32,384]{3,2,1,0:T(8,128)(2,1)S(1)}, bf16[4,1,32,384]{3,2,1,0:T(8,128)(2,1)S(1)}, u32[]{:S(2)}, u32[]{:S(2)}) collective-permute-start(bf16[4,1,32,384]{3,2,1,0:T(8,128)(2,1)S(1)} %get-tuple-element.47), channel_id=1, source_target_pairs={{4,0},{8,4},{12,8},{16,12},{20,16},{24,20},{28,24},{32,28},{36,32}... | collective-permute-start | bytes 294920 | tf_op jit(solution)/shard_map/ppermute | solution.py:36
  19.8 1.9 %collective-permute-start.1 = (bf16[4,1,32,384]{3,2,1,0:T(8,128)(2,1)S(1)}, bf16[4,1,32,384]{3,2,1,0:T(8,128)(2,1)S(1)}, u32[]{:S(2)}, u32[]{:S(2)}) collective-permute-start(bf16[4,1,32,384]{3,2,1,0:T(8,128)(2,1)S(1)} %get-tuple-element.46), channel_id=1, source_target_pairs={{0,4},{4,8},{8,12},{12,16},{16,20},{20,24},{24,28},{28,32},{32,36}... | collective-permute-start | bytes 294920 | tf_op jit(solution)/shard_map/ppermute | solution.py:35
  21.8 5.5 %collective-permute-done.1 = bf16[4,1,32,384]{3,2,1,0:T(8,128)(2,1)S(1)} collective-permute-done((bf16[4,1,32,384]{3,2,1,0:T(8,128)(2,1)S(1)}, bf16[4,1,32,384]{3,2,1,0:T(8,128)(2,1)S(1)}, u32[]{:S(2)}, u32[]{:S(2)}) %collective-permute-start.1) | collective-permute-done | bytes 98336 | tf_op jit(solution)/shard_map/ppermute | solution.py:35
  27.3 2.6 %collective-permute-start.3 = (bf16[4,6,1,384]{3,2,1,0:T(2,128)(2,1)S(1)}, bf16[4,6,1,384]{3,2,1,0:T(2,128)(2,1)S(1)}, u32[]{:S(2)}, u32[]{:S(2)}) collective-permute-start(bf16[4,6,1,384]{3,2,1,0:T(2,128)(2,1)S(1)} %get-tuple-element.34), channel_id=1, source_target_pairs={{0,1},{1,2},{2,3},{4,5},{5,6},{6,7},{8,9},{9,10},{10,11},{12,13},{... | collective-permute-start | bytes 55304 | tf_op jit(solution)/shard_map/ppermute | solution.py:35
  30.0 2.6 %collective-permute-start.4 = (bf16[4,6,1,384]{3,2,1,0:T(2,128)(2,1)S(1)}, bf16[4,6,1,384]{3,2,1,0:T(2,128)(2,1)S(1)}, u32[]{:S(2)}, u32[]{:S(2)}) collective-permute-start(bf16[4,6,1,384]{3,2,1,0:T(2,128)(2,1)S(1)} %get-tuple-element.35), channel_id=1, source_target_pairs={{1,0},{2,1},{3,2},{5,4},{6,5},{7,6},{9,8},{10,9},{11,10},{13,12},{... | collective-permute-start | bytes 55304 | tf_op jit(solution)/shard_map/ppermute | solution.py:36
  32.9 2.1 %collective-permute-done.4 = bf16[4,6,1,384]{3,2,1,0:T(2,128)(2,1)S(1)} collective-permute-done((bf16[4,6,1,384]{3,2,1,0:T(2,128)(2,1)S(1)}, bf16[4,6,1,384]{3,2,1,0:T(2,128)(2,1)S(1)}, u32[]{:S(2)}, u32[]{:S(2)}) %collective-permute-start.4) | collective-permute-done | bytes 18464 | tf_op jit(solution)/shard_map/ppermute | solution.py:36
  35.0 0.5 fusion.17
  35.9 0.4 maximum_maximum_fusion
  36.3 0.5 fusion.32
  36.8 1.1 slice-done.1
  38.2 0.3 convolution_add_fusion.22
  38.5 0.3 convolution_add_fusion.21
  38.8 0.3 convolution_add_fusion.20
  39.1 0.3 convolution_add_fusion.19
  39.7 0.3 convolution_add_fusion.17
  40.0 0.3 convolution_add_fusion.16
  40.3 0.3 convolution_add_fusion.15
  40.6 0.3 convolution_add_fusion.14
  40.9 0.3 convolution_add_fusion.13
  41.2 0.3 convolution_add_fusion.12
  41.5 0.3 convolution_add_fusion.11
  41.8 0.3 convolution_add_fusion.10
  42.1 0.3 convolution_add_fusion.9
  42.4 0.3 convolution_add_fusion.8
  42.7 0.3 convolution_add_fusion.7
  43.0 0.3 convolution_add_fusion.6
  43.3 0.3 convolution_add_fusion.5
  43.6 0.3 convolution_add_fusion.4
  43.9 0.3 convolution_add_fusion.3
  44.2 0.3 convolution_add_fusion.2
  44.8 0.3 convolution_add_fusion
  45.1 0.4 collective-permute-done.6.refs_2_
  45.7 2.4 %collective-permute-start.12 = (bf16[3,5,16,384]{3,2,1,0:T(8,128)(2,1)S(1)}, bf16[3,5,16,384]{3,2,1,0:T(8,128)(2,1)S(1)}, u32[]{:S(2)}, u32[]{:S(2)}) collective-permute-start(bf16[3,5,16,384]{3,2,1,0:T(8,128)(2,1)S(1)} %slice.300), channel_id=1, source_target_pairs={{0,12},{4,8},{8,4},{12,0},{1,13},{5,9},{9,5},{13,1},{2,14},{6,10},... | collective-permute-start | bytes 552968 | tf_op jit(solution)/shard_map/ppermute | solution.py:25
  48.2 3.1 %collective-permute-done.12 = bf16[3,5,16,384]{3,2,1,0:T(8,128)(2,1)S(1)} collective-permute-done((bf16[3,5,16,384]{3,2,1,0:T(8,128)(2,1)S(1)}, bf16[3,5,16,384]{3,2,1,0:T(8,128)(2,1)S(1)}, u32[]{:S(2)}, u32[]{:S(2)}) %collective-permute-start.12) | collective-permute-done | bytes 184352 | tf_op jit(solution)/shard_map/ppermute | solution.py:25
  51.4 2.0 %collective-permute-done.13 = bf16[3,5,24,384]{3,2,1,0:T(8,128)(2,1)S(1)} collective-permute-done((bf16[3,5,24,384]{3,2,1,0:T(8,128)(2,1)S(1)}, bf16[3,5,24,384]{3,2,1,0:T(8,128)(2,1)S(1)}, u32[]{:S(2)}, u32[]{:S(2)}) %collective-permute-start.13) | collective-permute-done | bytes 276512 | tf_op jit(solution)/shard_map/ppermute | solution.py:25
  53.5 1.3 pad_maximum_fusion
  54.8 0.3 fusion.25
  55.4 0.3 copy-done.6
  55.7 1.1 fusion.22
  56.8 1.1 convolution_convert_fusion
  58.0 3.6 %all-to-all-start = ((bf16[8,96,256]{2,1,0:T(8,128)(2,1)}), bf16[8,96,256]{2,1,0:T(8,128)(2,1)S(1)}, u32[]{:S(2)}, u32[]{:S(2)}) async-start(bf16[8,96,256]{2,1,0:T(8,128)(2,1)} %bitcast.201), calls=%async_computation | async-start | bytes 786432 | tf_op jit(solution)/shard_map/all_to_all | solution.py:152
  61.6 7.9 %all-to-all-done.scaled_ref = bf16[8,96,256]{2,1,0:T(8,128)(2,1)S(1)} async-done(((bf16[8,96,256]{2,1,0:T(8,128)(2,1)}), bf16[8,96,256]{2,1,0:T(8,128)(2,1)S(1)}, u32[]{:S(2)}, u32[]{:S(2)}) %all-to-all-start) | async-done | bytes 393248 | tf_op jit(solution)/shard_map/all_to_all | solution.py:152
  69.5 7.0 %shard_map.86 = bf16[4,14,24,384]{3,2,1,0:T(8,128)(2,1)S(1)} custom-call(s32[2]{0:T(128)S(1)} %pad_add_fusion.where_ref, bf16[8,96,256]{2,1,0:T(8,128)(2,1)S(1)} %all-to-all-done.scaled_ref, bf16[3,5,40,384]{3,2,1,0:T(8,128)(2,1)S(1)} %pad.4.refs_0_, bf16[3,5,40,384]{3,2,1,0:T(8,128)(2,1)S(1)} %collective-permute-done.5.refs_1_, ...), custom_call_target="tpu_custom_call" | custom-call | flops 2113929216 | bytes 9437184 | tf_op jit(solution)/shard_map/pallas_call | solution.py:82
  76.6 17.0 %all_to_all.20 = bf16[4,14,24,384]{3,2,1,0:T(8,128)(2,1)S(1)} all-to-all(bf16[4,14,24,384]{3,2,1,0:T(8,128)(2,1)S(1)} %shard_map.86), channel_id=1, replica_groups=mesh['zh'=2,'co'=2,'x'=4,'y'=4,'z'=4] {'x'}, dimensions={0} | all-to-all | bytes 2064384 | tf_op jit(solution)/shard_map/all_to_all | solution.py:152
  93.9 20.8 %all_to_all.21 = bf16[8,42,384]{2,1,0:T(8,128)(2,1)S(1)} all-to-all(bf16[8,42,384]{2,1,0:T(8,128)(2,1)S(1)} %reshape.153), channel_id=1, replica_groups=mesh['zh'=2,'co'=2,'x'=4,'y'=4,'z'=4] {'zh','z'}, dimensions={0} | all-to-all | bytes 516096 | tf_op jit(solution)/shard_map/all_to_all | solution.py:152
  114.7 0.7 broadcast_in_dim.4
  115.5 4.8 %all-to-all-start.3 = ((bf16[8,42,384]{2,1,0:T(8,128)(2,1)}), bf16[8,42,384]{2,1,0:T(8,128)(2,1)S(1)}, u32[]{:S(2)}, u32[]{:S(2)}) async-start(bf16[8,42,384]{2,1,0:T(8,128)(2,1)} %broadcast_in_dim.4), calls=%async_computation.3 | async-start | bytes 589824 | tf_op jit(solution)/shard_map/all_to_all | solution.py:152
  120.3 2.4 %collective-permute-start.8 = (bf16[2,1,32,384]{3,2,1,0:T(8,128)(2,1)S(1)}, bf16[2,1,32,384]{3,2,1,0:T(8,128)(2,1)S(1)}, u32[]{:S(2)}, u32[]{:S(2)}) collective-permute-start(bf16[2,1,32,384]{3,2,1,0:T(8,128)(2,1)S(1)} %get-tuple-element.51), channel_id=1, source_target_pairs={{4,0},{8,4},{12,8},{16,12},{20,16},{24,20},{28,24},{32,28},{36,32}... | collective-permute-start | bytes 147464 | tf_op jit(solution)/shard_map/ppermute | solution.py:21
  122.7 2.9 %collective-permute-start.7 = (bf16[2,1,32,384]{3,2,1,0:T(8,128)(2,1)S(1)}, bf16[2,1,32,384]{3,2,1,0:T(8,128)(2,1)S(1)}, u32[]{:S(2)}, u32[]{:S(2)}) collective-permute-start(bf16[2,1,32,384]{3,2,1,0:T(8,128)(2,1)S(1)} %get-tuple-element.50), channel_id=1, source_target_pairs={{0,4},{4,8},{8,12},{12,16},{16,20},{20,24},{24,28},{28,32},{32,36}... | collective-permute-start | bytes 147464 | tf_op jit(solution)/shard_map/ppermute | solution.py:21
  125.6 4.0 %collective-permute-done.7 = bf16[2,1,32,384]{3,2,1,0:T(8,128)(2,1)S(1)} collective-permute-done((bf16[2,1,32,384]{3,2,1,0:T(8,128)(2,1)S(1)}, bf16[2,1,32,384]{3,2,1,0:T(8,128)(2,1)S(1)}, u32[]{:S(2)}, u32[]{:S(2)}) %collective-permute-start.7) | collective-permute-done | bytes 49184 | tf_op jit(solution)/shard_map/ppermute | solution.py:21
  129.7 2.3 %collective-permute-start.10 = (bf16[2,6,1,384]{3,2,1,0:T(2,128)(2,1)S(1)}, bf16[2,6,1,384]{3,2,1,0:T(2,128)(2,1)S(1)}, u32[]{:S(2)}, u32[]{:S(2)}) collective-permute-start(bf16[2,6,1,384]{3,2,1,0:T(2,128)(2,1)S(1)} %get-tuple-element.49), channel_id=1, source_target_pairs={{1,0},{2,1},{3,2},{5,4},{6,5},{7,6},{9,8},{10,9},{11,10},{13,12},{... | collective-permute-start | bytes 27656 | tf_op jit(solution)/shard_map/ppermute | solution.py:21
  132.0 3.0 %collective-permute-start.9 = (bf16[2,6,1,384]{3,2,1,0:T(2,128)(2,1)S(1)}, bf16[2,6,1,384]{3,2,1,0:T(2,128)(2,1)S(1)}, u32[]{:S(2)}, u32[]{:S(2)}) collective-permute-start(bf16[2,6,1,384]{3,2,1,0:T(2,128)(2,1)S(1)} %get-tuple-element.48), channel_id=1, source_target_pairs={{0,1},{1,2},{2,3},{4,5},{5,6},{6,7},{8,9},{9,10},{10,11},{12,13},{... | collective-permute-start | bytes 27656 | tf_op jit(solution)/shard_map/ppermute | solution.py:21
  135.0 1.5 collective-permute-done.9
  136.5 0.9 pad_maximum_fusion.3.rim_ref
  137.4 6.6 %shard_map.84 = bf16[2,128,384]{2,1,0:T(8,128)(2,1)} custom-call(bf16[2,6,34,384]{3,2,1,0:T(8,128)(2,1)} %pad_maximum_fusion.3.rim_ref, bf16[3,3,3,384,384]{4,3,2,1,0:T(8,128)(2,1)} %bitcast.164), custom_call_target="tpu_custom_call" | custom-call | flops 1019215872 | bytes 6291456 | tf_op jit(solution)/shard_map/pallas_call | solution.py:132
  144.0 8.4 %collective-permute-start.11 = (bf16[2,128,384]{2,1,0:T(8,128)(2,1)}, bf16[2,128,384]{2,1,0:T(8,128)(2,1)S(1)}, u32[]{:S(2)}, u32[]{:S(2)}) collective-permute-start(bf16[2,128,384]{2,1,0:T(8,128)(2,1)} %shard_map.84), channel_id=1, source_target_pairs={{64,0},{128,64},{192,128},{65,1},{129,65},{193,129},{66,2},{130,66... | collective-permute-start | bytes 589832 | tf_op jit(solution)/shard_map/ppermute | solution.py:21
  152.6 10.9 %collective-permute-done.11.refs_0_ = bf16[2,128,384]{2,1,0:T(8,128)(2,1)S(1)} collective-permute-done((bf16[2,128,384]{2,1,0:T(8,128)(2,1)}, bf16[2,128,384]{2,1,0:T(8,128)(2,1)S(1)}, u32[]{:S(2)}, u32[]{:S(2)}) %collective-permute-start.11) | collective-permute-done | bytes 196640 | tf_op jit(solution)/shard_map/ppermute | solution.py:21
  163.5 0.7 copy-done.4
  164.1 6.7 %shard_map.85 = bf16[2,128,384]{2,1,0:T(8,128)(2,1)} custom-call(bf16[2,6,34,384]{3,2,1,0:T(8,128)(2,1)} %pad_maximum_fusion.3.rim_ref, bf16[2,128,384]{2,1,0:T(8,128)(2,1)} %copy-done.4, bf16[3,3,3,384,384]{4,3,2,1,0:T(8,128)(2,1)} %bitcast.165), custom_call_target="tpu_custom_call" | custom-call | flops 1019215872 | bytes 6291456 | tf_op jit(solution)/shard_map/pallas_call | solution.py:132
  171.0 1.0 convert_bitcast_fusion
  (59 shorter events, 3.1 us)
Async XLA Ops:
  0.6 21.1 %copy-start = (bf16[2,4,32,384]{3,2,1,0:T(8,128)(2,1)S(1)}, bf16[2,4,32,384]{3,2,1,0:T(8,128)(2,1)}, u32[]{:S(2)}) copy-start(bf16[2,4,32,384]{3,2,1,0:T(8,128)(2,1)} %param.5) | copy-start | bytes 589828
  0.6 13.6 %collective-permute-start = (bf16[2,4,32,384]{3,2,1,0:T(8,128)(2,1)}, bf16[2,4,32,384]{3,2,1,0:T(8,128)(2,1)S(1)}, u32[]{:S(2)}, u32[]{:S(2)}) collective-permute-start(bf16[2,4,32,384]{3,2,1,0:T(8,128)(2,1)} %param.5), channel_id=1, source_target_pairs={{0,64},{64,128},{128,192},{1,65},{65,129},{129,193},{2,66},{66,130... | collective-permute-start | bytes 589832 | tf_op jit(solution)/shard_map/ppermute | solution.py:21
  15.2 6.6 %collective-permute-start.2 = (bf16[4,1,32,384]{3,2,1,0:T(8,128)(2,1)S(1)}, bf16[4,1,32,384]{3,2,1,0:T(8,128)(2,1)S(1)}, u32[]{:S(2)}, u32[]{:S(2)}) collective-permute-start(bf16[4,1,32,384]{3,2,1,0:T(8,128)(2,1)S(1)} %get-tuple-element.47), channel_id=1, source_target_pairs={{4,0},{8,4},{12,8},{16,12},{20,16},{24,20},{28,24},{32,28},{36,32}... | collective-permute-start | bytes 294920 | tf_op jit(solution)/shard_map/ppermute | solution.py:36
  19.8 7.5 %collective-permute-start.1 = (bf16[4,1,32,384]{3,2,1,0:T(8,128)(2,1)S(1)}, bf16[4,1,32,384]{3,2,1,0:T(8,128)(2,1)S(1)}, u32[]{:S(2)}, u32[]{:S(2)}) collective-permute-start(bf16[4,1,32,384]{3,2,1,0:T(8,128)(2,1)S(1)} %get-tuple-element.46), channel_id=1, source_target_pairs={{0,4},{4,8},{8,12},{12,16},{16,20},{20,24},{24,28},{28,32},{32,36}... | collective-permute-start | bytes 294920 | tf_op jit(solution)/shard_map/ppermute | solution.py:35
  27.3 5.6 %collective-permute-start.3 = (bf16[4,6,1,384]{3,2,1,0:T(2,128)(2,1)S(1)}, bf16[4,6,1,384]{3,2,1,0:T(2,128)(2,1)S(1)}, u32[]{:S(2)}, u32[]{:S(2)}) collective-permute-start(bf16[4,6,1,384]{3,2,1,0:T(2,128)(2,1)S(1)} %get-tuple-element.34), channel_id=1, source_target_pairs={{0,1},{1,2},{2,3},{4,5},{5,6},{6,7},{8,9},{9,10},{10,11},{12,13},{... | collective-permute-start | bytes 55304 | tf_op jit(solution)/shard_map/ppermute | solution.py:35
  30.0 5.0 %collective-permute-start.4 = (bf16[4,6,1,384]{3,2,1,0:T(2,128)(2,1)S(1)}, bf16[4,6,1,384]{3,2,1,0:T(2,128)(2,1)S(1)}, u32[]{:S(2)}, u32[]{:S(2)}) collective-permute-start(bf16[4,6,1,384]{3,2,1,0:T(2,128)(2,1)S(1)} %get-tuple-element.35), channel_id=1, source_target_pairs={{1,0},{2,1},{3,2},{5,4},{6,5},{7,6},{9,8},{10,9},{11,10},{13,12},{... | collective-permute-start | bytes 55304 | tf_op jit(solution)/shard_map/ppermute | solution.py:36
  32.7 4.1 %slice-start = ((s8[7962624]{0:T(1024)(128)(4,1)}), s8[4194304]{0:T(1024)(128)(4,1)S(1)}, s32[]{:S(2)}) async-start(s8[7962624]{0:T(1024)(128)(4,1)} %bitcast.166), calls=%async_computation.4 | async-start | bytes 8388608
  35.6 9.5 %collective-permute-start.5 = (bf16[3,5,40,384]{3,2,1,0:T(8,128)(2,1)S(1)}, bf16[3,5,40,384]{3,2,1,0:T(8,128)(2,1)S(1)}, u32[]{:S(2)}, u32[]{:S(2)}) collective-permute-start(bf16[3,5,40,384]{3,2,1,0:T(8,128)(2,1)S(1)} %pad.4.refs_0_), channel_id=1, source_target_pairs={{0,4},{4,0},{8,12},{12,8},{1,5},{5,1},{9,13},{13,9},{2,6},{6,2},{1... | collective-permute-start | bytes 1382408 | tf_op jit(solution)/shard_map/ppermute | solution.py:25
  35.7 9.9 %collective-permute-start.6 = (bf16[3,5,40,384]{3,2,1,0:T(8,128)(2,1)S(1)}, bf16[3,5,40,384]{3,2,1,0:T(8,128)(2,1)S(1)}, u32[]{:S(2)}, u32[]{:S(2)}) collective-permute-start(bf16[3,5,40,384]{3,2,1,0:T(8,128)(2,1)S(1)} %pad.4.refs_0_), channel_id=1, source_target_pairs={{0,12},{4,8},{8,4},{12,0},{1,13},{5,9},{9,5},{13,1},{2,14},{6,10},... | collective-permute-start | bytes 1382408 | tf_op jit(solution)/shard_map/ppermute | solution.py:25
  35.9 2.1 %slice-start.1 = ((s8[7962624]{0:T(1024)(128)(4,1)}), s8[3768320]{0:T(1024)(128)(4,1)S(1)}, s32[]{:S(2)}) async-start(s8[7962624]{0:T(1024)(128)(4,1)} %bitcast.166), calls=%async_computation.5 | async-start | bytes 7536640
  36.3 1.9 %copy-start.5 = (f32[384]{0:T(512)S(1)}, f32[384]{0:T(512)}, u32[]{:S(2)}) copy-start(f32[384]{0:T(512)} %param.8) | copy-start | bytes 4612
  45.7 5.7 %collective-permute-start.12 = (bf16[3,5,16,384]{3,2,1,0:T(8,128)(2,1)S(1)}, bf16[3,5,16,384]{3,2,1,0:T(8,128)(2,1)S(1)}, u32[]{:S(2)}, u32[]{:S(2)}) collective-permute-start(bf16[3,5,16,384]{3,2,1,0:T(8,128)(2,1)S(1)} %slice.300), channel_id=1, source_target_pairs={{0,12},{4,8},{8,4},{12,0},{1,13},{5,9},{9,5},{13,1},{2,14},{6,10},... | collective-permute-start | bytes 552968 | tf_op jit(solution)/shard_map/ppermute | solution.py:25
  48.0 5.4 %collective-permute-start.13 = (bf16[3,5,24,384]{3,2,1,0:T(8,128)(2,1)S(1)}, bf16[3,5,24,384]{3,2,1,0:T(8,128)(2,1)S(1)}, u32[]{:S(2)}, u32[]{:S(2)}) collective-permute-start(bf16[3,5,24,384]{3,2,1,0:T(8,128)(2,1)S(1)} %slice.301), channel_id=1, source_target_pairs={{0,4},{4,0},{8,12},{12,8},{1,5},{5,1},{9,13},{13,9},{2,6},{6,2},{1... | collective-permute-start | bytes 829448 | tf_op jit(solution)/shard_map/ppermute | solution.py:25
  54.8 0.9 copy-start.6
  54.8 14.7 %collective-permute-start.14 = (bf16[4,2,5,40,384]{4,3,2,1,0:T(8,128)(2,1)}, bf16[4,2,5,40,384]{4,3,2,1,0:T(8,128)(2,1)S(1)}, u32[]{:S(2)}, u32[]{:S(2)}) collective-permute-start(bf16[4,2,5,40,384]{4,3,2,1,0:T(8,128)(2,1)} %pad_maximum_fusion), channel_id=1, source_target_pairs={{0,64},{64,0},{1,65},{65,1},{2,66},{66,2},{3,67},{67,3},{4,68},{68... | collective-permute-start | bytes 3686408 | tf_op jit(solution)/shard_map/ppermute | solution.py:25
  55.7 1.1 copy-start.3
  56.8 1.1 copy-start.1
  58.0 11.5 %all-to-all-start = ((bf16[8,96,256]{2,1,0:T(8,128)(2,1)}), bf16[8,96,256]{2,1,0:T(8,128)(2,1)S(1)}, u32[]{:S(2)}, u32[]{:S(2)}) async-start(bf16[8,96,256]{2,1,0:T(8,128)(2,1)} %bitcast.201), calls=%async_computation | async-start | bytes 786432 | tf_op jit(solution)/shard_map/all_to_all | solution.py:152
  93.8 26.5 %copy-start.2 = (bf16[256,384]{1,0:T(8,128)(2,1)S(1)}, bf16[256,384]{1,0:T(8,128)(2,1)}, u32[]{:S(2)}) copy-start(bf16[256,384]{1,0:T(8,128)(2,1)} %copy-done.1) | copy-start | bytes 589828
  115.5 36.9 %all-to-all-start.3 = ((bf16[8,42,384]{2,1,0:T(8,128)(2,1)}), bf16[8,42,384]{2,1,0:T(8,128)(2,1)S(1)}, u32[]{:S(2)}, u32[]{:S(2)}) async-start(bf16[8,42,384]{2,1,0:T(8,128)(2,1)} %broadcast_in_dim.4), calls=%async_computation.3 | async-start | bytes 589824 | tf_op jit(solution)/shard_map/all_to_all | solution.py:152
  120.3 5.3 %collective-permute-start.8 = (bf16[2,1,32,384]{3,2,1,0:T(8,128)(2,1)S(1)}, bf16[2,1,32,384]{3,2,1,0:T(8,128)(2,1)S(1)}, u32[]{:S(2)}, u32[]{:S(2)}) collective-permute-start(bf16[2,1,32,384]{3,2,1,0:T(8,128)(2,1)S(1)} %get-tuple-element.51), channel_id=1, source_target_pairs={{4,0},{8,4},{12,8},{16,12},{20,16},{24,20},{28,24},{32,28},{36,32}... | collective-permute-start | bytes 147464 | tf_op jit(solution)/shard_map/ppermute | solution.py:21
  122.7 6.9 %collective-permute-start.7 = (bf16[2,1,32,384]{3,2,1,0:T(8,128)(2,1)S(1)}, bf16[2,1,32,384]{3,2,1,0:T(8,128)(2,1)S(1)}, u32[]{:S(2)}, u32[]{:S(2)}) collective-permute-start(bf16[2,1,32,384]{3,2,1,0:T(8,128)(2,1)S(1)} %get-tuple-element.50), channel_id=1, source_target_pairs={{0,4},{4,8},{8,12},{12,16},{16,20},{20,24},{24,28},{28,32},{32,36}... | collective-permute-start | bytes 147464 | tf_op jit(solution)/shard_map/ppermute | solution.py:21
  129.7 5.3 %collective-permute-start.10 = (bf16[2,6,1,384]{3,2,1,0:T(2,128)(2,1)S(1)}, bf16[2,6,1,384]{3,2,1,0:T(2,128)(2,1)S(1)}, u32[]{:S(2)}, u32[]{:S(2)}) collective-permute-start(bf16[2,6,1,384]{3,2,1,0:T(2,128)(2,1)S(1)} %get-tuple-element.49), channel_id=1, source_target_pairs={{1,0},{2,1},{3,2},{5,4},{6,5},{7,6},{9,8},{10,9},{11,10},{13,12},{... | collective-permute-start | bytes 27656 | tf_op jit(solution)/shard_map/ppermute | solution.py:21
  132.0 4.5 %collective-permute-start.9 = (bf16[2,6,1,384]{3,2,1,0:T(2,128)(2,1)S(1)}, bf16[2,6,1,384]{3,2,1,0:T(2,128)(2,1)S(1)}, u32[]{:S(2)}, u32[]{:S(2)}) collective-permute-start(bf16[2,6,1,384]{3,2,1,0:T(2,128)(2,1)S(1)} %get-tuple-element.48), channel_id=1, source_target_pairs={{0,1},{1,2},{2,3},{4,5},{5,6},{6,7},{8,9},{9,10},{10,11},{12,13},{... | collective-permute-start | bytes 27656 | tf_op jit(solution)/shard_map/ppermute | solution.py:21
  144.0 19.5 %collective-permute-start.11 = (bf16[2,128,384]{2,1,0:T(8,128)(2,1)}, bf16[2,128,384]{2,1,0:T(8,128)(2,1)S(1)}, u32[]{:S(2)}, u32[]{:S(2)}) collective-permute-start(bf16[2,128,384]{2,1,0:T(8,128)(2,1)} %shard_map.84), channel_id=1, source_target_pairs={{64,0},{128,64},{192,128},{65,1},{129,65},{193,129},{66,2},{130,66... | collective-permute-start | bytes 589832 | tf_op jit(solution)/shard_map/ppermute | solution.py:21
  152.5 18.4 %collective-permute-start.15 = (bf16[14,24,384]{2,1,0:T(8,128)(2,1)S(1)}, bf16[14,24,384]{2,1,0:T(8,128)(2,1)S(1)}, u32[]{:S(2)}, u32[]{:S(2)}) collective-permute-start(bf16[14,24,384]{2,1,0:T(8,128)(2,1)S(1)} %reshape.154), channel_id=1, source_target_pairs={{0,64},{64,0},{1,65},{65,1},{2,66},{66,2},{3,67},{67,3},{4,68},{68... | collective-permute-start | bytes 774152 | tf_op jit(solution)/shard_map/ppermute | solution.py:25
  163.5 0.7 copy-start.4
